TPU v7x, 32 devices: a whole 2x2x4 slice. The times are simulated.
32 devices in a mesh: groups: 2 (over y), row: 8 (over z, x), col: 2 (over core).
Axes of the slice: x: 2, y: 2, z: 4, core: 2. Of those that a mesh axis runs over, the one named last changes fastest.
Arguments:
- object_slices: float32 [4, 2, 2048, 512], P(None, None, ('groups', 'row'), 'col'), parts along dimension 2, may hold values from -4 to 4
- probe: float32 [16, 2, 128, 128], P('groups'), parts along dimension 0, may hold values from -3 to 3
- taps: float32 [2, 63], replicated, may hold values from -0.5 to 0.5
- measured: float32 [64, 128, 128], P(('groups', 'row', 'col')), parts along dimension 0, may hold values from 0.5 to 16
- positions: int32 [64, 2], P(('groups', 'row', 'col')), parts along dimension 0, may hold values from -64 to 959, as said below
Outputs:
- object_grad: float32 [4, 2, 2048, 512], P(None, None, ('groups', 'row'), 'col'), parts along dimension 2
- new_probe: float32 [16, 2, 16384], P('groups', None, ('row', 'col')), parts along dimension 0
There are 2 independent parts, one for each index of `groups`. A program takes and returns all parts, laid end to end along the dimension named above; an argument that names none is the same for every part. Nothing has to cross between parts.
Inputs may be any that keep to these rules, and one draw needn't show every extreme that they name: `positions`: record r belongs to device d = r // 2 in row-major order over the (row, col) device grid, with tile indices (i, q); its row lies in [i * 128 - 128/2, (i + 1) * 128 - 128/2) and its column in [q * 256 - 128/2, (q + 1) * 256 - 128/2).
All inputs are finite; a program needn't handle non-finite values.
Results may differ from a plain program's by a relative error of at most 0.0003.
Values sent between devices are 32-bit elements; how exact they have to be, the bound alone decides.
No kernel may reach another device: no remote copies, remote signals or barrier semaphores. Data moves between devices by JAX's collectives and lax.ppermute only.
A program may use at most 64 MiB of HBM per device.

v0:
```python
import math

import jax
import jax.numpy as jnp
from jax import lax
from jax.sharding import PartitionSpec as P

highest_mode = lax.Precision.HIGHEST


def from_behind(value, axis, steps):
    count = lax.axis_size(axis)
    first, last = (max(0, -steps), min(count, count - steps))
    return lax.ppermute(value, axis, [(source, source + steps) for source in range(first, last)])


def with_halo(array, sides, width):
    for axis, dim in sides:
        devices, length = (lax.axis_size(axis), array.shape[dim])
        up = [(i, (i + 1) % devices) for i in range(devices - 1)]
        down = [(j, i) for i, j in up]
        last = lax.slice_in_dim(array, length - width, length, axis=dim)
        first = lax.slice_in_dim(array, 0, width, axis=dim)
        before = lax.ppermute(last, axis, up)
        after = lax.ppermute(first, axis, down)
        array = jnp.concatenate([before, array, after], axis=dim)
    return array


def einsum_exact(form, first, second):
    return jnp.einsum(form, first, second, precision=highest_mode)


def make_tables(taps, width):
    reach = taps.shape[1] // 2
    pixel_idx = lax.iota(jnp.int32, width)
    offset = pixel_idx[None, :] - pixel_idx[:, None] + reach
    tap_idx = lax.iota(jnp.int32, taps.shape[1])
    one_hot = (offset[:, :, None] == tap_idx[None, None, :]).astype(jnp.float32)
    band_re = einsum_exact("abt,t->ab", one_hot, taps[0])
    band_im = einsum_exact("abt,t->ab", one_hot, taps[1])
    phase_idx = pixel_idx[:, None] * pixel_idx[None, :] % width
    angle = 2.0 * math.pi / width * phase_idx.astype(jnp.float32)
    norm_factor = 1.0 / math.sqrt(width)
    return (band_re, band_im, jnp.cos(angle) * norm_factor, -jnp.sin(angle) * norm_factor)


def both_sides(mat_re, mat_im, wave_re, wave_im):
    left_re = einsum_exact("ab,kbc->kac", mat_re, wave_re) - einsum_exact(
        "ab,kbc->kac", mat_im, wave_im
    )
    left_im = einsum_exact("ab,kbc->kac", mat_re, wave_im) + einsum_exact(
        "ab,kbc->kac", mat_im, wave_re
    )
    out_re = einsum_exact("kac,dc->kad", left_re, mat_re) - einsum_exact(
        "kac,dc->kad", left_im, mat_im
    )
    out_im = einsum_exact("kac,dc->kad", left_re, mat_im) + einsum_exact(
        "kac,dc->kad", left_im, mat_re
    )
    return (out_re, out_im)


def record_loss(probe, patch, measured_one, tables):
    band_re, band_im, dft_re, dft_im = tables
    wave_re = probe[:, 0]
    wave_im = probe[:, 1]
    layers = patch.shape[0]
    for layer_idx in range(layers):
        obj_re = patch[layer_idx, 0]
        obj_im = patch[layer_idx, 1]
        wave_re, wave_im = (
            wave_re * obj_re - wave_im * obj_im,
            wave_re * obj_im + wave_im * obj_re,
        )
        if layer_idx + 1 < layers:
            wave_re, wave_im = both_sides(band_re, band_im, wave_re, wave_im)
    far_re, far_im = both_sides(dft_re, dft_im, wave_re, wave_im)
    intensity = jnp.sum(far_re * far_re + far_im * far_im, axis=0)
    weight = 1.0 / (8.0 * probe.shape[0])
    return 0.5 * weight * jnp.sum((intensity - measured_one) ** 2)


def accumulate(grid, probe, measured, places, tables, patch_width):
    sizes = (grid.shape[0], 2, patch_width, patch_width)

    def one_record(carry, item):
        grad_grid, grad_probe = carry
        place, measured_one = item
        zero_idx = jnp.zeros((), jnp.int32)
        starts = (zero_idx, zero_idx, place[0], place[1])
        patch = lax.dynamic_slice(grid, starts, sizes)
        grad_wave, grad_patch = jax.grad(record_loss, argnums=(0, 1))(
            probe, patch, measured_one, tables
        )
        current = lax.dynamic_slice(grad_grid, starts, sizes)
        grad_grid = lax.dynamic_update_slice(grad_grid, current + grad_patch, starts)
        return ((grad_grid, grad_probe + grad_wave), None)

    init = (jnp.zeros(grid.shape, jnp.float32), jnp.zeros(probe.shape, jnp.float32))
    (grad_grid, grad_probe), unused = lax.scan(one_record, init, (places, measured))
    return (grad_grid, grad_probe)


def gram_of(first, second):
    stacked = jnp.concatenate([first, second], axis=0)
    col_re = stacked[:, 0]
    col_im = stacked[:, 1]
    gram_re = einsum_exact("ax,bx->ab", col_re, col_re) + einsum_exact("ax,bx->ab", col_im, col_im)
    gram_im = einsum_exact("ax,bx->ab", col_re, col_im) - einsum_exact("ax,bx->ab", col_im, col_re)
    return (gram_re, gram_im)


def complex_cholesky(herm_re, herm_im):
    count = herm_re.shape[0]
    order_idx = lax.iota(jnp.int32, count)
    cols_re = []
    cols_im = []
    for col_idx in range(count):
        numer_re = herm_re[:, col_idx]
        numer_im = herm_im[:, col_idx]
        for prev_idx in range(col_idx):
            vec_re = cols_re[prev_idx]
            vec_im = cols_im[prev_idx]
            pivot_re = vec_re[col_idx]
            pivot_im = vec_im[col_idx]
            numer_re = numer_re - (vec_re * pivot_re + vec_im * pivot_im)
            numer_im = numer_im - (vec_im * pivot_re - vec_re * pivot_im)
        diag_val = jnp.sqrt(numer_re[col_idx])
        below = order_idx > col_idx
        at_diag = order_idx == col_idx
        cols_re.append(
            jnp.where(below, numer_re / diag_val, 0.0) + jnp.where(at_diag, diag_val, 0.0)
        )
        cols_im.append(jnp.where(below, numer_im / diag_val, 0.0))
    return (jnp.stack(cols_re, axis=1), jnp.stack(cols_im, axis=1))


def lower_inverse(low_re, low_im):
    count = low_re.shape[0]
    unit = jnp.eye(count, dtype=low_re.dtype)
    rows_re = []
    rows_im = []
    for row_idx in range(count):
        acc_re = unit[row_idx]
        acc_im = jnp.zeros_like(unit[row_idx])
        for prev_idx in range(row_idx):
            coef_re = low_re[row_idx, prev_idx]
            coef_im = low_im[row_idx, prev_idx]
            acc_re = acc_re - (coef_re * rows_re[prev_idx] - coef_im * rows_im[prev_idx])
            acc_im = acc_im - (coef_re * rows_im[prev_idx] + coef_im * rows_re[prev_idx])
        rows_re.append(acc_re / low_re[row_idx, row_idx])
        rows_im.append(acc_im / low_re[row_idx, row_idx])
    return (jnp.stack(rows_re, axis=0), jnp.stack(rows_im, axis=0))


def orthonormalize(probe_cols, grad_cols, gram_re, gram_im, scale_out):
    modes = probe_cols.shape[0]
    trace_pp = jnp.trace(gram_re[:modes, :modes])
    trace_gg = jnp.trace(gram_re[modes:, modes:])
    factor = 0.5 * jnp.sqrt(trace_pp / (trace_gg + 1e-06))
    new_re = (
        gram_re[:modes, :modes]
        - factor * (gram_re[:modes, modes:] + gram_re[modes:, :modes])
        + factor * factor * gram_re[modes:, modes:]
    )
    new_im = (
        gram_im[:modes, :modes]
        - factor * (gram_im[:modes, modes:] + gram_im[modes:, :modes])
        + factor * factor * gram_im[modes:, modes:]
    )
    low_re, low_im = complex_cholesky(new_re, new_im)
    inv_re, inv_im = lower_inverse(low_re, low_im)
    right_re = inv_re.T
    right_im = -inv_im.T
    moved = probe_cols - factor * grad_cols
    moved_re = moved[:, 0]
    moved_im = moved[:, 1]
    out_re = einsum_exact("kx,kj->jx", moved_re, right_re) - einsum_exact(
        "kx,kj->jx", moved_im, right_im
    )
    out_im = einsum_exact("kx,kj->jx", moved_re, right_im) + einsum_exact(
        "kx,kj->jx", moved_im, right_re
    )
    return jnp.stack([out_re, out_im], axis=1) * scale_out


def fold_axis(grad, dim, half):
    full = grad.shape[dim]
    inner = full - 2 * half
    core = lax.slice_in_dim(grad, half, half + inner, axis=dim)
    for step_by in (1, -1):
        if step_by == 1:
            sent = lax.slice_in_dim(grad, half + inner, full, axis=dim)
        else:
            sent = lax.slice_in_dim(grad, 0, half, axis=dim)
        if dim == 2:
            arrived = from_behind(sent, "row", step_by)
        else:
            arrived = from_behind(sent, "col", step_by)
        widths = [(0, 0)] * grad.ndim
        if step_by == 1:
            widths[dim] = (0, inner - half)
        else:
            widths[dim] = (inner - half, 0)
        core = core + jnp.pad(arrived, widths)
    return core


def per_device(object_slices, probe, taps, measured, positions):
    width = probe.shape[-1]
    half = width // 2
    tile_rows = object_slices.shape[2]
    tile_cols = object_slices.shape[3]
    tables = make_tables(taps, width)
    extended = with_halo(object_slices, (("row", 2), ("col", 3)), half)
    anchor = jnp.stack(
        [lax.axis_index("row") * tile_rows - half, lax.axis_index("col") * tile_cols - half]
    )
    places = positions - anchor[None, :]
    grad_ext, grad_probe = accumulate(extended, probe, measured, places, tables, width)
    folded = fold_axis(fold_axis(grad_ext, 2, half), 3, half)
    modes = probe.shape[0]
    pixels = width * width
    probe_cols = probe.reshape(modes, 2, pixels)
    grad_cols = grad_probe.reshape(modes, 2, pixels)
    share = pixels // (lax.axis_size("row") * lax.axis_size("col"))
    start = lax.axis_index(("row", "col")) * share
    own_probe = lax.dynamic_slice_in_dim(probe_cols, start, share, 2)
    total_grad = lax.psum(grad_cols, ("row", "col"))
    gram_re, gram_im = gram_of(probe_cols, total_grad)
    own_grad = lax.dynamic_slice_in_dim(total_grad, start, share, 2)
    new_probe = orthonormalize(own_probe, own_grad, gram_re, gram_im, float(width))
    return (folded, new_probe)


def solution(mesh):
    placed = (
        P(None, None, ("groups", "row"), "col"),
        P("groups", None, None, None),
        P(),
        P(("groups", "row", "col"), None, None),
        P(("groups", "row", "col"), None),
    )
    return jax.shard_map(
        per_device,
        mesh=mesh,
        in_specs=placed,
        out_specs=(P(None, None, ("groups", "row"), "col"), P("groups", None, ("row", "col"))),
        check_vma=False,
    )
```

profile of v0, /device:TPU:0, one launch (start us, length us, event | category | flops | bytes accessed | tf_op | source)
XLA Modules:
  0.0 651.0 jit_solution(16764180511014686650)
XLA Ops:
  8.5 4.9 collective-permute-start
  18.0 17.8 %collective-permute-done = f32[4,2,64,256]{3,2,1,0:T(8,128)S(1)} collective-permute-done((f32[4,2,64,256]{3,2,1,0:T(8,128)S(1)}, f32[4,2,64,256]{3,2,1,0:T(8,128)S(1)}, u32[]{:S(2)}, u32[]{:S(2)}) %collective-permute-start) | collective-permute-done | bytes 524320 | tf_op jit(solution)/shard_map/ppermute | solution.py:24
  44.0 3.3 fusion.235
  47.3 3.2 fusion.233
  50.5 3.8 pad_maximum_fusion
  56.2 173.4 %while.16 = (s32[]{:T(128)}, f32[4,2,256,384]{3,2,1,0:T(8,128)}, f32[8,2,128,128]{2,3,0,1:T(8,128)}, s32[2,2]{1,0:T(2,128)S(1)}, f32[8,2,128,128]{2,3,0,1:T(8,12...) while((s32[]{:T(128)}, f32[4,2,256,384]{3,2,1,0:T(8,128)}, ...), condition=%wide.region_18.19_spmd.clone.clone, body=%wide.region_0.18_spmd.clone.clone.sunk | while | flops 12914802688 | bytes 137233312 | solution.py:101
  90.1 2.5 fusion.624
  130.8 7.7 %dynamic_update_slice.9 = f32[4,2,256,384]{3,2,1,0:T(8,128)} dynamic-update-slice(f32[4,2,256,384]{3,2,1,0:T(8,128)} %get-tuple-element.615, f32[4,2,128,128]{3,2,1,0:T(8,128)S(1)} %add_add_fusion.2, s32[]{:T(128)} %constant.94.clone.1..sunk, s32[]{:T(128)} %constant.94.clone.1..sunk, s32[]{:T(128)S(6)} %select_n.471, s32[]{:T(128)S(6)} %select_n.472) | dynamic-update-slice | bytes 1048580 | tf_op jit(solution)/shard_map/while/body/eval_jaxpr/dynamic_update_slice | solution.py:97
  214.8 7.3 %dynamic_update_slice.9 = f32[4,2,256,384]{3,2,1,0:T(8,128)} dynamic-update-slice(f32[4,2,256,384]{3,2,1,0:T(8,128)} %get-tuple-element.615, f32[4,2,128,128]{3,2,1,0:T(8,128)S(1)} %add_add_fusion.2, s32[]{:T(128)} %constant.94.clone.1..sunk, s32[]{:T(128)} %constant.94.clone.1..sunk, s32[]{:T(128)S(6)} %select_n.471, s32[]{:T(128)S(6)} %select_n.472) | dynamic-update-slice | bytes 1048580 | tf_op jit(solution)/shard_map/while/body/eval_jaxpr/dynamic_update_slice | solution.py:97
  233.2 2.7 fusion.298
  235.8 4.2 collective-permute-start.4
  241.3 91.9 %all-reduce.16.cloned.1.call-done = f32[8,2,16384]{2,0,1:T(8,128)} async-done(((f32[8,2,16384]{2,0,1:T(8,128)}), f32[8,2,16384]{2,0,1:T(8,128)}) %all-reduce.16.cloned.1.call-update) | async-done | bytes 1048592 | tf_op jit(solution)/shard_map/psum | solution.py:230
  333.2 2.7 fusion.295
  335.9 2.7 convolution_add_fusion.25
  362.9 3.8 fusion.286
  368.1 3.8 compare_select_fusion.15
  374.6 5.0 fusion.282
  381.0 5.1 compare_select_fusion.13
  388.7 6.2 add_subtract_fusion.2
  396.1 6.2 compare_select_fusion.11
  404.8 7.6 %add_subtract_fusion.1 = f32[8]{0:T(128)S(1)} fusion(f32[8]{0:T(128)S(1)} %compare_select_fusion.11, f32[8]{0:T(128)S(1)} %compare_select_fusion.13, f32[8]{0:T(128)S(1)} %compare_select_fusion.15, f32[8]{0:T(128)S(1)} %compare_select_fusion.17, f32[8]{0:T(128)S(1)} %compare_select_fusion.19, f32[8]{0:T(128)S(1)} %get-tuple-element.459, ...), kind=kLoop, calls=%fused_computation.455 | loop fusion | flops 432 | bytes 516 | tf_op jit(solution)/shard_map/sub | solution.py:127
  413.7 7.6 %compare_select_fusion.9 = f32[8]{0:T(128)S(1)} fusion(f32[8]{0:T(128)S(1)} %compare_select_fusion.11, f32[8]{0:T(128)S(1)} %compare_select_fusion.13, f32[8]{0:T(128)S(1)} %compare_select_fusion.15, f32[8]{0:T(128)S(1)} %compare_select_fusion.17, f32[8]{0:T(128)S(1)} %compare_select_fusion.19, f32[8]{0:T(128)S(1)} %get-tuple-element.460, ...), kind=kLoop, calls=%fused_computation.391 | loop fusion | flops 456 | bytes 520 | tf_op jit(solution)/shard_map/jit(_where)/select_n | solution.py:135
  423.1 8.8 %add_subtract_fusion = f32[8]{0:T(128)S(1)} fusion(f32[8]{0:T(128)S(1)} %compare_select_fusion.9, f32[8]{0:T(128)S(1)} %compare_select_fusion.11, f32[8]{0:T(128)S(1)} %compare_select_fusion.13, f32[8]{0:T(128)S(1)} %compare_select_fusion.15, f32[8]{0:T(128)S(1)} %compare_select_fusion.17, f32[8]{0:T(128)S(1)} %compare_select_fusion.19, ...), kind=kLoop, calls=%fused_computation.454 | loop fusion | flops 512 | bytes 592 | tf_op jit(solution)/shard_map/sub | solution.py:127
  433.7 39.2 %subtract_divide_fusion.1 = (f32[1,8]{0,1:T(8,128)S(1)}, f32[1,8]{0,1:T(8,128)S(1)}, f32[1,8]{0,1:T(8,128)S(1)}, f32[1,8]{0,1:T(8,128)S(1)}, f32[1,8]{0,1:T(8,128)S(1)}) fusion(f32[8,8]{0,1:T(8,128)S(1)} %fusion.251, f32[]{:T(128)} %bitcast.99, f32[]{:T(128)} %bitcast.67, f32[]{:T(128)S(6)} %mul.2504, f32[]{:T(128)} %bitcast.96, f32[]{:T(128)} %bitcast.94, ...), kind=kLoop, calls=%fused_computation.360 | loop fusion | flops 1576 | bytes 720 | tf_op jit(solution)/shard_map/div | solution.py:152
  472.9 27.4 %subtract_divide_fusion.3 = f32[1,8]{0,1:T(8,128)S(1)} fusion(f32[]{:T(128)} %bitcast.81, f32[1,8]{0,1:T(8,128)S(1)} %get-tuple-element.353, f32[1,8]{0,1:T(8,128)S(1)} %get-tuple-element.354, f32[1,8]{0,1:T(8,128)S(1)} %get-tuple-element.355, f32[1,8]{0,1:T(8,128)S(1)} %get-tuple-element.356, f32[]{:T(128)} %bitcast.53, f32[8,8]{0,1:T(8,128)S(1)} %fusion.251, ...), kind=kLoop, calls=%fused_computation.362 | loop fusion | flops 960 | bytes 464 | tf_op jit(solution)/shard_map/div | solution.py:152
  500.3 19.0 %subtract_divide_fusion.5 = f32[1,8]{0,1:T(8,128)S(1)} fusion(f32[1,8]{0,1:T(8,128)S(1)} %get-tuple-element.354, f32[1,8]{0,1:T(8,128)S(1)} %get-tuple-element.355, f32[1,8]{0,1:T(8,128)S(1)} %get-tuple-element.356, f32[1,8]{0,1:T(8,128)S(1)} %get-tuple-element.353, f32[8,8]{0,1:T(8,128)S(1)} %fusion.251, f32[]{:T(128)} %bitcast.65, f32[]{:T(128)} %bitcast.41, ...), kind=kLoop, calls=%fused_computation.365 | loop fusion | flops 608 | bytes 372 | tf_op jit(solution)/shard_map/div | solution.py:152
  519.3 12.3 %subtract_divide_fusion.7 = f32[1,8]{0,1:T(8,128)S(1)} fusion(f32[1,8]{0,1:T(8,128)S(1)} %get-tuple-element.353, f32[1,8]{0,1:T(8,128)S(1)} %get-tuple-element.354, f32[1,8]{0,1:T(8,128)S(1)} %get-tuple-element.355, f32[1,8]{0,1:T(8,128)S(1)} %get-tuple-element.356, f32[8,8]{0,1:T(8,128)S(1)} %fusion.251, f32[]{:T(128)} %bitcast.51, f32[]{:T(128)} %bitcast.31, ...), kind=kLoop, calls=%fused_computation.368 | loop fusion | flops 320 | bytes 288 | tf_op jit(solution)/shard_map/div | solution.py:152
  532.2 27.3 %subtract_divide_fusion.2 = f32[1,8]{0,1:T(8,128)S(1)} fusion(f32[1,8]{0,1:T(8,128)S(1)} %get-tuple-element.353, f32[1,8]{0,1:T(8,128)S(1)} %get-tuple-element.354, f32[1,8]{0,1:T(8,128)S(1)} %get-tuple-element.355, f32[1,8]{0,1:T(8,128)S(1)} %get-tuple-element.356, f32[]{:T(128)} %bitcast.67, f32[]{:T(128)S(6)} %mul.2504, f32[]{:T(128)} %bitcast.81, ...), kind=kLoop, calls=%fused_computation.361 | loop fusion | flops 960 | bytes 432 | tf_op jit(solution)/shard_map/div | solution.py:153
  559.4 19.0 %subtract_divide_fusion.4 = f32[1,8]{0,1:T(8,128)S(1)} fusion(f32[1,8]{0,1:T(8,128)S(1)} %get-tuple-element.353, f32[1,8]{0,1:T(8,128)S(1)} %get-tuple-element.354, f32[1,8]{0,1:T(8,128)S(1)} %get-tuple-element.355, f32[1,8]{0,1:T(8,128)S(1)} %get-tuple-element.356, f32[]{:T(128)} %bitcast.53, f32[]{:T(128)S(6)} %mul.2430, f32[]{:T(128)} %bitcast.65, ...), kind=kLoop, calls=%fused_computation.363 | loop fusion | flops 608 | bytes 340 | tf_op jit(solution)/shard_map/div | solution.py:153
  578.4 7.2 %subtract_divide_fusion.8 = (f32[1,8]{0,1:T(8,128)S(1)}, f32[1,8]{0,1:T(8,128)S(1)}, f32[1,8]{0,1:T(8,128)S(1)}) fusion(f32[1,8]{0,1:T(8,128)S(1)} %get-tuple-element.354, f32[1,8]{0,1:T(8,128)S(1)} %get-tuple-element.355, f32[1,8]{0,1:T(8,128)S(1)} %get-tuple-element.356, f32[]{:T(128)} %bitcast.31, f32[]{:T(128)S(6)} %mul.2318, f32[]{:T(128)} %bitcast.39, ...), kind=kLoop, calls=%fused_computation.369 | loop fusion | flops 192 | bytes 252 | tf_op jit(solution)/shard_map/div | solution.py:153
  585.6 36.6 %subtract_divide_fusion = f32[1,8]{0,1:T(8,128)S(1)} fusion(f32[1,8]{0,1:T(8,128)S(1)} %get-tuple-element.353, f32[1,8]{0,1:T(8,128)S(1)} %get-tuple-element.354, f32[1,8]{0,1:T(8,128)S(1)} %get-tuple-element.355, f32[1,8]{0,1:T(8,128)S(1)} %get-tuple-element.356, f32[]{:T(128)} %bitcast.83, f32[]{:T(128)S(6)} %mul.2550, f32[]{:T(128)} %bitcast.99, ...), kind=kLoop, calls=%fused_computation.359 | loop fusion | flops 1376 | bytes 532 | tf_op jit(solution)/shard_map/div | solution.py:153
  622.3 12.2 %subtract_divide_fusion.6 = f32[1,8]{0,1:T(8,128)S(1)} fusion(f32[1,8]{0,1:T(8,128)S(1)} %get-tuple-element.353, f32[1,8]{0,1:T(8,128)S(1)} %get-tuple-element.354, f32[1,8]{0,1:T(8,128)S(1)} %get-tuple-element.355, f32[1,8]{0,1:T(8,128)S(1)} %get-tuple-element.356, f32[]{:T(128)} %bitcast.41, f32[]{:T(128)S(6)} %mul.2368, f32[]{:T(128)} %bitcast.51, ...), kind=kLoop, calls=%fused_computation.366 | loop fusion | flops 320 | bytes 256 | tf_op jit(solution)/shard_map/div | solution.py:153
  (339 shorter events, 193.5 us)
Async XLA Ops:
  7.2 326.0 %all-reduce.16.cloned.1.call-start = ((), (), s32[]{:S(2)}) async-start(), calls=%async_computation | async-start | bytes 2097152 | tf_op jit(solution)/shard_map/psum | solution.py:230
  8.5 27.2 %collective-permute-start = (f32[4,2,64,256]{3,2,1,0:T(8,128)S(1)}, f32[4,2,64,256]{3,2,1,0:T(8,128)S(1)}, u32[]{:S(2)}, u32[]{:S(2)}) collective-permute-start(f32[4,2,64,256]{3,2,1,0:T(8,128)S(1)} %get-tuple-element.392), channel_id=1, source_target_pairs={{0,2},{2,4},{4,6},{6,8},{8,10},{10,12},{12,14},{1,3},{3,5},{5,7},{... | collective-permute-start | bytes 1572872 | tf_op jit(solution)/shard_map/ppermute | solution.py:24
  13.4 22.7 %collective-permute-start.1 = (f32[4,2,64,256]{3,2,1,0:T(8,128)S(1)}, f32[4,2,64,256]{3,2,1,0:T(8,128)}, u32[]{:S(2)}, u32[]{:S(2)}) collective-permute-start(f32[4,2,64,256]{3,2,1,0:T(8,128)S(1)} %get-tuple-element.393), channel_id=1, source_target_pairs={{2,0},{4,2},{6,4},{8,6},{10,8},{12,10},{14,12},{3,1},{5,3},{7,5},{... | collective-permute-start | bytes 1572872 | tf_op jit(solution)/shard_map/ppermute | solution.py:25
  36.1 6.2 copy-start.23
  37.5 4.9 copy-start.9
  37.5 6.4 copy-start.24
  39.0 11.5 %collective-permute-start.2 = (f32[4,2,256,64]{2,3,1,0:T(8,128)}, f32[4,2,256,64]{2,3,1,0:T(8,128)}, u32[]{:S(2)}, u32[]{:S(2)}) collective-permute-start(f32[4,2,256,64]{2,3,1,0:T(8,128)} %get-tuple-element.388), channel_id=1, source_target_pairs={{0,1},{2,3},{4,5},{6,7},{8,9},{10,11},{12,13},{14,15},{16,17},{18,... | collective-permute-start | bytes 1572872 | tf_op jit(solution)/shard_map/ppermute | solution.py:24
  41.1 9.5 %collective-permute-start.3 = (f32[4,2,256,64]{2,3,1,0:T(8,128)}, f32[4,2,256,64]{2,3,1,0:T(8,128)}, u32[]{:S(2)}, u32[]{:S(2)}) collective-permute-start(f32[4,2,256,64]{2,3,1,0:T(8,128)} %get-tuple-element.389), channel_id=1, source_target_pairs={{1,0},{3,2},{5,4},{7,6},{9,8},{11,10},{13,12},{15,14},{17,16},{19,... | collective-permute-start | bytes 1572872 | tf_op jit(solution)/shard_map/ppermute | solution.py:25
  44.0 6.6 %copy-start.10 = (f32[4,2,64,256]{2,3,1,0:T(8,128)S(1)}, f32[4,2,64,256]{2,3,1,0:T(8,128)}, u32[]{:S(2)}) copy-start(f32[4,2,64,256]{2,3,1,0:T(8,128)} %copy-done.9) | copy-start | bytes 1572868
  56.2 9.2 %copy-start = (f32[8,2,128,128]{2,3,0,1:T(8,128)}, f32[8,2,128,128]{2,3,0,1:T(8,128)S(1)}, u32[]{:S(2)}) copy-start(f32[8,2,128,128]{2,3,0,1:T(8,128)S(1)} %get-tuple-element.634) | copy-start | bytes 3145732 | tf_op jit(solution)/shard_map/while
  63.1 3.4 copy-start.6
  90.1 4.6 copy-start.2
  90.1 4.6 copy-start.3
  97.2 4.6 copy-start.22
  122.8 3.6 copy-start.5
  122.8 3.6 copy-start.7
  138.9 9.2 %copy-start = (f32[8,2,128,128]{2,3,0,1:T(8,128)}, f32[8,2,128,128]{2,3,0,1:T(8,128)S(1)}, u32[]{:S(2)}) copy-start(f32[8,2,128,128]{2,3,0,1:T(8,128)S(1)} %get-tuple-element.634) | copy-start | bytes 3145732 | tf_op jit(solution)/shard_map/while
  145.8 3.4 copy-start.6
  172.8 4.4 copy-start.2
  172.8 4.4 copy-start.3
  179.6 4.5 copy-start.22
  205.4 3.6 copy-start.5
  205.4 3.6 copy-start.7
  209.1 3.7 copy-start.11
  209.1 3.7 copy-start.12
  209.1 3.7 copy-start.13
  209.1 3.7 copy-start.14
  235.8 399.3 %collective-permute-start.4 = (f32[4,2,64,384]{3,2,1,0:T(8,128)}, f32[4,2,64,384]{3,2,1,0:T(8,128)S(1)}, u32[]{:S(2)}, u32[]{:S(2)}) collective-permute-start(f32[4,2,64,384]{3,2,1,0:T(8,128)} %get-tuple-element.386), channel_id=1, source_target_pairs={{0,2},{2,4},{4,6},{6,8},{8,10},{10,12},{12,14},{1,3},{3,5},{5,7},{... | collective-permute-start | bytes 2359304 | tf_op jit(solution)/shard_map/ppermute | solution.py:14
  240.0 395.1 %collective-permute-start.5 = (f32[4,2,64,384]{3,2,1,0:T(8,128)}, f32[4,2,64,384]{3,2,1,0:T(8,128)}, u32[]{:S(2)}, u32[]{:S(2)}) collective-permute-start(f32[4,2,64,384]{3,2,1,0:T(8,128)} %get-tuple-element.387), channel_id=1, source_target_pairs={{2,0},{4,2},{6,4},{8,6},{10,8},{12,10},{14,12},{3,1},{5,3},{7,5},{... | collective-permute-start | bytes 2359304 | tf_op jit(solution)/shard_map/ppermute | solution.py:14
  333.2 8.8 %copy-start.8 = (f32[8,2,16384]{2,0,1:T(8,128)S(1)}, f32[8,2,16384]{2,0,1:T(8,128)}, u32[]{:S(2)}) copy-start(f32[8,2,16384]{2,0,1:T(8,128)} %all-reduce.16.cloned.1.call-done) | copy-start | bytes 3145732
  637.2 3.8 collective-permute-start.6
  638.5 3.8 collective-permute-start.7
  (21 other events, 47.2 us)
Sparse Core Ops, SparseCore 0:
  232.6 100.5 all-reduce.15
where the time goes:
time: 663 us; the launch traced here: 651 us
  other arithmetic  279 us (42%)
  matrix products  135 us (20%)
  waiting for transfers between devices  111 us (17%)
  local copies, waits for them, and re-layouts  60 us (9%)
  between operations  31.1 us (5%)
  starting transfers between devices  17.7 us (3%)
  loops' own time  17.6 us (3%)
    dot_general x138, matrix products, einsum_exact(): return jnp.einsum(form, first, second, precision=highest_mode)  135 us
    div x5, other arithmetic, lower_inverse(): rows_im.append(acc_im / low_re[row_idx, row_idx])  102 us
    div x4, other arithmetic, lower_inverse(): rows_re.append(acc_re / low_re[row_idx, row_idx])  97.9 us
    psum x1, waiting for transfers between devices, per_device(): total_grad = lax.psum(grad_cols, ('row', 'col'))  91.9 us
    sub x7, other arithmetic, complex_cholesky(): numer_re = numer_re - (vec_re * pivot_re + vec_im * pivot_im)  34.9 us
    select_n x7, other arithmetic, complex_cholesky(): cols_im.append(jnp.where(below, numer_im / diag_val, 0.0))  26.1 us
    ppermute x2, waiting for transfers between devices, with_halo(): before = lax.ppermute(last, axis, up)  17.8 us
    another operation x1, loops' own time, accumulate(): lax.scan(one_record, init, (places, measured))  17.6 us
  transfers between devices with their start and end apart: 9, of which 3 were waited for; matrix products, arithmetic and copies ran while one was open for 46% of the time, Pallas kernels for 0%

commit v1 on v0

v1 whole, which is shorter than its diff:
```python
import math

import jax
import jax.numpy as jnp
import numpy as np
from jax import lax
from jax.experimental import pallas as pl
from jax.experimental.pallas import tpu as pltpu
from jax.sharding import PartitionSpec as P

F32 = jnp.float32
BF16 = jnp.bfloat16
LANES = 128
SUBLANES = 8


def shifted(value, axis, step):
    count = lax.axis_size(axis)
    pairs = [(i, i + step) for i in range(count) if 0 <= i + step < count]
    return lax.ppermute(value, axis, pairs)


def swapped(value, axis, bit):
    count = lax.axis_size(axis)
    return lax.ppermute(value, axis, [(i, i ^ bit) for i in range(count)])


def hi_lo(value):
    high = lax.reduce_precision(value, 8, 7)
    return high.astype(BF16), (value - high).astype(BF16)


def block_tables(taps, width):
    reach = taps.shape[1] // 2
    padded = jnp.pad(taps, ((0, 0), (width, width)))
    idx = lax.iota(jnp.int32, width)
    offset = idx[None, :] - idx[:, None] + reach
    tap_idx = lax.iota(jnp.int32, taps.shape[1])
    hot = (offset[None, :, :] == tap_idx[:, None, None]).astype(F32)
    band_re = jnp.sum(hot * taps[0][:, None, None], axis=0)
    band_im = jnp.sum(hot * taps[1][:, None, None], axis=0)
    phase = np.arange(width)[:, None] * np.arange(width)[None, :] % width
    angle = 2.0 * math.pi / width * phase
    norm = 1.0 / math.sqrt(width)
    dft_re = jnp.asarray(np.cos(angle) * norm, F32)
    dft_im = jnp.asarray(-np.sin(angle) * norm, F32)

    def block(re, im):
        return jnp.concatenate(
            [jnp.concatenate([re, -im], axis=1), jnp.concatenate([im, re], axis=1)], axis=0
        )

    band, dft = block(band_re, band_im), block(dft_re, dft_im)
    parts = []
    for matrix in (band, band.T, dft, dft.T):
        parts.extend(hi_lo(matrix))
    return jnp.stack(parts)


def split(value):
    high = value.astype(BF16)
    return high, (value - high.astype(F32)).astype(BF16)


def mxu(a, b):
    return lax.dot_general(a, b, (((1,), (0,)), ((), ())), preferred_element_type=F32)


def left_product(tab, which, x):
    high, low = split(x)
    w_high, w_low = tab[2 * which], tab[2 * which + 1]
    return mxu(w_high, high) + (mxu(w_high, low) + mxu(w_low, high))


def right_product(tab, which, x):
    high, low = split(x)
    w_high, w_low = tab[2 * which], tab[2 * which + 1]
    return mxu(high, w_high) + (mxu(low, w_high) + mxu(high, w_low))


def to_rows(y):
    n = LANES
    return jnp.concatenate(
        [
            jnp.concatenate([y[:n, :n], y[n:, :n]], axis=1),
            jnp.concatenate([y[:n, n:], y[n:, n:]], axis=1),
        ],
        axis=0,
    )


def two_sided(tab, forward, x):
    base, adjoint = forward
    return right_product(tab, adjoint, to_rows(left_product(tab, base, x)))


BAND, BAND_ADJ, DFT, DFT_ADJ = range(4)


def field_kernel(
    places, side, own, above, below, beside, probe, tab, measured,
    gown, gside, gprobe, ext, gext, patch, waves, far, intensity, gpatch,
):
    rec = pl.program_id(0)
    slices = own.shape[0]
    modes = probe.shape[0]
    n = LANES
    tile_cols = own.shape[3]
    half = above.shape[2]
    tile_rows = own.shape[2]
    weight = 1.0 / (8.0 * modes)

    @pl.when(rec == 0)
    def _():
        gext[...] = jnp.zeros(gext.shape, F32)
        gprobe[...] = jnp.zeros(gprobe.shape, F32)
        ext[:, :, :half, n : n + tile_cols] = above[...]
        ext[:, :, half : half + tile_rows, n : n + tile_cols] = own[...]
        ext[:, :, half + tile_rows :, n : n + tile_cols] = below[...]
        nothing = jnp.zeros(beside.shape, F32)

        @pl.when(side[0] == 0)
        def _():
            ext[:, :, :, :n] = nothing
            ext[:, :, :, n + tile_cols :] = beside[...]

        @pl.when(side[0] != 0)
        def _():
            ext[:, :, :, :n] = beside[...]
            ext[:, :, :, n + tile_cols :] = nothing

    row = places[rec, 0]
    col = places[rec, 1]
    lane_tile = pl.multiple_of(col // n * n, n)
    shift = col % n
    row_tile = pl.multiple_of(row // SUBLANES * SUBLANES, SUBLANES)
    drop = row % SUBLANES
    for s in range(slices):
        for c in range(2):
            window = ext[s, c, pl.ds(row_tile, n + SUBLANES), pl.ds(lane_tile, 2 * n)]
            window = pltpu.roll(window, (2 * n - shift) % (2 * n), 1)[:, :n]
            patch[s, c] = pltpu.roll(window, (n + SUBLANES - drop) % (n + SUBLANES), 0)[:n]

    def wave_in(s, mode):
        if s == 0:
            return probe[mode, 0], probe[mode, 1]
        block = waves[s - 1, mode * n : (mode + 1) * n, :]
        return block[:, :n], block[:, n:]

    intensity[...] = jnp.zeros(intensity.shape, F32)
    for s in range(slices):
        last = s + 1 == slices
        obj_re, obj_im = patch[s, 0], patch[s, 1]
        for pair in range(modes // 2):
            res, ims = [], []
            for mode in (2 * pair, 2 * pair + 1):
                re, im = wave_in(s, mode)
                res.append(re * obj_re - im * obj_im)
                ims.append(re * obj_im + im * obj_re)
            x = jnp.concatenate(
                [jnp.concatenate(res, axis=1), jnp.concatenate(ims, axis=1)], axis=0
            )
            z = two_sided(tab, (DFT, DFT_ADJ) if last else (BAND, BAND_ADJ), x)
            if last:
                far[pair * 2 * n : (pair + 1) * 2 * n, :] = z
                squares = z * z
                both = squares[:n] + squares[n:]
                intensity[...] += both[:, :n] + both[:, n:]
            else:
                waves[s, pair * 2 * n : (pair + 1) * 2 * n, :] = z

    factor = 2.0 * weight * (intensity[...] - measured[0])
    for pair in range(modes // 2):
        block = far[pair * 2 * n : (pair + 1) * 2 * n, :]
        scale = jnp.concatenate([jnp.concatenate([factor, factor], axis=1)] * 2, axis=0)
        far[pair * 2 * n : (pair + 1) * 2 * n, :] = two_sided(
            tab, (DFT_ADJ, DFT), to_rows(block * scale)
        )
    for s in reversed(range(slices)):
        obj_re, obj_im = patch[s, 0], patch[s, 1]
        for pair in range(modes // 2):
            res, ims = [], []
            sum_re = sum_im = None
            for mode in (2 * pair, 2 * pair + 1):
                block = far[mode * n : (mode + 1) * n, :]
                g_re, g_im = block[:, :n], block[:, n:]
                re, im = wave_in(s, mode)
                add_re = g_re * re + g_im * im
                add_im = g_im * re - g_re * im
                sum_re = add_re if sum_re is None else sum_re + add_re
                sum_im = add_im if sum_im is None else sum_im + add_im
                res.append(g_re * obj_re + g_im * obj_im)
                ims.append(g_im * obj_re - g_re * obj_im)
            if pair == 0:
                gpatch[0] = sum_re
                gpatch[1] = sum_im
            else:
                gpatch[0] += sum_re
                gpatch[1] += sum_im
            if s > 0:
                x = jnp.concatenate(
                    [jnp.concatenate(res, axis=1), jnp.concatenate(ims, axis=1)], axis=0
                )
                far[pair * 2 * n : (pair + 1) * 2 * n, :] = two_sided(tab, (BAND_ADJ, BAND), x)
            else:
                for k, mode in enumerate((2 * pair, 2 * pair + 1)):
                    gprobe[mode, 0] += res[k]
                    gprobe[mode, 1] += ims[k]
        for c in range(2):
            tall = jnp.concatenate([gpatch[c], jnp.zeros((SUBLANES, n), F32)], axis=0)
            tall = pltpu.roll(tall, drop, 0)
            wide = jnp.concatenate([tall, jnp.zeros(tall.shape, F32)], axis=1)
            wide = pltpu.roll(wide, shift, 1)
            gext[s, c, pl.ds(row_tile, n + SUBLANES), pl.ds(lane_tile, 2 * n)] += wide

    @pl.when(rec == pl.num_programs(0) - 1)
    def _():
        gown[...] = gext[:, :, :, n : n + tile_cols]

        @pl.when(side[0] == 0)
        def _():
            gside[...] = gext[:, :, :, n + tile_cols :]

        @pl.when(side[0] != 0)
        def _():
            gside[...] = gext[:, :, :, :n]


def fields(places, side, own, above, below, beside, probe, tab, measured):
    slices, _, tile_rows, tile_cols = own.shape
    modes, _, n, _ = probe.shape
    rows = tile_rows + 2 * above.shape[2]
    records = measured.shape[0]

    def whole(shape):
        return pl.BlockSpec(shape, lambda r, *_: (0,) * len(shape))

    inputs = (own, above, below, beside, probe, tab)
    outs = [(slices, 2, rows, tile_cols), (slices, 2, rows, n), (modes, 2, n, n)]
    return pl.pallas_call(
        field_kernel,
        out_shape=[jax.ShapeDtypeStruct(s, F32) for s in outs],
        grid_spec=pltpu.PrefetchScalarGridSpec(
            num_scalar_prefetch=2,
            grid=(records,),
            in_specs=[whole(x.shape) for x in inputs]
            + [pl.BlockSpec((1, n, n), lambda r, *_: (r, 0, 0))],
            out_specs=[whole(s) for s in outs],
            scratch_shapes=[
                pltpu.VMEM((slices, 2, rows, tile_cols + 2 * n), F32),
                pltpu.VMEM((slices, 2, rows, tile_cols + 2 * n), F32),
                pltpu.VMEM((slices, 2, n, n), F32),
                pltpu.VMEM((slices - 1, modes * n, 2 * n), F32),
                pltpu.VMEM((modes * n, 2 * n), F32),
                pltpu.VMEM((n, n), F32),
                pltpu.VMEM((2, n, n), F32),
            ],
        ),
        compiler_params=pltpu.CompilerParams(vmem_limit_bytes=56 << 20),
        name="fields",
    )(places, side, *inputs, measured)


def gram_kernel(probe, grad, out):
    rows = jnp.concatenate([probe[...], grad[...]], axis=0)
    out[...] = lax.dot_general(
        rows, rows, (((1,), (1,)), ((), ())), precision=lax.Precision.HIGHEST,
        preferred_element_type=F32,
    )


def gram(probe, grad):
    rows = probe.shape[0] + grad.shape[0]
    return pl.pallas_call(
        gram_kernel, out_shape=jax.ShapeDtypeStruct((rows, rows), F32), name="gram"
    )(probe, grad)


def ortho_kernel(gram_ref, probe, grad, out, *, modes, scale):
    m = modes
    s = gram_ref[...]

    def part(a, b):
        return s[a * m : (a + 1) * m, b * m : (b + 1) * m]

    def complex_part(a, b):
        re = part(2 * a, 2 * b) + part(2 * a + 1, 2 * b + 1)
        im = part(2 * a, 2 * b + 1) - part(2 * a + 1, 2 * b)
        return re, im

    pp, pg, gp, gg = (complex_part(a, b) for a, b in ((0, 0), (0, 1), (1, 0), (1, 1)))
    eye = (
        lax.broadcasted_iota(jnp.int32, (m, m), 0) == lax.broadcasted_iota(jnp.int32, (m, m), 1)
    ).astype(F32)

    def trace(x):
        return jnp.sum(jnp.sum(x * eye, axis=1, keepdims=True), axis=0, keepdims=True)

    factor = 0.5 * jnp.sqrt(trace(pp[0]) / (trace(gg[0]) + 1e-06))
    new_re = pp[0] - factor * (pg[0] + gp[0]) + factor * factor * gg[0]
    new_im = pp[1] - factor * (pg[1] + gp[1]) + factor * factor * gg[1]
    a_re = jnp.concatenate([new_re, eye], axis=1)
    a_im = jnp.concatenate([new_im, jnp.zeros((m, m), F32)], axis=1)
    row_idx = lax.broadcasted_iota(jnp.int32, (m, 1), 0)
    for j in range(m):
        inv = 1.0 / jnp.sqrt(a_re[j : j + 1, j : j + 1])
        r_re = a_re[j : j + 1, :] * inv
        r_im = a_im[j : j + 1, :] * inv
        c_re = jnp.where(row_idx > j, a_re[:, j : j + 1] * inv, 0.0)
        c_im = jnp.where(row_idx > j, a_im[:, j : j + 1] * inv, 0.0)
        at = row_idx == j
        a_re, a_im = (
            jnp.where(at, r_re, a_re - (c_re * r_re - c_im * r_im)),
            jnp.where(at, r_im, a_im - (c_re * r_im + c_im * r_re)),
        )
    inv_re = a_re[:, m:] * scale
    inv_im = a_im[:, m:] * scale
    moved = probe[...] - factor * grad[...]
    mix = jnp.concatenate(
        [
            jnp.concatenate([inv_re, inv_im], axis=1),
            jnp.concatenate([-inv_im, inv_re], axis=1),
        ],
        axis=0,
    )
    out[...] = lax.dot_general(
        mix, moved, (((1,), (0,)), ((), ())), precision=lax.Precision.HIGHEST,
        preferred_element_type=F32,
    )


def ortho(gram_all, probe, grad, modes, scale):
    def body(*refs):
        ortho_kernel(*refs, modes=modes, scale=scale)

    return pl.pallas_call(
        body, out_shape=jax.ShapeDtypeStruct(probe.shape, F32), name="ortho"
    )(gram_all, probe, grad)


def per_device(object_slices, probe, taps, measured, positions):
    width = probe.shape[-1]
    half = width // 2
    slices, _, tile_rows, tile_cols = object_slices.shape
    modes = probe.shape[0]
    row_devices = lax.axis_size("row")
    col_devices = lax.axis_size("col")
    row_idx = lax.axis_index("row")
    col_idx = lax.axis_index("col")

    above = shifted(object_slices[:, :, tile_rows - half :], "row", 1)
    below = shifted(object_slices[:, :, :half], "row", -1)
    near = (1 - col_idx) * (tile_cols - LANES)
    strip = jnp.concatenate([
        lax.dynamic_slice_in_dim(x, near, LANES, 3) for x in (above, object_slices, below)
    ], axis=2)
    beside = swapped(strip, "col", 1)

    tab = block_tables(taps, width)
    anchor = jnp.stack([row_idx * tile_rows - half, col_idx * tile_cols - LANES])
    places = (positions - anchor[None, :]).astype(jnp.int32)
    side = col_idx.astype(jnp.int32).reshape(1)
    gown, gside, gprobe = fields(
        places, side, object_slices, above, below, beside, probe, tab, measured
    )

    devices = row_devices * col_devices
    share = width // devices
    index = row_idx * col_devices + col_idx
    total = gprobe.reshape(modes * 2, width, width)
    lows = [("col", 1, 1)]
    bit = 1
    while bit < row_devices:
        lows.append(("row", bit, bit * col_devices))
        bit *= 2
    span = width
    lows = [lows[0], lows[1]] + lows[:1:-1]
    shape = (modes * 2,) + (2,) * len(lows) + (share, width)
    total = total.reshape(shape)
    dims = list(range(len(lows) - 1, -1, -1))
    for axis, bit, global_bit in lows:
        which = dims.index(global_bit.bit_length() - 1)
        mine = (index // global_bit) % 2
        keep = lax.dynamic_index_in_dim(total, mine, which + 1, keepdims=False)
        send = lax.dynamic_index_in_dim(total, 1 - mine, which + 1, keepdims=False)
        total = keep + swapped(send, axis, bit)
        dims.pop(which)

    def by_part(x):
        return x.reshape(modes, 2, share * width).transpose(1, 0, 2).reshape(2 * modes, -1)

    own_probe = lax.dynamic_slice_in_dim(probe, index * share, share, 2)
    p_rows = by_part(own_probe)
    g_rows = by_part(total)
    gram_all = gram(p_rows, g_rows)
    for axis, bit, _ in lows:
        gram_all = gram_all + swapped(gram_all, axis, bit)
    new_rows = ortho(gram_all, p_rows, g_rows, modes, float(width))
    new_probe = new_rows.reshape(2, modes, share * width).transpose(1, 0, 2)

    got = swapped(gside, "col", 1)
    folded = lax.dynamic_update_slice_in_dim(
        gown, lax.dynamic_slice_in_dim(gown, near, LANES, 3) + got, near, 3
    )
    from_above = shifted(folded[:, :, half + tile_rows :], "row", 1)
    from_below = shifted(folded[:, :, :half], "row", -1)
    middle = folded[:, :, half : half + tile_rows]
    object_grad = middle + jnp.concatenate([from_above, from_below], axis=2)
    return (object_grad, new_probe)


def solution(mesh):
    placed = (
        P(None, None, ("groups", "row"), "col"),
        P("groups", None, None, None),
        P(),
        P(("groups", "row", "col"), None, None),
        P(("groups", "row", "col"), None),
    )
    return jax.shard_map(
        per_device,
        mesh=mesh,
        in_specs=placed,
        out_specs=(P(None, None, ("groups", "row"), "col"), P("groups", None, ("row", "col"))),
        check_vma=False,
    )
```

time: 663 us -> 123 us (0.19); the launches traced: 651 us -> 122 us
  other arithmetic: 279 us -> 8.38 us
  matrix products: 135 us -> 0 us
  waiting for transfers between devices: 111 us -> 44.2 us
  local copies, waits for them, and re-layouts: 60 us -> 14.6 us
  between operations: 31.1 us -> 1 us
  Pallas kernels: 0 us -> 27.1 us
  loops' own time: 17.6 us -> 0 us
  starting transfers between devices: 17.7 us -> 27 us
    div x9 -> x0, other arithmetic: 200 us -> none  [the longest x5 102 us: lower_inverse(): rows_im.append(acc_im / low_re[row_idx, row_idx])]
    dot_general x138 -> x0, matrix products: 135 us -> none  [einsum_exact(): return jnp.einsum(form, first, second, precision=highest_mode)]
    psum x1 -> x0, waiting for transfers between devices: 91.9 us -> none  [per_device(): total_grad = lax.psum(grad_cols, ('row', 'col'))]
    sub x9 -> x1, other arithmetic: 34.9 us -> 0.61 us  [per_device(): places = (positions - anchor[None, :]).astype(jnp.int32)]
    pallas_call x0 -> x3, Pallas kernels: none -> 27.1 us  [the longest x1 22.5 us: fields(): pl.pallas_call(field_kernel, out_shape=[jax.ShapeDtypeStruct(s, F32) for...]
    select_n x7 -> x0, other arithmetic: 26.1 us -> none  [complex_cholesky(): cols_im.append(jnp.where(below, numer_im / diag_val, 0.0))]
    ppermute x8 -> x14, waiting for transfers between devices: 19.1 us -> 44.2 us  [the longest x10 24.7 us: swapped(): return lax.ppermute(value, axis, [(i, i ^ bit) for i in range(count)])]
    slice x30 -> x2, local copies, waits for them, and re-layouts: 24.3 us -> 3.26 us  [the longest x1 2.37 us: per_device(): below = shifted(object_slices[:, :, :half], 'row', -1)]
  transfers between devices with their start and end apart: 9 -> 14, of which waited for: 3 -> 9; matrix products, arithmetic and copies ran while one was open for 46% -> 13% of each run, Pallas kernels for 0% -> 4%
where the time goes in v1:
time: 123 us; the launch traced here: 122 us
  waiting for transfers between devices  44.2 us (36%)
  Pallas kernels  27.1 us (22%)
  starting transfers between devices  27 us (22%)
  local copies, waits for them, and re-layouts  14.6 us (12%)
  other arithmetic  8.38 us (7%)
    ppermute x10, waiting for transfers between devices, swapped(): return lax.ppermute(value, axis, [(i, i ^ bit) for i in range(count)])  24.7 us
    pallas_call x1, Pallas kernels, fields(): pl.pallas_call(field_kernel, out_shape=[jax.ShapeDtypeStruct(s, F32) for...  22.5 us
    ppermute x4, waiting for transfers between devices, shifted(): return lax.ppermute(value, axis, pairs)  19.4 us
    ppermute x10, starting transfers between devices, swapped(): return lax.ppermute(value, axis, [(i, i ^ bit) for i in range(count)])  14.2 us
    ppermute x4, starting transfers between devices, shifted(): return lax.ppermute(value, axis, pairs)  12.8 us
    unnamed x19, local copies, waits for them, and re-layouts  3.16 us
    pallas_call x1, Pallas kernels, ortho(): pl.pallas_call(body, out_shape=jax.ShapeDtypeStruct(probe.shape, F32), na...  2.87 us
  transfers between devices with their start and end apart: 14, of which 9 were waited for; matrix products, arithmetic and copies ran while one was open for 13% of the time, Pallas kernels for 4%

profile of v1, /device:TPU:0, one launch (start us, length us, event | category | flops | bytes accessed | tf_op | source)
XLA Modules:
  0.0 122.3 jit_solution(17425814480350501516)
XLA Ops:
  0.7 2.4 %fusion.5 = (f32[4,2,64,256]{3,2,1,0:T(8,128)}, f32[4,2,64,256]{3,2,1,0:T(8,128)}) fusion(f32[4,2,128,256]{3,2,1,0:T(8,128)} %own.1), kind=kLoop, calls=%fused_computation.48 | loop fusion | bytes 2097152 | tf_op jit(solution)/shard_map/slice | solution.py:352
  3.0 4.9 %collective-permute-start = (f32[4,2,64,256]{3,2,1,0:T(8,128)}, f32[4,2,64,256]{3,2,1,0:T(8,128)S(1)}, u32[]{:S(2)}, u32[]{:S(2)}) collective-permute-start(f32[4,2,64,256]{3,2,1,0:T(8,128)} %get-tuple-element.15), channel_id=1, source_target_pairs={{0,2},{2,4},{4,6},{6,8},{8,10},{10,12},{12,14},{1,3},{3,5},{5,7},{... | collective-permute-start | bytes 1572872 | tf_op jit(solution)/shard_map/ppermute | solution.py:20
  7.9 1.3 %collective-permute-start.1 = (f32[4,2,64,256]{3,2,1,0:T(8,128)}, f32[4,2,64,256]{3,2,1,0:T(8,128)S(1)}, u32[]{:S(2)}, u32[]{:S(2)}) collective-permute-start(f32[4,2,64,256]{3,2,1,0:T(8,128)} %get-tuple-element.14), channel_id=1, source_target_pairs={{2,0},{4,2},{6,4},{8,6},{10,8},{12,10},{14,12},{3,1},{5,3},{7,5},{... | collective-permute-start | bytes 1572872 | tf_op jit(solution)/shard_map/ppermute | solution.py:20
  11.1 12.3 %collective-permute-done.1.below = f32[4,2,64,256]{3,2,1,0:T(8,128)S(1)} collective-permute-done((f32[4,2,64,256]{3,2,1,0:T(8,128)}, f32[4,2,64,256]{3,2,1,0:T(8,128)S(1)}, u32[]{:S(2)}, u32[]{:S(2)}) %collective-permute-start.1) | collective-permute-done | bytes 524320 | tf_op jit(solution)/shard_map/ppermute | solution.py:20
  23.4 7.2 %collective-permute-done.above = f32[4,2,64,256]{3,2,1,0:T(8,128)S(1)} collective-permute-done((f32[4,2,64,256]{3,2,1,0:T(8,128)}, f32[4,2,64,256]{3,2,1,0:T(8,128)S(1)}, u32[]{:S(2)}, u32[]{:S(2)}) %collective-permute-start) | collective-permute-done | bytes 524320 | tf_op jit(solution)/shard_map/ppermute | solution.py:20
  30.8 1.0 copy.29
  31.9 0.9 constant_dynamic-update-slice_fusion.3
  32.9 0.9 constant_dynamic-update-slice_fusion.2
  33.8 0.9 constant_dynamic-update-slice_fusion.1
  34.7 0.9 constant_dynamic-update-slice_fusion.tab
  36.6 22.5 %fields.1 = (f32[4,2,256,256]{3,2,1,0:T(8,128)}, f32[4,2,256,128]{3,2,1,0:T(8,128)}, f32[8,2,128,128]{3,2,1,0:T(8,128)}) custom-call(s32[2,2]{1,0:T(2,128)} %broadcast_subtract_fusion.places, s32[1]{0:T(128)} %bitcast.2.side, f32[4,2,128,256]{3,2,1,0:T(8,128)} %own.1, f32[4,2,64,256]{3,2,1,0:T(8,128)} %copy-done.3, f32[4,2,64,256]{3,2,1,0:T(8,128)} %copy-done.4, ...), custom_call_target="tpu_custom_call" | custom-call | tf_op jit(solution)/shard_map/fields/pallas_call | solution.py:240
  59.2 1.3 %constant_dynamic-slice_fusion.1 = (f32[16,2,2,2,1,8,128]{6,5,4,3,2,1,0:T(8,128)S(1)}, f32[16,2,2,2,1,8,128]{6,5,4,3,2,1,0:T(8,128)S(1)}) fusion(f32[16,2,2,2,2,8,128]{6,5,4,3,2,1,0:T(8,128)} %bitcast.62, s32[]{:T(128)S(6)} %select_n.71, s32[]{:T(128)S(6)} %select_n.72), kind=kLoop, calls=%fused_computation.38 | loop fusion | bytes 2097160 | tf_op jit(solution)/shard_map/jit(dynamic_index_in_dim)/dynamic_slice | solution.py:384
  61.9 1.9 %collective-permute-done.6 = f32[16,2,2,2,8,128]{5,4,2,1,0,3:T(8,128)} collective-permute-done((f32[16,2,2,2,8,128]{5,4,2,1,0,3:T(8,128)}, f32[16,2,2,2,8,128]{5,4,2,1,0,3:T(8,128)}, u32[]{:S(2)}, u32[]{:S(2)}) %collective-permute-start.6) | collective-permute-done | bytes 524320 | tf_op jit(solution)/shard_map/ppermute | solution.py:25
  63.7 1.1 bitcast_add_fusion
  64.9 2.5 %collective-permute-start.7 = (f32[16,2,2,8,128]{4,3,2,1,0:T(8,128)S(1)}, f32[16,2,2,8,128]{4,3,2,1,0:T(8,128)S(1)}, u32[]{:S(2)}, u32[]{:S(2)}) collective-permute-start(f32[16,2,2,8,128]{4,3,2,1,0:T(8,128)S(1)} %dynamic-slice_bitcast_fusion), channel_id=1, source_target_pairs={{0,2},{2,0},{4,6},{6,4},{8,10},{10,8},{12,14},{14,12},{1,3},{3,1},... | collective-permute-start | bytes 786440 | tf_op jit(solution)/shard_map/ppermute | solution.py:25
  67.3 6.8 %collective-permute-done.7 = f32[16,2,2,8,128]{4,3,2,1,0:T(8,128)S(1)} collective-permute-done((f32[16,2,2,8,128]{4,3,2,1,0:T(8,128)S(1)}, f32[16,2,2,8,128]{4,3,2,1,0:T(8,128)S(1)}, u32[]{:S(2)}, u32[]{:S(2)}) %collective-permute-start.7) | collective-permute-done | bytes 262176 | tf_op jit(solution)/shard_map/ppermute | solution.py:25
  74.2 3.8 %collective-permute-start.8 = (f32[16,2,8,128]{3,2,1,0:T(8,128)S(1)}, f32[16,2,8,128]{3,2,1,0:T(8,128)S(1)}, u32[]{:S(2)}, u32[]{:S(2)}) collective-permute-start(f32[16,2,8,128]{3,2,1,0:T(8,128)S(1)} %dynamic-slice_bitcast_fusion.1), channel_id=1, source_target_pairs={{0,8},{2,10},{4,12},{6,14},{8,0},{10,2},{12,4},{14,6},{1,9},{3,11}... | collective-permute-start | bytes 393224 | tf_op jit(solution)/shard_map/ppermute | solution.py:25
  78.1 1.4 %add_dynamic-update-slice_fusion = f32[4,2,256,256]{3,2,1,0:T(8,128)S(1)} fusion(f32[4,2,256,256]{3,2,1,0:T(8,128)S(1)} %copy-done.1, s32[]{:T(128)S(6)} %select_n.68, f32[4,2,256,128]{3,2,1,0:T(8,128)} %collective-permute-done.3), kind=kLoop, calls=%fused_computation.5 | loop fusion | flops 262144 | bytes 3145732 | tf_op jit(solution)/shard_map/dynamic_update_slice | solution.py:402
  80.4 1.3 %collective-permute-start.5 = (f32[4,2,64,256]{3,2,1,0:T(8,128)}, f32[4,2,64,256]{3,2,1,0:T(8,128)S(1)}, u32[]{:S(2)}, u32[]{:S(2)}) collective-permute-start(f32[4,2,64,256]{3,2,1,0:T(8,128)} %get-tuple-element.11), channel_id=1, source_target_pairs={{2,0},{4,2},{6,4},{8,6},{10,8},{12,10},{14,12},{3,1},{5,3},{7,5},{... | collective-permute-start | bytes 1572872 | tf_op jit(solution)/shard_map/ppermute | solution.py:20
  81.7 5.4 %collective-permute-start.4 = (f32[4,2,64,256]{3,2,1,0:T(8,128)S(1)}, f32[4,2,64,256]{3,2,1,0:T(8,128)}, u32[]{:S(2)}, u32[]{:S(2)}) collective-permute-start(f32[4,2,64,256]{3,2,1,0:T(8,128)S(1)} %get-tuple-element.10), channel_id=1, source_target_pairs={{0,2},{2,4},{4,6},{6,8},{8,10},{10,12},{12,14},{1,3},{3,5},{5,7},{... | collective-permute-start | bytes 1572872 | tf_op jit(solution)/shard_map/ppermute | solution.py:20
  89.5 7.5 %collective-permute-done.9 = f32[16,8,128]{2,1,0:T(8,128)S(1)} collective-permute-done((f32[16,8,128]{2,1,0:T(8,128)S(1)}, f32[16,8,128]{2,1,0:T(8,128)S(1)}, u32[]{:S(2)}, u32[]{:S(2)}) %collective-permute-start.9) | collective-permute-done | bytes 65568 | tf_op jit(solution)/shard_map/ppermute | solution.py:25
  97.7 1.7 %gram.1 = f32[32,32]{1,0:T(8,128)} custom-call(f32[16,1024]{1,0:T(8,128)} %bitcast.63, f32[16,1024]{1,0:T(8,128)} %bitcast.65), custom_call_target="tpu_custom_call" | custom-call | tf_op jit(solution)/shard_map/gram/pallas_call | solution.py:274
  99.4 1.4 %collective-permute-done.10 = f32[32,32]{1,0:T(8,128)S(1)} collective-permute-done((f32[32,32]{1,0:T(8,128)}, f32[32,32]{1,0:T(8,128)S(1)}, u32[]{:S(2)}, u32[]{:S(2)}) %collective-permute-start.10) | collective-permute-done | bytes 4128 | tf_op jit(solution)/shard_map/ppermute | solution.py:25
  101.5 2.4 %collective-permute-start.11 = (f32[32,32]{1,0:T(8,128)S(1)}, f32[32,32]{1,0:T(8,128)S(1)}, u32[]{:S(2)}, u32[]{:S(2)}) collective-permute-start(f32[32,32]{1,0:T(8,128)S(1)} %add.129), channel_id=1, source_target_pairs={{0,2},{2,0},{4,6},{6,4},{8,10},{10,8},{12,14},{14,12},{1,3},{3,1},... | collective-permute-start | bytes 12296 | tf_op jit(solution)/shard_map/ppermute | solution.py:25
  104.0 2.2 %collective-permute-done.11 = f32[32,32]{1,0:T(8,128)S(1)} collective-permute-done((f32[32,32]{1,0:T(8,128)S(1)}, f32[32,32]{1,0:T(8,128)S(1)}, u32[]{:S(2)}, u32[]{:S(2)}) %collective-permute-start.11) | collective-permute-done | bytes 4128 | tf_op jit(solution)/shard_map/ppermute | solution.py:25
  106.1 1.4 %collective-permute-start.12 = (f32[32,32]{1,0:T(8,128)S(1)}, f32[32,32]{1,0:T(8,128)S(1)}, u32[]{:S(2)}, u32[]{:S(2)}) collective-permute-start(f32[32,32]{1,0:T(8,128)S(1)} %add.130), channel_id=1, source_target_pairs={{0,8},{2,10},{4,12},{6,14},{8,0},{10,2},{12,4},{14,6},{1,9},{3,11}... | collective-permute-start | bytes 12296 | tf_op jit(solution)/shard_map/ppermute | solution.py:25
  107.5 3.3 %collective-permute-done.12 = f32[32,32]{1,0:T(8,128)S(1)} collective-permute-done((f32[32,32]{1,0:T(8,128)S(1)}, f32[32,32]{1,0:T(8,128)S(1)}, u32[]{:S(2)}, u32[]{:S(2)}) %collective-permute-start.12) | collective-permute-done | bytes 4128 | tf_op jit(solution)/shard_map/ppermute | solution.py:25
  110.8 2.7 %collective-permute-start.13 = (f32[32,32]{1,0:T(8,128)S(1)}, f32[32,32]{1,0:T(8,128)S(1)}, u32[]{:S(2)}, u32[]{:S(2)}) collective-permute-start(f32[32,32]{1,0:T(8,128)S(1)} %add.131), channel_id=1, source_target_pairs={{0,4},{2,6},{4,0},{6,2},{8,12},{10,14},{12,8},{14,10},{1,5},{3,7},... | collective-permute-start | bytes 12296 | tf_op jit(solution)/shard_map/ppermute | solution.py:25
  113.4 1.7 %collective-permute-done.13 = f32[32,32]{1,0:T(8,128)S(1)} collective-permute-done((f32[32,32]{1,0:T(8,128)S(1)}, f32[32,32]{1,0:T(8,128)S(1)}, u32[]{:S(2)}, u32[]{:S(2)}) %collective-permute-start.13) | collective-permute-done | bytes 4128 | tf_op jit(solution)/shard_map/ppermute | solution.py:25
  115.7 2.9 %ortho.1 = f32[16,1024]{1,0:T(8,128)} custom-call(f32[32,32]{1,0:T(8,128)} %add.132.refs_0_, f32[16,1024]{1,0:T(8,128)} %bitcast.64, f32[16,1024]{1,0:T(8,128)} %bitcast.66), custom_call_target="tpu_custom_call" | custom-call | tf_op jit(solution)/shard_map/ortho/pallas_call | solution.py:336
  118.6 1.5 %copy.43 = f32[2,8,1024]{2,0,1:T(2,128)} copy(f32[2,8,1024]{2,1,0:T(8,128)} %bitcast.67) | data formatting | bytes 131072 | tf_op jit(solution)/shard_map/reshape | solution.py:399
  120.1 2.2 %slice_add_fusion = f32[4,2,128,256]{3,2,1,0:T(8,128)} fusion(f32[4,2,256,256]{3,2,1,0:T(8,128)S(1)} %add_dynamic-update-slice_fusion, f32[4,2,64,256]{3,2,1,0:T(8,128)S(1)} %collective-permute-done.5, f32[4,2,64,256]{3,2,1,0:T(8,128)} %collective-permute-done.4), kind=kLoop, calls=%fused_computation.3 | loop fusion | flops 524288 | bytes 3145728 | tf_op jit(solution)/shard_map/add | solution.py:408
  (60 shorter events, 10.0 us)
Async XLA Ops:
  0.6 10.4 %copy-start = (f32[4,2,128,256]{3,2,1,0:T(8,128)S(1)}, f32[4,2,128,256]{3,2,1,0:T(8,128)}, u32[]{:S(2)}) copy-start(f32[4,2,128,256]{3,2,1,0:T(8,128)} %own.1) | copy-start | bytes 3145732
  0.6 8.6 %copy-start.5 = (f32[2,63]{1,0:T(2,128)S(1)}, f32[2,63]{1,0:T(2,128)}, u32[]{:S(2)}) copy-start(f32[2,63]{1,0:T(2,128)} %param.9) | copy-start | bytes 1516
  3.0 27.6 %collective-permute-start = (f32[4,2,64,256]{3,2,1,0:T(8,128)}, f32[4,2,64,256]{3,2,1,0:T(8,128)S(1)}, u32[]{:S(2)}, u32[]{:S(2)}) collective-permute-start(f32[4,2,64,256]{3,2,1,0:T(8,128)} %get-tuple-element.15), channel_id=1, source_target_pairs={{0,2},{2,4},{4,6},{6,8},{8,10},{10,12},{12,14},{1,3},{3,5},{5,7},{... | collective-permute-start | bytes 1572872 | tf_op jit(solution)/shard_map/ppermute | solution.py:20
  7.9 15.5 %collective-permute-start.1 = (f32[4,2,64,256]{3,2,1,0:T(8,128)}, f32[4,2,64,256]{3,2,1,0:T(8,128)S(1)}, u32[]{:S(2)}, u32[]{:S(2)}) collective-permute-start(f32[4,2,64,256]{3,2,1,0:T(8,128)} %get-tuple-element.14), channel_id=1, source_target_pairs={{2,0},{4,2},{6,4},{8,6},{10,8},{12,10},{14,12},{3,1},{5,3},{7,5},{... | collective-permute-start | bytes 1572872 | tf_op jit(solution)/shard_map/ppermute | solution.py:20
  23.4 8.6 %copy-start.4 = (f32[4,2,64,256]{3,2,1,0:T(8,128)}, f32[4,2,64,256]{3,2,1,0:T(8,128)S(1)}, u32[]{:S(2)}) copy-start(f32[4,2,64,256]{3,2,1,0:T(8,128)S(1)} %collective-permute-done.1.below) | copy-start | bytes 1572868
  30.6 3.2 %copy-start.3 = (f32[4,2,64,256]{3,2,1,0:T(8,128)}, f32[4,2,64,256]{3,2,1,0:T(8,128)S(1)}, u32[]{:S(2)}) copy-start(f32[4,2,64,256]{3,2,1,0:T(8,128)S(1)} %collective-permute-done.above) | copy-start | bytes 1572868
  30.6 5.0 %copy-start.6 = (s32[2,2]{1,0:T(2,128)S(1)}, s32[2,2]{1,0:T(2,128)}, u32[]{:S(2)}) copy-start(s32[2,2]{1,0:T(2,128)} %param.11) | copy-start | bytes 52
  30.7 5.6 %collective-permute-start.2 = (f32[4,2,256,128]{3,2,1,0:T(8,128)S(1)}, f32[4,2,256,128]{3,2,1,0:T(8,128)}, u32[]{:S(2)}, u32[]{:S(2)}) collective-permute-start(f32[4,2,256,128]{3,2,1,0:T(8,128)S(1)} %pad_maximum_fusion), channel_id=1, source_target_pairs={{0,1},{1,0},{2,3},{3,2},{4,5},{5,4},{6,7},{7,6},{8,9},{9,8},{10,11... | collective-permute-start | bytes 3145736 | tf_op jit(solution)/shard_map/ppermute | solution.py:25
  35.7 1.0 copy-start.2
  60.5 17.6 %copy-start.1 = (f32[4,2,256,256]{3,2,1,0:T(8,128)S(1)}, f32[4,2,256,256]{3,2,1,0:T(8,128)}, u32[]{:S(2)}) copy-start(f32[4,2,256,256]{3,2,1,0:T(8,128)} %get-tuple-element.5) | copy-start | bytes 6291460
  61.3 2.4 %collective-permute-start.6 = (f32[16,2,2,2,8,128]{5,4,2,1,0,3:T(8,128)}, f32[16,2,2,2,8,128]{5,4,2,1,0,3:T(8,128)}, u32[]{:S(2)}, u32[]{:S(2)}) collective-permute-start(f32[16,2,2,2,8,128]{5,4,2,1,0,3:T(8,128)} %bitcast.58), channel_id=1, source_target_pairs={{0,1},{1,0},{2,3},{3,2},{4,5},{5,4},{6,7},{7,6},{8,9},{9,8},{10,11... | collective-permute-start | bytes 1572872 | tf_op jit(solution)/shard_map/ppermute | solution.py:25
  61.8 16.2 %collective-permute-start.3 = (f32[4,2,256,128]{3,2,1,0:T(8,128)}, f32[4,2,256,128]{3,2,1,0:T(8,128)}, u32[]{:S(2)}, u32[]{:S(2)}) collective-permute-start(f32[4,2,256,128]{3,2,1,0:T(8,128)} %get-tuple-element.6), channel_id=1, source_target_pairs={{0,1},{1,0},{2,3},{3,2},{4,5},{5,4},{6,7},{7,6},{8,9},{9,8},{10,11... | collective-permute-start | bytes 3145736 | tf_op jit(solution)/shard_map/ppermute | solution.py:25
  64.9 9.3 %collective-permute-start.7 = (f32[16,2,2,8,128]{4,3,2,1,0:T(8,128)S(1)}, f32[16,2,2,8,128]{4,3,2,1,0:T(8,128)S(1)}, u32[]{:S(2)}, u32[]{:S(2)}) collective-permute-start(f32[16,2,2,8,128]{4,3,2,1,0:T(8,128)S(1)} %dynamic-slice_bitcast_fusion), channel_id=1, source_target_pairs={{0,2},{2,0},{4,6},{6,4},{8,10},{10,8},{12,14},{14,12},{1,3},{3,1},... | collective-permute-start | bytes 786440 | tf_op jit(solution)/shard_map/ppermute | solution.py:25
  74.2 12.8 %collective-permute-start.8 = (f32[16,2,8,128]{3,2,1,0:T(8,128)S(1)}, f32[16,2,8,128]{3,2,1,0:T(8,128)S(1)}, u32[]{:S(2)}, u32[]{:S(2)}) collective-permute-start(f32[16,2,8,128]{3,2,1,0:T(8,128)S(1)} %dynamic-slice_bitcast_fusion.1), channel_id=1, source_target_pairs={{0,8},{2,10},{4,12},{6,14},{8,0},{10,2},{12,4},{14,6},{1,9},{3,11}... | collective-permute-start | bytes 393224 | tf_op jit(solution)/shard_map/ppermute | solution.py:25
  80.4 39.7 %collective-permute-start.5 = (f32[4,2,64,256]{3,2,1,0:T(8,128)}, f32[4,2,64,256]{3,2,1,0:T(8,128)S(1)}, u32[]{:S(2)}, u32[]{:S(2)}) collective-permute-start(f32[4,2,64,256]{3,2,1,0:T(8,128)} %get-tuple-element.11), channel_id=1, source_target_pairs={{2,0},{4,2},{6,4},{8,6},{10,8},{12,10},{14,12},{3,1},{5,3},{7,5},{... | collective-permute-start | bytes 1572872 | tf_op jit(solution)/shard_map/ppermute | solution.py:20
  81.7 38.4 %collective-permute-start.4 = (f32[4,2,64,256]{3,2,1,0:T(8,128)S(1)}, f32[4,2,64,256]{3,2,1,0:T(8,128)}, u32[]{:S(2)}, u32[]{:S(2)}) collective-permute-start(f32[4,2,64,256]{3,2,1,0:T(8,128)S(1)} %get-tuple-element.10), channel_id=1, source_target_pairs={{0,2},{2,4},{4,6},{6,8},{8,10},{10,12},{12,14},{1,3},{3,5},{5,7},{... | collective-permute-start | bytes 1572872 | tf_op jit(solution)/shard_map/ppermute | solution.py:20
  87.1 9.9 %collective-permute-start.9 = (f32[16,8,128]{2,1,0:T(8,128)S(1)}, f32[16,8,128]{2,1,0:T(8,128)S(1)}, u32[]{:S(2)}, u32[]{:S(2)}) collective-permute-start(f32[16,8,128]{2,1,0:T(8,128)S(1)} %dynamic-slice_bitcast_fusion.2), channel_id=1, source_target_pairs={{0,4},{2,6},{4,0},{6,2},{8,12},{10,14},{12,8},{14,10},{1,5},{3,7},... | collective-permute-start | bytes 196616 | tf_op jit(solution)/shard_map/ppermute | solution.py:25
  99.4 1.4 %collective-permute-start.10 = (f32[32,32]{1,0:T(8,128)}, f32[32,32]{1,0:T(8,128)S(1)}, u32[]{:S(2)}, u32[]{:S(2)}) collective-permute-start(f32[32,32]{1,0:T(8,128)} %gram.1), channel_id=1, source_target_pairs={{0,1},{1,0},{2,3},{3,2},{4,5},{5,4},{6,7},{7,6},{8,9},{9,8},{10,11... | collective-permute-start | bytes 12296 | tf_op jit(solution)/shard_map/ppermute | solution.py:25
  101.5 4.6 %collective-permute-start.11 = (f32[32,32]{1,0:T(8,128)S(1)}, f32[32,32]{1,0:T(8,128)S(1)}, u32[]{:S(2)}, u32[]{:S(2)}) collective-permute-start(f32[32,32]{1,0:T(8,128)S(1)} %add.129), channel_id=1, source_target_pairs={{0,2},{2,0},{4,6},{6,4},{8,10},{10,8},{12,14},{14,12},{1,3},{3,1},... | collective-permute-start | bytes 12296 | tf_op jit(solution)/shard_map/ppermute | solution.py:25
  106.1 4.6 %collective-permute-start.12 = (f32[32,32]{1,0:T(8,128)S(1)}, f32[32,32]{1,0:T(8,128)S(1)}, u32[]{:S(2)}, u32[]{:S(2)}) collective-permute-start(f32[32,32]{1,0:T(8,128)S(1)} %add.130), channel_id=1, source_target_pairs={{0,8},{2,10},{4,12},{6,14},{8,0},{10,2},{12,4},{14,6},{1,9},{3,11}... | collective-permute-start | bytes 12296 | tf_op jit(solution)/shard_map/ppermute | solution.py:25
  110.8 4.4 %collective-permute-start.13 = (f32[32,32]{1,0:T(8,128)S(1)}, f32[32,32]{1,0:T(8,128)S(1)}, u32[]{:S(2)}, u32[]{:S(2)}) collective-permute-start(f32[32,32]{1,0:T(8,128)S(1)} %add.131), channel_id=1, source_target_pairs={{0,4},{2,6},{4,0},{6,2},{8,12},{10,14},{12,8},{14,10},{1,5},{3,7},... | collective-permute-start | bytes 12296 | tf_op jit(solution)/shard_map/ppermute | solution.py:25

commit v2 on v1

v2 whole, which is shorter than its diff:
```python
import math

import jax
import jax.numpy as jnp
import numpy as np
from jax import lax
from jax.experimental import pallas as pl
from jax.experimental.pallas import tpu as pltpu
from jax.sharding import PartitionSpec as P

F32 = jnp.float32
BF16 = jnp.bfloat16
LANES = 128
SUBLANES = 8


def shifted(value, axis, step):
    count = lax.axis_size(axis)
    pairs = [(i, i + step) for i in range(count) if 0 <= i + step < count]
    return lax.ppermute(value, axis, pairs)


def swapped(value, axis, bit):
    count = lax.axis_size(axis)
    return lax.ppermute(value, axis, [(i, i ^ bit) for i in range(count)])


def hi_lo(value):
    high = lax.reduce_precision(value, 8, 7)
    return high.astype(BF16), (value - high).astype(BF16)


def block_tables(taps, width):
    reach = taps.shape[1] // 2
    padded = jnp.pad(taps, ((0, 0), (width, width)))
    idx = lax.iota(jnp.int32, width)
    offset = idx[None, :] - idx[:, None] + reach
    tap_idx = lax.iota(jnp.int32, taps.shape[1])
    hot = (offset[None, :, :] == tap_idx[:, None, None]).astype(F32)
    band_re = jnp.sum(hot * taps[0][:, None, None], axis=0)
    band_im = jnp.sum(hot * taps[1][:, None, None], axis=0)
    phase = np.arange(width)[:, None] * np.arange(width)[None, :] % width
    angle = 2.0 * math.pi / width * phase
    norm = 1.0 / math.sqrt(width)
    dft_re = jnp.asarray(np.cos(angle) * norm, F32)
    dft_im = jnp.asarray(-np.sin(angle) * norm, F32)

    def block(re, im):
        return jnp.concatenate(
            [jnp.concatenate([re, -im], axis=1), jnp.concatenate([im, re], axis=1)], axis=0
        )

    band, dft = block(band_re, band_im), block(dft_re, dft_im)
    parts = []
    for matrix in (band, band.T, dft, dft.T):
        parts.extend(hi_lo(matrix))
    return jnp.stack(parts)


def split(value):
    high = value.astype(BF16)
    return high, (value - high.astype(F32)).astype(BF16)


def mxu(a, b):
    return lax.dot_general(a, b, (((1,), (0,)), ((), ())), preferred_element_type=F32)


def left_product(tab, which, x):
    high, low = split(x)
    w_high, w_low = tab[2 * which], tab[2 * which + 1]
    return mxu(w_high, high) + (mxu(w_high, low) + mxu(w_low, high))


def right_product(tab, which, x):
    high, low = split(x)
    w_high, w_low = tab[2 * which], tab[2 * which + 1]
    return mxu(high, w_high) + (mxu(low, w_high) + mxu(high, w_low))


def to_rows(y):
    n = LANES
    return jnp.concatenate(
        [
            jnp.concatenate([y[:n, :n], y[n:, :n]], axis=1),
            jnp.concatenate([y[:n, n:], y[n:, n:]], axis=1),
        ],
        axis=0,
    )


def two_sided(tab, forward, x):
    base, adjoint = forward
    return right_product(tab, adjoint, to_rows(left_product(tab, base, x)))


BAND, BAND_ADJ, DFT, DFT_ADJ = range(4)


def cut_windows(rec, places, side, own, above, below, beside, ext, patch):
    slices, _, tile_rows, tile_cols = own.shape
    half = above.shape[2]
    n = LANES

    @pl.when(rec == 0)
    def _():
        ext[:, :, :half, n : n + tile_cols] = above[...]
        ext[:, :, half : half + tile_rows, n : n + tile_cols] = own[...]
        ext[:, :, half + tile_rows :, n : n + tile_cols] = below[...]
        nothing = jnp.zeros(beside.shape, F32)

        @pl.when(side[0] == 0)
        def _():
            ext[:, :, :, :n] = nothing
            ext[:, :, :, n + tile_cols :] = beside[...]

        @pl.when(side[0] != 0)
        def _():
            ext[:, :, :, :n] = beside[...]
            ext[:, :, :, n + tile_cols :] = nothing

    row_tile, drop, lane_tile, shift = window_place(places, rec)
    for s in range(slices):
        for c in range(2):
            window = ext[s, c, pl.ds(row_tile, n + SUBLANES), pl.ds(lane_tile, 2 * n)]
            window = pltpu.roll(window, (2 * n - shift) % (2 * n), 1)[:, :n]
            patch[s, c] = pltpu.roll(window, (n + SUBLANES - drop) % (n + SUBLANES), 0)[:n]


def window_place(places, rec):
    row, col = places[rec, 0], places[rec, 1]
    lane_tile = pl.multiple_of(col // LANES * LANES, LANES)
    row_tile = pl.multiple_of(row // SUBLANES * SUBLANES, SUBLANES)
    return row_tile, row % SUBLANES, lane_tile, col % LANES


def through_slice(wave, patch, pair):
    obj_re, obj_im = patch[0], patch[1]
    res, ims = [], []
    for mode in (2 * pair, 2 * pair + 1):
        re, im = wave(mode)
        res.append(re * obj_re - im * obj_im)
        ims.append(re * obj_im + im * obj_re)
    return jnp.concatenate([jnp.concatenate(res, axis=1), jnp.concatenate(ims, axis=1)], axis=0)


def probe_waves(probe):
    return lambda mode: (probe[mode, 0], probe[mode, 1])


def row_waves(waves):
    n = LANES

    def wave(mode):
        block = waves[mode * n : (mode + 1) * n, :]
        return block[:, :n], block[:, n:]

    return wave


def forward_kernel(
    places, side, own, above, below, beside, probe, tab, waves, patches, ext
):
    rec = pl.program_id(0)
    n = LANES
    patch = patches.at[0]
    cut_windows(rec, places, side, own, above, below, beside, ext, patch)
    for s in range(own.shape[0]):
        wave = probe_waves(probe) if s == 0 else row_waves(waves.at[0, s - 1])
        for pair in range(probe.shape[0] // 2):
            x = through_slice(wave, patch.at[s], pair)
            z = two_sided(tab, (BAND, BAND_ADJ), x)
            waves[0, s, pair * 2 * n : (pair + 1) * 2 * n, :] = z


def backward_kernel(
    places, side, own, above, below, beside, probe, tab, measured, waves, patches,
    gown, gside, gprobe, ext, gext, last_patch, far, intensity, gpatch,
):
    rec = pl.program_id(0)
    modes = probe.shape[0]
    n = LANES
    tile_cols = own.shape[3]
    weight = 1.0 / (8.0 * modes)
    slices = waves.shape[1] + 1

    @pl.when(rec == 0)
    def _():
        gext[...] = jnp.zeros(gext.shape, F32)
        gprobe[...] = jnp.zeros(gprobe.shape, F32)

    cut_windows(rec, places, side, own, above, below, beside, ext, last_patch)
    row_tile, drop, lane_tile, shift = window_place(places, rec)

    def wave_into(s):
        return probe_waves(probe) if s == 0 else row_waves(waves.at[0, s - 1])

    def patch_of(s):
        return last_patch.at[0] if s + 1 == slices else patches.at[0, s]

    intensity[...] = jnp.zeros(intensity.shape, F32)
    for pair in range(modes // 2):
        x = through_slice(wave_into(slices - 1), patch_of(slices - 1), pair)
        z = two_sided(tab, (DFT, DFT_ADJ), x)
        far[pair * 2 * n : (pair + 1) * 2 * n, :] = z
        squares = z * z
        both = squares[:n] + squares[n:]
        intensity[...] += both[:, :n] + both[:, n:]

    factor = 2.0 * weight * (intensity[...] - measured[0])
    for pair in range(modes // 2):
        block = far[pair * 2 * n : (pair + 1) * 2 * n, :]
        scale = jnp.concatenate([jnp.concatenate([factor, factor], axis=1)] * 2, axis=0)
        far[pair * 2 * n : (pair + 1) * 2 * n, :] = two_sided(
            tab, (DFT_ADJ, DFT), to_rows(block * scale)
        )
    for s in reversed(range(slices)):
        patch = patch_of(s)
        obj_re, obj_im = patch[0], patch[1]
        wave = wave_into(s)
        for pair in range(modes // 2):
            res, ims = [], []
            sum_re = sum_im = None
            for mode in (2 * pair, 2 * pair + 1):
                g_re, g_im = row_waves(far)(mode)
                re, im = wave(mode)
                add_re = g_re * re + g_im * im
                add_im = g_im * re - g_re * im
                sum_re = add_re if sum_re is None else sum_re + add_re
                sum_im = add_im if sum_im is None else sum_im + add_im
                res.append(g_re * obj_re + g_im * obj_im)
                ims.append(g_im * obj_re - g_re * obj_im)
            if pair == 0:
                gpatch[0] = sum_re
                gpatch[1] = sum_im
            else:
                gpatch[0] += sum_re
                gpatch[1] += sum_im
            if s > 0:
                x = jnp.concatenate(
                    [jnp.concatenate(res, axis=1), jnp.concatenate(ims, axis=1)], axis=0
                )
                far[pair * 2 * n : (pair + 1) * 2 * n, :] = two_sided(tab, (BAND_ADJ, BAND), x)
            else:
                for k, mode in enumerate((2 * pair, 2 * pair + 1)):
                    for c, part in enumerate((res[k], ims[k])):
                        gprobe[:, c * modes + mode] += part.reshape(
                            n // SUBLANES, SUBLANES, n
                        )
        for c in range(2):
            tall = jnp.concatenate([gpatch[c], jnp.zeros((SUBLANES, n), F32)], axis=0)
            tall = pltpu.roll(tall, drop, 0)
            wide = jnp.concatenate([tall, jnp.zeros(tall.shape, F32)], axis=1)
            wide = pltpu.roll(wide, shift, 1)
            gext[s, c, pl.ds(row_tile, n + SUBLANES), pl.ds(lane_tile, 2 * n)] += wide

    @pl.when(rec == pl.num_programs(0) - 1)
    def _():
        gown[...] = gext[:, :, :, n : n + tile_cols]

        @pl.when(side[0] == 0)
        def _():
            gside[...] = gext[:, :, :, n + tile_cols :]

        @pl.when(side[0] != 0)
        def _():
            gside[...] = gext[:, :, :, :n]


def whole(shape):
    return pl.BlockSpec(shape, lambda r, *_: (0,) * len(shape))


def one_record(shape):
    return pl.BlockSpec((1,) + shape[1:], lambda r, *_: (r,) + (0,) * (len(shape) - 1))


def forward(places, side, objects, halo, probe, tab):
    above, below, beside = halo
    slices = above.shape[0]
    tile_rows, tile_cols = objects.shape[2:]
    modes, _, n, _ = probe.shape
    rows = tile_rows + 2 * above.shape[2]
    records = places.shape[0]
    outs = [(records, slices, modes * n, 2 * n), (records, slices, 2, n, n)]
    return pl.pallas_call(
        forward_kernel,
        out_shape=[jax.ShapeDtypeStruct(s, F32) for s in outs],
        grid_spec=pltpu.PrefetchScalarGridSpec(
            num_scalar_prefetch=2,
            grid=(records,),
            in_specs=[whole((slices,) + objects.shape[1:])]
            + [whole(x.shape) for x in (above, below, beside, probe, tab)],
            out_specs=[one_record(s) for s in outs],
            scratch_shapes=[pltpu.VMEM((slices, 2, rows, tile_cols + 2 * n), F32)],
        ),
        compiler_params=pltpu.CompilerParams(vmem_limit_bytes=56 << 20),
        name="forward",
    )(places, side, objects, above, below, beside, probe, tab)


def backward(places, side, objects, halo, probe, tab, measured, waves, patches):
    above, below, beside = halo
    slices, _, tile_rows, tile_cols = objects.shape
    modes, _, n, _ = probe.shape
    rows = tile_rows + 2 * above.shape[2]
    records = measured.shape[0]
    last = (1,) + objects.shape[1:]
    outs = [(slices, 2, rows, tile_cols), (slices, 2, rows, n)]
    outs.append((n // SUBLANES, 2 * modes, SUBLANES, n))
    return pl.pallas_call(
        backward_kernel,
        out_shape=[jax.ShapeDtypeStruct(s, F32) for s in outs],
        grid_spec=pltpu.PrefetchScalarGridSpec(
            num_scalar_prefetch=2,
            grid=(records,),
            in_specs=[pl.BlockSpec(last, lambda r, *_: (slices - 1, 0, 0, 0))]
            + [whole(x.shape) for x in (above, below, beside, probe, tab)]
            + [one_record(x.shape) for x in (measured, waves, patches)],
            out_specs=[whole(s) for s in outs],
            scratch_shapes=[
                pltpu.VMEM((1, 2, rows, tile_cols + 2 * n), F32),
                pltpu.VMEM((slices, 2, rows, tile_cols + 2 * n), F32),
                pltpu.VMEM((1, 2, n, n), F32),
                pltpu.VMEM((modes * n, 2 * n), F32),
                pltpu.VMEM((n, n), F32),
                pltpu.VMEM((2, n, n), F32),
            ],
        ),
        compiler_params=pltpu.CompilerParams(vmem_limit_bytes=56 << 20),
        name="backward",
    )(places, side, objects, above, below, beside, probe, tab, measured, waves, patches)


def gram_kernel(which, probe, first, second, out, own):
    total = None
    for b in range(probe.shape[0]):
        for i in range(probe.shape[2]):
            grad = first[b, :, i, :] + second[b, :, i, :]
            rows = jnp.concatenate([probe[b, :, i, :], grad], axis=0)
            one = lax.dot_general(
                rows, rows, (((1,), (1,)), ((), ())), precision=lax.Precision.HIGHEST,
                preferred_element_type=F32,
            )
            total = one if total is None else total + one
    out[...] = total
    own[...] = first[which[0]] + second[which[0]]


def gram(which, probe, first, second):
    rows = 2 * probe.shape[1]
    specs = [pl.BlockSpec(memory_space=pltpu.VMEM)] * 3
    return pl.pallas_call(
        gram_kernel,
        in_specs=[pl.BlockSpec(memory_space=pltpu.SMEM)] + specs,
        out_specs=[specs[0]] * 2,
        out_shape=[
            jax.ShapeDtypeStruct((rows, rows), F32),
            jax.ShapeDtypeStruct(probe.shape[1:], F32),
        ],
        name="gram",
    )(which, probe, first, second)


def ortho_kernel(*refs, modes, scale):
    *grams, probe, grad, out = refs
    m = modes
    s = grams[0][...]
    for other in grams[1:]:
        s = s + other[...]

    def part(a, b):
        return s[a * m : (a + 1) * m, b * m : (b + 1) * m]

    def complex_part(a, b):
        re = part(2 * a, 2 * b) + part(2 * a + 1, 2 * b + 1)
        im = part(2 * a, 2 * b + 1) - part(2 * a + 1, 2 * b)
        return re, im

    pp, pg, gp, gg = (complex_part(a, b) for a, b in ((0, 0), (0, 1), (1, 0), (1, 1)))
    eye = (
        lax.broadcasted_iota(jnp.int32, (m, m), 0) == lax.broadcasted_iota(jnp.int32, (m, m), 1)
    ).astype(F32)

    def trace(x):
        return jnp.sum(jnp.sum(x * eye, axis=1, keepdims=True), axis=0, keepdims=True)

    factor = 0.5 * jnp.sqrt(trace(pp[0]) / (trace(gg[0]) + 1e-06))
    new_re = pp[0] - factor * (pg[0] + gp[0]) + factor * factor * gg[0]
    new_im = pp[1] - factor * (pg[1] + gp[1]) + factor * factor * gg[1]
    a_re = jnp.concatenate([new_re, eye], axis=1)
    a_im = jnp.concatenate([new_im, jnp.zeros((m, m), F32)], axis=1)
    row_idx = lax.broadcasted_iota(jnp.int32, (m, 1), 0)
    for j in range(m):
        inv = 1.0 / jnp.sqrt(a_re[j : j + 1, j : j + 1])
        r_re = a_re[j : j + 1, :] * inv
        r_im = a_im[j : j + 1, :] * inv
        c_re = jnp.where(row_idx > j, a_re[:, j : j + 1] * inv, 0.0)
        c_im = jnp.where(row_idx > j, a_im[:, j : j + 1] * inv, 0.0)
        at = row_idx == j
        a_re, a_im = (
            jnp.where(at, r_re, a_re - (c_re * r_re - c_im * r_im)),
            jnp.where(at, r_im, a_im - (c_re * r_im + c_im * r_re)),
        )
    inv_re = a_re[:, m:] * scale
    inv_im = a_im[:, m:] * scale
    mix = jnp.concatenate(
        [
            jnp.concatenate([inv_re, inv_im], axis=1),
            jnp.concatenate([-inv_im, inv_re], axis=1),
        ],
        axis=0,
    )
    n = probe.shape[2]
    for i in range(probe.shape[1]):
        moved = probe[:, i, :] - factor * grad[:, i, :]
        new = lax.dot_general(
            mix, moved, (((1,), (0,)), ((), ())), precision=lax.Precision.HIGHEST,
            preferred_element_type=F32,
        )
        out[:, 0, i * n : (i + 1) * n] = new[:m]
        out[:, 1, i * n : (i + 1) * n] = new[m:]


def ortho(grams, probe, grad, modes, scale):
    def body(*refs):
        ortho_kernel(*refs, modes=modes, scale=scale)

    pixels = probe.shape[1] * probe.shape[2]
    return pl.pallas_call(
        body, out_shape=jax.ShapeDtypeStruct((modes, 2, pixels), F32), name="ortho"
    )(*grams, probe, grad)


def take(array, which, dim):
    return lax.dynamic_index_in_dim(array, which, dim, keepdims=False)


def updates(probe, grad, bottom, top, middle):
    modes, _, width, _ = probe.shape
    row_devices = lax.axis_size("row")
    col_devices = lax.axis_size("col")
    devices = row_devices * col_devices
    share = width // devices
    index = lax.axis_index("row") * col_devices + lax.axis_index("col")
    if share != SUBLANES:
        grad = grad.transpose(0, 2, 1, 3).reshape(devices, share, 2 * modes, width)
        grad = grad.transpose(0, 2, 1, 3)

    bits = devices.bit_length() - 1
    grad = grad.reshape((2,) * bits + (2 * modes, share, width))
    row_bits = [1 << b for b in range(bits - 1)]
    order = [("col", 1, 0)] + [("row", bit, bit.bit_length()) for bit in row_bits[1:]]
    left = list(range(bits))[::-1]
    parts = [grad]
    for axis, bit, place in order:
        dim = left.index(place)
        mine = (index >> place) % 2
        send = sum(take(p, 1 - mine, dim) for p in parts)
        keep = sum(take(p, mine, dim) for p in parts)
        received = swapped(send, axis, bit)
        left.pop(dim)
        if len(left) == bits - 2:
            received, bottom, top = lax.optimization_barrier((received, bottom, top))
        parts = [keep, received]
    from_above = shifted(bottom, "row", 1)
    from_below = shifted(top, "row", -1)
    first = sum(parts)
    second = swapped(first, "row", 1)
    mine = (index >> 1) % 2
    base = index - 2 * mine
    blocks = jnp.stack([
        lax.dynamic_slice_in_dim(probe, (base + 2 * k) * share, share, 2) for k in range(2)
    ])
    blocks = blocks.transpose(0, 2, 1, 3, 4).reshape(2, 2 * modes, share, width)
    total, own_grad = gram(mine.astype(jnp.int32).reshape(1), blocks, first, second)
    own_probe = take(blocks, mine, 0)
    left = row_bits[1:]
    while left:
        if len(left) > 1:
            a, b, *left = left
            total = (total + swapped(total, "row", a)) + (
                swapped(total, "row", b) + swapped(total, "row", a ^ b)
            )
        else:
            total = total + swapped(total, "row", left.pop())
    object_grad = middle + jnp.concatenate([from_above, from_below], axis=2)
    total, object_grad = lax.optimization_barrier((total, object_grad))
    grams = [total, swapped(total, "col", 1)]
    return ortho(grams, own_probe, own_grad, modes, float(width)), object_grad


def row_halo(objects, half):
    rows = objects.shape[2]
    above = shifted(objects[:, :, rows - half :], "row", 1)
    below = shifted(objects[:, :, :half], "row", -1)
    return above, below


def with_strip(objects, above, below, near):
    strip = jnp.concatenate([
        lax.dynamic_slice_in_dim(x, near, LANES, 3) for x in (above, objects, below)
    ], axis=2)
    return above, below, swapped(strip, "col", 1)


def per_device(object_slices, probe, taps, measured, positions):
    width = probe.shape[-1]
    half = width // 2
    slices, _, tile_rows, tile_cols = object_slices.shape
    row_idx = lax.axis_index("row")
    col_idx = lax.axis_index("col")
    near = (1 - col_idx) * (tile_cols - LANES)

    lead, last = object_slices[: slices - 1], object_slices[slices - 1 :]
    lead_rows = row_halo(lead, half)
    last_rows = row_halo(last, half)
    tab = block_tables(taps, width)
    anchor = jnp.stack([row_idx * tile_rows - half, col_idx * tile_cols - LANES])
    places = (positions - anchor[None, :]).astype(jnp.int32)
    side = col_idx.astype(jnp.int32).reshape(1)
    lead_rows, tab = lax.optimization_barrier((lead_rows, tab))
    waves, patches = forward(
        places, side, object_slices, with_strip(lead, *lead_rows, near), probe, tab
    )
    last_rows, waves = lax.optimization_barrier((last_rows, waves))
    gown, gside, gprobe = backward(
        places, side, object_slices, with_strip(last, *last_rows, near), probe, tab,
        measured, waves, patches,
    )

    got = swapped(gside, "col", 1)
    folded = lax.dynamic_update_slice_in_dim(
        gown, lax.dynamic_slice_in_dim(gown, near, LANES, 3) + got, near, 3
    )
    bottom, top = folded[:, :, half + tile_rows :], folded[:, :, :half]
    middle = folded[:, :, half : half + tile_rows]
    new_probe, object_grad = updates(probe, gprobe, bottom, top, middle)
    return (object_grad, new_probe)


def solution(mesh):
    placed = (
        P(None, None, ("groups", "row"), "col"),
        P("groups", None, None, None),
        P(),
        P(("groups", "row", "col"), None, None),
        P(("groups", "row", "col"), None),
    )
    return jax.shard_map(
        per_device,
        mesh=mesh,
        in_specs=placed,
        out_specs=(P(None, None, ("groups", "row"), "col"), P("groups", None, ("row", "col"))),
        check_vma=False,
    )
```

time: 123 us -> 134 us (1.089)
  Pallas kernels: 27.1 us -> 34.9 us
  waiting for transfers between devices: 44.2 us -> 36.5 us
  starting transfers between devices: 27 us -> 33 us
  local copies, waits for them, and re-layouts: 14.6 us -> 17.9 us
    ppermute x4 -> x6, waiting for transfers between devices: 19.4 us -> 7.59 us  [shifted(): return lax.ppermute(value, axis, pairs)]
    pallas_call x3 -> x4, Pallas kernels: 27.1 us -> 34.9 us  [the longest x1 18.5 us: backward(): pl.pallas_call(backward_kernel, out_shape=[jax.ShapeDtypeStruct(s, F32) f...]
    ppermute x10 -> x11, waiting for transfers between devices: 24.7 us -> 28.9 us  [swapped(): return lax.ppermute(value, axis, [(i, i ^ bit) for i in range(count)])]
    ppermute x4 -> x6, starting transfers between devices: 12.8 us -> 16.7 us  [shifted(): return lax.ppermute(value, axis, pairs)]
    squeeze x3 -> x2, local copies, waits for them, and re-layouts: 0.06 us -> 2.54 us  [take(): return lax.dynamic_index_in_dim(array, which, dim, keepdims=False)]
    unnamed x19 -> x29, local copies, waits for them, and re-layouts: 3.16 us -> 5.45 us
    reshape x4 -> x0, local copies, waits for them, and re-layouts: 2.24 us -> none  [the longest x1 1.52 us: per_device(): new_probe = new_rows.reshape(2, modes, share * width).transpose(1, 0, 2)]
    ppermute x10 -> x11, starting transfers between devices: 14.2 us -> 16.3 us  [swapped(): return lax.ppermute(value, axis, [(i, i ^ bit) for i in range(count)])]
  transfers between devices with their start and end apart: 14 -> 17, of which waited for: 9 -> 8; matrix products, arithmetic and copies ran while one was open for 13% -> 15% of each run, Pallas kernels for 4% -> 10%
where the time goes in v2:
time: 134 us; the launch traced here: 133 us
  waiting for transfers between devices  36.5 us (27%)
  Pallas kernels  34.9 us (26%)
  starting transfers between devices  33 us (25%)
  local copies, waits for them, and re-layouts  17.9 us (13%)
  other arithmetic  9.72 us (7%)
    ppermute x11, waiting for transfers between devices, swapped(): return lax.ppermute(value, axis, [(i, i ^ bit) for i in range(count)])  28.9 us
    pallas_call x1, Pallas kernels, backward(): pl.pallas_call(backward_kernel, out_shape=[jax.ShapeDtypeStruct(s, F32) f...  18.5 us
    ppermute x6, starting transfers between devices, shifted(): return lax.ppermute(value, axis, pairs)  16.7 us
    ppermute x11, starting transfers between devices, swapped(): return lax.ppermute(value, axis, [(i, i ^ bit) for i in range(count)])  16.3 us
    pallas_call x1, Pallas kernels, forward(): pl.pallas_call(forward_kernel, out_shape=[jax.ShapeDtypeStruct(s, F32) fo...  11.4 us
    ppermute x6, waiting for transfers between devices, shifted(): return lax.ppermute(value, axis, pairs)  7.59 us
    unnamed x29, local copies, waits for them, and re-layouts  5.45 us
    pallas_call x1, Pallas kernels, ortho(): pl.pallas_call(body, out_shape=jax.ShapeDtypeStruct((modes, 2, pixels), F...  2.92 us
  transfers between devices with their start and end apart: 17, of which 8 were waited for; matrix products, arithmetic and copies ran while one was open for 15% of the time, Pallas kernels for 10%

profile of v2, /device:TPU:0, one launch (start us, length us, event | category | flops | bytes accessed | tf_op | source)
XLA Modules:
  0.0 133.1 jit_solution(13031327573252731499)
XLA Ops:
  0.6 2.1 %fusion.5 = (f32[3,2,64,256]{3,2,1,0:T(8,128)}, f32[3,2,64,256]{3,2,1,0:T(8,128)}) fusion(f32[4,2,128,256]{3,2,1,0:T(8,128)} %own.3), kind=kLoop, calls=%fused_computation.49 | loop fusion | bytes 1572864 | tf_op jit(solution)/shard_map/slice | solution.py:496
  2.8 5.6 %collective-permute-start.2 = (f32[3,2,64,256]{3,2,1,0:T(8,128)}, f32[3,2,64,256]{3,2,1,0:T(8,128)}, u32[]{:S(2)}, u32[]{:S(2)}) collective-permute-start(f32[3,2,64,256]{3,2,1,0:T(8,128)} %get-tuple-element.45), channel_id=1, source_target_pairs={{0,2},{2,4},{4,6},{6,8},{8,10},{10,12},{12,14},{1,3},{3,5},{5,7},{... | collective-permute-start | bytes 1179656 | tf_op jit(solution)/shard_map/ppermute | solution.py:20
  8.4 1.3 collective-permute-start.3
  12.3 1.0 copy.26
  17.1 7.6 %collective-permute-done.2.above = f32[3,2,64,256]{3,2,1,0:T(8,128)} collective-permute-done((f32[3,2,64,256]{3,2,1,0:T(8,128)}, f32[3,2,64,256]{3,2,1,0:T(8,128)}, u32[]{:S(2)}, u32[]{:S(2)}) %collective-permute-start.2) | collective-permute-done | bytes 393248 | tf_op jit(solution)/shard_map/ppermute | solution.py:20
  24.7 1.0 constant_dynamic-slice_fusion.4
  26.6 4.4 %collective-permute-start = (f32[1,2,64,256]{3,2,1,0:T(8,128)}, f32[1,2,64,256]{3,2,1,0:T(8,128)S(1)}, u32[]{:S(2)}, u32[]{:S(2)}) collective-permute-start(f32[1,2,64,256]{3,2,1,0:T(8,128)} %get-tuple-element.47), channel_id=1, source_target_pairs={{0,2},{2,4},{4,6},{6,8},{8,10},{10,12},{12,14},{1,3},{3,5},{5,7},{... | collective-permute-start | bytes 393224 | tf_op jit(solution)/shard_map/ppermute | solution.py:20
  31.0 1.3 collective-permute-start.1
  33.0 11.4 %forward.1 = (f32[2,3,1024,256]{3,2,1,0:T(8,128)}, f32[2,3,2,128,128]{4,3,2,1,0:T(8,128)}) custom-call(s32[2,2]{1,0:T(2,128)} %broadcast_subtract_fusion.places, s32[1]{0:T(128)} %bitcast.7.side, f32[4,2,128,256]{3,2,1,0:T(8,128)} %own.3, f32[3,2,64,256]{3,2,1,0:T(8,128)} %collective-permute-done.2.above, f32[3,2,64,256]{3,2,1,0:T(8,128)} %collective-permute-done.3.below, ...), custom_call_target="tpu_custom_call" | custom-call | tf_op jit(solution)/shard_map/forward/pallas_call | solution.py:286
  44.7 1.4 %collective-permute-done.5.beside = f32[1,2,256,128]{3,2,1,0:T(8,128)S(1)} collective-permute-done((f32[1,2,256,128]{3,2,1,0:T(8,128)S(1)}, f32[1,2,256,128]{3,2,1,0:T(8,128)S(1)}, u32[]{:S(2)}, u32[]{:S(2)}) %collective-permute-start.5) | collective-permute-done | bytes 262176 | tf_op jit(solution)/shard_map/ppermute | solution.py:25
  46.8 18.5 %backward.1 = (f32[4,2,256,256]{3,2,1,0:T(8,128)}, f32[4,2,256,128]{3,2,1,0:T(8,128)}, f32[16,16,8,128]{3,2,1,0:T(8,128)}) custom-call(s32[2,2]{1,0:T(2,128)} %broadcast_subtract_fusion.places, s32[1]{0:T(128)} %bitcast.7.side, f32[4,2,128,256]{3,2,1,0:T(8,128)} %own.3, f32[1,2,64,256]{3,2,1,0:T(8,128)} %copy-done.4, f32[1,2,64,256]{3,2,1,0:T(8,128)} %copy-done.5, ...), custom_call_target="tpu_custom_call" | custom-call | tf_op jit(solution)/shard_map/backward/pallas_call | solution.py:311
  65.3 1.1 copy_bitcast_fusion
  66.9 1.8 %collective-permute-done.6 = f32[2,2,2,16,8,128]{5,4,3,2,0,1:T(8,128)S(1)} collective-permute-done((f32[2,2,2,16,8,128]{5,4,3,2,0,1:T(8,128)S(1)}, f32[2,2,2,16,8,128]{5,4,3,2,0,1:T(8,128)S(1)}, u32[]{:S(2)}, u32[]{:S(2)}) %collective-permute-start.6) | collective-permute-done | bytes 524320 | tf_op jit(solution)/shard_map/ppermute | solution.py:25
  68.6 1.1 bitcast_add_fusion.1
  69.7 4.5 %collective-permute-start.7 = (f32[2,2,16,8,128]{4,3,2,1,0:T(8,128)S(1)}, f32[2,2,16,8,128]{4,3,2,1,0:T(8,128)S(1)}, u32[]{:S(2)}, u32[]{:S(2)}) collective-permute-start(f32[2,2,16,8,128]{4,3,2,1,0:T(8,128)S(1)} %get-tuple-element.43), channel_id=1, source_target_pairs={{0,4},{2,6},{4,0},{6,2},{8,12},{10,14},{12,8},{14,10},{1,5},{3,7},... | collective-permute-start | bytes 786440 | tf_op jit(solution)/shard_map/ppermute | solution.py:25
  74.2 2.3 %add_dynamic-update-slice_fusion = f32[4,2,256,256]{3,2,1,0:T(8,128)} fusion(f32[4,2,256,256]{3,2,1,0:T(8,128)} %get-tuple-element.29, s32[]{:T(128)S(6)} %select_n.73, f32[4,2,256,128]{3,2,1,0:T(8,128)S(1)} %collective-permute-done.8), kind=kLoop, calls=%fused_computation.4 | loop fusion | flops 262144 | bytes 3145732 | tf_op jit(solution)/shard_map/dynamic_update_slice | solution.py:533
  76.6 1.4 %fusion.4 = (f32[4,2,64,256]{3,2,1,0:T(8,128)S(1)}, f32[4,2,64,256]{3,2,1,0:T(8,128)S(1)}) fusion(f32[4,2,256,256]{3,2,1,0:T(8,128)} %add_dynamic-update-slice_fusion), kind=kLoop, calls=%fused_computation.48 | loop fusion | bytes 2097152 | tf_op jit(solution)/shard_map/slice | solution.py:536
  78.0 2.8 %collective-permute-done.7 = f32[2,2,16,8,128]{4,3,2,1,0:T(8,128)S(1)} collective-permute-done((f32[2,2,16,8,128]{4,3,2,1,0:T(8,128)S(1)}, f32[2,2,16,8,128]{4,3,2,1,0:T(8,128)S(1)}, u32[]{:S(2)}, u32[]{:S(2)}) %collective-permute-start.7) | collective-permute-done | bytes 262176 | tf_op jit(solution)/shard_map/ppermute | solution.py:25
  81.6 2.9 %collective-permute-start.9 = (f32[2,16,8,128]{3,2,1,0:T(8,128)S(1)}, f32[2,16,8,128]{3,2,1,0:T(8,128)}, u32[]{:S(2)}, u32[]{:S(2)}) collective-permute-start(f32[2,16,8,128]{3,2,1,0:T(8,128)S(1)} %add_bitcast_fusion), channel_id=1, source_target_pairs={{0,8},{2,10},{4,12},{6,14},{8,0},{10,2},{12,4},{14,6},{1,9},{3,11}... | collective-permute-start | bytes 393224 | tf_op jit(solution)/shard_map/ppermute | solution.py:25
  84.5 2.9 %collective-permute-start.14 = (f32[4,2,64,256]{3,2,1,0:T(8,128)S(1)}, f32[4,2,64,256]{3,2,1,0:T(8,128)}, u32[]{:S(2)}, u32[]{:S(2)}) collective-permute-start(f32[4,2,64,256]{3,2,1,0:T(8,128)S(1)} %get-tuple-element.33), channel_id=1, source_target_pairs={{0,2},{2,4},{4,6},{6,8},{8,10},{10,12},{12,14},{1,3},{3,5},{5,7},{... | collective-permute-start | bytes 1572872 | tf_op jit(solution)/shard_map/ppermute | solution.py:20
  87.3 1.3 collective-permute-start.15
  88.6 1.9 %collective-permute-done.9 = f32[2,16,8,128]{3,2,1,0:T(8,128)} collective-permute-done((f32[2,16,8,128]{3,2,1,0:T(8,128)S(1)}, f32[2,16,8,128]{3,2,1,0:T(8,128)}, u32[]{:S(2)}, u32[]{:S(2)}) %collective-permute-start.9) | collective-permute-done | bytes 131104 | tf_op jit(solution)/shard_map/ppermute | solution.py:25
  90.5 1.0 bitcast_add_fusion.2.first
  94.0 17.0 %collective-permute-done.10.second = f32[2,16,8,128]{3,2,1,0:T(8,128)S(1)} collective-permute-done((f32[2,16,8,128]{3,2,1,0:T(8,128)S(1)}, f32[2,16,8,128]{3,2,1,0:T(8,128)S(1)}, u32[]{:S(2)}, u32[]{:S(2)}) %collective-permute-start.10) | collective-permute-done | bytes 131104 | tf_op jit(solution)/shard_map/ppermute | solution.py:25
  111.7 2.2 %gram.1 = (f32[32,32]{1,0:T(8,128)}, f32[16,8,128]{2,1,0:T(8,128)}) custom-call(s32[1]{0:T(128)} %bitcast.which, f32[2,16,8,128]{3,2,1,0:T(8,128)} %bitcast.60, f32[2,16,8,128]{3,2,1,0:T(8,128)} %copy-done.3, f32[2,16,8,128]{3,2,1,0:T(8,128)} %copy-done.8), custom_call_target="tpu_custom_call" | custom-call | tf_op jit(solution)/shard_map/gram/pallas_call | solution.py:353
  113.9 4.7 %collective-permute-start.11 = (f32[32,32]{1,0:T(8,128)}, f32[32,32]{1,0:T(8,128)S(1)}, u32[]{:S(2)}, u32[]{:S(2)}) collective-permute-start(f32[32,32]{1,0:T(8,128)} %get-tuple-element.32), channel_id=1, source_target_pairs={{0,4},{2,6},{4,0},{6,2},{8,12},{10,14},{12,8},{14,10},{1,5},{3,7},... | collective-permute-start | bytes 12296 | tf_op jit(solution)/shard_map/ppermute | solution.py:25
  119.3 1.7 %collective-permute-start.13 = (f32[32,32]{1,0:T(8,128)}, f32[32,32]{1,0:T(8,128)S(1)}, u32[]{:S(2)}, u32[]{:S(2)}) collective-permute-start(f32[32,32]{1,0:T(8,128)} %get-tuple-element.32), channel_id=1, source_target_pairs={{0,12},{2,14},{4,8},{6,10},{8,4},{10,6},{12,0},{14,2},{1,13},{3,15... | collective-permute-start | bytes 12296 | tf_op jit(solution)/shard_map/ppermute | solution.py:25
  121.0 2.5 %collective-permute-done.12 = f32[32,32]{1,0:T(8,128)S(1)} collective-permute-done((f32[32,32]{1,0:T(8,128)}, f32[32,32]{1,0:T(8,128)S(1)}, u32[]{:S(2)}, u32[]{:S(2)}) %collective-permute-start.12) | collective-permute-done | bytes 4128 | tf_op jit(solution)/shard_map/ppermute | solution.py:25
  123.4 1.6 %collective-permute-done.13 = f32[32,32]{1,0:T(8,128)S(1)} collective-permute-done((f32[32,32]{1,0:T(8,128)}, f32[32,32]{1,0:T(8,128)S(1)}, u32[]{:S(2)}, u32[]{:S(2)}) %collective-permute-start.13) | collective-permute-done | bytes 4128 | tf_op jit(solution)/shard_map/ppermute | solution.py:25
  125.8 2.3 %slice_add_fusion = f32[4,2,128,256]{3,2,1,0:T(8,128)} fusion(f32[4,2,256,256]{3,2,1,0:T(8,128)S(1)} %copy-done.2, f32[4,2,64,256]{3,2,1,0:T(8,128)} %collective-permute-done.15, f32[4,2,64,256]{3,2,1,0:T(8,128)} %collective-permute-done.14), kind=kLoop, calls=%fused_computation.3 | loop fusion | flops 524288 | bytes 3145728 | tf_op jit(solution)/shard_map/add | solution.py:487
  128.1 1.5 %dynamic-slice_bitcast_fusion.refs_2_ = f32[16,8,128]{2,1,0:T(8,128)} fusion(f32[2,16,8,128]{3,2,1,0:T(8,128)} %bitcast.61, s32[]{:T(128)S(6)} %select_n.86), kind=kLoop, calls=%fused_computation.26 | loop fusion | bytes 131076 | tf_op jit(solution)/shard_map/jit(dynamic_index_in_dim)/squeeze | solution.py:436
  130.1 2.9 %ortho.1 = f32[8,2,1024]{2,1,0:T(2,128)} custom-call(f32[32,32]{1,0:T(8,128)} %copy-done.9, f32[32,32]{1,0:T(8,128)} %copy-done.10, f32[16,8,128]{2,1,0:T(8,128)} %dynamic-slice_bitcast_fusion.refs_2_, f32[16,8,128]{2,1,0:T(8,128)} %get-tuple-element.37.refs_3_), custom_call_target="tpu_custom_call" | custom-call | tf_op jit(solution)/shard_map/ortho/pallas_call | solution.py:430
  (75 shorter events, 15.2 us)
Async XLA Ops:
  0.6 16.4 %slice-start = ((f32[4,2,128,256]{3,2,1,0:T(8,128)}), f32[3,2,128,256]{3,2,1,0:T(8,128)S(1)}, s32[]{:S(2)}) async-start(f32[4,2,128,256]{3,2,1,0:T(8,128)} %own.3), calls=%async_computation | async-start | bytes 1572864 | tf_op jit(solution)/shard_map/slice | solution.py:515
  2.8 21.9 %collective-permute-start.2 = (f32[3,2,64,256]{3,2,1,0:T(8,128)}, f32[3,2,64,256]{3,2,1,0:T(8,128)}, u32[]{:S(2)}, u32[]{:S(2)}) collective-permute-start(f32[3,2,64,256]{3,2,1,0:T(8,128)} %get-tuple-element.45), channel_id=1, source_target_pairs={{0,2},{2,4},{4,6},{6,8},{8,10},{10,12},{12,14},{1,3},{3,5},{5,7},{... | collective-permute-start | bytes 1179656 | tf_op jit(solution)/shard_map/ppermute | solution.py:20
  8.4 16.4 %collective-permute-start.3 = (f32[3,2,64,256]{3,2,1,0:T(8,128)}, f32[3,2,64,256]{3,2,1,0:T(8,128)}, u32[]{:S(2)}, u32[]{:S(2)}) collective-permute-start(f32[3,2,64,256]{3,2,1,0:T(8,128)} %get-tuple-element.44), channel_id=1, source_target_pairs={{2,0},{4,2},{6,4},{8,6},{10,8},{12,10},{14,12},{3,1},{5,3},{7,5},{... | collective-permute-start | bytes 1179656 | tf_op jit(solution)/shard_map/ppermute | solution.py:20
  11.4 14.5 %copy-start = (f32[4,2,128,256]{3,2,1,0:T(8,128)S(1)}, f32[4,2,128,256]{3,2,1,0:T(8,128)}, u32[]{:S(2)}) copy-start(f32[4,2,128,256]{3,2,1,0:T(8,128)} %own.3) | copy-start | bytes 3145732
  12.1 20.3 %copy-start.11 = (s32[2,2]{1,0:T(2,128)S(1)}, s32[2,2]{1,0:T(2,128)}, u32[]{:S(2)}) copy-start(s32[2,2]{1,0:T(2,128)} %param.11) | copy-start | bytes 52
  12.2 20.7 %slice-start.1 = ((f32[4,2,128,256]{3,2,1,0:T(8,128)}), f32[1,2,128,256]{3,2,1,0:T(8,128)S(1)}, s32[]{:S(2)}) async-start(f32[4,2,128,256]{3,2,1,0:T(8,128)} %own.3), calls=%async_computation.1 | async-start | bytes 524288 | tf_op jit(solution)/shard_map/slice | solution.py:515
  17.1 15.9 %copy-start.1 = (bf16[8,256,256]{2,1,0:T(8,128)(2,1)}, bf16[8,256,256]{2,1,0:T(8,128)(2,1)S(1)}, u32[]{:S(2)}) copy-start(bf16[8,256,256]{2,1,0:T(8,128)(2,1)S(1)} %constant_dynamic-update-slice_fusion.tab) | copy-start | bytes 3145732
  25.8 7.1 %collective-permute-start.4 = (f32[3,2,256,128]{3,2,1,0:T(8,128)S(1)}, f32[3,2,256,128]{3,2,1,0:T(8,128)}, u32[]{:S(2)}, u32[]{:S(2)}) collective-permute-start(f32[3,2,256,128]{3,2,1,0:T(8,128)S(1)} %pad_maximum_fusion), channel_id=1, source_target_pairs={{0,1},{1,0},{2,3},{3,2},{4,5},{5,4},{6,7},{7,6},{8,9},{9,8},{10,11... | collective-permute-start | bytes 2359304 | tf_op jit(solution)/shard_map/ppermute | solution.py:25
  26.6 17.7 %collective-permute-start = (f32[1,2,64,256]{3,2,1,0:T(8,128)}, f32[1,2,64,256]{3,2,1,0:T(8,128)S(1)}, u32[]{:S(2)}, u32[]{:S(2)}) collective-permute-start(f32[1,2,64,256]{3,2,1,0:T(8,128)} %get-tuple-element.47), channel_id=1, source_target_pairs={{0,2},{2,4},{4,6},{6,8},{8,10},{10,12},{12,14},{1,3},{3,5},{5,7},{... | collective-permute-start | bytes 393224 | tf_op jit(solution)/shard_map/ppermute | solution.py:20
  31.0 13.4 %collective-permute-start.1 = (f32[1,2,64,256]{3,2,1,0:T(8,128)S(1)}, f32[1,2,64,256]{3,2,1,0:T(8,128)S(1)}, u32[]{:S(2)}, u32[]{:S(2)}) collective-permute-start(f32[1,2,64,256]{3,2,1,0:T(8,128)S(1)} %get-tuple-element.46), channel_id=1, source_target_pairs={{2,0},{4,2},{6,4},{8,6},{10,8},{12,10},{14,12},{3,1},{5,3},{7,5},{... | collective-permute-start | bytes 393224 | tf_op jit(solution)/shard_map/ppermute | solution.py:20
  44.4 1.7 %copy-start.4 = (f32[1,2,64,256]{3,2,1,0:T(8,128)}, f32[1,2,64,256]{3,2,1,0:T(8,128)S(1)}, u32[]{:S(2)}) copy-start(f32[1,2,64,256]{3,2,1,0:T(8,128)S(1)} %collective-permute-done.above) | copy-start | bytes 393220
  44.4 1.7 %copy-start.5 = (f32[1,2,64,256]{3,2,1,0:T(8,128)}, f32[1,2,64,256]{3,2,1,0:T(8,128)S(1)}, u32[]{:S(2)}) copy-start(f32[1,2,64,256]{3,2,1,0:T(8,128)S(1)} %collective-permute-done.1.below) | copy-start | bytes 393220
  44.5 1.6 %collective-permute-start.5 = (f32[1,2,256,128]{3,2,1,0:T(8,128)S(1)}, f32[1,2,256,128]{3,2,1,0:T(8,128)S(1)}, u32[]{:S(2)}, u32[]{:S(2)}) collective-permute-start(f32[1,2,256,128]{3,2,1,0:T(8,128)S(1)} %pad_maximum_fusion.2), channel_id=1, source_target_pairs={{0,1},{1,0},{2,3},{3,2},{4,5},{5,4},{6,7},{7,6},{8,9},{9,8},{10,11... | collective-permute-start | bytes 786440 | tf_op jit(solution)/shard_map/ppermute | solution.py:25
  46.1 0.7 copy-start.6
  65.2 9.0 %collective-permute-start.8 = (f32[4,2,256,128]{3,2,1,0:T(8,128)}, f32[4,2,256,128]{3,2,1,0:T(8,128)S(1)}, u32[]{:S(2)}, u32[]{:S(2)}) collective-permute-start(f32[4,2,256,128]{3,2,1,0:T(8,128)} %get-tuple-element.30), channel_id=1, source_target_pairs={{0,1},{1,0},{2,3},{3,2},{4,5},{5,4},{6,7},{7,6},{8,9},{9,8},{10,11... | collective-permute-start | bytes 3145736 | tf_op jit(solution)/shard_map/ppermute | solution.py:25
  66.4 2.2 %collective-permute-start.6 = (f32[2,2,2,16,8,128]{5,4,3,2,0,1:T(8,128)S(1)}, f32[2,2,2,16,8,128]{5,4,3,2,0,1:T(8,128)S(1)}, u32[]{:S(2)}, u32[]{:S(2)}) collective-permute-start(f32[2,2,2,16,8,128]{5,4,3,2,0,1:T(8,128)S(1)} %copy_bitcast_fusion), channel_id=1, source_target_pairs={{0,1},{1,0},{2,3},{3,2},{4,5},{5,4},{6,7},{7,6},{8,9},{9,8},{10,11... | collective-permute-start | bytes 1572872 | tf_op jit(solution)/shard_map/ppermute | solution.py:25
  69.7 11.2 %collective-permute-start.7 = (f32[2,2,16,8,128]{4,3,2,1,0:T(8,128)S(1)}, f32[2,2,16,8,128]{4,3,2,1,0:T(8,128)S(1)}, u32[]{:S(2)}, u32[]{:S(2)}) collective-permute-start(f32[2,2,16,8,128]{4,3,2,1,0:T(8,128)S(1)} %get-tuple-element.43), channel_id=1, source_target_pairs={{0,4},{2,6},{4,0},{6,2},{8,12},{10,14},{12,8},{14,10},{1,5},{3,7},... | collective-permute-start | bytes 786440 | tf_op jit(solution)/shard_map/ppermute | solution.py:25
  76.6 49.2 %copy-start.2 = (f32[4,2,256,256]{3,2,1,0:T(8,128)S(1)}, f32[4,2,256,256]{3,2,1,0:T(8,128)}, u32[]{:S(2)}) copy-start(f32[4,2,256,256]{3,2,1,0:T(8,128)} %add_dynamic-update-slice_fusion) | copy-start | bytes 6291460
  80.9 0.7 copy-start.7
  81.6 8.9 %collective-permute-start.9 = (f32[2,16,8,128]{3,2,1,0:T(8,128)S(1)}, f32[2,16,8,128]{3,2,1,0:T(8,128)}, u32[]{:S(2)}, u32[]{:S(2)}) collective-permute-start(f32[2,16,8,128]{3,2,1,0:T(8,128)S(1)} %add_bitcast_fusion), channel_id=1, source_target_pairs={{0,8},{2,10},{4,12},{6,14},{8,0},{10,2},{12,4},{14,6},{1,9},{3,11}... | collective-permute-start | bytes 393224 | tf_op jit(solution)/shard_map/ppermute | solution.py:25
  84.5 41.3 %collective-permute-start.14 = (f32[4,2,64,256]{3,2,1,0:T(8,128)S(1)}, f32[4,2,64,256]{3,2,1,0:T(8,128)}, u32[]{:S(2)}, u32[]{:S(2)}) collective-permute-start(f32[4,2,64,256]{3,2,1,0:T(8,128)S(1)} %get-tuple-element.33), channel_id=1, source_target_pairs={{0,2},{2,4},{4,6},{6,8},{8,10},{10,12},{12,14},{1,3},{3,5},{5,7},{... | collective-permute-start | bytes 1572872 | tf_op jit(solution)/shard_map/ppermute | solution.py:20
  87.3 38.4 %collective-permute-start.15 = (f32[4,2,64,256]{3,2,1,0:T(8,128)S(1)}, f32[4,2,64,256]{3,2,1,0:T(8,128)}, u32[]{:S(2)}, u32[]{:S(2)}) collective-permute-start(f32[4,2,64,256]{3,2,1,0:T(8,128)S(1)} %get-tuple-element.34), channel_id=1, source_target_pairs={{2,0},{4,2},{6,4},{8,6},{10,8},{12,10},{14,12},{3,1},{5,3},{7,5},{... | collective-permute-start | bytes 1572872 | tf_op jit(solution)/shard_map/ppermute | solution.py:20
  91.5 20.2 %copy-start.3 = (f32[2,16,8,128]{3,2,1,0:T(8,128)}, f32[2,16,8,128]{3,2,1,0:T(8,128)S(1)}, u32[]{:S(2)}) copy-start(f32[2,16,8,128]{3,2,1,0:T(8,128)S(1)} %bitcast_add_fusion.2.first) | copy-start | bytes 393220
  91.5 19.5 %collective-permute-start.10 = (f32[2,16,8,128]{3,2,1,0:T(8,128)S(1)}, f32[2,16,8,128]{3,2,1,0:T(8,128)S(1)}, u32[]{:S(2)}, u32[]{:S(2)}) collective-permute-start(f32[2,16,8,128]{3,2,1,0:T(8,128)S(1)} %bitcast_add_fusion.2.first), channel_id=1, source_target_pairs={{0,2},{2,0},{4,6},{6,4},{8,10},{10,8},{12,14},{14,12},{1,3},{3,1},... | collective-permute-start | bytes 393224 | tf_op jit(solution)/shard_map/ppermute | solution.py:25
  111.0 0.6 copy-start.8
  113.9 7.1 %collective-permute-start.11 = (f32[32,32]{1,0:T(8,128)}, f32[32,32]{1,0:T(8,128)S(1)}, u32[]{:S(2)}, u32[]{:S(2)}) collective-permute-start(f32[32,32]{1,0:T(8,128)} %get-tuple-element.32), channel_id=1, source_target_pairs={{0,4},{2,6},{4,0},{6,2},{8,12},{10,14},{12,8},{14,10},{1,5},{3,7},... | collective-permute-start | bytes 12296 | tf_op jit(solution)/shard_map/ppermute | solution.py:25
  118.6 4.8 %collective-permute-start.12 = (f32[32,32]{1,0:T(8,128)}, f32[32,32]{1,0:T(8,128)S(1)}, u32[]{:S(2)}, u32[]{:S(2)}) collective-permute-start(f32[32,32]{1,0:T(8,128)} %get-tuple-element.32), channel_id=1, source_target_pairs={{0,8},{2,10},{4,12},{6,14},{8,0},{10,2},{12,4},{14,6},{1,9},{3,11}... | collective-permute-start | bytes 12296 | tf_op jit(solution)/shard_map/ppermute | solution.py:25
  119.3 5.7 %collective-permute-start.13 = (f32[32,32]{1,0:T(8,128)}, f32[32,32]{1,0:T(8,128)S(1)}, u32[]{:S(2)}, u32[]{:S(2)}) collective-permute-start(f32[32,32]{1,0:T(8,128)} %get-tuple-element.32), channel_id=1, source_target_pairs={{0,12},{2,14},{4,8},{6,10},{8,4},{10,6},{12,0},{14,2},{1,13},{3,15... | collective-permute-start | bytes 12296 | tf_op jit(solution)/shard_map/ppermute | solution.py:25
  125.7 3.8 %copy-start.9 = (f32[32,32]{1,0:T(8,128)}, f32[32,32]{1,0:T(8,128)S(1)}, u32[]{:S(2)}) copy-start(f32[32,32]{1,0:T(8,128)S(1)} %add_add_fusion.refs_0_) | copy-start | bytes 12292
  128.1 1.5 %collective-permute-start.16 = (f32[32,32]{1,0:T(8,128)S(1)}, f32[32,32]{1,0:T(8,128)S(1)}, u32[]{:S(2)}, u32[]{:S(2)}) collective-permute-start(f32[32,32]{1,0:T(8,128)S(1)} %add_add_fusion.refs_0_), channel_id=1, source_target_pairs={{0,1},{1,0},{2,3},{3,2},{4,5},{5,4},{6,7},{7,6},{8,9},{9,8},{10,11... | collective-permute-start | bytes 12296 | tf_op jit(solution)/shard_map/ppermute | solution.py:25
  129.5 0.6 copy-start.10

commit v3 on v1

--- a/solution.py
+++ b/solution.py
@@ -204,8 +204,10 @@
                 far[pair * 2 * n : (pair + 1) * 2 * n, :] = two_sided(tab, (BAND_ADJ, BAND), x)
             else:
                 for k, mode in enumerate((2 * pair, 2 * pair + 1)):
-                    gprobe[mode, 0] += res[k]
-                    gprobe[mode, 1] += ims[k]
+                    for c, part in enumerate((res[k], ims[k])):
+                        gprobe[:, c * modes + mode] += part.reshape(
+                            n // SUBLANES, SUBLANES, n
+                        )
         for c in range(2):
             tall = jnp.concatenate([gpatch[c], jnp.zeros((SUBLANES, n), F32)], axis=0)
             tall = pltpu.roll(tall, drop, 0)
@@ -236,7 +238,8 @@
         return pl.BlockSpec(shape, lambda r, *_: (0,) * len(shape))
 
     inputs = (own, above, below, beside, probe, tab)
-    outs = [(slices, 2, rows, tile_cols), (slices, 2, rows, n), (modes, 2, n, n)]
+    outs = [(slices, 2, rows, tile_cols), (slices, 2, rows, n)]
+    outs.append((n // SUBLANES, 2 * modes, SUBLANES, n))
     return pl.pallas_call(
         field_kernel,
         out_shape=[jax.ShapeDtypeStruct(s, F32) for s in outs],
@@ -261,24 +264,42 @@
     )(places, side, *inputs, measured)
 
 
-def gram_kernel(probe, grad, out):
-    rows = jnp.concatenate([probe[...], grad[...]], axis=0)
-    out[...] = lax.dot_general(
-        rows, rows, (((1,), (1,)), ((), ())), precision=lax.Precision.HIGHEST,
-        preferred_element_type=F32,
-    )
-
-
-def gram(probe, grad):
-    rows = probe.shape[0] + grad.shape[0]
+def gram_kernel(which, probe, first, second, out, own):
+    total = None
+    for b in range(probe.shape[0]):
+        for i in range(probe.shape[2]):
+            grad = first[b, :, i, :] + second[b, :, i, :]
+            rows = jnp.concatenate([probe[b, :, i, :], grad], axis=0)
+            one = lax.dot_general(
+                rows, rows, (((1,), (1,)), ((), ())), precision=lax.Precision.HIGHEST,
+                preferred_element_type=F32,
+            )
+            total = one if total is None else total + one
+    out[...] = total
+    own[...] = first[which[0]] + second[which[0]]
+
+
+def gram(which, probe, first, second):
+    rows = 2 * probe.shape[1]
+    specs = [pl.BlockSpec(memory_space=pltpu.VMEM)] * 3
     return pl.pallas_call(
-        gram_kernel, out_shape=jax.ShapeDtypeStruct((rows, rows), F32), name="gram"
-    )(probe, grad)
-
-
-def ortho_kernel(gram_ref, probe, grad, out, *, modes, scale):
+        gram_kernel,
+        in_specs=[pl.BlockSpec(memory_space=pltpu.SMEM)] + specs,
+        out_specs=[specs[0]] * 2,
+        out_shape=[
+            jax.ShapeDtypeStruct((rows, rows), F32),
+            jax.ShapeDtypeStruct(probe.shape[1:], F32),
+        ],
+        name="gram",
+    )(which, probe, first, second)
+
+
+def ortho_kernel(*refs, modes, scale):
+    *grams, probe, grad, out = refs
     m = modes
-    s = gram_ref[...]
+    s = grams[0][...]
+    for other in grams[1:]:
+        s = s + other[...]
 
     def part(a, b):
         return s[a * m : (a + 1) * m, b * m : (b + 1) * m]
@@ -315,7 +336,6 @@
         )
     inv_re = a_re[:, m:] * scale
     inv_im = a_im[:, m:] * scale
-    moved = probe[...] - factor * grad[...]
     mix = jnp.concatenate(
         [
             jnp.concatenate([inv_re, inv_im], axis=1),
@@ -323,40 +343,97 @@
         ],
         axis=0,
     )
-    out[...] = lax.dot_general(
-        mix, moved, (((1,), (0,)), ((), ())), precision=lax.Precision.HIGHEST,
-        preferred_element_type=F32,
-    )
-
-
-def ortho(gram_all, probe, grad, modes, scale):
+    n = probe.shape[2]
+    for i in range(probe.shape[1]):
+        moved = probe[:, i, :] - factor * grad[:, i, :]
+        new = lax.dot_general(
+            mix, moved, (((1,), (0,)), ((), ())), precision=lax.Precision.HIGHEST,
+            preferred_element_type=F32,
+        )
+        out[:, 0, i * n : (i + 1) * n] = new[:m]
+        out[:, 1, i * n : (i + 1) * n] = new[m:]
+
+
+def ortho(grams, probe, grad, modes, scale):
     def body(*refs):
         ortho_kernel(*refs, modes=modes, scale=scale)
 
+    pixels = probe.shape[1] * probe.shape[2]
     return pl.pallas_call(
-        body, out_shape=jax.ShapeDtypeStruct(probe.shape, F32), name="ortho"
-    )(gram_all, probe, grad)
+        body, out_shape=jax.ShapeDtypeStruct((modes, 2, pixels), F32), name="ortho"
+    )(*grams, probe, grad)
+
+
+def take(array, which, dim):
+    return lax.dynamic_index_in_dim(array, which, dim, keepdims=False)
+
+
+def updates(probe, grad, bottom, top, middle):
+    modes, _, width, _ = probe.shape
+    row_devices = lax.axis_size("row")
+    col_devices = lax.axis_size("col")
+    devices = row_devices * col_devices
+    share = width // devices
+    index = lax.axis_index("row") * col_devices + lax.axis_index("col")
+    if share != SUBLANES:
+        grad = grad.transpose(0, 2, 1, 3).reshape(devices, share, 2 * modes, width)
+        grad = grad.transpose(0, 2, 1, 3)
+
+    bits = devices.bit_length() - 1
+    grad = grad.reshape((2,) * bits + (2 * modes, share, width))
+    row_bits = [1 << b for b in range(bits - 1)]
+    order = [("col", 1, 0)] + [("row", bit, bit.bit_length()) for bit in row_bits[:-1]]
+    left = list(range(bits))[::-1]
+    parts = [grad]
+    for axis, bit, place in order:
+        dim = left.index(place)
+        mine = (index >> place) % 2
+        send = sum(take(p, 1 - mine, dim) for p in parts)
+        keep = sum(take(p, mine, dim) for p in parts)
+        received = swapped(send, axis, bit)
+        left.pop(dim)
+        if len(left) == bits - 2:
+            received, bottom, top = lax.optimization_barrier((received, bottom, top))
+        parts = [keep, received]
+    from_above = shifted(bottom, "row", 1)
+    from_below = shifted(top, "row", -1)
+    first = sum(parts)
+    second = swapped(first, "row", row_bits[-1])
+    place = left[0]
+    mine = (index >> place) % 2
+    base = index - (mine << place)
+    blocks = jnp.stack([
+        lax.dynamic_slice_in_dim(probe, (base + (k << place)) * share, share, 2) for k in range(2)
+    ])
+    blocks = blocks.transpose(0, 2, 1, 3, 4).reshape(2, 2 * modes, share, width)
+    total, own_grad = gram(mine.astype(jnp.int32).reshape(1), blocks, first, second)
+    own_probe = take(blocks, mine, 0)
+    total = total + swapped(total, "col", 1)
+    for bit in row_bits[-2:0:-1]:
+        total = total + swapped(total, "row", bit)
+    grams = [total, swapped(total, "row", 1)]
+    new_probe = ortho(grams, own_probe, own_grad, modes, float(width))
+    object_grad = middle() + jnp.concatenate([from_above, from_below], axis=2)
+    return new_probe, object_grad
 
 
 def per_device(object_slices, probe, taps, measured, positions):
     width = probe.shape[-1]
     half = width // 2
     slices, _, tile_rows, tile_cols = object_slices.shape
-    modes = probe.shape[0]
-    row_devices = lax.axis_size("row")
-    col_devices = lax.axis_size("col")
     row_idx = lax.axis_index("row")
     col_idx = lax.axis_index("col")
 
     above = shifted(object_slices[:, :, tile_rows - half :], "row", 1)
     below = shifted(object_slices[:, :, :half], "row", -1)
+    tab = block_tables(taps, width)
+    above, below, tab = lax.optimization_barrier((above, below, tab))
     near = (1 - col_idx) * (tile_cols - LANES)
     strip = jnp.concatenate([
         lax.dynamic_slice_in_dim(x, near, LANES, 3) for x in (above, object_slices, below)
     ], axis=2)
     beside = swapped(strip, "col", 1)
 
-    tab = block_tables(taps, width)
     anchor = jnp.stack([row_idx * tile_rows - half, col_idx * tile_cols - LANES])
     places = (positions - anchor[None, :]).astype(jnp.int32)
     side = col_idx.astype(jnp.int32).reshape(1)
@@ -364,48 +441,19 @@
         places, side, object_slices, above, below, beside, probe, tab, measured
     )
 
-    devices = row_devices * col_devices
-    share = width // devices
-    index = row_idx * col_devices + col_idx
-    total = gprobe.reshape(modes * 2, width, width)
-    lows = [("col", 1, 1)]
-    bit = 1
-    while bit < row_devices:
-        lows.append(("row", bit, bit * col_devices))
-        bit *= 2
-    span = width
-    lows = [lows[0], lows[1]] + lows[:1:-1]
-    shape = (modes * 2,) + (2,) * len(lows) + (share, width)
-    total = total.reshape(shape)
-    dims = list(range(len(lows) - 1, -1, -1))
-    for axis, bit, global_bit in lows:
-        which = dims.index(global_bit.bit_length() - 1)
-        mine = (index // global_bit) % 2
-        keep = lax.dynamic_index_in_dim(total, mine, which + 1, keepdims=False)
-        send = lax.dynamic_index_in_dim(total, 1 - mine, which + 1, keepdims=False)
-        total = keep + swapped(send, axis, bit)
-        dims.pop(which)
-
-    def by_part(x):
-        return x.reshape(modes, 2, share * width).transpose(1, 0, 2).reshape(2 * modes, -1)
-
-    own_probe = lax.dynamic_slice_in_dim(probe, index * share, share, 2)
-    p_rows = by_part(own_probe)
-    g_rows = by_part(total)
-    gram_all = gram(p_rows, g_rows)
-    for axis, bit, _ in lows:
-        gram_all = gram_all + swapped(gram_all, axis, bit)
-    new_rows = ortho(gram_all, p_rows, g_rows, modes, float(width))
-    new_probe = new_rows.reshape(2, modes, share * width).transpose(1, 0, 2)
-
     got = swapped(gside, "col", 1)
-    folded = lax.dynamic_update_slice_in_dim(
-        gown, lax.dynamic_slice_in_dim(gown, near, LANES, 3) + got, near, 3
-    )
-    from_above = shifted(folded[:, :, half + tile_rows :], "row", 1)
-    from_below = shifted(folded[:, :, :half], "row", -1)
-    middle = folded[:, :, half : half + tile_rows]
-    object_grad = middle + jnp.concatenate([from_above, from_below], axis=2)
+
+    def folded(first, last):
+        part = got[:, :, first:last]
+        low = jnp.where(col_idx == 0, 0.0, part)
+        high = jnp.where(col_idx == 0, part, 0.0)
+        inner = jnp.zeros(part.shape[:3] + (tile_cols - 2 * LANES,), F32)
+        return gown[:, :, first:last] + jnp.concatenate([low, inner, high], axis=3)
+
+    bottom, top = folded(half + tile_rows, tile_rows + 2 * half), folded(0, half)
+    new_probe, object_grad = updates(
+        probe, gprobe, bottom, top, lambda: folded(half, half + tile_rows)
+    )
     return (object_grad, new_probe)
 
 

time: 123 us -> 119 us (0.967)
  starting transfers between devices: 27 us -> 21.3 us
  other arithmetic: 8.38 us -> 9.84 us
    ppermute x4, waiting for transfers between devices: 19.4 us -> 14.7 us  [shifted(): return lax.ppermute(value, axis, pairs)]
    ppermute x10 -> x9, waiting for transfers between devices: 24.7 us -> 28.5 us  [swapped(): return lax.ppermute(value, axis, [(i, i ^ bit) for i in range(count)])]
    ppermute x10 -> x9, starting transfers between devices: 14.2 us -> 10.6 us  [swapped(): return lax.ppermute(value, axis, [(i, i ^ bit) for i in range(count)])]
    squeeze x3 -> x2, local copies, waits for them, and re-layouts: 0.06 us -> 3.35 us  [take(): return lax.dynamic_index_in_dim(array, which, dim, keepdims=False)]
    reshape x4 -> x0, local copies, waits for them, and re-layouts: 2.24 us -> none  [the longest x1 1.52 us: per_device(): new_probe = new_rows.reshape(2, modes, share * width).transpose(1, 0, 2)]
    ppermute x4, starting transfers between devices: 12.8 us -> 10.7 us  [shifted(): return lax.ppermute(value, axis, pairs)]
    dynamic_slice x3 -> x1, local copies, waits for them, and re-layouts: 2.98 us -> 1.21 us  [take(): return lax.dynamic_index_in_dim(array, which, dim, keepdims=False)]
    add x9 -> x7, other arithmetic: 4.67 us -> 6.3 us  [the longest x1 2.34 us: updates(): object_grad = middle() + jnp.concatenate([from_above, from_below], axis=2)]
  transfers between devices with their start and end apart: 14 -> 13, of which waited for: 9 -> 8; matrix products, arithmetic and copies ran while one was open for 13% -> 16% of each run, Pallas kernels for 4% -> 4%
where the time goes in v3:
time: 119 us; the launch traced here: 118 us
  waiting for transfers between devices  43.2 us (36%)
  Pallas kernels  27.7 us (23%)
  starting transfers between devices  21.3 us (18%)
  local copies, waits for them, and re-layouts  15.5 us (13%)
  other arithmetic  9.84 us (8%)
    ppermute x9, waiting for transfers between devices, swapped(): return lax.ppermute(value, axis, [(i, i ^ bit) for i in range(count)])  28.5 us
    pallas_call x1, Pallas kernels, fields(): pl.pallas_call(field_kernel, out_shape=[jax.ShapeDtypeStruct(s, F32) for...  22.6 us
    ppermute x4, waiting for transfers between devices, shifted(): return lax.ppermute(value, axis, pairs)  14.7 us
    ppermute x4, starting transfers between devices, shifted(): return lax.ppermute(value, axis, pairs)  10.7 us
    ppermute x9, starting transfers between devices, swapped(): return lax.ppermute(value, axis, [(i, i ^ bit) for i in range(count)])  10.6 us
    unnamed x31, local copies, waits for them, and re-layouts  4.78 us
    squeeze x2, local copies, waits for them, and re-layouts, take(): return lax.dynamic_index_in_dim(array, which, dim, keepdims=False)  3.35 us
    pallas_call x1, Pallas kernels, ortho(): pl.pallas_call(body, out_shape=jax.ShapeDtypeStruct((modes, 2, pixels), F...  2.92 us
  transfers between devices with their start and end apart: 13, of which 8 were waited for; matrix products, arithmetic and copies ran while one was open for 16% of the time, Pallas kernels for 4%

profile of v3, /device:TPU:0, one launch (start us, length us, event | category | flops | bytes accessed | tf_op | source)
XLA Modules:
  0.0 118.4 jit_solution(2188891195249344334)
XLA Ops:
  0.6 2.3 %fusion.7 = (f32[4,2,64,256]{3,2,1,0:T(8,128)}, f32[4,2,64,256]{3,2,1,0:T(8,128)}) fusion(f32[4,2,128,256]{3,2,1,0:T(8,128)} %own.1), kind=kLoop, calls=%fused_computation.55 | loop fusion | bytes 2097152 | tf_op jit(solution)/shard_map/slice | solution.py:428
  2.9 4.9 %collective-permute-start = (f32[4,2,64,256]{3,2,1,0:T(8,128)}, f32[4,2,64,256]{3,2,1,0:T(8,128)S(1)}, u32[]{:S(2)}, u32[]{:S(2)}) collective-permute-start(f32[4,2,64,256]{3,2,1,0:T(8,128)} %get-tuple-element.39), channel_id=1, source_target_pairs={{0,2},{2,4},{4,6},{6,8},{8,10},{10,12},{12,14},{1,3},{3,5},{5,7},{... | collective-permute-start | bytes 1572872 | tf_op jit(solution)/shard_map/ppermute | solution.py:20
  7.8 1.3 %collective-permute-start.1 = (f32[4,2,64,256]{3,2,1,0:T(8,128)}, f32[4,2,64,256]{3,2,1,0:T(8,128)S(1)}, u32[]{:S(2)}, u32[]{:S(2)}) collective-permute-start(f32[4,2,64,256]{3,2,1,0:T(8,128)} %get-tuple-element.38), channel_id=1, source_target_pairs={{2,0},{4,2},{6,4},{8,6},{10,8},{12,10},{14,12},{3,1},{5,3},{7,5},{... | collective-permute-start | bytes 1572872 | tf_op jit(solution)/shard_map/ppermute | solution.py:20
  11.0 1.0 copy.25
  12.0 0.9 constant_dynamic-update-slice_fusion.3
  13.0 0.9 constant_dynamic-update-slice_fusion.2
  13.9 0.9 constant_dynamic-update-slice_fusion.1
  14.8 0.9 constant_dynamic-update-slice_fusion.tab
  15.8 14.7 %collective-permute-done.above = f32[4,2,64,256]{3,2,1,0:T(8,128)S(1)} collective-permute-done((f32[4,2,64,256]{3,2,1,0:T(8,128)}, f32[4,2,64,256]{3,2,1,0:T(8,128)S(1)}, u32[]{:S(2)}, u32[]{:S(2)}) %collective-permute-start) | collective-permute-done | bytes 524320 | tf_op jit(solution)/shard_map/ppermute | solution.py:20
  31.4 2.1 %collective-permute-done.2.beside = f32[4,2,256,128]{3,2,1,0:T(8,128)} collective-permute-done((f32[4,2,256,128]{3,2,1,0:T(8,128)S(1)}, f32[4,2,256,128]{3,2,1,0:T(8,128)}, u32[]{:S(2)}, u32[]{:S(2)}) %collective-permute-start.2) | collective-permute-done | bytes 1048608 | tf_op jit(solution)/shard_map/ppermute | solution.py:25
  33.5 22.6 %fields.1 = (f32[4,2,256,256]{3,2,1,0:T(8,128)}, f32[4,2,256,128]{3,2,1,0:T(8,128)}, f32[16,16,8,128]{3,2,1,0:T(8,128)}) custom-call(s32[2,2]{1,0:T(2,128)} %broadcast_subtract_fusion.places, s32[1]{0:T(128)} %bitcast.2.side, f32[4,2,128,256]{3,2,1,0:T(8,128)} %own.1, f32[4,2,64,256]{3,2,1,0:T(8,128)} %copy-done.3, f32[4,2,64,256]{3,2,1,0:T(8,128)} %copy-done.4, ...), custom_call_target="tpu_custom_call" | custom-call | tf_op jit(solution)/shard_map/fields/pallas_call | solution.py:243
  56.3 1.9 %copy_bitcast_fusion = f32[2,2,2,16,8,128]{5,4,3,0,1,2:T(8,128)} fusion(f32[2,2,2,2,16,8,128]{6,5,4,3,2,1,0:T(8,128)} %bitcast.58, s32[]{:T(128)S(6)} %select_n.111), kind=kLoop, calls=%fused_computation.8 | loop fusion | bytes 1048580 | tf_op jit(solution)/shard_map/jit(dynamic_index_in_dim)/squeeze | solution.py:368
  58.5 1.2 %constant_dynamic-slice_fusion = (f32[2,2,1,1,16,8,128]{6,5,4,3,2,1,0:T(8,128)S(1)}, f32[2,2,1,1,16,8,128]{6,5,4,3,2,1,0:T(8,128)S(1)}) fusion(f32[2,2,2,2,16,8,128]{6,5,4,3,2,1,0:T(8,128)} %bitcast.59, s32[]{:T(128)S(6)} %select_n.121, s32[]{:T(128)S(6)} %select_n.110, s32[]{:T(128)S(6)} %select_n.107), kind=kLoop, calls=%fused_computation.45 | loop fusion | bytes 1048588 | tf_op jit(solution)/shard_map/jit(dynamic_index_in_dim)/dynamic_slice | solution.py:368
  60.4 1.1 fusion.3
  61.5 2.5 %collective-permute-start.5 = (f32[2,2,16,8,128]{4,3,2,0,1:T(8,128)S(1)}, f32[2,2,16,8,128]{4,3,2,0,1:T(8,128)S(1)}, u32[]{:S(2)}, u32[]{:S(2)}) collective-permute-start(f32[2,2,16,8,128]{4,3,2,0,1:T(8,128)S(1)} %get-tuple-element.41), channel_id=1, source_target_pairs={{0,2},{2,0},{4,6},{6,4},{8,10},{10,8},{12,14},{14,12},{1,3},{3,1},... | collective-permute-start | bytes 786440 | tf_op jit(solution)/shard_map/ppermute | solution.py:25
  64.1 1.2 maximum_add_fusion.2
  65.3 5.5 %collective-permute-done.5 = f32[2,2,16,8,128]{4,3,2,0,1:T(8,128)S(1)} collective-permute-done((f32[2,2,16,8,128]{4,3,2,0,1:T(8,128)S(1)}, f32[2,2,16,8,128]{4,3,2,0,1:T(8,128)S(1)}, u32[]{:S(2)}, u32[]{:S(2)}) %collective-permute-start.5) | collective-permute-done | bytes 262176 | tf_op jit(solution)/shard_map/ppermute | solution.py:25
  71.5 2.8 %collective-permute-start.8 = (f32[2,16,8,128]{3,2,1,0:T(8,128)S(1)}, f32[2,16,8,128]{3,2,1,0:T(8,128)S(1)}, u32[]{:S(2)}, u32[]{:S(2)}) collective-permute-start(f32[2,16,8,128]{3,2,1,0:T(8,128)S(1)} %add_bitcast_fusion), channel_id=1, source_target_pairs={{0,4},{2,6},{4,0},{6,2},{8,12},{10,14},{12,8},{14,10},{1,5},{3,7},... | collective-permute-start | bytes 393224 | tf_op jit(solution)/shard_map/ppermute | solution.py:25
  74.3 3.2 %collective-permute-start.6 = (f32[4,2,64,256]{3,2,1,0:T(8,128)}, f32[4,2,64,256]{3,2,1,0:T(8,128)}, u32[]{:S(2)}, u32[]{:S(2)}) collective-permute-start(f32[4,2,64,256]{3,2,1,0:T(8,128)} %get-tuple-element.19), channel_id=1, source_target_pairs={{0,2},{2,4},{4,6},{6,8},{8,10},{10,12},{12,14},{1,3},{3,5},{5,7},{... | collective-permute-start | bytes 1572872 | tf_op jit(solution)/shard_map/ppermute | solution.py:20
  77.5 1.3 %collective-permute-start.7 = (f32[4,2,64,256]{3,2,1,0:T(8,128)}, f32[4,2,64,256]{3,2,1,0:T(8,128)}, u32[]{:S(2)}, u32[]{:S(2)}) collective-permute-start(f32[4,2,64,256]{3,2,1,0:T(8,128)} %get-tuple-element.20), channel_id=1, source_target_pairs={{2,0},{4,2},{6,4},{8,6},{10,8},{12,10},{14,12},{3,1},{5,3},{7,5},{... | collective-permute-start | bytes 1572872 | tf_op jit(solution)/shard_map/ppermute | solution.py:20
  78.8 0.9 bitcast_add_fusion.first
  79.8 4.8 %collective-permute-start.9 = (f32[2,16,8,128]{3,2,1,0:T(8,128)S(1)}, f32[2,16,8,128]{3,2,1,0:T(8,128)S(1)}, u32[]{:S(2)}, u32[]{:S(2)}) collective-permute-start(f32[2,16,8,128]{3,2,1,0:T(8,128)S(1)} %bitcast_add_fusion.first), channel_id=1, source_target_pairs={{0,8},{2,10},{4,12},{6,14},{8,0},{10,2},{12,4},{14,6},{1,9},{3,11}... | collective-permute-start | bytes 393224 | tf_op jit(solution)/shard_map/ppermute | solution.py:25
  84.5 0.9 dynamic-slice_bitcast_fusion.2
  86.1 14.0 %collective-permute-done.9.second = f32[2,16,8,128]{3,2,1,0:T(8,128)S(1)} collective-permute-done((f32[2,16,8,128]{3,2,1,0:T(8,128)S(1)}, f32[2,16,8,128]{3,2,1,0:T(8,128)S(1)}, u32[]{:S(2)}, u32[]{:S(2)}) %collective-permute-start.9) | collective-permute-done | bytes 131104 | tf_op jit(solution)/shard_map/ppermute | solution.py:25
  100.7 2.2 %gram.1 = (f32[32,32]{1,0:T(8,128)}, f32[16,8,128]{2,1,0:T(8,128)}) custom-call(s32[1]{0:T(128)} %bitcast.14.which, f32[2,16,8,128]{3,2,1,0:T(8,128)} %bitcast.60, f32[2,16,8,128]{3,2,1,0:T(8,128)} %copy-done.6, f32[2,16,8,128]{3,2,1,0:T(8,128)} %copy-done.8), custom_call_target="tpu_custom_call" | custom-call | tf_op jit(solution)/shard_map/gram/pallas_call | solution.py:285
  102.9 1.4 %collective-permute-done.10 = f32[32,32]{1,0:T(8,128)S(1)} collective-permute-done((f32[32,32]{1,0:T(8,128)}, f32[32,32]{1,0:T(8,128)S(1)}, u32[]{:S(2)}, u32[]{:S(2)}) %collective-permute-start.10) | collective-permute-done | bytes 4128 | tf_op jit(solution)/shard_map/ppermute | solution.py:25
  105.1 1.5 %dynamic-slice_bitcast_fusion.refs_2_ = f32[16,8,128]{2,1,0:T(8,128)} fusion(f32[2,16,8,128]{3,2,1,0:T(8,128)} %bitcast.61, s32[]{:T(128)S(6)} %select_n.125), kind=kLoop, calls=%fused_computation.35 | loop fusion | bytes 131076 | tf_op jit(solution)/shard_map/jit(dynamic_index_in_dim)/squeeze | solution.py:368
  106.5 2.3 %collective-permute-done.11 = f32[32,32]{1,0:T(8,128)S(1)} collective-permute-done((f32[32,32]{1,0:T(8,128)S(1)}, f32[32,32]{1,0:T(8,128)S(1)}, u32[]{:S(2)}, u32[]{:S(2)}) %collective-permute-start.11) | collective-permute-done | bytes 4128 | tf_op jit(solution)/shard_map/ppermute | solution.py:25
  108.8 1.1 slice_select_fusion.1
  110.0 2.6 %collective-permute-done.12.refs_1_ = f32[32,32]{1,0:T(8,128)S(1)} collective-permute-done((f32[32,32]{1,0:T(8,128)S(1)}, f32[32,32]{1,0:T(8,128)S(1)}, u32[]{:S(2)}, u32[]{:S(2)}) %collective-permute-start.12) | collective-permute-done | bytes 4128 | tf_op jit(solution)/shard_map/ppermute | solution.py:25
  113.1 2.9 %ortho.1 = f32[8,2,1024]{2,1,0:T(2,128)} custom-call(f32[32,32]{1,0:T(8,128)} %copy-done.9, f32[32,32]{1,0:T(8,128)} %copy-done.10, f32[16,8,128]{2,1,0:T(8,128)} %dynamic-slice_bitcast_fusion.refs_2_, f32[16,8,128]{2,1,0:T(8,128)} %get-tuple-element.23.refs_3_), custom_call_target="tpu_custom_call" | custom-call | tf_op jit(solution)/shard_map/ortho/pallas_call | solution.py:362
  116.1 2.3 %fusion = f32[4,2,128,256]{3,2,1,0:T(8,128)} fusion(f32[4,2,128,128]{3,2,1,0:T(8,128)S(1)} %get-tuple-element.37, f32[4,2,128,128]{3,2,1,0:T(8,128)S(1)} %get-tuple-element.36, f32[4,2,64,256]{3,2,1,0:T(8,128)} %collective-permute-done.7, f32[4,2,64,256]{3,2,1,0:T(8,128)} %collective-permute-done.6, f32[4,2,256,256]{3,2,1,0:T(8,128)S(1)} %copy-done.1), kind=kLoop, calls=%fused_computation.5 | loop fusion | flops 1048576 | bytes 4194304 | tf_op jit(solution)/shard_map/add | solution.py:416
  (62 shorter events, 7.5 us)
Async XLA Ops:
  0.6 8.5 %copy-start.11 = (f32[2,63]{1,0:T(2,128)S(1)}, f32[2,63]{1,0:T(2,128)}, u32[]{:S(2)}) copy-start(f32[2,63]{1,0:T(2,128)} %param.9) | copy-start | bytes 1516
  2.9 27.6 %collective-permute-start = (f32[4,2,64,256]{3,2,1,0:T(8,128)}, f32[4,2,64,256]{3,2,1,0:T(8,128)S(1)}, u32[]{:S(2)}, u32[]{:S(2)}) collective-permute-start(f32[4,2,64,256]{3,2,1,0:T(8,128)} %get-tuple-element.39), channel_id=1, source_target_pairs={{0,2},{2,4},{4,6},{6,8},{8,10},{10,12},{12,14},{1,3},{3,5},{5,7},{... | collective-permute-start | bytes 1572872 | tf_op jit(solution)/shard_map/ppermute | solution.py:20
  7.8 22.7 %collective-permute-start.1 = (f32[4,2,64,256]{3,2,1,0:T(8,128)}, f32[4,2,64,256]{3,2,1,0:T(8,128)S(1)}, u32[]{:S(2)}, u32[]{:S(2)}) collective-permute-start(f32[4,2,64,256]{3,2,1,0:T(8,128)} %get-tuple-element.38), channel_id=1, source_target_pairs={{2,0},{4,2},{6,4},{8,6},{10,8},{12,10},{14,12},{3,1},{5,3},{7,5},{... | collective-permute-start | bytes 1572872 | tf_op jit(solution)/shard_map/ppermute | solution.py:20
  9.9 5.8 %copy-start = (f32[4,2,128,256]{3,2,1,0:T(8,128)S(1)}, f32[4,2,128,256]{3,2,1,0:T(8,128)}, u32[]{:S(2)}) copy-start(f32[4,2,128,256]{3,2,1,0:T(8,128)} %own.1) | copy-start | bytes 3145732
  15.7 14.9 %copy-start.2 = (bf16[8,256,256]{2,1,0:T(8,128)(2,1)}, bf16[8,256,256]{2,1,0:T(8,128)(2,1)S(1)}, u32[]{:S(2)}) copy-start(bf16[8,256,256]{2,1,0:T(8,128)(2,1)S(1)} %constant_dynamic-update-slice_fusion.tab) | copy-start | bytes 3145732
  15.8 15.0 %copy-start.12 = (s32[2,2]{1,0:T(2,128)S(1)}, s32[2,2]{1,0:T(2,128)}, u32[]{:S(2)}) copy-start(s32[2,2]{1,0:T(2,128)} %param.11) | copy-start | bytes 52
  30.5 3.0 %copy-start.3 = (f32[4,2,64,256]{3,2,1,0:T(8,128)}, f32[4,2,64,256]{3,2,1,0:T(8,128)S(1)}, u32[]{:S(2)}) copy-start(f32[4,2,64,256]{3,2,1,0:T(8,128)S(1)} %collective-permute-done.above) | copy-start | bytes 1572868
  30.5 3.0 %copy-start.4 = (f32[4,2,64,256]{3,2,1,0:T(8,128)}, f32[4,2,64,256]{3,2,1,0:T(8,128)S(1)}, u32[]{:S(2)}) copy-start(f32[4,2,64,256]{3,2,1,0:T(8,128)S(1)} %collective-permute-done.1.below) | copy-start | bytes 1572868
  30.6 2.9 %collective-permute-start.2 = (f32[4,2,256,128]{3,2,1,0:T(8,128)S(1)}, f32[4,2,256,128]{3,2,1,0:T(8,128)}, u32[]{:S(2)}, u32[]{:S(2)}) collective-permute-start(f32[4,2,256,128]{3,2,1,0:T(8,128)S(1)} %pad_maximum_fusion), channel_id=1, source_target_pairs={{0,1},{1,0},{2,3},{3,2},{4,5},{5,4},{6,7},{7,6},{8,9},{9,8},{10,11... | collective-permute-start | bytes 3145736 | tf_op jit(solution)/shard_map/ppermute | solution.py:25
  56.1 7.9 %collective-permute-start.3 = (f32[4,2,256,128]{3,2,1,0:T(8,128)}, f32[4,2,256,128]{3,2,1,0:T(8,128)S(1)}, u32[]{:S(2)}, u32[]{:S(2)}) collective-permute-start(f32[4,2,256,128]{3,2,1,0:T(8,128)} %get-tuple-element.17), channel_id=1, source_target_pairs={{0,1},{1,0},{2,3},{3,2},{4,5},{5,4},{6,7},{7,6},{8,9},{9,8},{10,11... | collective-permute-start | bytes 3145736 | tf_op jit(solution)/shard_map/ppermute | solution.py:25
  58.1 2.3 %collective-permute-start.4 = (f32[2,2,2,16,8,128]{5,4,3,0,1,2:T(8,128)}, f32[2,2,2,16,8,128]{5,4,3,0,1,2:T(8,128)}, u32[]{:S(2)}, u32[]{:S(2)}) collective-permute-start(f32[2,2,2,16,8,128]{5,4,3,0,1,2:T(8,128)} %copy_bitcast_fusion), channel_id=1, source_target_pairs={{0,1},{1,0},{2,3},{3,2},{4,5},{5,4},{6,7},{7,6},{8,9},{9,8},{10,11... | collective-permute-start | bytes 1572872 | tf_op jit(solution)/shard_map/ppermute | solution.py:25
  58.5 5.6 %copy-start.1 = (f32[4,2,256,256]{3,2,1,0:T(8,128)S(1)}, f32[4,2,256,256]{3,2,1,0:T(8,128)}, u32[]{:S(2)}) copy-start(f32[4,2,256,256]{3,2,1,0:T(8,128)} %get-tuple-element.16) | copy-start | bytes 6291460
  61.5 9.3 %collective-permute-start.5 = (f32[2,2,16,8,128]{4,3,2,0,1:T(8,128)S(1)}, f32[2,2,16,8,128]{4,3,2,0,1:T(8,128)S(1)}, u32[]{:S(2)}, u32[]{:S(2)}) collective-permute-start(f32[2,2,16,8,128]{4,3,2,0,1:T(8,128)S(1)} %get-tuple-element.41), channel_id=1, source_target_pairs={{0,2},{2,0},{4,6},{6,4},{8,10},{10,8},{12,14},{14,12},{1,3},{3,1},... | collective-permute-start | bytes 786440 | tf_op jit(solution)/shard_map/ppermute | solution.py:25
  64.0 1.3 %copy-start.5 = (f32[4,2,256,128]{3,2,1,0:T(8,128)}, f32[4,2,256,128]{3,2,1,0:T(8,128)S(1)}, u32[]{:S(2)}) copy-start(f32[4,2,256,128]{3,2,1,0:T(8,128)S(1)} %collective-permute-done.3) | copy-start | bytes 3145732
  70.8 0.7 copy-start.7
  71.5 7.3 %collective-permute-start.8 = (f32[2,16,8,128]{3,2,1,0:T(8,128)S(1)}, f32[2,16,8,128]{3,2,1,0:T(8,128)S(1)}, u32[]{:S(2)}, u32[]{:S(2)}) collective-permute-start(f32[2,16,8,128]{3,2,1,0:T(8,128)S(1)} %add_bitcast_fusion), channel_id=1, source_target_pairs={{0,4},{2,6},{4,0},{6,2},{8,12},{10,14},{12,8},{14,10},{1,5},{3,7},... | collective-permute-start | bytes 393224 | tf_op jit(solution)/shard_map/ppermute | solution.py:25
  74.3 41.7 %collective-permute-start.6 = (f32[4,2,64,256]{3,2,1,0:T(8,128)}, f32[4,2,64,256]{3,2,1,0:T(8,128)}, u32[]{:S(2)}, u32[]{:S(2)}) collective-permute-start(f32[4,2,64,256]{3,2,1,0:T(8,128)} %get-tuple-element.19), channel_id=1, source_target_pairs={{0,2},{2,4},{4,6},{6,8},{8,10},{10,12},{12,14},{1,3},{3,5},{5,7},{... | collective-permute-start | bytes 1572872 | tf_op jit(solution)/shard_map/ppermute | solution.py:20
  77.5 38.5 %collective-permute-start.7 = (f32[4,2,64,256]{3,2,1,0:T(8,128)}, f32[4,2,64,256]{3,2,1,0:T(8,128)}, u32[]{:S(2)}, u32[]{:S(2)}) collective-permute-start(f32[4,2,64,256]{3,2,1,0:T(8,128)} %get-tuple-element.20), channel_id=1, source_target_pairs={{2,0},{4,2},{6,4},{8,6},{10,8},{12,10},{14,12},{3,1},{5,3},{7,5},{... | collective-permute-start | bytes 1572872 | tf_op jit(solution)/shard_map/ppermute | solution.py:20
  79.8 20.3 %copy-start.6 = (f32[2,16,8,128]{3,2,1,0:T(8,128)}, f32[2,16,8,128]{3,2,1,0:T(8,128)S(1)}, u32[]{:S(2)}) copy-start(f32[2,16,8,128]{3,2,1,0:T(8,128)S(1)} %bitcast_add_fusion.first) | copy-start | bytes 393220
  79.8 20.3 %collective-permute-start.9 = (f32[2,16,8,128]{3,2,1,0:T(8,128)S(1)}, f32[2,16,8,128]{3,2,1,0:T(8,128)S(1)}, u32[]{:S(2)}, u32[]{:S(2)}) collective-permute-start(f32[2,16,8,128]{3,2,1,0:T(8,128)S(1)} %bitcast_add_fusion.first), channel_id=1, source_target_pairs={{0,8},{2,10},{4,12},{6,14},{8,0},{10,2},{12,4},{14,6},{1,9},{3,11}... | collective-permute-start | bytes 393224 | tf_op jit(solution)/shard_map/ppermute | solution.py:25
  100.1 0.7 copy-start.8
  102.9 1.4 %collective-permute-start.10 = (f32[32,32]{1,0:T(8,128)}, f32[32,32]{1,0:T(8,128)S(1)}, u32[]{:S(2)}, u32[]{:S(2)}) collective-permute-start(f32[32,32]{1,0:T(8,128)} %get-tuple-element.22), channel_id=1, source_target_pairs={{0,1},{1,0},{2,3},{3,2},{4,5},{5,4},{6,7},{7,6},{8,9},{9,8},{10,11... | collective-permute-start | bytes 12296 | tf_op jit(solution)/shard_map/ppermute | solution.py:25
  105.0 3.7 %collective-permute-start.11 = (f32[32,32]{1,0:T(8,128)S(1)}, f32[32,32]{1,0:T(8,128)S(1)}, u32[]{:S(2)}, u32[]{:S(2)}) collective-permute-start(f32[32,32]{1,0:T(8,128)S(1)} %add.157), channel_id=1, source_target_pairs={{0,4},{2,6},{4,0},{6,2},{8,12},{10,14},{12,8},{14,10},{1,5},{3,7},... | collective-permute-start | bytes 12296 | tf_op jit(solution)/shard_map/ppermute | solution.py:25
  108.8 3.7 %copy-start.9 = (f32[32,32]{1,0:T(8,128)}, f32[32,32]{1,0:T(8,128)S(1)}, u32[]{:S(2)}) copy-start(f32[32,32]{1,0:T(8,128)S(1)} %add.158.refs_0_) | copy-start | bytes 12292
  108.8 3.7 %collective-permute-start.12 = (f32[32,32]{1,0:T(8,128)S(1)}, f32[32,32]{1,0:T(8,128)S(1)}, u32[]{:S(2)}, u32[]{:S(2)}) collective-permute-start(f32[32,32]{1,0:T(8,128)S(1)} %add.158.refs_0_), channel_id=1, source_target_pairs={{0,2},{2,0},{4,6},{6,4},{8,10},{10,8},{12,14},{14,12},{1,3},{3,1},... | collective-permute-start | bytes 12296 | tf_op jit(solution)/shard_map/ppermute | solution.py:25
  112.5 0.6 copy-start.10

commit v4 on v3

--- a/solution.py
+++ b/solution.py
@@ -99,7 +99,7 @@
 
 def field_kernel(
     places, side, own, above, below, beside, probe, tab, measured,
-    gown, gside, gprobe, ext, gext, patch, waves, far, intensity, gpatch,
+    gown, gside, gkeep, gsend, ext, gext, gprobe, patch, waves, far, intensity, gpatch,
 ):
     rec = pl.program_id(0)
     slices = own.shape[0]
@@ -205,9 +205,7 @@
             else:
                 for k, mode in enumerate((2 * pair, 2 * pair + 1)):
                     for c, part in enumerate((res[k], ims[k])):
-                        gprobe[:, c * modes + mode] += part.reshape(
-                            n // SUBLANES, SUBLANES, n
-                        )
+                        gprobe[:, :, c * modes + mode] += part.reshape(gprobe.shape[:2] + (SUBLANES, n))
         for c in range(2):
             tall = jnp.concatenate([gpatch[c], jnp.zeros((SUBLANES, n), F32)], axis=0)
             tall = pltpu.roll(tall, drop, 0)
@@ -222,10 +220,14 @@
         @pl.when(side[0] == 0)
         def _():
             gside[...] = gext[:, :, :, n + tile_cols :]
+            gkeep[...] = gprobe[:, 0]
+            gsend[...] = gprobe[:, 1]
 
         @pl.when(side[0] != 0)
         def _():
             gside[...] = gext[:, :, :, :n]
+            gkeep[...] = gprobe[:, 1]
+            gsend[...] = gprobe[:, 0]
 
 
 def fields(places, side, own, above, below, beside, probe, tab, measured):
@@ -239,7 +241,8 @@
 
     inputs = (own, above, below, beside, probe, tab)
     outs = [(slices, 2, rows, tile_cols), (slices, 2, rows, n)]
-    outs.append((n // SUBLANES, 2 * modes, SUBLANES, n))
+    halves = (n // SUBLANES // 2, 2 * modes, SUBLANES, n)
+    outs.extend([halves, halves])
     return pl.pallas_call(
         field_kernel,
         out_shape=[jax.ShapeDtypeStruct(s, F32) for s in outs],
@@ -252,6 +255,7 @@
             scratch_shapes=[
                 pltpu.VMEM((slices, 2, rows, tile_cols + 2 * n), F32),
                 pltpu.VMEM((slices, 2, rows, tile_cols + 2 * n), F32),
+                pltpu.VMEM((n // SUBLANES // 2, 2, 2 * modes, SUBLANES, n), F32),
                 pltpu.VMEM((slices, 2, n, n), F32),
                 pltpu.VMEM((slices - 1, modes * n, 2 * n), F32),
                 pltpu.VMEM((modes * n, 2 * n), F32),
@@ -264,34 +268,33 @@
     )(places, side, *inputs, measured)
 
 
-def gram_kernel(which, probe, first, second, out, own):
+def gram_kernel(*refs):
+    probe, *parts, out, own = refs
+    grad = parts[0][...]
+    for part in parts[1:]:
+        grad = grad + part[...]
+    own[...] = grad
     total = None
-    for b in range(probe.shape[0]):
-        for i in range(probe.shape[2]):
-            grad = first[b, :, i, :] + second[b, :, i, :]
-            rows = jnp.concatenate([probe[b, :, i, :], grad], axis=0)
-            one = lax.dot_general(
-                rows, rows, (((1,), (1,)), ((), ())), precision=lax.Precision.HIGHEST,
-                preferred_element_type=F32,
-            )
-            total = one if total is None else total + one
+    for i in range(probe.shape[1]):
+        rows = jnp.concatenate([probe[:, i, :], own[:, i, :]], axis=0)
+        one = lax.dot_general(
+            rows, rows, (((1,), (1,)), ((), ())), precision=lax.Precision.HIGHEST,
+            preferred_element_type=F32,
+        )
+        total = one if total is None else total + one
     out[...] = total
-    own[...] = first[which[0]] + second[which[0]]
-
-
-def gram(which, probe, first, second):
-    rows = 2 * probe.shape[1]
-    specs = [pl.BlockSpec(memory_space=pltpu.VMEM)] * 3
+
+
+def gram(probe, parts):
+    rows = 2 * probe.shape[0]
     return pl.pallas_call(
         gram_kernel,
-        in_specs=[pl.BlockSpec(memory_space=pltpu.SMEM)] + specs,
-        out_specs=[specs[0]] * 2,
         out_shape=[
             jax.ShapeDtypeStruct((rows, rows), F32),
-            jax.ShapeDtypeStruct(probe.shape[1:], F32),
+            jax.ShapeDtypeStruct(probe.shape, F32),
         ],
         name="gram",
-    )(which, probe, first, second)
+    )(probe, *parts)
 
 
 def ortho_kernel(*refs, modes, scale):
@@ -368,50 +371,47 @@
     return lax.dynamic_index_in_dim(array, which, dim, keepdims=False)
 
 
-def updates(probe, grad, bottom, top, middle):
+def updates(probe, keep, send, bottom, top, middle):
     modes, _, width, _ = probe.shape
     row_devices = lax.axis_size("row")
     col_devices = lax.axis_size("col")
     devices = row_devices * col_devices
     share = width // devices
-    index = lax.axis_index("row") * col_devices + lax.axis_index("col")
-    if share != SUBLANES:
-        grad = grad.transpose(0, 2, 1, 3).reshape(devices, share, 2 * modes, width)
-        grad = grad.transpose(0, 2, 1, 3)
-
-    bits = devices.bit_length() - 1
-    grad = grad.reshape((2,) * bits + (2 * modes, share, width))
-    row_bits = [1 << b for b in range(bits - 1)]
-    order = [("col", 1, 0)] + [("row", bit, bit.bit_length()) for bit in row_bits[:-1]]
-    left = list(range(bits))[::-1]
-    parts = [grad]
-    for axis, bit, place in order:
-        dim = left.index(place)
-        mine = (index >> place) % 2
-        send = sum(take(p, 1 - mine, dim) for p in parts)
-        keep = sum(take(p, mine, dim) for p in parts)
-        received = swapped(send, axis, bit)
-        left.pop(dim)
-        if len(left) == bits - 2:
-            received, bottom, top = lax.optimization_barrier((received, bottom, top))
-        parts = [keep, received]
+    row_idx, col_idx = lax.axis_index("row"), lax.axis_index("col")
+    index = row_idx * col_devices + col_idx
+    row_bits = [1 << b for b in range(row_devices.bit_length() - 1)]
+
+    if share == SUBLANES and row_devices <= 8:
+        received = swapped(send, "col", 1)
+        parts = []
+        for k in range(row_devices):
+            block = take(keep, row_idx ^ k, 0) + take(received, row_idx ^ k, 0)
+            parts.append(swapped(block, "row", k) if k else block)
+    else:
+        even, odd = jnp.where(col_idx == 0, keep, send), jnp.where(col_idx == 0, send, keep)
+        grad = jnp.stack([even, odd], axis=1).transpose(0, 1, 3, 2, 4)
+        grad = grad.reshape(row_devices, col_devices, share, 2 * modes, width)
+        grad = grad.transpose(1, 0, 3, 2, 4)
+        grad = take(grad, col_idx, 0) + swapped(take(grad, 1 - col_idx, 0), "col", 1)
+        for bit in reversed(row_bits):
+            grad = grad.reshape((2, bit) + grad.shape[-3:])
+            mine = (row_idx // bit) % 2
+            grad = take(grad, mine, 0) + swapped(take(grad, 1 - mine, 0), "row", bit)
+        parts = [grad.reshape(2 * modes, share, width)]
+
+    parts, bottom, top = lax.optimization_barrier((parts, bottom, top))
     from_above = shifted(bottom, "row", 1)
     from_below = shifted(top, "row", -1)
-    first = sum(parts)
-    second = swapped(first, "row", row_bits[-1])
-    place = left[0]
-    mine = (index >> place) % 2
-    base = index - (mine << place)
-    blocks = jnp.stack([
-        lax.dynamic_slice_in_dim(probe, (base + (k << place)) * share, share, 2) for k in range(2)
-    ])
-    blocks = blocks.transpose(0, 2, 1, 3, 4).reshape(2, 2 * modes, share, width)
-    total, own_grad = gram(mine.astype(jnp.int32).reshape(1), blocks, first, second)
-    own_probe = take(blocks, mine, 0)
+    own_probe = lax.dynamic_slice_in_dim(probe, index * share, share, 2)
+    own_probe = own_probe.transpose(1, 0, 2, 3).reshape(2 * modes, share, width)
+    total, own_grad = gram(own_probe, parts)
     total = total + swapped(total, "col", 1)
-    for bit in row_bits[-2:0:-1]:
-        total = total + swapped(total, "row", bit)
-    grams = [total, swapped(total, "row", 1)]
+    if len(row_bits) % 2:
+        total = total + swapped(total, "row", row_bits.pop(0))
+    while row_bits:
+        a, b, *row_bits = row_bits
+        grams = [total] + [swapped(total, "row", k) for k in (a, b, a ^ b)]
+        total = (grams[0] + grams[1]) + (grams[2] + grams[3])
     new_probe = ortho(grams, own_probe, own_grad, modes, float(width))
     object_grad = middle() + jnp.concatenate([from_above, from_below], axis=2)
     return new_probe, object_grad
@@ -437,7 +437,7 @@
     anchor = jnp.stack([row_idx * tile_rows - half, col_idx * tile_cols - LANES])
     places = (positions - anchor[None, :]).astype(jnp.int32)
     side = col_idx.astype(jnp.int32).reshape(1)
-    gown, gside, gprobe = fields(
+    gown, gside, gkeep, gsend = fields(
         places, side, object_slices, above, below, beside, probe, tab, measured
     )
 
@@ -452,7 +452,7 @@
 
     bottom, top = folded(half + tile_rows, tile_rows + 2 * half), folded(0, half)
     new_probe, object_grad = updates(
-        probe, gprobe, bottom, top, lambda: folded(half, half + tile_rows)
+        probe, gkeep, gsend, bottom, top, lambda: folded(half, half + tile_rows)
     )
     return (object_grad, new_probe)
 

time: 119 us -> 124 us (1.042)
  starting transfers between devices: 21.3 us -> 31.2 us
  local copies, waits for them, and re-layouts: 15.5 us -> 10.1 us
    ppermute x9 -> x15, starting transfers between devices: 10.6 us -> 21.1 us  [swapped(): return lax.ppermute(value, axis, [(i, i ^ bit) for i in range(count)])]
    squeeze x2 -> x0, local copies, waits for them, and re-layouts: 3.35 us -> none  [take(): return lax.dynamic_index_in_dim(array, which, dim, keepdims=False)]
    unnamed x31 -> x43, local copies, waits for them, and re-layouts: 4.78 us -> 4.06 us
    ppermute x9 -> x15, waiting for transfers between devices: 28.5 us -> 28.5 us  [swapped(): return lax.ppermute(value, axis, [(i, i ^ bit) for i in range(count)])]
  transfers between devices with their start and end apart: 13 -> 19, of which waited for: 8 -> 10; matrix products, arithmetic and copies ran while one was open for 16% -> 11% of each run, Pallas kernels for 4% -> 4%
where the time goes in v4:
time: 124 us; the launch traced here: 123 us
  waiting for transfers between devices  43.2 us (35%)
  starting transfers between devices  31.2 us (25%)
  Pallas kernels  27.7 us (22%)
  local copies, waits for them, and re-layouts  10.1 us (8%)
  other arithmetic  9.63 us (8%)
    ppermute x15, waiting for transfers between devices, swapped(): return lax.ppermute(value, axis, [(i, i ^ bit) for i in range(count)])  28.5 us
    pallas_call x1, Pallas kernels, fields(): pl.pallas_call(field_kernel, out_shape=[jax.ShapeDtypeStruct(s, F32) for...  22.6 us
    ppermute x15, starting transfers between devices, swapped(): return lax.ppermute(value, axis, [(i, i ^ bit) for i in range(count)])  21.1 us
    ppermute x4, waiting for transfers between devices, shifted(): return lax.ppermute(value, axis, pairs)  14.7 us
    ppermute x4, starting transfers between devices, shifted(): return lax.ppermute(value, axis, pairs)  10.2 us
    unnamed x43, local copies, waits for them, and re-layouts  4.06 us
    pallas_call x1, Pallas kernels, ortho(): pl.pallas_call(body, out_shape=jax.ShapeDtypeStruct((modes, 2, pixels), F...  2.95 us
  transfers between devices with their start and end apart: 19, of which 10 were waited for; matrix products, arithmetic and copies ran while one was open for 11% of the time, Pallas kernels for 4%

profile of v4, /device:TPU:0, one launch (start us, length us, event | category | flops | bytes accessed | tf_op | source)
XLA Modules:
  0.0 122.9 jit_solution(868881928576264115)
XLA Ops:
  0.6 2.3 %fusion.5 = (f32[4,2,64,256]{3,2,1,0:T(8,128)}, f32[4,2,64,256]{3,2,1,0:T(8,128)}) fusion(f32[4,2,128,256]{3,2,1,0:T(8,128)} %own.1), kind=kLoop, calls=%fused_computation.50 | loop fusion | bytes 2097152 | tf_op jit(solution)/shard_map/slice | solution.py:428
  2.9 4.9 %collective-permute-start = (f32[4,2,64,256]{3,2,1,0:T(8,128)}, f32[4,2,64,256]{3,2,1,0:T(8,128)S(1)}, u32[]{:S(2)}, u32[]{:S(2)}) collective-permute-start(f32[4,2,64,256]{3,2,1,0:T(8,128)} %get-tuple-element.59), channel_id=1, source_target_pairs={{0,2},{2,4},{4,6},{6,8},{8,10},{10,12},{12,14},{1,3},{3,5},{5,7},{... | collective-permute-start | bytes 1572872 | tf_op jit(solution)/shard_map/ppermute | solution.py:20
  7.8 1.3 %collective-permute-start.1 = (f32[4,2,64,256]{3,2,1,0:T(8,128)}, f32[4,2,64,256]{3,2,1,0:T(8,128)S(1)}, u32[]{:S(2)}, u32[]{:S(2)}) collective-permute-start(f32[4,2,64,256]{3,2,1,0:T(8,128)} %get-tuple-element.58), channel_id=1, source_target_pairs={{2,0},{4,2},{6,4},{8,6},{10,8},{12,10},{14,12},{3,1},{5,3},{7,5},{... | collective-permute-start | bytes 1572872 | tf_op jit(solution)/shard_map/ppermute | solution.py:20
  11.0 1.0 copy.17
  12.0 0.9 constant_dynamic-update-slice_fusion.3
  13.9 0.9 constant_dynamic-update-slice_fusion.1
  15.8 14.7 %collective-permute-done.above = f32[4,2,64,256]{3,2,1,0:T(8,128)S(1)} collective-permute-done((f32[4,2,64,256]{3,2,1,0:T(8,128)}, f32[4,2,64,256]{3,2,1,0:T(8,128)S(1)}, u32[]{:S(2)}, u32[]{:S(2)}) %collective-permute-start) | collective-permute-done | bytes 524320 | tf_op jit(solution)/shard_map/ppermute | solution.py:20
  31.4 2.1 %collective-permute-done.2.beside = f32[4,2,256,128]{3,2,1,0:T(8,128)} collective-permute-done((f32[4,2,256,128]{3,2,1,0:T(8,128)S(1)}, f32[4,2,256,128]{3,2,1,0:T(8,128)}, u32[]{:S(2)}, u32[]{:S(2)}) %collective-permute-start.2) | collective-permute-done | bytes 1048608 | tf_op jit(solution)/shard_map/ppermute | solution.py:25
  33.5 22.6 %fields.1 = (f32[4,2,256,256]{3,2,1,0:T(8,128)}, f32[4,2,256,128]{3,2,1,0:T(8,128)}, f32[8,16,8,128]{3,2,1,0:T(8,128)}, f32[8,16,8,128]{3,2,1,0:T(8,128)}) custom-call(s32[2,2]{1,0:T(2,128)} %broadcast_subtract_fusion.places, s32[1]{0:T(128)} %bitcast.2.side, f32[4,2,128,256]{3,2,1,0:T(8,128)} %own.1, f32[4,2,64,256]{3,2,1,0:T(8,128)} %copy-done.3, ...), custom_call_target="tpu_custom_call" | custom-call | tf_op jit(solution)/shard_map/fields/pallas_call | solution.py:246
  56.6 3.2 %collective-permute-done.4 = f32[8,16,8,128]{3,2,1,0:T(8,128)} collective-permute-done((f32[8,16,8,128]{3,2,1,0:T(8,128)}, f32[8,16,8,128]{3,2,1,0:T(8,128)}, u32[]{:S(2)}, u32[]{:S(2)}) %collective-permute-start.4) | collective-permute-done | bytes 524320 | tf_op jit(solution)/shard_map/ppermute | solution.py:25
  59.9 1.9 %add_bitcast_fusion = (f32[16,8,128]{2,1,0:T(8,128)S(1)}, f32[16,8,128]{2,1,0:T(8,128)S(1)}, f32[16,8,128]{2,1,0:T(8,128)S(1)}, f32[16,8,128]{2,1,0:T(8,128)S(1)...) fusion(f32[8,16,8,128]{3,2,1,0:T(8,128)} %collective-permute-don, ...), kind=kLoop, calls=%fused_computation.28 | loop fusion | flops 131072 | bytes 1572896 | tf_op jit(solution)/shard_map/add | solution.py:388
  61.8 5.4 %collective-permute-start.10 = (f32[16,8,128]{2,1,0:T(8,128)S(1)}, f32[16,8,128]{2,1,0:T(8,128)S(1)}, u32[]{:S(2)}, u32[]{:S(2)}) collective-permute-start(f32[16,8,128]{2,1,0:T(8,128)S(1)} %get-tuple-element.49), channel_id=1, source_target_pairs={{0,12},{2,14},{4,8},{6,10},{8,4},{10,6},{12,0},{14,2},{1,13},{3,15... | collective-permute-start | bytes 196616 | tf_op jit(solution)/shard_map/ppermute | solution.py:25
  67.5 1.2 collective-permute-start.5
  68.7 2.3 %collective-permute-start.7 = (f32[16,8,128]{2,1,0:T(8,128)S(1)}, f32[16,8,128]{2,1,0:T(8,128)S(1)}, u32[]{:S(2)}, u32[]{:S(2)}) collective-permute-start(f32[16,8,128]{2,1,0:T(8,128)S(1)} %get-tuple-element.52), channel_id=1, source_target_pairs={{0,6},{2,4},{4,2},{6,0},{8,14},{10,12},{12,10},{14,8},{1,7},{3,5},... | collective-permute-start | bytes 196616 | tf_op jit(solution)/shard_map/ppermute | solution.py:25
  71.1 2.2 %collective-permute-start.8 = (f32[16,8,128]{2,1,0:T(8,128)S(1)}, f32[16,8,128]{2,1,0:T(8,128)S(1)}, u32[]{:S(2)}, u32[]{:S(2)}) collective-permute-start(f32[16,8,128]{2,1,0:T(8,128)S(1)} %get-tuple-element.51), channel_id=1, source_target_pairs={{0,8},{2,10},{4,12},{6,14},{8,0},{10,2},{12,4},{14,6},{1,9},{3,11}... | collective-permute-start | bytes 196616 | tf_op jit(solution)/shard_map/ppermute | solution.py:25
  73.3 1.2 collective-permute-done.11.refs_8_
  74.5 1.1 collective-permute-start.9
  75.6 1.1 maximum_add_fusion.2
  76.8 1.5 %collective-permute-done.8.refs_5_ = f32[16,8,128]{2,1,0:T(8,128)S(1)} collective-permute-done((f32[16,8,128]{2,1,0:T(8,128)S(1)}, f32[16,8,128]{2,1,0:T(8,128)S(1)}, u32[]{:S(2)}, u32[]{:S(2)}) %collective-permute-start.8) | collective-permute-done | bytes 65568 | tf_op jit(solution)/shard_map/ppermute | solution.py:25
  78.3 2.6 %collective-permute-done.9.refs_6_ = f32[16,8,128]{2,1,0:T(8,128)S(1)} collective-permute-done((f32[16,8,128]{2,1,0:T(8,128)S(1)}, f32[16,8,128]{2,1,0:T(8,128)S(1)}, u32[]{:S(2)}, u32[]{:S(2)}) %collective-permute-start.9) | collective-permute-done | bytes 65568 | tf_op jit(solution)/shard_map/ppermute | solution.py:25
  81.6 2.7 %collective-permute-start.12 = (f32[4,2,64,256]{3,2,1,0:T(8,128)}, f32[4,2,64,256]{3,2,1,0:T(8,128)}, u32[]{:S(2)}, u32[]{:S(2)}) collective-permute-start(f32[4,2,64,256]{3,2,1,0:T(8,128)} %get-tuple-element.28), channel_id=1, source_target_pairs={{0,2},{2,4},{4,6},{6,8},{8,10},{10,12},{12,14},{1,3},{3,5},{5,7},{... | collective-permute-start | bytes 1572872 | tf_op jit(solution)/shard_map/ppermute | solution.py:20
  84.3 1.3 %collective-permute-start.13 = (f32[4,2,64,256]{3,2,1,0:T(8,128)}, f32[4,2,64,256]{3,2,1,0:T(8,128)}, u32[]{:S(2)}, u32[]{:S(2)}) collective-permute-start(f32[4,2,64,256]{3,2,1,0:T(8,128)} %get-tuple-element.29), channel_id=1, source_target_pairs={{2,0},{4,2},{6,4},{8,6},{10,8},{12,10},{14,12},{3,1},{5,3},{7,5},{... | collective-permute-start | bytes 1572872 | tf_op jit(solution)/shard_map/ppermute | solution.py:20
  87.1 2.1 %gram.1 = (f32[32,32]{1,0:T(8,128)}, f32[16,8,128]{2,1,0:T(8,128)}) custom-call(f32[16,8,128]{2,1,0:T(8,128)} %bitcast.48, f32[16,8,128]{2,1,0:T(8,128)} %get-tuple-element.30.refs_1_, f32[16,8,128]{2,1,0:T(8,128)} %copy-done.8, f32[16,8,128]{2,1,0:T(8,128)} %copy-done.9, f32[16,8,128]{2,1,0:T(8,128)} %copy-done.10, f32[16,8,128]{2,1,0:T(8,128)} %copy-done.11, ...), custom_call_target="tpu_custom_call" | custom-call | tf_op jit(solution)/shard_map/gram/pallas_call | solution.py:290
  89.2 1.4 %collective-permute-done.14 = f32[32,32]{1,0:T(8,128)S(1)} collective-permute-done((f32[32,32]{1,0:T(8,128)}, f32[32,32]{1,0:T(8,128)S(1)}, u32[]{:S(2)}, u32[]{:S(2)}) %collective-permute-start.14) | collective-permute-done | bytes 4128 | tf_op jit(solution)/shard_map/ppermute | solution.py:25
  91.3 2.6 %collective-permute-start.15 = (f32[32,32]{1,0:T(8,128)S(1)}, f32[32,32]{1,0:T(8,128)S(1)}, u32[]{:S(2)}, u32[]{:S(2)}) collective-permute-start(f32[32,32]{1,0:T(8,128)S(1)} %add.157), channel_id=1, source_target_pairs={{0,2},{2,0},{4,6},{6,4},{8,10},{10,8},{12,14},{14,12},{1,3},{3,1},... | collective-permute-start | bytes 12296 | tf_op jit(solution)/shard_map/ppermute | solution.py:25
  93.9 12.1 %collective-permute-done.15 = f32[32,32]{1,0:T(8,128)S(1)} collective-permute-done((f32[32,32]{1,0:T(8,128)S(1)}, f32[32,32]{1,0:T(8,128)S(1)}, u32[]{:S(2)}, u32[]{:S(2)}) %collective-permute-start.15) | collective-permute-done | bytes 4128 | tf_op jit(solution)/shard_map/ppermute | solution.py:25
  106.1 2.2 %collective-permute-start.16 = (f32[32,32]{1,0:T(8,128)S(1)}, f32[32,32]{1,0:T(8,128)S(1)}, u32[]{:S(2)}, u32[]{:S(2)}) collective-permute-start(f32[32,32]{1,0:T(8,128)S(1)} %add.158.refs_0_), channel_id=1, source_target_pairs={{0,4},{2,6},{4,0},{6,2},{8,12},{10,14},{12,8},{14,10},{1,5},{3,7},... | collective-permute-start | bytes 12296 | tf_op jit(solution)/shard_map/ppermute | solution.py:25
  108.3 3.1 %collective-permute-start.17 = (f32[32,32]{1,0:T(8,128)S(1)}, f32[32,32]{1,0:T(8,128)S(1)}, u32[]{:S(2)}, u32[]{:S(2)}) collective-permute-start(f32[32,32]{1,0:T(8,128)S(1)} %add.158.refs_0_), channel_id=1, source_target_pairs={{0,8},{2,10},{4,12},{6,14},{8,0},{10,2},{12,4},{14,6},{1,9},{3,11}... | collective-permute-start | bytes 12296 | tf_op jit(solution)/shard_map/ppermute | solution.py:25
  111.4 1.1 slice_select_fusion.1
  113.1 3.8 %collective-permute-done.18.refs_3_ = f32[32,32]{1,0:T(8,128)S(1)} collective-permute-done((f32[32,32]{1,0:T(8,128)S(1)}, f32[32,32]{1,0:T(8,128)S(1)}, u32[]{:S(2)}, u32[]{:S(2)}) %collective-permute-start.18) | collective-permute-done | bytes 4128 | tf_op jit(solution)/shard_map/ppermute | solution.py:25
  117.5 3.0 %ortho.1 = f32[8,2,1024]{2,1,0:T(2,128)} custom-call(f32[32,32]{1,0:T(8,128)} %copy-done.13, f32[32,32]{1,0:T(8,128)} %copy-done.14, f32[32,32]{1,0:T(8,128)} %copy-done.15, f32[32,32]{1,0:T(8,128)} %copy-done.16, f32[16,8,128]{2,1,0:T(8,128)} %bitcast.49, f32[16,8,128]{2,1,0:T(8,128)} %get-tuple-element.39.refs_5_), custom_call_target="tpu_custom_call" | custom-call | tf_op jit(solution)/shard_map/ortho/pallas_call | solution.py:365
  120.5 2.3 %fusion = f32[4,2,128,256]{3,2,1,0:T(8,128)} fusion(f32[4,2,128,128]{3,2,1,0:T(8,128)S(1)} %get-tuple-element.57, f32[4,2,128,128]{3,2,1,0:T(8,128)S(1)} %get-tuple-element.56, f32[4,2,64,256]{3,2,1,0:T(8,128)} %collective-permute-done.13, f32[4,2,64,256]{3,2,1,0:T(8,128)} %collective-permute-done.12, f32[4,2,256,256]{3,2,1,0:T(8,128)S(1)} %copy-done.1), kind=kLoop, calls=%fused_computation.5 | loop fusion | flops 1048576 | bytes 4194304 | tf_op jit(solution)/shard_map/add | solution.py:416
  (80 shorter events, 9.5 us)
Async XLA Ops:
  0.6 8.5 %copy-start.17 = (f32[2,63]{1,0:T(2,128)S(1)}, f32[2,63]{1,0:T(2,128)}, u32[]{:S(2)}) copy-start(f32[2,63]{1,0:T(2,128)} %param.9) | copy-start | bytes 1516
  2.9 27.6 %collective-permute-start = (f32[4,2,64,256]{3,2,1,0:T(8,128)}, f32[4,2,64,256]{3,2,1,0:T(8,128)S(1)}, u32[]{:S(2)}, u32[]{:S(2)}) collective-permute-start(f32[4,2,64,256]{3,2,1,0:T(8,128)} %get-tuple-element.59), channel_id=1, source_target_pairs={{0,2},{2,4},{4,6},{6,8},{8,10},{10,12},{12,14},{1,3},{3,5},{5,7},{... | collective-permute-start | bytes 1572872 | tf_op jit(solution)/shard_map/ppermute | solution.py:20
  7.8 22.7 %collective-permute-start.1 = (f32[4,2,64,256]{3,2,1,0:T(8,128)}, f32[4,2,64,256]{3,2,1,0:T(8,128)S(1)}, u32[]{:S(2)}, u32[]{:S(2)}) collective-permute-start(f32[4,2,64,256]{3,2,1,0:T(8,128)} %get-tuple-element.58), channel_id=1, source_target_pairs={{2,0},{4,2},{6,4},{8,6},{10,8},{12,10},{14,12},{3,1},{5,3},{7,5},{... | collective-permute-start | bytes 1572872 | tf_op jit(solution)/shard_map/ppermute | solution.py:20
  9.9 5.8 %copy-start = (f32[4,2,128,256]{3,2,1,0:T(8,128)S(1)}, f32[4,2,128,256]{3,2,1,0:T(8,128)}, u32[]{:S(2)}) copy-start(f32[4,2,128,256]{3,2,1,0:T(8,128)} %own.1) | copy-start | bytes 3145732
  15.7 14.9 %copy-start.2 = (bf16[8,256,256]{2,1,0:T(8,128)(2,1)}, bf16[8,256,256]{2,1,0:T(8,128)(2,1)S(1)}, u32[]{:S(2)}) copy-start(bf16[8,256,256]{2,1,0:T(8,128)(2,1)S(1)} %constant_dynamic-update-slice_fusion.tab) | copy-start | bytes 3145732
  15.8 15.0 %copy-start.18 = (s32[2,2]{1,0:T(2,128)S(1)}, s32[2,2]{1,0:T(2,128)}, u32[]{:S(2)}) copy-start(s32[2,2]{1,0:T(2,128)} %param.11) | copy-start | bytes 52
  30.6 2.9 %collective-permute-start.2 = (f32[4,2,256,128]{3,2,1,0:T(8,128)S(1)}, f32[4,2,256,128]{3,2,1,0:T(8,128)}, u32[]{:S(2)}, u32[]{:S(2)}) collective-permute-start(f32[4,2,256,128]{3,2,1,0:T(8,128)S(1)} %pad_maximum_fusion), channel_id=1, source_target_pairs={{0,1},{1,0},{2,3},{3,2},{4,5},{5,4},{6,7},{7,6},{8,9},{9,8},{10,11... | collective-permute-start | bytes 3145736 | tf_op jit(solution)/shard_map/ppermute | solution.py:25
  56.1 19.5 %copy-start.1 = (f32[4,2,256,256]{3,2,1,0:T(8,128)S(1)}, f32[4,2,256,256]{3,2,1,0:T(8,128)}, u32[]{:S(2)}) copy-start(f32[4,2,256,256]{3,2,1,0:T(8,128)} %get-tuple-element.24) | copy-start | bytes 6291460
  56.1 12.6 %collective-permute-start.3 = (f32[4,2,256,128]{3,2,1,0:T(8,128)}, f32[4,2,256,128]{3,2,1,0:T(8,128)S(1)}, u32[]{:S(2)}, u32[]{:S(2)}) collective-permute-start(f32[4,2,256,128]{3,2,1,0:T(8,128)} %get-tuple-element.25), channel_id=1, source_target_pairs={{0,1},{1,0},{2,3},{3,2},{4,5},{5,4},{6,7},{7,6},{8,9},{9,8},{10,11... | collective-permute-start | bytes 3145736 | tf_op jit(solution)/shard_map/ppermute | solution.py:25
  56.3 3.6 %collective-permute-start.4 = (f32[8,16,8,128]{3,2,1,0:T(8,128)}, f32[8,16,8,128]{3,2,1,0:T(8,128)}, u32[]{:S(2)}, u32[]{:S(2)}) collective-permute-start(f32[8,16,8,128]{3,2,1,0:T(8,128)} %get-tuple-element.27), channel_id=1, source_target_pairs={{0,1},{1,0},{2,3},{3,2},{4,5},{5,4},{6,7},{7,6},{8,9},{9,8},{10,11... | collective-permute-start | bytes 1572872 | tf_op jit(solution)/shard_map/ppermute | solution.py:25
  61.8 9.3 %collective-permute-start.10 = (f32[16,8,128]{2,1,0:T(8,128)S(1)}, f32[16,8,128]{2,1,0:T(8,128)S(1)}, u32[]{:S(2)}, u32[]{:S(2)}) collective-permute-start(f32[16,8,128]{2,1,0:T(8,128)S(1)} %get-tuple-element.49), channel_id=1, source_target_pairs={{0,12},{2,14},{4,8},{6,10},{8,4},{10,6},{12,0},{14,2},{1,13},{3,15... | collective-permute-start | bytes 196616 | tf_op jit(solution)/shard_map/ppermute | solution.py:25
  67.2 7.3 %collective-permute-start.11 = (f32[16,8,128]{2,1,0:T(8,128)S(1)}, f32[16,8,128]{2,1,0:T(8,128)S(1)}, u32[]{:S(2)}, u32[]{:S(2)}) collective-permute-start(f32[16,8,128]{2,1,0:T(8,128)S(1)} %get-tuple-element.48), channel_id=1, source_target_pairs={{0,14},{2,12},{4,10},{6,8},{8,6},{10,4},{12,2},{14,0},{1,15},{3,13... | collective-permute-start | bytes 196616 | tf_op jit(solution)/shard_map/ppermute | solution.py:25
  67.5 9.3 %collective-permute-start.5 = (f32[16,8,128]{2,1,0:T(8,128)S(1)}, f32[16,8,128]{2,1,0:T(8,128)S(1)}, u32[]{:S(2)}, u32[]{:S(2)}) collective-permute-start(f32[16,8,128]{2,1,0:T(8,128)S(1)} %get-tuple-element.54), channel_id=1, source_target_pairs={{0,2},{2,0},{4,6},{6,4},{8,10},{10,8},{12,14},{14,12},{1,3},{3,1},... | collective-permute-start | bytes 196616 | tf_op jit(solution)/shard_map/ppermute | solution.py:25
  68.7 8.1 %collective-permute-start.6 = (f32[16,8,128]{2,1,0:T(8,128)S(1)}, f32[16,8,128]{2,1,0:T(8,128)S(1)}, u32[]{:S(2)}, u32[]{:S(2)}) collective-permute-start(f32[16,8,128]{2,1,0:T(8,128)S(1)} %get-tuple-element.53), channel_id=1, source_target_pairs={{0,4},{2,6},{4,0},{6,2},{8,12},{10,14},{12,8},{14,10},{1,5},{3,7},... | collective-permute-start | bytes 196616 | tf_op jit(solution)/shard_map/ppermute | solution.py:25
  68.7 8.1 %copy-start.5 = (f32[4,2,256,128]{3,2,1,0:T(8,128)}, f32[4,2,256,128]{3,2,1,0:T(8,128)S(1)}, u32[]{:S(2)}) copy-start(f32[4,2,256,128]{3,2,1,0:T(8,128)S(1)} %collective-permute-done.3) | copy-start | bytes 3145732
  68.7 8.1 %collective-permute-start.7 = (f32[16,8,128]{2,1,0:T(8,128)S(1)}, f32[16,8,128]{2,1,0:T(8,128)S(1)}, u32[]{:S(2)}, u32[]{:S(2)}) collective-permute-start(f32[16,8,128]{2,1,0:T(8,128)S(1)} %get-tuple-element.52), channel_id=1, source_target_pairs={{0,6},{2,4},{4,2},{6,0},{8,14},{10,12},{12,10},{14,8},{1,7},{3,5},... | collective-permute-start | bytes 196616 | tf_op jit(solution)/shard_map/ppermute | solution.py:25
  71.1 15.9 %copy-start.6 = (f32[16,8,128]{2,1,0:T(8,128)}, f32[16,8,128]{2,1,0:T(8,128)S(1)}, u32[]{:S(2)}) copy-start(f32[16,8,128]{2,1,0:T(8,128)S(1)} %collective-permute-done.10.refs_7_) | copy-start | bytes 196612
  71.1 7.2 %collective-permute-start.8 = (f32[16,8,128]{2,1,0:T(8,128)S(1)}, f32[16,8,128]{2,1,0:T(8,128)S(1)}, u32[]{:S(2)}, u32[]{:S(2)}) collective-permute-start(f32[16,8,128]{2,1,0:T(8,128)S(1)} %get-tuple-element.51), channel_id=1, source_target_pairs={{0,8},{2,10},{4,12},{6,14},{8,0},{10,2},{12,4},{14,6},{1,9},{3,11}... | collective-permute-start | bytes 196616 | tf_op jit(solution)/shard_map/ppermute | solution.py:25
  74.5 12.6 %copy-start.7 = (f32[16,8,128]{2,1,0:T(8,128)}, f32[16,8,128]{2,1,0:T(8,128)S(1)}, u32[]{:S(2)}) copy-start(f32[16,8,128]{2,1,0:T(8,128)S(1)} %collective-permute-done.11.refs_8_) | copy-start | bytes 196612
  74.5 6.4 %collective-permute-start.9 = (f32[16,8,128]{2,1,0:T(8,128)S(1)}, f32[16,8,128]{2,1,0:T(8,128)S(1)}, u32[]{:S(2)}, u32[]{:S(2)}) collective-permute-start(f32[16,8,128]{2,1,0:T(8,128)S(1)} %get-tuple-element.50), channel_id=1, source_target_pairs={{0,10},{2,8},{4,14},{6,12},{8,2},{10,0},{12,6},{14,4},{1,11},{3,9}... | collective-permute-start | bytes 196616 | tf_op jit(solution)/shard_map/ppermute | solution.py:25
  76.8 10.3 %copy-start.8 = (f32[16,8,128]{2,1,0:T(8,128)}, f32[16,8,128]{2,1,0:T(8,128)S(1)}, u32[]{:S(2)}) copy-start(f32[16,8,128]{2,1,0:T(8,128)S(1)} %collective-permute-done.5.refs_2_) | copy-start | bytes 196612
  76.8 10.3 %copy-start.9 = (f32[16,8,128]{2,1,0:T(8,128)}, f32[16,8,128]{2,1,0:T(8,128)S(1)}, u32[]{:S(2)}) copy-start(f32[16,8,128]{2,1,0:T(8,128)S(1)} %collective-permute-done.6.refs_3_) | copy-start | bytes 196612
  76.8 10.3 %copy-start.10 = (f32[16,8,128]{2,1,0:T(8,128)}, f32[16,8,128]{2,1,0:T(8,128)S(1)}, u32[]{:S(2)}) copy-start(f32[16,8,128]{2,1,0:T(8,128)S(1)} %collective-permute-done.7.refs_4_) | copy-start | bytes 196612
  78.3 8.7 %copy-start.11 = (f32[16,8,128]{2,1,0:T(8,128)}, f32[16,8,128]{2,1,0:T(8,128)S(1)}, u32[]{:S(2)}) copy-start(f32[16,8,128]{2,1,0:T(8,128)S(1)} %collective-permute-done.8.refs_5_) | copy-start | bytes 196612
  81.6 39.0 %collective-permute-start.12 = (f32[4,2,64,256]{3,2,1,0:T(8,128)}, f32[4,2,64,256]{3,2,1,0:T(8,128)}, u32[]{:S(2)}, u32[]{:S(2)}) collective-permute-start(f32[4,2,64,256]{3,2,1,0:T(8,128)} %get-tuple-element.28), channel_id=1, source_target_pairs={{0,2},{2,4},{4,6},{6,8},{8,10},{10,12},{12,14},{1,3},{3,5},{5,7},{... | collective-permute-start | bytes 1572872 | tf_op jit(solution)/shard_map/ppermute | solution.py:20
  84.3 36.2 %collective-permute-start.13 = (f32[4,2,64,256]{3,2,1,0:T(8,128)}, f32[4,2,64,256]{3,2,1,0:T(8,128)}, u32[]{:S(2)}, u32[]{:S(2)}) collective-permute-start(f32[4,2,64,256]{3,2,1,0:T(8,128)} %get-tuple-element.29), channel_id=1, source_target_pairs={{2,0},{4,2},{6,4},{8,6},{10,8},{12,10},{14,12},{3,1},{5,3},{7,5},{... | collective-permute-start | bytes 1572872 | tf_op jit(solution)/shard_map/ppermute | solution.py:20
  89.2 1.4 %collective-permute-start.14 = (f32[32,32]{1,0:T(8,128)}, f32[32,32]{1,0:T(8,128)S(1)}, u32[]{:S(2)}, u32[]{:S(2)}) collective-permute-start(f32[32,32]{1,0:T(8,128)} %get-tuple-element.38), channel_id=1, source_target_pairs={{0,1},{1,0},{2,3},{3,2},{4,5},{5,4},{6,7},{7,6},{8,9},{9,8},{10,11... | collective-permute-start | bytes 12296 | tf_op jit(solution)/shard_map/ppermute | solution.py:25
  91.3 14.8 %collective-permute-start.15 = (f32[32,32]{1,0:T(8,128)S(1)}, f32[32,32]{1,0:T(8,128)S(1)}, u32[]{:S(2)}, u32[]{:S(2)}) collective-permute-start(f32[32,32]{1,0:T(8,128)S(1)} %add.157), channel_id=1, source_target_pairs={{0,2},{2,0},{4,6},{6,4},{8,10},{10,8},{12,14},{14,12},{1,3},{3,1},... | collective-permute-start | bytes 12296 | tf_op jit(solution)/shard_map/ppermute | solution.py:25
  106.1 10.9 %copy-start.13 = (f32[32,32]{1,0:T(8,128)}, f32[32,32]{1,0:T(8,128)S(1)}, u32[]{:S(2)}) copy-start(f32[32,32]{1,0:T(8,128)S(1)} %add.158.refs_0_) | copy-start | bytes 12292
  106.1 6.5 %collective-permute-start.16 = (f32[32,32]{1,0:T(8,128)S(1)}, f32[32,32]{1,0:T(8,128)S(1)}, u32[]{:S(2)}, u32[]{:S(2)}) collective-permute-start(f32[32,32]{1,0:T(8,128)S(1)} %add.158.refs_0_), channel_id=1, source_target_pairs={{0,4},{2,6},{4,0},{6,2},{8,12},{10,14},{12,8},{14,10},{1,5},{3,7},... | collective-permute-start | bytes 12296 | tf_op jit(solution)/shard_map/ppermute | solution.py:25
  108.3 4.9 %collective-permute-start.17 = (f32[32,32]{1,0:T(8,128)S(1)}, f32[32,32]{1,0:T(8,128)S(1)}, u32[]{:S(2)}, u32[]{:S(2)}) collective-permute-start(f32[32,32]{1,0:T(8,128)S(1)} %add.158.refs_0_), channel_id=1, source_target_pairs={{0,8},{2,10},{4,12},{6,14},{8,0},{10,2},{12,4},{14,6},{1,9},{3,11}... | collective-permute-start | bytes 12296 | tf_op jit(solution)/shard_map/ppermute | solution.py:25
  111.4 5.5 %collective-permute-start.18 = (f32[32,32]{1,0:T(8,128)S(1)}, f32[32,32]{1,0:T(8,128)S(1)}, u32[]{:S(2)}, u32[]{:S(2)}) collective-permute-start(f32[32,32]{1,0:T(8,128)S(1)} %add.158.refs_0_), channel_id=1, source_target_pairs={{0,12},{2,14},{4,8},{6,10},{8,4},{10,6},{12,0},{14,2},{1,13},{3,15... | collective-permute-start | bytes 12296 | tf_op jit(solution)/shard_map/ppermute | solution.py:25
  (6 other events, 15.4 us)

commit v5 on v4

--- a/solution.py
+++ b/solution.py
@@ -406,12 +406,14 @@
     own_probe = own_probe.transpose(1, 0, 2, 3).reshape(2 * modes, share, width)
     total, own_grad = gram(own_probe, parts)
     total = total + swapped(total, "col", 1)
-    if len(row_bits) % 2:
-        total = total + swapped(total, "row", row_bits.pop(0))
-    while row_bits:
-        a, b, *row_bits = row_bits
-        grams = [total] + [swapped(total, "row", k) for k in (a, b, a ^ b)]
-        total = (grams[0] + grams[1]) + (grams[2] + grams[3])
+    high_bits = row_bits[1:]
+    if len(high_bits) % 2:
+        total = total + swapped(total, "row", high_bits.pop())
+    while high_bits:
+        a, b, *high_bits = high_bits
+        near, far, both = (swapped(total, "row", k) for k in (a, b, a ^ b))
+        total = (total + near) + (far + both)
+    grams = [total, swapped(total, "row", row_bits[0])]
     new_probe = ortho(grams, own_probe, own_grad, modes, float(width))
     object_grad = middle() + jnp.concatenate([from_above, from_below], axis=2)
     return new_probe, object_grad

time: 124 us -> 112 us (0.903)
  waiting for transfers between devices: 43.2 us -> 34.6 us
  starting transfers between devices: 31.2 us -> 29.2 us
    ppermute x15, waiting for transfers between devices: 28.5 us -> 19.9 us  [swapped(): return lax.ppermute(value, axis, [(i, i ^ bit) for i in range(count)])]
    ppermute x15, starting transfers between devices: 21.1 us -> 19 us  [swapped(): return lax.ppermute(value, axis, [(i, i ^ bit) for i in range(count)])]
    unnamed x43 -> x39, local copies, waits for them, and re-layouts: 4.06 us -> 3.44 us
  transfers between devices with their start and end apart: 19 -> 19, of which waited for: 10 -> 11; matrix products, arithmetic and copies ran while one was open for 11% -> 12% of each run, Pallas kernels for 4% -> 4%
where the time goes in v5:
time: 112 us
  waiting for transfers between devices  34.6 us (31%)
  starting transfers between devices  29.2 us (26%)
  Pallas kernels  27.6 us (25%)
  other arithmetic  9.64 us (9%)
  local copies, waits for them, and re-layouts  9.51 us (8%)
    pallas_call x1, Pallas kernels, fields(): pl.pallas_call(field_kernel, out_shape=[jax.ShapeDtypeStruct(s, F32) for...  22.6 us
    ppermute x15, waiting for transfers between devices, swapped(): return lax.ppermute(value, axis, [(i, i ^ bit) for i in range(count)])  19.9 us
    ppermute x15, starting transfers between devices, swapped(): return lax.ppermute(value, axis, [(i, i ^ bit) for i in range(count)])  19 us
    ppermute x4, waiting for transfers between devices, shifted(): return lax.ppermute(value, axis, pairs)  14.7 us
    ppermute x4, starting transfers between devices, shifted(): return lax.ppermute(value, axis, pairs)  10.2 us
    unnamed x39, local copies, waits for them, and re-layouts  3.44 us
    pallas_call x1, Pallas kernels, ortho(): pl.pallas_call(body, out_shape=jax.ShapeDtypeStruct((modes, 2, pixels), F...  2.92 us
    add x1, other arithmetic, updates(): object_grad = middle() + jnp.concatenate([from_above, from_below], axis=2)  2.34 us
  transfers between devices with their start and end apart: 19, of which 11 were waited for; matrix products, arithmetic and copies ran while one was open for 12% of the time, Pallas kernels for 4%

profile of v5, /device:TPU:0, one launch (start us, length us, event | category | flops | bytes accessed | tf_op | source)
XLA Modules:
  0.0 111.6 jit_solution(1331575072237291734)
XLA Ops:
  0.6 2.3 %fusion.5 = (f32[4,2,64,256]{3,2,1,0:T(8,128)}, f32[4,2,64,256]{3,2,1,0:T(8,128)}) fusion(f32[4,2,128,256]{3,2,1,0:T(8,128)} %own.1), kind=kLoop, calls=%fused_computation.51 | loop fusion | bytes 2097152 | tf_op jit(solution)/shard_map/slice | solution.py:430
  2.9 4.9 %collective-permute-start = (f32[4,2,64,256]{3,2,1,0:T(8,128)}, f32[4,2,64,256]{3,2,1,0:T(8,128)S(1)}, u32[]{:S(2)}, u32[]{:S(2)}) collective-permute-start(f32[4,2,64,256]{3,2,1,0:T(8,128)} %get-tuple-element.59), channel_id=1, source_target_pairs={{0,2},{2,4},{4,6},{6,8},{8,10},{10,12},{12,14},{1,3},{3,5},{5,7},{... | collective-permute-start | bytes 1572872 | tf_op jit(solution)/shard_map/ppermute | solution.py:20
  7.8 1.3 %collective-permute-start.1 = (f32[4,2,64,256]{3,2,1,0:T(8,128)}, f32[4,2,64,256]{3,2,1,0:T(8,128)S(1)}, u32[]{:S(2)}, u32[]{:S(2)}) collective-permute-start(f32[4,2,64,256]{3,2,1,0:T(8,128)} %get-tuple-element.58), channel_id=1, source_target_pairs={{2,0},{4,2},{6,4},{8,6},{10,8},{12,10},{14,12},{3,1},{5,3},{7,5},{... | collective-permute-start | bytes 1572872 | tf_op jit(solution)/shard_map/ppermute | solution.py:20
  11.0 1.0 copy.17
  12.1 0.9 constant_dynamic-update-slice_fusion.3
  13.0 0.9 constant_dynamic-update-slice_fusion.2
  15.8 14.7 %collective-permute-done.above = f32[4,2,64,256]{3,2,1,0:T(8,128)S(1)} collective-permute-done((f32[4,2,64,256]{3,2,1,0:T(8,128)}, f32[4,2,64,256]{3,2,1,0:T(8,128)S(1)}, u32[]{:S(2)}, u32[]{:S(2)}) %collective-permute-start) | collective-permute-done | bytes 524320 | tf_op jit(solution)/shard_map/ppermute | solution.py:20
  31.4 2.1 %collective-permute-done.2.beside = f32[4,2,256,128]{3,2,1,0:T(8,128)} collective-permute-done((f32[4,2,256,128]{3,2,1,0:T(8,128)S(1)}, f32[4,2,256,128]{3,2,1,0:T(8,128)}, u32[]{:S(2)}, u32[]{:S(2)}) %collective-permute-start.2) | collective-permute-done | bytes 1048608 | tf_op jit(solution)/shard_map/ppermute | solution.py:25
  33.5 22.6 %fields.1 = (f32[4,2,256,256]{3,2,1,0:T(8,128)}, f32[4,2,256,128]{3,2,1,0:T(8,128)}, f32[8,16,8,128]{3,2,1,0:T(8,128)}, f32[8,16,8,128]{3,2,1,0:T(8,128)}) custom-call(s32[2,2]{1,0:T(2,128)} %broadcast_subtract_fusion.places, s32[1]{0:T(128)} %bitcast.2.side, f32[4,2,128,256]{3,2,1,0:T(8,128)} %own.1, f32[4,2,64,256]{3,2,1,0:T(8,128)} %copy-done.3, ...), custom_call_target="tpu_custom_call" | custom-call | tf_op jit(solution)/shard_map/fields/pallas_call | solution.py:246
  56.7 3.2 %collective-permute-done.4 = f32[8,16,8,128]{3,2,1,0:T(8,128)} collective-permute-done((f32[8,16,8,128]{3,2,1,0:T(8,128)}, f32[8,16,8,128]{3,2,1,0:T(8,128)}, u32[]{:S(2)}, u32[]{:S(2)}) %collective-permute-start.4) | collective-permute-done | bytes 524320 | tf_op jit(solution)/shard_map/ppermute | solution.py:25
  59.9 1.9 %add_bitcast_fusion = (f32[16,8,128]{2,1,0:T(8,128)S(1)}, f32[16,8,128]{2,1,0:T(8,128)S(1)}, f32[16,8,128]{2,1,0:T(8,128)S(1)}, f32[16,8,128]{2,1,0:T(8,128)S(1)...) fusion(f32[8,16,8,128]{3,2,1,0:T(8,128)} %collective-permute-don, ...), kind=kLoop, calls=%fused_computation.28 | loop fusion | flops 131072 | bytes 1572896 | tf_op jit(solution)/shard_map/add | solution.py:388
  61.8 5.3 %collective-permute-start.10 = (f32[16,8,128]{2,1,0:T(8,128)S(1)}, f32[16,8,128]{2,1,0:T(8,128)S(1)}, u32[]{:S(2)}, u32[]{:S(2)}) collective-permute-start(f32[16,8,128]{2,1,0:T(8,128)S(1)} %get-tuple-element.49), channel_id=1, source_target_pairs={{0,12},{2,14},{4,8},{6,10},{8,4},{10,6},{12,0},{14,2},{1,13},{3,15... | collective-permute-start | bytes 196616 | tf_op jit(solution)/shard_map/ppermute | solution.py:25
  67.5 1.2 %collective-permute-start.5 = (f32[16,8,128]{2,1,0:T(8,128)S(1)}, f32[16,8,128]{2,1,0:T(8,128)S(1)}, u32[]{:S(2)}, u32[]{:S(2)}) collective-permute-start(f32[16,8,128]{2,1,0:T(8,128)S(1)} %get-tuple-element.54), channel_id=1, source_target_pairs={{0,2},{2,0},{4,6},{6,4},{8,10},{10,8},{12,14},{14,12},{1,3},{3,1},... | collective-permute-start | bytes 196616 | tf_op jit(solution)/shard_map/ppermute | solution.py:25
  68.7 2.3 %collective-permute-start.7 = (f32[16,8,128]{2,1,0:T(8,128)S(1)}, f32[16,8,128]{2,1,0:T(8,128)S(1)}, u32[]{:S(2)}, u32[]{:S(2)}) collective-permute-start(f32[16,8,128]{2,1,0:T(8,128)S(1)} %get-tuple-element.52), channel_id=1, source_target_pairs={{0,6},{2,4},{4,2},{6,0},{8,14},{10,12},{12,10},{14,8},{1,7},{3,5},... | collective-permute-start | bytes 196616 | tf_op jit(solution)/shard_map/ppermute | solution.py:25
  71.1 2.1 %collective-permute-start.8 = (f32[16,8,128]{2,1,0:T(8,128)S(1)}, f32[16,8,128]{2,1,0:T(8,128)S(1)}, u32[]{:S(2)}, u32[]{:S(2)}) collective-permute-start(f32[16,8,128]{2,1,0:T(8,128)S(1)} %get-tuple-element.51), channel_id=1, source_target_pairs={{0,8},{2,10},{4,12},{6,14},{8,0},{10,2},{12,4},{14,6},{1,9},{3,11}... | collective-permute-start | bytes 196616 | tf_op jit(solution)/shard_map/ppermute | solution.py:25
  73.2 1.3 %collective-permute-done.11.refs_8_ = f32[16,8,128]{2,1,0:T(8,128)S(1)} collective-permute-done((f32[16,8,128]{2,1,0:T(8,128)S(1)}, f32[16,8,128]{2,1,0:T(8,128)S(1)}, u32[]{:S(2)}, u32[]{:S(2)}) %collective-permute-start.11) | collective-permute-done | bytes 65568 | tf_op jit(solution)/shard_map/ppermute | solution.py:25
  74.5 1.1 collective-permute-start.9
  75.5 1.1 %maximum_add_fusion.2 = (f32[4,2,64,256]{3,2,1,0:T(8,128)}, f32[4,2,64,256]{3,2,1,0:T(8,128)}) fusion(f32[4,2,64,128]{3,2,1,0:T(8,128)S(1)} %get-tuple-element.46, f32[4,2,64,128]{3,2,1,0:T(8,128)S(1)} %get-tuple-element.44, f32[4,2,256,256]{3,2,1,0:T(8,128)S(1)} %copy-done.1, f32[4,2,64,128]{3,2,1,0:T(8,128)S(1)} %get-tuple-element.45, ...), kind=kLoop, calls=%fused_computation.7 | loop fusion | flops 524288 | bytes 3145728 | tf_op jit(solution)/shard_map/add | solution.py:453
  76.7 1.6 %collective-permute-done.8.refs_5_ = f32[16,8,128]{2,1,0:T(8,128)S(1)} collective-permute-done((f32[16,8,128]{2,1,0:T(8,128)S(1)}, f32[16,8,128]{2,1,0:T(8,128)S(1)}, u32[]{:S(2)}, u32[]{:S(2)}) %collective-permute-start.8) | collective-permute-done | bytes 65568 | tf_op jit(solution)/shard_map/ppermute | solution.py:25
  78.3 2.6 %collective-permute-done.9.refs_6_ = f32[16,8,128]{2,1,0:T(8,128)S(1)} collective-permute-done((f32[16,8,128]{2,1,0:T(8,128)S(1)}, f32[16,8,128]{2,1,0:T(8,128)S(1)}, u32[]{:S(2)}, u32[]{:S(2)}) %collective-permute-start.9) | collective-permute-done | bytes 65568 | tf_op jit(solution)/shard_map/ppermute | solution.py:25
  80.9 2.8 %collective-permute-start.12 = (f32[4,2,64,256]{3,2,1,0:T(8,128)}, f32[4,2,64,256]{3,2,1,0:T(8,128)}, u32[]{:S(2)}, u32[]{:S(2)}) collective-permute-start(f32[4,2,64,256]{3,2,1,0:T(8,128)} %get-tuple-element.28), channel_id=1, source_target_pairs={{0,2},{2,4},{4,6},{6,8},{8,10},{10,12},{12,14},{1,3},{3,5},{5,7},{... | collective-permute-start | bytes 1572872 | tf_op jit(solution)/shard_map/ppermute | solution.py:20
  83.7 1.3 %collective-permute-start.13 = (f32[4,2,64,256]{3,2,1,0:T(8,128)}, f32[4,2,64,256]{3,2,1,0:T(8,128)}, u32[]{:S(2)}, u32[]{:S(2)}) collective-permute-start(f32[4,2,64,256]{3,2,1,0:T(8,128)} %get-tuple-element.29), channel_id=1, source_target_pairs={{2,0},{4,2},{6,4},{8,6},{10,8},{12,10},{14,12},{3,1},{5,3},{7,5},{... | collective-permute-start | bytes 1572872 | tf_op jit(solution)/shard_map/ppermute | solution.py:20
  86.5 2.1 %gram.1 = (f32[32,32]{1,0:T(8,128)}, f32[16,8,128]{2,1,0:T(8,128)}) custom-call(f32[16,8,128]{2,1,0:T(8,128)} %bitcast.48, f32[16,8,128]{2,1,0:T(8,128)} %get-tuple-element.30.refs_1_, f32[16,8,128]{2,1,0:T(8,128)} %copy-done.9, f32[16,8,128]{2,1,0:T(8,128)} %copy-done.10, f32[16,8,128]{2,1,0:T(8,128)} %copy-done.11, f32[16,8,128]{2,1,0:T(8,128)} %copy-done.12, ...), custom_call_target="tpu_custom_call" | custom-call | tf_op jit(solution)/shard_map/gram/pallas_call | solution.py:290
  88.5 1.4 %collective-permute-done.14 = f32[32,32]{1,0:T(8,128)S(1)} collective-permute-done((f32[32,32]{1,0:T(8,128)}, f32[32,32]{1,0:T(8,128)S(1)}, u32[]{:S(2)}, u32[]{:S(2)}) %collective-permute-start.14) | collective-permute-done | bytes 4128 | tf_op jit(solution)/shard_map/ppermute | solution.py:25
  90.7 2.6 %collective-permute-start.15 = (f32[32,32]{1,0:T(8,128)S(1)}, f32[32,32]{1,0:T(8,128)S(1)}, u32[]{:S(2)}, u32[]{:S(2)}) collective-permute-start(f32[32,32]{1,0:T(8,128)S(1)} %add.163), channel_id=1, source_target_pairs={{0,4},{2,6},{4,0},{6,2},{8,12},{10,14},{12,8},{14,10},{1,5},{3,7},... | collective-permute-start | bytes 12296 | tf_op jit(solution)/shard_map/ppermute | solution.py:25
  93.2 3.1 %collective-permute-start.16 = (f32[32,32]{1,0:T(8,128)S(1)}, f32[32,32]{1,0:T(8,128)S(1)}, u32[]{:S(2)}, u32[]{:S(2)}) collective-permute-start(f32[32,32]{1,0:T(8,128)S(1)} %add.163), channel_id=1, source_target_pairs={{0,8},{2,10},{4,12},{6,14},{8,0},{10,2},{12,4},{14,6},{1,9},{3,11}... | collective-permute-start | bytes 12296 | tf_op jit(solution)/shard_map/ppermute | solution.py:25
  96.3 2.0 %collective-permute-done.15 = f32[32,32]{1,0:T(8,128)S(1)} collective-permute-done((f32[32,32]{1,0:T(8,128)S(1)}, f32[32,32]{1,0:T(8,128)S(1)}, u32[]{:S(2)}, u32[]{:S(2)}) %collective-permute-start.15) | collective-permute-done | bytes 4128 | tf_op jit(solution)/shard_map/ppermute | solution.py:25
  99.2 2.7 %collective-permute-done.17 = f32[32,32]{1,0:T(8,128)S(1)} collective-permute-done((f32[32,32]{1,0:T(8,128)S(1)}, f32[32,32]{1,0:T(8,128)S(1)}, u32[]{:S(2)}, u32[]{:S(2)}) %collective-permute-start.17) | collective-permute-done | bytes 4128 | tf_op jit(solution)/shard_map/ppermute | solution.py:25
  102.3 1.1 %slice_select_fusion.1 = (f32[4,2,128,128]{3,2,1,0:T(8,128)S(1)}, f32[4,2,128,128]{3,2,1,0:T(8,128)S(1)}) fusion(f32[4,2,256,128]{3,2,1,0:T(8,128)} %copy-done.5, pred[]{:T(512)S(6)} %eq.30), kind=kLoop, calls=%fused_computation.9 | loop fusion | flops 262144 | bytes 1572865 | tf_op jit(solution)/shard_map/jit(_where)/select_n | solution.py:450
  103.4 2.2 %collective-permute-done.18.refs_1_ = f32[32,32]{1,0:T(8,128)S(1)} collective-permute-done((f32[32,32]{1,0:T(8,128)S(1)}, f32[32,32]{1,0:T(8,128)S(1)}, u32[]{:S(2)}, u32[]{:S(2)}) %collective-permute-start.18) | collective-permute-done | bytes 4128 | tf_op jit(solution)/shard_map/ppermute | solution.py:25
  106.3 2.9 %ortho.1 = f32[8,2,1024]{2,1,0:T(2,128)} custom-call(f32[32,32]{1,0:T(8,128)} %copy-done.6, f32[32,32]{1,0:T(8,128)} %copy-done.14, f32[16,8,128]{2,1,0:T(8,128)} %bitcast.49, f32[16,8,128]{2,1,0:T(8,128)} %get-tuple-element.39.refs_3_), custom_call_target="tpu_custom_call" | custom-call | tf_op jit(solution)/shard_map/ortho/pallas_call | solution.py:365
  109.2 2.3 %fusion = f32[4,2,128,256]{3,2,1,0:T(8,128)} fusion(f32[4,2,128,128]{3,2,1,0:T(8,128)S(1)} %get-tuple-element.57, f32[4,2,128,128]{3,2,1,0:T(8,128)S(1)} %get-tuple-element.56, f32[4,2,64,256]{3,2,1,0:T(8,128)} %collective-permute-done.13, f32[4,2,64,256]{3,2,1,0:T(8,128)} %collective-permute-done.12, f32[4,2,256,256]{3,2,1,0:T(8,128)S(1)} %copy-done.1), kind=kLoop, calls=%fused_computation.5 | loop fusion | flops 1048576 | bytes 4194304 | tf_op jit(solution)/shard_map/add | solution.py:418
  (76 shorter events, 9.7 us)
Async XLA Ops:
  0.6 8.5 %copy-start.15 = (f32[2,63]{1,0:T(2,128)S(1)}, f32[2,63]{1,0:T(2,128)}, u32[]{:S(2)}) copy-start(f32[2,63]{1,0:T(2,128)} %param.9) | copy-start | bytes 1516
  2.9 27.6 %collective-permute-start = (f32[4,2,64,256]{3,2,1,0:T(8,128)}, f32[4,2,64,256]{3,2,1,0:T(8,128)S(1)}, u32[]{:S(2)}, u32[]{:S(2)}) collective-permute-start(f32[4,2,64,256]{3,2,1,0:T(8,128)} %get-tuple-element.59), channel_id=1, source_target_pairs={{0,2},{2,4},{4,6},{6,8},{8,10},{10,12},{12,14},{1,3},{3,5},{5,7},{... | collective-permute-start | bytes 1572872 | tf_op jit(solution)/shard_map/ppermute | solution.py:20
  7.8 22.7 %collective-permute-start.1 = (f32[4,2,64,256]{3,2,1,0:T(8,128)}, f32[4,2,64,256]{3,2,1,0:T(8,128)S(1)}, u32[]{:S(2)}, u32[]{:S(2)}) collective-permute-start(f32[4,2,64,256]{3,2,1,0:T(8,128)} %get-tuple-element.58), channel_id=1, source_target_pairs={{2,0},{4,2},{6,4},{8,6},{10,8},{12,10},{14,12},{3,1},{5,3},{7,5},{... | collective-permute-start | bytes 1572872 | tf_op jit(solution)/shard_map/ppermute | solution.py:20
  9.9 5.8 %copy-start = (f32[4,2,128,256]{3,2,1,0:T(8,128)S(1)}, f32[4,2,128,256]{3,2,1,0:T(8,128)}, u32[]{:S(2)}) copy-start(f32[4,2,128,256]{3,2,1,0:T(8,128)} %own.1) | copy-start | bytes 3145732
  15.8 14.9 %copy-start.2 = (bf16[8,256,256]{2,1,0:T(8,128)(2,1)}, bf16[8,256,256]{2,1,0:T(8,128)(2,1)S(1)}, u32[]{:S(2)}) copy-start(bf16[8,256,256]{2,1,0:T(8,128)(2,1)S(1)} %constant_dynamic-update-slice_fusion.tab) | copy-start | bytes 3145732
  15.8 15.0 %copy-start.16 = (s32[2,2]{1,0:T(2,128)S(1)}, s32[2,2]{1,0:T(2,128)}, u32[]{:S(2)}) copy-start(s32[2,2]{1,0:T(2,128)} %param.11) | copy-start | bytes 52
  30.6 2.9 %collective-permute-start.2 = (f32[4,2,256,128]{3,2,1,0:T(8,128)S(1)}, f32[4,2,256,128]{3,2,1,0:T(8,128)}, u32[]{:S(2)}, u32[]{:S(2)}) collective-permute-start(f32[4,2,256,128]{3,2,1,0:T(8,128)S(1)} %pad_maximum_fusion), channel_id=1, source_target_pairs={{0,1},{1,0},{2,3},{3,2},{4,5},{5,4},{6,7},{7,6},{8,9},{9,8},{10,11... | collective-permute-start | bytes 3145736 | tf_op jit(solution)/shard_map/ppermute | solution.py:25
  56.1 19.4 %copy-start.1 = (f32[4,2,256,256]{3,2,1,0:T(8,128)S(1)}, f32[4,2,256,256]{3,2,1,0:T(8,128)}, u32[]{:S(2)}) copy-start(f32[4,2,256,256]{3,2,1,0:T(8,128)} %get-tuple-element.24) | copy-start | bytes 6291460
  56.2 12.5 %collective-permute-start.3 = (f32[4,2,256,128]{3,2,1,0:T(8,128)}, f32[4,2,256,128]{3,2,1,0:T(8,128)S(1)}, u32[]{:S(2)}, u32[]{:S(2)}) collective-permute-start(f32[4,2,256,128]{3,2,1,0:T(8,128)} %get-tuple-element.25), channel_id=1, source_target_pairs={{0,1},{1,0},{2,3},{3,2},{4,5},{5,4},{6,7},{7,6},{8,9},{9,8},{10,11... | collective-permute-start | bytes 3145736 | tf_op jit(solution)/shard_map/ppermute | solution.py:25
  56.3 3.6 %collective-permute-start.4 = (f32[8,16,8,128]{3,2,1,0:T(8,128)}, f32[8,16,8,128]{3,2,1,0:T(8,128)}, u32[]{:S(2)}, u32[]{:S(2)}) collective-permute-start(f32[8,16,8,128]{3,2,1,0:T(8,128)} %get-tuple-element.27), channel_id=1, source_target_pairs={{0,1},{1,0},{2,3},{3,2},{4,5},{5,4},{6,7},{7,6},{8,9},{9,8},{10,11... | collective-permute-start | bytes 1572872 | tf_op jit(solution)/shard_map/ppermute | solution.py:25
  61.8 9.3 %collective-permute-start.10 = (f32[16,8,128]{2,1,0:T(8,128)S(1)}, f32[16,8,128]{2,1,0:T(8,128)S(1)}, u32[]{:S(2)}, u32[]{:S(2)}) collective-permute-start(f32[16,8,128]{2,1,0:T(8,128)S(1)} %get-tuple-element.49), channel_id=1, source_target_pairs={{0,12},{2,14},{4,8},{6,10},{8,4},{10,6},{12,0},{14,2},{1,13},{3,15... | collective-permute-start | bytes 196616 | tf_op jit(solution)/shard_map/ppermute | solution.py:25
  67.2 7.3 %collective-permute-start.11 = (f32[16,8,128]{2,1,0:T(8,128)S(1)}, f32[16,8,128]{2,1,0:T(8,128)S(1)}, u32[]{:S(2)}, u32[]{:S(2)}) collective-permute-start(f32[16,8,128]{2,1,0:T(8,128)S(1)} %get-tuple-element.48), channel_id=1, source_target_pairs={{0,14},{2,12},{4,10},{6,8},{8,6},{10,4},{12,2},{14,0},{1,15},{3,13... | collective-permute-start | bytes 196616 | tf_op jit(solution)/shard_map/ppermute | solution.py:25
  67.5 9.2 %collective-permute-start.5 = (f32[16,8,128]{2,1,0:T(8,128)S(1)}, f32[16,8,128]{2,1,0:T(8,128)S(1)}, u32[]{:S(2)}, u32[]{:S(2)}) collective-permute-start(f32[16,8,128]{2,1,0:T(8,128)S(1)} %get-tuple-element.54), channel_id=1, source_target_pairs={{0,2},{2,0},{4,6},{6,4},{8,10},{10,8},{12,14},{14,12},{1,3},{3,1},... | collective-permute-start | bytes 196616 | tf_op jit(solution)/shard_map/ppermute | solution.py:25
  68.7 8.0 %collective-permute-start.6 = (f32[16,8,128]{2,1,0:T(8,128)S(1)}, f32[16,8,128]{2,1,0:T(8,128)S(1)}, u32[]{:S(2)}, u32[]{:S(2)}) collective-permute-start(f32[16,8,128]{2,1,0:T(8,128)S(1)} %get-tuple-element.53), channel_id=1, source_target_pairs={{0,4},{2,6},{4,0},{6,2},{8,12},{10,14},{12,8},{14,10},{1,5},{3,7},... | collective-permute-start | bytes 196616 | tf_op jit(solution)/shard_map/ppermute | solution.py:25
  68.7 8.0 %copy-start.5 = (f32[4,2,256,128]{3,2,1,0:T(8,128)}, f32[4,2,256,128]{3,2,1,0:T(8,128)S(1)}, u32[]{:S(2)}) copy-start(f32[4,2,256,128]{3,2,1,0:T(8,128)S(1)} %collective-permute-done.3) | copy-start | bytes 3145732
  68.7 8.0 %collective-permute-start.7 = (f32[16,8,128]{2,1,0:T(8,128)S(1)}, f32[16,8,128]{2,1,0:T(8,128)S(1)}, u32[]{:S(2)}, u32[]{:S(2)}) collective-permute-start(f32[16,8,128]{2,1,0:T(8,128)S(1)} %get-tuple-element.52), channel_id=1, source_target_pairs={{0,6},{2,4},{4,2},{6,0},{8,14},{10,12},{12,10},{14,8},{1,7},{3,5},... | collective-permute-start | bytes 196616 | tf_op jit(solution)/shard_map/ppermute | solution.py:25
  71.1 15.3 %copy-start.7 = (f32[16,8,128]{2,1,0:T(8,128)}, f32[16,8,128]{2,1,0:T(8,128)S(1)}, u32[]{:S(2)}) copy-start(f32[16,8,128]{2,1,0:T(8,128)S(1)} %collective-permute-done.10.refs_7_) | copy-start | bytes 196612
  71.1 7.2 %collective-permute-start.8 = (f32[16,8,128]{2,1,0:T(8,128)S(1)}, f32[16,8,128]{2,1,0:T(8,128)S(1)}, u32[]{:S(2)}, u32[]{:S(2)}) collective-permute-start(f32[16,8,128]{2,1,0:T(8,128)S(1)} %get-tuple-element.51), channel_id=1, source_target_pairs={{0,8},{2,10},{4,12},{6,14},{8,0},{10,2},{12,4},{14,6},{1,9},{3,11}... | collective-permute-start | bytes 196616 | tf_op jit(solution)/shard_map/ppermute | solution.py:25
  74.5 11.9 %copy-start.8 = (f32[16,8,128]{2,1,0:T(8,128)}, f32[16,8,128]{2,1,0:T(8,128)S(1)}, u32[]{:S(2)}) copy-start(f32[16,8,128]{2,1,0:T(8,128)S(1)} %collective-permute-done.11.refs_8_) | copy-start | bytes 196612
  74.5 6.4 %collective-permute-start.9 = (f32[16,8,128]{2,1,0:T(8,128)S(1)}, f32[16,8,128]{2,1,0:T(8,128)S(1)}, u32[]{:S(2)}, u32[]{:S(2)}) collective-permute-start(f32[16,8,128]{2,1,0:T(8,128)S(1)} %get-tuple-element.50), channel_id=1, source_target_pairs={{0,10},{2,8},{4,14},{6,12},{8,2},{10,0},{12,6},{14,4},{1,11},{3,9}... | collective-permute-start | bytes 196616 | tf_op jit(solution)/shard_map/ppermute | solution.py:25
  76.7 9.8 %copy-start.9 = (f32[16,8,128]{2,1,0:T(8,128)}, f32[16,8,128]{2,1,0:T(8,128)S(1)}, u32[]{:S(2)}) copy-start(f32[16,8,128]{2,1,0:T(8,128)S(1)} %collective-permute-done.5.refs_2_) | copy-start | bytes 196612
  76.7 9.7 %copy-start.10 = (f32[16,8,128]{2,1,0:T(8,128)}, f32[16,8,128]{2,1,0:T(8,128)S(1)}, u32[]{:S(2)}) copy-start(f32[16,8,128]{2,1,0:T(8,128)S(1)} %collective-permute-done.6.refs_3_) | copy-start | bytes 196612
  76.7 9.7 %copy-start.11 = (f32[16,8,128]{2,1,0:T(8,128)}, f32[16,8,128]{2,1,0:T(8,128)S(1)}, u32[]{:S(2)}) copy-start(f32[16,8,128]{2,1,0:T(8,128)S(1)} %collective-permute-done.7.refs_4_) | copy-start | bytes 196612
  78.3 8.1 %copy-start.12 = (f32[16,8,128]{2,1,0:T(8,128)}, f32[16,8,128]{2,1,0:T(8,128)S(1)}, u32[]{:S(2)}) copy-start(f32[16,8,128]{2,1,0:T(8,128)S(1)} %collective-permute-done.8.refs_5_) | copy-start | bytes 196612
  80.9 5.5 %copy-start.13 = (f32[16,8,128]{2,1,0:T(8,128)}, f32[16,8,128]{2,1,0:T(8,128)S(1)}, u32[]{:S(2)}) copy-start(f32[16,8,128]{2,1,0:T(8,128)S(1)} %collective-permute-done.9.refs_6_) | copy-start | bytes 196612
  80.9 28.3 %collective-permute-start.12 = (f32[4,2,64,256]{3,2,1,0:T(8,128)}, f32[4,2,64,256]{3,2,1,0:T(8,128)}, u32[]{:S(2)}, u32[]{:S(2)}) collective-permute-start(f32[4,2,64,256]{3,2,1,0:T(8,128)} %get-tuple-element.28), channel_id=1, source_target_pairs={{0,2},{2,4},{4,6},{6,8},{8,10},{10,12},{12,14},{1,3},{3,5},{5,7},{... | collective-permute-start | bytes 1572872 | tf_op jit(solution)/shard_map/ppermute | solution.py:20
  83.7 25.5 %collective-permute-start.13 = (f32[4,2,64,256]{3,2,1,0:T(8,128)}, f32[4,2,64,256]{3,2,1,0:T(8,128)}, u32[]{:S(2)}, u32[]{:S(2)}) collective-permute-start(f32[4,2,64,256]{3,2,1,0:T(8,128)} %get-tuple-element.29), channel_id=1, source_target_pairs={{2,0},{4,2},{6,4},{8,6},{10,8},{12,10},{14,12},{3,1},{5,3},{7,5},{... | collective-permute-start | bytes 1572872 | tf_op jit(solution)/shard_map/ppermute | solution.py:20
  88.5 1.4 %collective-permute-start.14 = (f32[32,32]{1,0:T(8,128)}, f32[32,32]{1,0:T(8,128)S(1)}, u32[]{:S(2)}, u32[]{:S(2)}) collective-permute-start(f32[32,32]{1,0:T(8,128)} %get-tuple-element.38), channel_id=1, source_target_pairs={{0,1},{1,0},{2,3},{3,2},{4,5},{5,4},{6,7},{7,6},{8,9},{9,8},{10,11... | collective-permute-start | bytes 12296 | tf_op jit(solution)/shard_map/ppermute | solution.py:25
  90.7 7.6 %collective-permute-start.15 = (f32[32,32]{1,0:T(8,128)S(1)}, f32[32,32]{1,0:T(8,128)S(1)}, u32[]{:S(2)}, u32[]{:S(2)}) collective-permute-start(f32[32,32]{1,0:T(8,128)S(1)} %add.163), channel_id=1, source_target_pairs={{0,4},{2,6},{4,0},{6,2},{8,12},{10,14},{12,8},{14,10},{1,5},{3,7},... | collective-permute-start | bytes 12296 | tf_op jit(solution)/shard_map/ppermute | solution.py:25
  93.2 5.9 %collective-permute-start.16 = (f32[32,32]{1,0:T(8,128)S(1)}, f32[32,32]{1,0:T(8,128)S(1)}, u32[]{:S(2)}, u32[]{:S(2)}) collective-permute-start(f32[32,32]{1,0:T(8,128)S(1)} %add.163), channel_id=1, source_target_pairs={{0,8},{2,10},{4,12},{6,14},{8,0},{10,2},{12,4},{14,6},{1,9},{3,11}... | collective-permute-start | bytes 12296 | tf_op jit(solution)/shard_map/ppermute | solution.py:25
  96.3 5.5 %collective-permute-start.17 = (f32[32,32]{1,0:T(8,128)S(1)}, f32[32,32]{1,0:T(8,128)S(1)}, u32[]{:S(2)}, u32[]{:S(2)}) collective-permute-start(f32[32,32]{1,0:T(8,128)S(1)} %add.163), channel_id=1, source_target_pairs={{0,12},{2,14},{4,8},{6,10},{8,4},{10,6},{12,0},{14,2},{1,13},{3,15... | collective-permute-start | bytes 12296 | tf_op jit(solution)/shard_map/ppermute | solution.py:25
  101.9 3.8 %collective-permute-start.18 = (f32[32,32]{1,0:T(8,128)S(1)}, f32[32,32]{1,0:T(8,128)S(1)}, u32[]{:S(2)}, u32[]{:S(2)}) collective-permute-start(f32[32,32]{1,0:T(8,128)S(1)} %add_add_fusion.refs_0_), channel_id=1, source_target_pairs={{0,2},{2,0},{4,6},{6,4},{8,10},{10,8},{12,14},{14,12},{1,3},{3,1},... | collective-permute-start | bytes 12296 | tf_op jit(solution)/shard_map/ppermute | solution.py:25
  (4 other events, 10.4 us)

commit v6 on v5

--- a/solution.py
+++ b/solution.py
@@ -371,22 +371,34 @@
     return lax.dynamic_index_in_dim(array, which, dim, keepdims=False)
 
 
-def updates(probe, keep, send, bottom, top, middle):
+def own_block(probe):
     modes, _, width, _ = probe.shape
+    devices = lax.axis_size("row") * lax.axis_size("col")
+    share = width // devices
+    index = lax.axis_index(("row", "col"))
+    block = lax.dynamic_slice_in_dim(probe, index * share, share, 2)
+    return block.transpose(1, 0, 2, 3).reshape(2 * modes, share, width)
+
+
+def updates(own_probe, keep, send, bottom, top, middle):
+    rows, share, width = own_probe.shape
+    modes = rows // 2
     row_devices = lax.axis_size("row")
     col_devices = lax.axis_size("col")
-    devices = row_devices * col_devices
-    share = width // devices
     row_idx, col_idx = lax.axis_index("row"), lax.axis_index("col")
-    index = row_idx * col_devices + col_idx
     row_bits = [1 << b for b in range(row_devices.bit_length() - 1)]
 
     if share == SUBLANES and row_devices <= 8:
         received = swapped(send, "col", 1)
+        pairs = (row_devices // 2, 2) + keep.shape[1:]
+        keep, received = keep.reshape(pairs), received.reshape(pairs)
+        low, high = row_idx % 2, row_idx // 2
+        send = take(keep, 1 - low, 1) + take(received, 1 - low, 1)
+        keep, received = take(keep, low, 1) + take(received, low, 1), swapped(send, "row", 1)
         parts = []
-        for k in range(row_devices):
-            block = take(keep, row_idx ^ k, 0) + take(received, row_idx ^ k, 0)
-            parts.append(swapped(block, "row", k) if k else block)
+        for k in range(row_devices // 2):
+            block = take(keep, high ^ k, 0) + take(received, high ^ k, 0)
+            parts.append(swapped(block, "row", 2 * k) if k else block)
     else:
         even, odd = jnp.where(col_idx == 0, keep, send), jnp.where(col_idx == 0, send, keep)
         grad = jnp.stack([even, odd], axis=1).transpose(0, 1, 3, 2, 4)
@@ -402,8 +414,6 @@
     parts, bottom, top = lax.optimization_barrier((parts, bottom, top))
     from_above = shifted(bottom, "row", 1)
     from_below = shifted(top, "row", -1)
-    own_probe = lax.dynamic_slice_in_dim(probe, index * share, share, 2)
-    own_probe = own_probe.transpose(1, 0, 2, 3).reshape(2 * modes, share, width)
     total, own_grad = gram(own_probe, parts)
     total = total + swapped(total, "col", 1)
     high_bits = row_bits[1:]
@@ -426,10 +436,14 @@
     row_idx = lax.axis_index("row")
     col_idx = lax.axis_index("col")
 
-    above = shifted(object_slices[:, :, tile_rows - half :], "row", 1)
-    below = shifted(object_slices[:, :, :half], "row", -1)
+    bottom_rows, later = lax.optimization_barrier(
+        (object_slices[:, :, tile_rows - half :], object_slices)
+    )
+    above = shifted(bottom_rows, "row", 1)
+    below = shifted(later[:, :, :half], "row", -1)
     tab = block_tables(taps, width)
-    above, below, tab = lax.optimization_barrier((above, below, tab))
+    own_probe = own_block(probe)
+    above, below, tab, own_probe = lax.optimization_barrier((above, below, tab, own_probe))
     near = (1 - col_idx) * (tile_cols - LANES)
     strip = jnp.concatenate([
         lax.dynamic_slice_in_dim(x, near, LANES, 3) for x in (above, object_slices, below)
@@ -454,7 +468,7 @@
 
     bottom, top = folded(half + tile_rows, tile_rows + 2 * half), folded(0, half)
     new_probe, object_grad = updates(
-        probe, gkeep, gsend, bottom, top, lambda: folded(half, half + tile_rows)
+        own_probe, gkeep, gsend, bottom, top, lambda: folded(half, half + tile_rows)
     )
     return (object_grad, new_probe)
 

time: 112 us -> 115 us (1.027)
  waiting for transfers between devices: 34.6 us -> 38.3 us
  starting transfers between devices: 29.2 us -> 25.8 us
  other arithmetic: 9.64 us -> 11.2 us
  local copies, waits for them, and re-layouts: 9.51 us -> 10.9 us
    ppermute x15 -> x12, starting transfers between devices: 19 us -> 12.3 us  [swapped(): return lax.ppermute(value, axis, [(i, i ^ bit) for i in range(count)])]
    ppermute x15 -> x12, waiting for transfers between devices: 19.9 us -> 24.8 us  [swapped(): return lax.ppermute(value, axis, [(i, i ^ bit) for i in range(count)])]
    ppermute x4, starting transfers between devices: 10.2 us -> 13.4 us  [shifted(): return lax.ppermute(value, axis, pairs)]
    add x1 -> x3, other arithmetic: 1.92 us -> 3.49 us  [the longest x1 1.76 us: updates(): send = take(keep, 1 - low, 1) + take(received, 1 - low, 1)]
    slice x1 -> x2, local copies, waits for them, and re-layouts: 2.3 us -> 3.75 us  [the longest x1 1.88 us: per_device(): object_slices[:, :, tile_rows - half:]]
    ppermute x4, waiting for transfers between devices: 14.7 us -> 13.4 us  [shifted(): return lax.ppermute(value, axis, pairs)]
    unnamed x39 -> x31, local copies, waits for them, and re-layouts: 3.44 us -> 3.42 us
  transfers between devices with their start and end apart: 19 -> 16, of which waited for: 11 -> 12; matrix products, arithmetic and copies ran while one was open for 12% -> 13% of each run, Pallas kernels for 4% -> 4%
where the time goes in v6:
time: 115 us
  waiting for transfers between devices  38.3 us (33%)
  Pallas kernels  27.4 us (24%)
  starting transfers between devices  25.8 us (22%)
  other arithmetic  11.2 us (10%)
  local copies, waits for them, and re-layouts  10.9 us (9%)
    ppermute x12, waiting for transfers between devices, swapped(): return lax.ppermute(value, axis, [(i, i ^ bit) for i in range(count)])  24.8 us
    pallas_call x1, Pallas kernels, fields(): pl.pallas_call(field_kernel, out_shape=[jax.ShapeDtypeStruct(s, F32) for...  22.6 us
    ppermute x4, waiting for transfers between devices, shifted(): return lax.ppermute(value, axis, pairs)  13.4 us
    ppermute x4, starting transfers between devices, shifted(): return lax.ppermute(value, axis, pairs)  13.4 us
    ppermute x12, starting transfers between devices, swapped(): return lax.ppermute(value, axis, [(i, i ^ bit) for i in range(count)])  12.3 us
    unnamed x31, local copies, waits for them, and re-layouts  3.42 us
    pallas_call x1, Pallas kernels, ortho(): pl.pallas_call(body, out_shape=jax.ShapeDtypeStruct((modes, 2, pixels), F...  2.92 us
    add x1, other arithmetic, updates(): object_grad = middle() + jnp.concatenate([from_above, from_below], axis=2)  2.34 us
  transfers between devices with their start and end apart: 16, of which 12 were waited for; matrix products, arithmetic and copies ran while one was open for 13% of the time, Pallas kernels for 4%

profile of v6, /device:TPU:0, one launch (start us, length us, event | category | flops | bytes accessed | tf_op | source)
XLA Modules:
  0.0 114.6 jit_solution(8426835319802411783)
XLA Ops:
  0.6 1.9 %slice.30 = f32[4,2,64,256]{3,2,1,0:T(8,128)} slice(f32[4,2,128,256]{3,2,1,0:T(8,128)} %own.1), slice={[0:4], [0:2], [64:128], [0:256]} | slice | bytes 1048576 | tf_op jit(solution)/shard_map/slice | solution.py:440
  2.5 1.9 %slice.31 = f32[4,2,64,256]{3,2,1,0:T(8,128)} slice(f32[4,2,128,256]{3,2,1,0:T(8,128)} %own.1), slice={[0:4], [0:2], [0:64], [0:256]} | slice | bytes 1048576 | tf_op jit(solution)/shard_map/slice | solution.py:443
  4.4 1.3 %collective-permute-start.1 = (f32[4,2,64,256]{3,2,1,0:T(8,128)}, f32[4,2,64,256]{3,2,1,0:T(8,128)S(1)}, u32[]{:S(2)}, u32[]{:S(2)}) collective-permute-start(f32[4,2,64,256]{3,2,1,0:T(8,128)} %slice.31), channel_id=1, source_target_pairs={{2,0},{4,2},{6,4},{8,6},{10,8},{12,10},{14,12},{3,1},{5,3},{7,5},{... | collective-permute-start | bytes 1572872 | tf_op jit(solution)/shard_map/ppermute | solution.py:20
  5.7 5.5 %collective-permute-start = (f32[4,2,64,256]{3,2,1,0:T(8,128)}, f32[4,2,64,256]{3,2,1,0:T(8,128)S(1)}, u32[]{:S(2)}, u32[]{:S(2)}) collective-permute-start(f32[4,2,64,256]{3,2,1,0:T(8,128)} %slice.30), channel_id=1, source_target_pairs={{0,2},{2,4},{4,6},{6,8},{8,10},{10,12},{12,14},{1,3},{3,5},{5,7},{... | collective-permute-start | bytes 1572872 | tf_op jit(solution)/shard_map/ppermute | solution.py:20
  13.1 1.0 copy.22
  14.1 0.9 constant_dynamic-update-slice_fusion.3
  17.5 0.9 constant_dynamic-update-slice_fusion.1
  19.4 2.0 %collective-permute-done.1.below = f32[4,2,64,256]{3,2,1,0:T(8,128)S(1)} collective-permute-done((f32[4,2,64,256]{3,2,1,0:T(8,128)}, f32[4,2,64,256]{3,2,1,0:T(8,128)S(1)}, u32[]{:S(2)}, u32[]{:S(2)}) %collective-permute-start.1) | collective-permute-done | bytes 524320 | tf_op jit(solution)/shard_map/ppermute | solution.py:20
  21.4 11.5 %collective-permute-done.above = f32[4,2,64,256]{3,2,1,0:T(8,128)S(1)} collective-permute-done((f32[4,2,64,256]{3,2,1,0:T(8,128)}, f32[4,2,64,256]{3,2,1,0:T(8,128)S(1)}, u32[]{:S(2)}, u32[]{:S(2)}) %collective-permute-start) | collective-permute-done | bytes 524320 | tf_op jit(solution)/shard_map/ppermute | solution.py:20
  33.7 2.1 %collective-permute-done.2.beside = f32[4,2,256,128]{3,2,1,0:T(8,128)} collective-permute-done((f32[4,2,256,128]{3,2,1,0:T(8,128)S(1)}, f32[4,2,256,128]{3,2,1,0:T(8,128)}, u32[]{:S(2)}, u32[]{:S(2)}) %collective-permute-start.2) | collective-permute-done | bytes 1048608 | tf_op jit(solution)/shard_map/ppermute | solution.py:25
  35.8 22.6 %fields.1 = (f32[4,2,256,256]{3,2,1,0:T(8,128)}, f32[4,2,256,128]{3,2,1,0:T(8,128)}, f32[8,16,8,128]{3,2,1,0:T(8,128)}, f32[8,16,8,128]{3,2,1,0:T(8,128)}) custom-call(s32[2,2]{1,0:T(2,128)} %broadcast_subtract_fusion.places, s32[1]{0:T(128)} %bitcast.2.side, f32[4,2,128,256]{3,2,1,0:T(8,128)} %own.1, f32[4,2,64,256]{3,2,1,0:T(8,128)} %copy-done.4, ...), custom_call_target="tpu_custom_call" | custom-call | tf_op jit(solution)/shard_map/fields/pallas_call | solution.py:246
  59.0 3.2 %collective-permute-done.4 = f32[8,16,8,128]{3,2,1,0:T(8,128)} collective-permute-done((f32[8,16,8,128]{3,2,1,0:T(8,128)}, f32[8,16,8,128]{3,2,1,0:T(8,128)}, u32[]{:S(2)}, u32[]{:S(2)}) %collective-permute-start.4) | collective-permute-done | bytes 524320 | tf_op jit(solution)/shard_map/ppermute | solution.py:25
  62.2 1.8 %fusion.3 = f32[4,16,8,128]{3,2,1,0:T(8,128)} fusion(f32[4,2,16,8,128]{4,3,2,1,0:T(8,128)} %bitcast.13, s32[]{:T(128)S(6)} %select_n.90, f32[4,2,16,8,128]{4,3,2,1,0:T(8,128)} %bitcast.68), kind=kLoop, calls=%fused_computation.19 | loop fusion | flops 65536 | bytes 786436 | tf_op jit(solution)/shard_map/add | solution.py:396
  64.0 2.4 %collective-permute-start.5 = (f32[4,16,8,128]{3,2,1,0:T(8,128)}, f32[4,16,8,128]{3,2,1,0:T(8,128)S(1)}, u32[]{:S(2)}, u32[]{:S(2)}) collective-permute-start(f32[4,16,8,128]{3,2,1,0:T(8,128)} %fusion.3), channel_id=1, source_target_pairs={{0,2},{2,0},{4,6},{6,4},{8,10},{10,8},{12,14},{14,12},{1,3},{3,1},... | collective-permute-start | bytes 786440 | tf_op jit(solution)/shard_map/ppermute | solution.py:25
  66.4 1.1 dynamic-slice_add_fusion
  67.4 5.8 %collective-permute-done.5 = f32[4,16,8,128]{3,2,1,0:T(8,128)S(1)} collective-permute-done((f32[4,16,8,128]{3,2,1,0:T(8,128)}, f32[4,16,8,128]{3,2,1,0:T(8,128)S(1)}, u32[]{:S(2)}, u32[]{:S(2)}) %collective-permute-start.5) | collective-permute-done | bytes 262176 | tf_op jit(solution)/shard_map/ppermute | solution.py:25
  73.9 1.6 %collective-permute-start.6 = (f32[16,8,128]{2,1,0:T(8,128)S(1)}, f32[16,8,128]{2,1,0:T(8,128)S(1)}, u32[]{:S(2)}, u32[]{:S(2)}) collective-permute-start(f32[16,8,128]{2,1,0:T(8,128)S(1)} %get-tuple-element.50), channel_id=1, source_target_pairs={{0,4},{2,6},{4,0},{6,2},{8,12},{10,14},{12,8},{14,10},{1,5},{3,7},... | collective-permute-start | bytes 196616 | tf_op jit(solution)/shard_map/ppermute | solution.py:25
  75.5 1.9 %collective-permute-start.7 = (f32[16,8,128]{2,1,0:T(8,128)S(1)}, f32[16,8,128]{2,1,0:T(8,128)S(1)}, u32[]{:S(2)}, u32[]{:S(2)}) collective-permute-start(f32[16,8,128]{2,1,0:T(8,128)S(1)} %get-tuple-element.49), channel_id=1, source_target_pairs={{0,8},{2,10},{4,12},{6,14},{8,0},{10,2},{12,4},{14,6},{1,9},{3,11}... | collective-permute-start | bytes 196616 | tf_op jit(solution)/shard_map/ppermute | solution.py:25
  78.4 1.2 %maximum_add_fusion.2 = (f32[4,2,64,256]{3,2,1,0:T(8,128)}, f32[4,2,64,256]{3,2,1,0:T(8,128)}) fusion(f32[4,2,64,128]{3,2,1,0:T(8,128)S(1)} %get-tuple-element.44, f32[4,2,64,128]{3,2,1,0:T(8,128)S(1)} %get-tuple-element.42, f32[4,2,256,256]{3,2,1,0:T(8,128)S(1)} %copy-done.1, f32[4,2,64,128]{3,2,1,0:T(8,128)S(1)} %get-tuple-element.43, ...), kind=kLoop, calls=%fused_computation.7 | loop fusion | flops 524288 | bytes 3145728 | tf_op jit(solution)/shard_map/add | solution.py:467
  79.6 2.9 %collective-permute-done.7.refs_3_ = f32[16,8,128]{2,1,0:T(8,128)S(1)} collective-permute-done((f32[16,8,128]{2,1,0:T(8,128)S(1)}, f32[16,8,128]{2,1,0:T(8,128)S(1)}, u32[]{:S(2)}, u32[]{:S(2)}) %collective-permute-start.7) | collective-permute-done | bytes 65568 | tf_op jit(solution)/shard_map/ppermute | solution.py:25
  82.5 1.0 collective-permute-done.8.refs_4_
  83.5 1.3 %collective-permute-start.10 = (f32[4,2,64,256]{3,2,1,0:T(8,128)}, f32[4,2,64,256]{3,2,1,0:T(8,128)}, u32[]{:S(2)}, u32[]{:S(2)}) collective-permute-start(f32[4,2,64,256]{3,2,1,0:T(8,128)} %get-tuple-element.30), channel_id=1, source_target_pairs={{2,0},{4,2},{6,4},{8,6},{10,8},{12,10},{14,12},{3,1},{5,3},{7,5},{... | collective-permute-start | bytes 1572872 | tf_op jit(solution)/shard_map/ppermute | solution.py:20
  84.8 5.3 %collective-permute-start.9 = (f32[4,2,64,256]{3,2,1,0:T(8,128)}, f32[4,2,64,256]{3,2,1,0:T(8,128)}, u32[]{:S(2)}, u32[]{:S(2)}) collective-permute-start(f32[4,2,64,256]{3,2,1,0:T(8,128)} %get-tuple-element.29), channel_id=1, source_target_pairs={{0,2},{2,4},{4,6},{6,8},{8,10},{10,12},{12,14},{1,3},{3,5},{5,7},{... | collective-permute-start | bytes 1572872 | tf_op jit(solution)/shard_map/ppermute | solution.py:20
  90.2 1.9 %gram.1 = (f32[32,32]{1,0:T(8,128)}, f32[16,8,128]{2,1,0:T(8,128)}) custom-call(f32[16,8,128]{2,1,0:T(8,128)} %bitcast.66, f32[16,8,128]{2,1,0:T(8,128)} %get-tuple-element.32.refs_1_, f32[16,8,128]{2,1,0:T(8,128)} %copy-done.7, f32[16,8,128]{2,1,0:T(8,128)} %copy-done.8, f32[16,8,128]{2,1,0:T(8,128)} %copy-done.9), custom_call_target="tpu_custom_call" | custom-call | tf_op jit(solution)/shard_map/gram/pallas_call | solution.py:290
  92.1 1.4 %collective-permute-done.11 = f32[32,32]{1,0:T(8,128)S(1)} collective-permute-done((f32[32,32]{1,0:T(8,128)}, f32[32,32]{1,0:T(8,128)S(1)}, u32[]{:S(2)}, u32[]{:S(2)}) %collective-permute-start.11) | collective-permute-done | bytes 4128 | tf_op jit(solution)/shard_map/ppermute | solution.py:25
  94.4 2.6 %collective-permute-start.13 = (f32[32,32]{1,0:T(8,128)S(1)}, f32[32,32]{1,0:T(8,128)S(1)}, u32[]{:S(2)}, u32[]{:S(2)}) collective-permute-start(f32[32,32]{1,0:T(8,128)S(1)} %add.142), channel_id=1, source_target_pairs={{0,8},{2,10},{4,12},{6,14},{8,0},{10,2},{12,4},{14,6},{1,9},{3,11}... | collective-permute-start | bytes 12296 | tf_op jit(solution)/shard_map/ppermute | solution.py:25
  97.0 1.6 %collective-permute-start.14 = (f32[32,32]{1,0:T(8,128)S(1)}, f32[32,32]{1,0:T(8,128)S(1)}, u32[]{:S(2)}, u32[]{:S(2)}) collective-permute-start(f32[32,32]{1,0:T(8,128)S(1)} %add.142), channel_id=1, source_target_pairs={{0,12},{2,14},{4,8},{6,10},{8,4},{10,6},{12,0},{14,2},{1,13},{3,15... | collective-permute-start | bytes 12296 | tf_op jit(solution)/shard_map/ppermute | solution.py:25
  99.3 3.2 %collective-permute-done.14 = f32[32,32]{1,0:T(8,128)S(1)} collective-permute-done((f32[32,32]{1,0:T(8,128)S(1)}, f32[32,32]{1,0:T(8,128)S(1)}, u32[]{:S(2)}, u32[]{:S(2)}) %collective-permute-start.14) | collective-permute-done | bytes 4128 | tf_op jit(solution)/shard_map/ppermute | solution.py:25
  103.1 1.1 slice_select_fusion.1
  104.2 4.5 %collective-permute-done.15.refs_1_ = f32[32,32]{1,0:T(8,128)S(1)} collective-permute-done((f32[32,32]{1,0:T(8,128)S(1)}, f32[32,32]{1,0:T(8,128)S(1)}, u32[]{:S(2)}, u32[]{:S(2)}) %collective-permute-start.15) | collective-permute-done | bytes 4128 | tf_op jit(solution)/shard_map/ppermute | solution.py:25
  109.3 2.9 %ortho.1 = f32[8,2,1024]{2,1,0:T(2,128)} custom-call(f32[32,32]{1,0:T(8,128)} %copy-done.6, f32[32,32]{1,0:T(8,128)} %copy-done.10, f32[16,8,128]{2,1,0:T(8,128)} %bitcast.67, f32[16,8,128]{2,1,0:T(8,128)} %get-tuple-element.37.refs_3_), custom_call_target="tpu_custom_call" | custom-call | tf_op jit(solution)/shard_map/ortho/pallas_call | solution.py:365
  112.2 2.3 %fusion = f32[4,2,128,256]{3,2,1,0:T(8,128)} fusion(f32[4,2,128,128]{3,2,1,0:T(8,128)S(1)} %get-tuple-element.47, f32[4,2,128,128]{3,2,1,0:T(8,128)S(1)} %get-tuple-element.46, f32[4,2,64,256]{3,2,1,0:T(8,128)} %collective-permute-done.10, f32[4,2,64,256]{3,2,1,0:T(8,128)} %collective-permute-done.9, f32[4,2,256,256]{3,2,1,0:T(8,128)S(1)} %copy-done.1), kind=kLoop, calls=%fused_computation.5 | loop fusion | flops 1048576 | bytes 4194304 | tf_op jit(solution)/shard_map/add | solution.py:428
  (65 shorter events, 11.1 us)
Async XLA Ops:
  0.6 10.6 %copy-start.11 = (f32[2,63]{1,0:T(2,128)S(1)}, f32[2,63]{1,0:T(2,128)}, u32[]{:S(2)}) copy-start(f32[2,63]{1,0:T(2,128)} %param.9) | copy-start | bytes 1516
  4.4 17.0 %collective-permute-start.1 = (f32[4,2,64,256]{3,2,1,0:T(8,128)}, f32[4,2,64,256]{3,2,1,0:T(8,128)S(1)}, u32[]{:S(2)}, u32[]{:S(2)}) collective-permute-start(f32[4,2,64,256]{3,2,1,0:T(8,128)} %slice.31), channel_id=1, source_target_pairs={{2,0},{4,2},{6,4},{8,6},{10,8},{12,10},{14,12},{3,1},{5,3},{7,5},{... | collective-permute-start | bytes 1572872 | tf_op jit(solution)/shard_map/ppermute | solution.py:20
  5.7 27.2 %collective-permute-start = (f32[4,2,64,256]{3,2,1,0:T(8,128)}, f32[4,2,64,256]{3,2,1,0:T(8,128)S(1)}, u32[]{:S(2)}, u32[]{:S(2)}) collective-permute-start(f32[4,2,64,256]{3,2,1,0:T(8,128)} %slice.30), channel_id=1, source_target_pairs={{0,2},{2,4},{4,6},{6,8},{8,10},{10,12},{12,14},{1,3},{3,5},{5,7},{... | collective-permute-start | bytes 1572872 | tf_op jit(solution)/shard_map/ppermute | solution.py:20
  12.1 7.2 %copy-start = (f32[4,2,128,256]{3,2,1,0:T(8,128)S(1)}, f32[4,2,128,256]{3,2,1,0:T(8,128)}, u32[]{:S(2)}) copy-start(f32[4,2,128,256]{3,2,1,0:T(8,128)} %own.1) | copy-start | bytes 3145732
  19.3 13.6 %copy-start.2 = (bf16[8,256,256]{2,1,0:T(8,128)(2,1)}, bf16[8,256,256]{2,1,0:T(8,128)(2,1)S(1)}, u32[]{:S(2)}) copy-start(bf16[8,256,256]{2,1,0:T(8,128)(2,1)S(1)} %constant_dynamic-update-slice_fusion.tab) | copy-start | bytes 3145732
  19.3 13.8 %copy-start.12 = (s32[2,2]{1,0:T(2,128)S(1)}, s32[2,2]{1,0:T(2,128)}, u32[]{:S(2)}) copy-start(s32[2,2]{1,0:T(2,128)} %param.11) | copy-start | bytes 52
  21.4 14.5 %copy-start.3 = (f32[4,2,64,256]{3,2,1,0:T(8,128)}, f32[4,2,64,256]{3,2,1,0:T(8,128)S(1)}, u32[]{:S(2)}) copy-start(f32[4,2,64,256]{3,2,1,0:T(8,128)S(1)} %collective-permute-done.1.below) | copy-start | bytes 1572868
  32.8 3.0 %copy-start.4 = (f32[4,2,64,256]{3,2,1,0:T(8,128)}, f32[4,2,64,256]{3,2,1,0:T(8,128)S(1)}, u32[]{:S(2)}) copy-start(f32[4,2,64,256]{3,2,1,0:T(8,128)S(1)} %collective-permute-done.above) | copy-start | bytes 1572868
  33.0 2.9 %collective-permute-start.2 = (f32[4,2,256,128]{3,2,1,0:T(8,128)S(1)}, f32[4,2,256,128]{3,2,1,0:T(8,128)}, u32[]{:S(2)}, u32[]{:S(2)}) collective-permute-start(f32[4,2,256,128]{3,2,1,0:T(8,128)S(1)} %pad_maximum_fusion), channel_id=1, source_target_pairs={{0,1},{1,0},{2,3},{3,2},{4,5},{5,4},{6,7},{7,6},{8,9},{9,8},{10,11... | collective-permute-start | bytes 3145736 | tf_op jit(solution)/shard_map/ppermute | solution.py:25
  58.4 20.0 %copy-start.1 = (f32[4,2,256,256]{3,2,1,0:T(8,128)S(1)}, f32[4,2,256,256]{3,2,1,0:T(8,128)}, u32[]{:S(2)}) copy-start(f32[4,2,256,256]{3,2,1,0:T(8,128)} %get-tuple-element.25) | copy-start | bytes 6291460
  58.4 19.8 %collective-permute-start.3 = (f32[4,2,256,128]{3,2,1,0:T(8,128)}, f32[4,2,256,128]{3,2,1,0:T(8,128)S(1)}, u32[]{:S(2)}, u32[]{:S(2)}) collective-permute-start(f32[4,2,256,128]{3,2,1,0:T(8,128)} %get-tuple-element.26), channel_id=1, source_target_pairs={{0,1},{1,0},{2,3},{3,2},{4,5},{5,4},{6,7},{7,6},{8,9},{9,8},{10,11... | collective-permute-start | bytes 3145736 | tf_op jit(solution)/shard_map/ppermute | solution.py:25
  58.6 3.6 %collective-permute-start.4 = (f32[8,16,8,128]{3,2,1,0:T(8,128)}, f32[8,16,8,128]{3,2,1,0:T(8,128)}, u32[]{:S(2)}, u32[]{:S(2)}) collective-permute-start(f32[8,16,8,128]{3,2,1,0:T(8,128)} %get-tuple-element.28), channel_id=1, source_target_pairs={{0,1},{1,0},{2,3},{3,2},{4,5},{5,4},{6,7},{7,6},{8,9},{9,8},{10,11... | collective-permute-start | bytes 1572872 | tf_op jit(solution)/shard_map/ppermute | solution.py:25
  64.0 9.2 %collective-permute-start.5 = (f32[4,16,8,128]{3,2,1,0:T(8,128)}, f32[4,16,8,128]{3,2,1,0:T(8,128)S(1)}, u32[]{:S(2)}, u32[]{:S(2)}) collective-permute-start(f32[4,16,8,128]{3,2,1,0:T(8,128)} %fusion.3), channel_id=1, source_target_pairs={{0,2},{2,0},{4,6},{6,4},{8,10},{10,8},{12,14},{14,12},{1,3},{3,1},... | collective-permute-start | bytes 786440 | tf_op jit(solution)/shard_map/ppermute | solution.py:25
  73.9 5.7 %collective-permute-start.6 = (f32[16,8,128]{2,1,0:T(8,128)S(1)}, f32[16,8,128]{2,1,0:T(8,128)S(1)}, u32[]{:S(2)}, u32[]{:S(2)}) collective-permute-start(f32[16,8,128]{2,1,0:T(8,128)S(1)} %get-tuple-element.50), channel_id=1, source_target_pairs={{0,4},{2,6},{4,0},{6,2},{8,12},{10,14},{12,8},{14,10},{1,5},{3,7},... | collective-permute-start | bytes 196616 | tf_op jit(solution)/shard_map/ppermute | solution.py:25
  75.5 7.1 %collective-permute-start.7 = (f32[16,8,128]{2,1,0:T(8,128)S(1)}, f32[16,8,128]{2,1,0:T(8,128)S(1)}, u32[]{:S(2)}, u32[]{:S(2)}) collective-permute-start(f32[16,8,128]{2,1,0:T(8,128)S(1)} %get-tuple-element.49), channel_id=1, source_target_pairs={{0,8},{2,10},{4,12},{6,14},{8,0},{10,2},{12,4},{14,6},{1,9},{3,11}... | collective-permute-start | bytes 196616 | tf_op jit(solution)/shard_map/ppermute | solution.py:25
  77.4 6.2 %collective-permute-start.8 = (f32[16,8,128]{2,1,0:T(8,128)S(1)}, f32[16,8,128]{2,1,0:T(8,128)S(1)}, u32[]{:S(2)}, u32[]{:S(2)}) collective-permute-start(f32[16,8,128]{2,1,0:T(8,128)S(1)} %get-tuple-element.48), channel_id=1, source_target_pairs={{0,12},{2,14},{4,8},{6,10},{8,4},{10,6},{12,0},{14,2},{1,13},{3,15... | collective-permute-start | bytes 196616 | tf_op jit(solution)/shard_map/ppermute | solution.py:25
  78.3 1.3 %copy-start.5 = (f32[4,2,256,128]{3,2,1,0:T(8,128)}, f32[4,2,256,128]{3,2,1,0:T(8,128)S(1)}, u32[]{:S(2)}) copy-start(f32[4,2,256,128]{3,2,1,0:T(8,128)S(1)} %collective-permute-done.3) | copy-start | bytes 3145732
  79.6 10.6 %copy-start.7 = (f32[16,8,128]{2,1,0:T(8,128)}, f32[16,8,128]{2,1,0:T(8,128)S(1)}, u32[]{:S(2)}) copy-start(f32[16,8,128]{2,1,0:T(8,128)S(1)} %collective-permute-done.6.refs_2_) | copy-start | bytes 196612
  82.5 7.6 %copy-start.8 = (f32[16,8,128]{2,1,0:T(8,128)}, f32[16,8,128]{2,1,0:T(8,128)S(1)}, u32[]{:S(2)}) copy-start(f32[16,8,128]{2,1,0:T(8,128)S(1)} %collective-permute-done.7.refs_3_) | copy-start | bytes 196612
  83.5 6.6 %copy-start.9 = (f32[16,8,128]{2,1,0:T(8,128)}, f32[16,8,128]{2,1,0:T(8,128)S(1)}, u32[]{:S(2)}) copy-start(f32[16,8,128]{2,1,0:T(8,128)S(1)} %collective-permute-done.8.refs_4_) | copy-start | bytes 196612
  83.5 28.7 %collective-permute-start.10 = (f32[4,2,64,256]{3,2,1,0:T(8,128)}, f32[4,2,64,256]{3,2,1,0:T(8,128)}, u32[]{:S(2)}, u32[]{:S(2)}) collective-permute-start(f32[4,2,64,256]{3,2,1,0:T(8,128)} %get-tuple-element.30), channel_id=1, source_target_pairs={{2,0},{4,2},{6,4},{8,6},{10,8},{12,10},{14,12},{3,1},{5,3},{7,5},{... | collective-permute-start | bytes 1572872 | tf_op jit(solution)/shard_map/ppermute | solution.py:20
  84.8 27.4 %collective-permute-start.9 = (f32[4,2,64,256]{3,2,1,0:T(8,128)}, f32[4,2,64,256]{3,2,1,0:T(8,128)}, u32[]{:S(2)}, u32[]{:S(2)}) collective-permute-start(f32[4,2,64,256]{3,2,1,0:T(8,128)} %get-tuple-element.29), channel_id=1, source_target_pairs={{0,2},{2,4},{4,6},{6,8},{8,10},{10,12},{12,14},{1,3},{3,5},{5,7},{... | collective-permute-start | bytes 1572872 | tf_op jit(solution)/shard_map/ppermute | solution.py:20
  92.1 1.4 %collective-permute-start.11 = (f32[32,32]{1,0:T(8,128)}, f32[32,32]{1,0:T(8,128)S(1)}, u32[]{:S(2)}, u32[]{:S(2)}) collective-permute-start(f32[32,32]{1,0:T(8,128)} %get-tuple-element.36), channel_id=1, source_target_pairs={{0,1},{1,0},{2,3},{3,2},{4,5},{5,4},{6,7},{7,6},{8,9},{9,8},{10,11... | collective-permute-start | bytes 12296 | tf_op jit(solution)/shard_map/ppermute | solution.py:25
  94.2 4.5 %collective-permute-start.12 = (f32[32,32]{1,0:T(8,128)S(1)}, f32[32,32]{1,0:T(8,128)S(1)}, u32[]{:S(2)}, u32[]{:S(2)}) collective-permute-start(f32[32,32]{1,0:T(8,128)S(1)} %add.142), channel_id=1, source_target_pairs={{0,4},{2,6},{4,0},{6,2},{8,12},{10,14},{12,8},{14,10},{1,5},{3,7},... | collective-permute-start | bytes 12296 | tf_op jit(solution)/shard_map/ppermute | solution.py:25
  94.4 4.9 %collective-permute-start.13 = (f32[32,32]{1,0:T(8,128)S(1)}, f32[32,32]{1,0:T(8,128)S(1)}, u32[]{:S(2)}, u32[]{:S(2)}) collective-permute-start(f32[32,32]{1,0:T(8,128)S(1)} %add.142), channel_id=1, source_target_pairs={{0,8},{2,10},{4,12},{6,14},{8,0},{10,2},{12,4},{14,6},{1,9},{3,11}... | collective-permute-start | bytes 12296 | tf_op jit(solution)/shard_map/ppermute | solution.py:25
  97.0 5.5 %collective-permute-start.14 = (f32[32,32]{1,0:T(8,128)S(1)}, f32[32,32]{1,0:T(8,128)S(1)}, u32[]{:S(2)}, u32[]{:S(2)}) collective-permute-start(f32[32,32]{1,0:T(8,128)S(1)} %add.142), channel_id=1, source_target_pairs={{0,12},{2,14},{4,8},{6,10},{8,4},{10,6},{12,0},{14,2},{1,13},{3,15... | collective-permute-start | bytes 12296 | tf_op jit(solution)/shard_map/ppermute | solution.py:25
  102.5 6.2 %copy-start.6 = (f32[32,32]{1,0:T(8,128)}, f32[32,32]{1,0:T(8,128)S(1)}, u32[]{:S(2)}) copy-start(f32[32,32]{1,0:T(8,128)S(1)} %add_add_fusion.refs_0_) | copy-start | bytes 12292
  102.5 6.2 %collective-permute-start.15 = (f32[32,32]{1,0:T(8,128)S(1)}, f32[32,32]{1,0:T(8,128)S(1)}, u32[]{:S(2)}, u32[]{:S(2)}) collective-permute-start(f32[32,32]{1,0:T(8,128)S(1)} %add_add_fusion.refs_0_), channel_id=1, source_target_pairs={{0,2},{2,0},{4,6},{6,4},{8,10},{10,8},{12,14},{14,12},{1,3},{3,1},... | collective-permute-start | bytes 12296 | tf_op jit(solution)/shard_map/ppermute | solution.py:25
  108.7 0.6 copy-start.10

commit v7 on v6

--- a/solution.py
+++ b/solution.py
@@ -388,17 +388,13 @@
     row_idx, col_idx = lax.axis_index("row"), lax.axis_index("col")
     row_bits = [1 << b for b in range(row_devices.bit_length() - 1)]
 
+    from_above = shifted(bottom, "row", 1)
     if share == SUBLANES and row_devices <= 8:
         received = swapped(send, "col", 1)
-        pairs = (row_devices // 2, 2) + keep.shape[1:]
-        keep, received = keep.reshape(pairs), received.reshape(pairs)
-        low, high = row_idx % 2, row_idx // 2
-        send = take(keep, 1 - low, 1) + take(received, 1 - low, 1)
-        keep, received = take(keep, low, 1) + take(received, low, 1), swapped(send, "row", 1)
         parts = []
-        for k in range(row_devices // 2):
-            block = take(keep, high ^ k, 0) + take(received, high ^ k, 0)
-            parts.append(swapped(block, "row", 2 * k) if k else block)
+        for k in range(row_devices):
+            block = take(keep, row_idx ^ k, 0) + take(received, row_idx ^ k, 0)
+            parts.append(swapped(block, "row", k) if k else block)
     else:
         even, odd = jnp.where(col_idx == 0, keep, send), jnp.where(col_idx == 0, send, keep)
         grad = jnp.stack([even, odd], axis=1).transpose(0, 1, 3, 2, 4)
@@ -411,8 +407,7 @@
             grad = take(grad, mine, 0) + swapped(take(grad, 1 - mine, 0), "row", bit)
         parts = [grad.reshape(2 * modes, share, width)]
 
-    parts, bottom, top = lax.optimization_barrier((parts, bottom, top))
-    from_above = shifted(bottom, "row", 1)
+    parts, top, from_above = lax.optimization_barrier((parts, top, from_above))
     from_below = shifted(top, "row", -1)
     total, own_grad = gram(own_probe, parts)
     total = total + swapped(total, "col", 1)
@@ -424,8 +419,9 @@
         near, far, both = (swapped(total, "row", k) for k in (a, b, a ^ b))
         total = (total + near) + (far + both)
     grams = [total, swapped(total, "row", row_bits[0])]
+    object_grad = middle() + jnp.concatenate([from_above, from_below], axis=2)
+    grams, object_grad = lax.optimization_barrier((grams, object_grad))
     new_probe = ortho(grams, own_probe, own_grad, modes, float(width))
-    object_grad = middle() + jnp.concatenate([from_above, from_below], axis=2)
     return new_probe, object_grad
 
 
@@ -436,11 +432,8 @@
     row_idx = lax.axis_index("row")
     col_idx = lax.axis_index("col")
 
-    bottom_rows, later = lax.optimization_barrier(
-        (object_slices[:, :, tile_rows - half :], object_slices)
-    )
-    above = shifted(bottom_rows, "row", 1)
-    below = shifted(later[:, :, :half], "row", -1)
+    above = shifted(object_slices[:, :, tile_rows - half :], "row", 1)
+    below = shifted(object_slices[:, :, :half], "row", -1)
     tab = block_tables(taps, width)
     own_probe = own_block(probe)
     above, below, tab, own_probe = lax.optimization_barrier((above, below, tab, own_probe))

time: 115 us -> 122 us (1.061)
  starting transfers between devices: 25.8 us -> 34.4 us
  other arithmetic: 11.2 us -> 9.82 us
    ppermute x12 -> x15, starting transfers between devices: 12.3 us -> 22.3 us  [swapped(): return lax.ppermute(value, axis, [(i, i ^ bit) for i in range(count)])]
    add x3 -> x1, other arithmetic: 3.49 us -> 1.92 us  [updates(): block = take(keep, row_idx ^ k, 0) + take(received, row_idx ^ k, 0)]
    slice x2 -> x1, local copies, waits for them, and re-layouts: 3.75 us -> 2.3 us  [per_device(): below = shifted(object_slices[:, :, :half], 'row', -1)]
    ppermute x4, starting transfers between devices: 13.4 us -> 12.1 us  [shifted(): return lax.ppermute(value, axis, pairs)]
    unnamed x31 -> x37, local copies, waits for them, and re-layouts: 3.42 us -> 4.05 us
    ppermute x12 -> x15, waiting for transfers between devices: 24.8 us -> 24.7 us  [swapped(): return lax.ppermute(value, axis, [(i, i ^ bit) for i in range(count)])]
  transfers between devices with their start and end apart: 16 -> 19, of which waited for: 12 -> 9; matrix products, arithmetic and copies ran while one was open for 13% -> 13% of each run, Pallas kernels for 4% -> 2%
where the time goes in v7:
time: 122 us; the launch traced here: 121 us
  waiting for transfers between devices  37.8 us (31%)
  starting transfers between devices  34.4 us (28%)
  Pallas kernels  27.7 us (23%)
  local copies, waits for them, and re-layouts  10.1 us (8%)
  other arithmetic  9.82 us (8%)
    ppermute x15, waiting for transfers between devices, swapped(): return lax.ppermute(value, axis, [(i, i ^ bit) for i in range(count)])  24.7 us
    pallas_call x1, Pallas kernels, fields(): pl.pallas_call(field_kernel, out_shape=[jax.ShapeDtypeStruct(s, F32) for...  22.7 us
    ppermute x15, starting transfers between devices, swapped(): return lax.ppermute(value, axis, [(i, i ^ bit) for i in range(count)])  22.3 us
    ppermute x4, waiting for transfers between devices, shifted(): return lax.ppermute(value, axis, pairs)  13.2 us
    ppermute x4, starting transfers between devices, shifted(): return lax.ppermute(value, axis, pairs)  12.1 us
    unnamed x37, local copies, waits for them, and re-layouts  4.05 us
    pallas_call x1, Pallas kernels, ortho(): pl.pallas_call(body, out_shape=jax.ShapeDtypeStruct((modes, 2, pixels), F...  2.92 us
  transfers between devices with their start and end apart: 19, of which 9 were waited for; matrix products, arithmetic and copies ran while one was open for 13% of the time, Pallas kernels for 2%

profile of v7, /device:TPU:0, one launch (start us, length us, event | category | flops | bytes accessed | tf_op | source)
XLA Modules:
  0.0 120.9 jit_solution(18269716811128718183)
XLA Ops:
  0.6 2.3 %fusion.5 = (f32[4,2,64,256]{3,2,1,0:T(8,128)}, f32[4,2,64,256]{3,2,1,0:T(8,128)}) fusion(f32[4,2,128,256]{3,2,1,0:T(8,128)} %own.1), kind=kLoop, calls=%fused_computation.51 | loop fusion | bytes 2097152 | tf_op jit(solution)/shard_map/slice | solution.py:436
  2.9 4.9 %collective-permute-start = (f32[4,2,64,256]{3,2,1,0:T(8,128)}, f32[4,2,64,256]{3,2,1,0:T(8,128)S(1)}, u32[]{:S(2)}, u32[]{:S(2)}) collective-permute-start(f32[4,2,64,256]{3,2,1,0:T(8,128)} %get-tuple-element.67), channel_id=1, source_target_pairs={{0,2},{2,4},{4,6},{6,8},{8,10},{10,12},{12,14},{1,3},{3,5},{5,7},{... | collective-permute-start | bytes 1572872 | tf_op jit(solution)/shard_map/ppermute | solution.py:20
  7.8 1.3 %collective-permute-start.1 = (f32[4,2,64,256]{3,2,1,0:T(8,128)}, f32[4,2,64,256]{3,2,1,0:T(8,128)S(1)}, u32[]{:S(2)}, u32[]{:S(2)}) collective-permute-start(f32[4,2,64,256]{3,2,1,0:T(8,128)} %get-tuple-element.66), channel_id=1, source_target_pairs={{2,0},{4,2},{6,4},{8,6},{10,8},{12,10},{14,12},{3,1},{5,3},{7,5},{... | collective-permute-start | bytes 1572872 | tf_op jit(solution)/shard_map/ppermute | solution.py:20
  11.0 1.0 copy.17
  12.1 0.9 constant_dynamic-update-slice_fusion.3
  13.0 0.9 dynamic-slice_bitcast_fusion
  14.5 0.9 constant_dynamic-update-slice_fusion.2
  15.4 0.9 constant_dynamic-update-slice_fusion.1
  16.3 0.9 constant_dynamic-update-slice_fusion.tab
  17.3 13.2 %collective-permute-done.above = f32[4,2,64,256]{3,2,1,0:T(8,128)S(1)} collective-permute-done((f32[4,2,64,256]{3,2,1,0:T(8,128)}, f32[4,2,64,256]{3,2,1,0:T(8,128)S(1)}, u32[]{:S(2)}, u32[]{:S(2)}) %collective-permute-start) | collective-permute-done | bytes 524320 | tf_op jit(solution)/shard_map/ppermute | solution.py:20
  31.4 2.1 %collective-permute-done.2.beside = f32[4,2,256,128]{3,2,1,0:T(8,128)} collective-permute-done((f32[4,2,256,128]{3,2,1,0:T(8,128)S(1)}, f32[4,2,256,128]{3,2,1,0:T(8,128)}, u32[]{:S(2)}, u32[]{:S(2)}) %collective-permute-start.2) | collective-permute-done | bytes 1048608 | tf_op jit(solution)/shard_map/ppermute | solution.py:25
  33.5 22.7 %fields.1 = (f32[4,2,256,256]{3,2,1,0:T(8,128)}, f32[4,2,256,128]{3,2,1,0:T(8,128)}, f32[8,16,8,128]{3,2,1,0:T(8,128)}, f32[8,16,8,128]{3,2,1,0:T(8,128)}) custom-call(s32[2,2]{1,0:T(2,128)} %broadcast_subtract_fusion.places, s32[1]{0:T(128)} %bitcast.11.side, f32[4,2,128,256]{3,2,1,0:T(8,128)} %own.1, f32[4,2,64,256]{3,2,1,0:T(8,128)} %copy-done.3, ...), custom_call_target="tpu_custom_call" | custom-call | tf_op jit(solution)/shard_map/fields/pallas_call | solution.py:246
  56.7 3.1 %collective-permute-done.11 = f32[4,2,256,128]{3,2,1,0:T(8,128)S(1)} collective-permute-done((f32[4,2,256,128]{3,2,1,0:T(8,128)}, f32[4,2,256,128]{3,2,1,0:T(8,128)S(1)}, u32[]{:S(2)}, u32[]{:S(2)}) %collective-permute-start.11) | collective-permute-done | bytes 1048608 | tf_op jit(solution)/shard_map/ppermute | solution.py:25
  59.9 2.3 %maximum_add_fusion.2 = (f32[4,2,64,256]{3,2,1,0:T(8,128)}, f32[4,2,64,256]{3,2,1,0:T(8,128)}) fusion(f32[4,2,64,128]{3,2,1,0:T(8,128)S(1)} %get-tuple-element.56, f32[4,2,64,128]{3,2,1,0:T(8,128)S(1)} %get-tuple-element.54, f32[4,2,256,256]{3,2,1,0:T(8,128)} %get-tuple-element.31, f32[4,2,64,128]{3,2,1,0:T(8,128)S(1)} %get-tuple-element.55, ...), kind=kLoop, calls=%fused_computation.7 | loop fusion | flops 524288 | bytes 3145728 | tf_op jit(solution)/shard_map/add | solution.py:460
  62.2 4.7 %collective-permute-start.12 = (f32[4,2,64,256]{3,2,1,0:T(8,128)}, f32[4,2,64,256]{3,2,1,0:T(8,128)}, u32[]{:S(2)}, u32[]{:S(2)}) collective-permute-start(f32[4,2,64,256]{3,2,1,0:T(8,128)} %get-tuple-element.50), channel_id=1, source_target_pairs={{0,2},{2,4},{4,6},{6,8},{8,10},{10,12},{12,14},{1,3},{3,5},{5,7},{... | collective-permute-start | bytes 1572872 | tf_op jit(solution)/shard_map/ppermute | solution.py:20
  67.0 1.9 %add_bitcast_fusion = (f32[16,8,128]{2,1,0:T(8,128)S(1)}, f32[16,8,128]{2,1,0:T(8,128)S(1)}, f32[16,8,128]{2,1,0:T(8,128)S(1)}, f32[16,8,128]{2,1,0:T(8,128)S(1)...) fusion(f32[8,16,8,128]{3,2,1,0:T(8,128)} %collective-permute-don, ...), kind=kLoop, calls=%fused_computation.27 | loop fusion | flops 131072 | bytes 1572896 | tf_op jit(solution)/shard_map/add | solution.py:396
  68.9 1.4 %collective-permute-start.4 = (f32[16,8,128]{2,1,0:T(8,128)S(1)}, f32[16,8,128]{2,1,0:T(8,128)S(1)}, u32[]{:S(2)}, u32[]{:S(2)}) collective-permute-start(f32[16,8,128]{2,1,0:T(8,128)S(1)} %get-tuple-element.64), channel_id=1, source_target_pairs={{0,2},{2,0},{4,6},{6,4},{8,10},{10,8},{12,14},{14,12},{1,3},{3,1},... | collective-permute-start | bytes 196616 | tf_op jit(solution)/shard_map/ppermute | solution.py:25
  70.3 2.4 %collective-permute-start.5 = (f32[16,8,128]{2,1,0:T(8,128)S(1)}, f32[16,8,128]{2,1,0:T(8,128)S(1)}, u32[]{:S(2)}, u32[]{:S(2)}) collective-permute-start(f32[16,8,128]{2,1,0:T(8,128)S(1)} %get-tuple-element.63), channel_id=1, source_target_pairs={{0,4},{2,6},{4,0},{6,2},{8,12},{10,14},{12,8},{14,10},{1,5},{3,7},... | collective-permute-start | bytes 196616 | tf_op jit(solution)/shard_map/ppermute | solution.py:25
  72.7 2.0 %collective-permute-start.7 = (f32[16,8,128]{2,1,0:T(8,128)S(1)}, f32[16,8,128]{2,1,0:T(8,128)S(1)}, u32[]{:S(2)}, u32[]{:S(2)}) collective-permute-start(f32[16,8,128]{2,1,0:T(8,128)S(1)} %get-tuple-element.61), channel_id=1, source_target_pairs={{0,8},{2,10},{4,12},{6,14},{8,0},{10,2},{12,4},{14,6},{1,9},{3,11}... | collective-permute-start | bytes 196616 | tf_op jit(solution)/shard_map/ppermute | solution.py:25
  74.7 6.0 %collective-permute-done.4.refs_2_ = f32[16,8,128]{2,1,0:T(8,128)S(1)} collective-permute-done((f32[16,8,128]{2,1,0:T(8,128)S(1)}, f32[16,8,128]{2,1,0:T(8,128)S(1)}, u32[]{:S(2)}, u32[]{:S(2)}) %collective-permute-start.4) | collective-permute-done | bytes 65568 | tf_op jit(solution)/shard_map/ppermute | solution.py:25
  80.6 4.9 %collective-permute-start.8 = (f32[16,8,128]{2,1,0:T(8,128)S(1)}, f32[16,8,128]{2,1,0:T(8,128)S(1)}, u32[]{:S(2)}, u32[]{:S(2)}) collective-permute-start(f32[16,8,128]{2,1,0:T(8,128)S(1)} %get-tuple-element.60), channel_id=1, source_target_pairs={{0,10},{2,8},{4,14},{6,12},{8,2},{10,0},{12,6},{14,4},{1,11},{3,9}... | collective-permute-start | bytes 196616 | tf_op jit(solution)/shard_map/ppermute | solution.py:25
  86.3 4.8 %collective-permute-start.10 = (f32[16,8,128]{2,1,0:T(8,128)S(1)}, f32[16,8,128]{2,1,0:T(8,128)S(1)}, u32[]{:S(2)}, u32[]{:S(2)}) collective-permute-start(f32[16,8,128]{2,1,0:T(8,128)S(1)} %get-tuple-element.58), channel_id=1, source_target_pairs={{0,14},{2,12},{4,10},{6,8},{8,6},{10,4},{12,2},{14,0},{1,15},{3,13... | collective-permute-start | bytes 196616 | tf_op jit(solution)/shard_map/ppermute | solution.py:25
  91.1 0.8 collective-permute-done.9.refs_7_
  91.9 2.5 %collective-permute-done.10.refs_8_ = f32[16,8,128]{2,1,0:T(8,128)S(1)} collective-permute-done((f32[16,8,128]{2,1,0:T(8,128)S(1)}, f32[16,8,128]{2,1,0:T(8,128)S(1)}, u32[]{:S(2)}, u32[]{:S(2)}) %collective-permute-start.10) | collective-permute-done | bytes 65568 | tf_op jit(solution)/shard_map/ppermute | solution.py:25
  95.0 1.3 %collective-permute-start.18 = (f32[4,2,64,256]{3,2,1,0:T(8,128)}, f32[4,2,64,256]{3,2,1,0:T(8,128)}, u32[]{:S(2)}, u32[]{:S(2)}) collective-permute-start(f32[4,2,64,256]{3,2,1,0:T(8,128)} %get-tuple-element.43), channel_id=1, source_target_pairs={{2,0},{4,2},{6,4},{8,6},{10,8},{12,10},{14,12},{3,1},{5,3},{7,5},{... | collective-permute-start | bytes 1572872 | tf_op jit(solution)/shard_map/ppermute | solution.py:20
  96.4 2.1 %gram.1 = (f32[32,32]{1,0:T(8,128)}, f32[16,8,128]{2,1,0:T(8,128)}) custom-call(f32[16,8,128]{2,1,0:T(8,128)} %bitcast.48, f32[16,8,128]{2,1,0:T(8,128)} %get-tuple-element.33.refs_1_, f32[16,8,128]{2,1,0:T(8,128)} %copy-done.6, f32[16,8,128]{2,1,0:T(8,128)} %copy-done.7, f32[16,8,128]{2,1,0:T(8,128)} %copy-done.8, f32[16,8,128]{2,1,0:T(8,128)} %copy-done.9, ...), custom_call_target="tpu_custom_call" | custom-call | tf_op jit(solution)/shard_map/gram/pallas_call | solution.py:290
  98.4 1.4 %collective-permute-done.13 = f32[32,32]{1,0:T(8,128)S(1)} collective-permute-done((f32[32,32]{1,0:T(8,128)}, f32[32,32]{1,0:T(8,128)S(1)}, u32[]{:S(2)}, u32[]{:S(2)}) %collective-permute-start.13) | collective-permute-done | bytes 4128 | tf_op jit(solution)/shard_map/ppermute | solution.py:25
  100.5 4.3 %collective-permute-start.15 = (f32[32,32]{1,0:T(8,128)S(1)}, f32[32,32]{1,0:T(8,128)S(1)}, u32[]{:S(2)}, u32[]{:S(2)}) collective-permute-start(f32[32,32]{1,0:T(8,128)S(1)} %add.161), channel_id=1, source_target_pairs={{0,8},{2,10},{4,12},{6,14},{8,0},{10,2},{12,4},{14,6},{1,9},{3,11}... | collective-permute-start | bytes 12296 | tf_op jit(solution)/shard_map/ppermute | solution.py:25
  106.0 7.5 %collective-permute-done.15 = f32[32,32]{1,0:T(8,128)S(1)} collective-permute-done((f32[32,32]{1,0:T(8,128)S(1)}, f32[32,32]{1,0:T(8,128)S(1)}, u32[]{:S(2)}, u32[]{:S(2)}) %collective-permute-start.15) | collective-permute-done | bytes 4128 | tf_op jit(solution)/shard_map/ppermute | solution.py:25
  113.7 2.4 %fusion = f32[4,2,128,256]{3,2,1,0:T(8,128)} fusion(f32[4,2,128,128]{3,2,1,0:T(8,128)S(1)} %get-tuple-element.53, f32[4,2,128,128]{3,2,1,0:T(8,128)S(1)} %get-tuple-element.52, f32[4,2,64,256]{3,2,1,0:T(8,128)} %collective-permute-done.18, f32[4,2,64,256]{3,2,1,0:T(8,128)} %collective-permute-done.12, f32[4,2,256,256]{3,2,1,0:T(8,128)S(1)} %copy-done.1), kind=kLoop, calls=%fused_computation.5 | loop fusion | flops 1048576 | bytes 4194304 | tf_op jit(solution)/shard_map/add | solution.py:422
  116.1 1.3 %collective-permute-done.17.refs_1_ = f32[32,32]{1,0:T(8,128)S(1)} collective-permute-done((f32[32,32]{1,0:T(8,128)S(1)}, f32[32,32]{1,0:T(8,128)S(1)}, u32[]{:S(2)}, u32[]{:S(2)}) %collective-permute-start.17) | collective-permute-done | bytes 4128 | tf_op jit(solution)/shard_map/ppermute | solution.py:25
  118.0 2.9 %ortho.1 = f32[8,2,1024]{2,1,0:T(2,128)} custom-call(f32[32,32]{1,0:T(8,128)} %copy-done.5, f32[32,32]{1,0:T(8,128)} %copy-done.13, f32[16,8,128]{2,1,0:T(8,128)} %bitcast.49, f32[16,8,128]{2,1,0:T(8,128)} %get-tuple-element.47.refs_3_), custom_call_target="tpu_custom_call" | custom-call | tf_op jit(solution)/shard_map/ortho/pallas_call | solution.py:365
  (74 shorter events, 8.0 us)
Async XLA Ops:
  0.6 8.5 %copy-start.14 = (f32[2,63]{1,0:T(2,128)S(1)}, f32[2,63]{1,0:T(2,128)}, u32[]{:S(2)}) copy-start(f32[2,63]{1,0:T(2,128)} %param.9) | copy-start | bytes 1516
  2.9 27.6 %collective-permute-start = (f32[4,2,64,256]{3,2,1,0:T(8,128)}, f32[4,2,64,256]{3,2,1,0:T(8,128)S(1)}, u32[]{:S(2)}, u32[]{:S(2)}) collective-permute-start(f32[4,2,64,256]{3,2,1,0:T(8,128)} %get-tuple-element.67), channel_id=1, source_target_pairs={{0,2},{2,4},{4,6},{6,8},{8,10},{10,12},{12,14},{1,3},{3,5},{5,7},{... | collective-permute-start | bytes 1572872 | tf_op jit(solution)/shard_map/ppermute | solution.py:20
  7.8 22.7 %collective-permute-start.1 = (f32[4,2,64,256]{3,2,1,0:T(8,128)}, f32[4,2,64,256]{3,2,1,0:T(8,128)S(1)}, u32[]{:S(2)}, u32[]{:S(2)}) collective-permute-start(f32[4,2,64,256]{3,2,1,0:T(8,128)} %get-tuple-element.66), channel_id=1, source_target_pairs={{2,0},{4,2},{6,4},{8,6},{10,8},{12,10},{14,12},{3,1},{5,3},{7,5},{... | collective-permute-start | bytes 1572872 | tf_op jit(solution)/shard_map/ppermute | solution.py:20
  10.0 7.2 %copy-start = (f32[4,2,128,256]{3,2,1,0:T(8,128)S(1)}, f32[4,2,128,256]{3,2,1,0:T(8,128)}, u32[]{:S(2)}) copy-start(f32[4,2,128,256]{3,2,1,0:T(8,128)} %own.1) | copy-start | bytes 3145732
  17.2 13.4 %copy-start.2 = (bf16[8,256,256]{2,1,0:T(8,128)(2,1)}, bf16[8,256,256]{2,1,0:T(8,128)(2,1)S(1)}, u32[]{:S(2)}) copy-start(bf16[8,256,256]{2,1,0:T(8,128)(2,1)S(1)} %constant_dynamic-update-slice_fusion.tab) | copy-start | bytes 3145732
  17.2 13.5 %copy-start.15 = (s32[2,2]{1,0:T(2,128)S(1)}, s32[2,2]{1,0:T(2,128)}, u32[]{:S(2)}) copy-start(s32[2,2]{1,0:T(2,128)} %param.11) | copy-start | bytes 52
  30.5 3.0 %copy-start.3 = (f32[4,2,64,256]{3,2,1,0:T(8,128)}, f32[4,2,64,256]{3,2,1,0:T(8,128)S(1)}, u32[]{:S(2)}) copy-start(f32[4,2,64,256]{3,2,1,0:T(8,128)S(1)} %collective-permute-done.above) | copy-start | bytes 1572868
  30.5 3.0 %copy-start.4 = (f32[4,2,64,256]{3,2,1,0:T(8,128)}, f32[4,2,64,256]{3,2,1,0:T(8,128)S(1)}, u32[]{:S(2)}) copy-start(f32[4,2,64,256]{3,2,1,0:T(8,128)S(1)} %collective-permute-done.1.below) | copy-start | bytes 1572868
  30.6 2.9 %collective-permute-start.2 = (f32[4,2,256,128]{3,2,1,0:T(8,128)S(1)}, f32[4,2,256,128]{3,2,1,0:T(8,128)}, u32[]{:S(2)}, u32[]{:S(2)}) collective-permute-start(f32[4,2,256,128]{3,2,1,0:T(8,128)S(1)} %pad_maximum_fusion), channel_id=1, source_target_pairs={{0,1},{1,0},{2,3},{3,2},{4,5},{5,4},{6,7},{7,6},{8,9},{9,8},{10,11... | collective-permute-start | bytes 3145736 | tf_op jit(solution)/shard_map/ppermute | solution.py:25
  56.2 3.6 %collective-permute-start.11 = (f32[4,2,256,128]{3,2,1,0:T(8,128)}, f32[4,2,256,128]{3,2,1,0:T(8,128)S(1)}, u32[]{:S(2)}, u32[]{:S(2)}) collective-permute-start(f32[4,2,256,128]{3,2,1,0:T(8,128)} %get-tuple-element.32), channel_id=1, source_target_pairs={{0,1},{1,0},{2,3},{3,2},{4,5},{5,4},{6,7},{7,6},{8,9},{9,8},{10,11... | collective-permute-start | bytes 3145736 | tf_op jit(solution)/shard_map/ppermute | solution.py:25
  56.3 10.7 %collective-permute-start.3 = (f32[8,16,8,128]{3,2,1,0:T(8,128)}, f32[8,16,8,128]{3,2,1,0:T(8,128)}, u32[]{:S(2)}, u32[]{:S(2)}) collective-permute-start(f32[8,16,8,128]{3,2,1,0:T(8,128)} %get-tuple-element.30), channel_id=1, source_target_pairs={{0,1},{1,0},{2,3},{3,2},{4,5},{5,4},{6,7},{7,6},{8,9},{9,8},{10,11... | collective-permute-start | bytes 1572872 | tf_op jit(solution)/shard_map/ppermute | solution.py:25
  62.2 51.4 %copy-start.1 = (f32[4,2,256,256]{3,2,1,0:T(8,128)S(1)}, f32[4,2,256,256]{3,2,1,0:T(8,128)}, u32[]{:S(2)}) copy-start(f32[4,2,256,256]{3,2,1,0:T(8,128)} %get-tuple-element.31) | copy-start | bytes 6291460
  62.2 32.8 %collective-permute-start.12 = (f32[4,2,64,256]{3,2,1,0:T(8,128)}, f32[4,2,64,256]{3,2,1,0:T(8,128)}, u32[]{:S(2)}, u32[]{:S(2)}) collective-permute-start(f32[4,2,64,256]{3,2,1,0:T(8,128)} %get-tuple-element.50), channel_id=1, source_target_pairs={{0,2},{2,4},{4,6},{6,8},{8,10},{10,12},{12,14},{1,3},{3,5},{5,7},{... | collective-permute-start | bytes 1572872 | tf_op jit(solution)/shard_map/ppermute | solution.py:20
  68.9 11.8 %collective-permute-start.4 = (f32[16,8,128]{2,1,0:T(8,128)S(1)}, f32[16,8,128]{2,1,0:T(8,128)S(1)}, u32[]{:S(2)}, u32[]{:S(2)}) collective-permute-start(f32[16,8,128]{2,1,0:T(8,128)S(1)} %get-tuple-element.64), channel_id=1, source_target_pairs={{0,2},{2,0},{4,6},{6,4},{8,10},{10,8},{12,14},{14,12},{1,3},{3,1},... | collective-permute-start | bytes 196616 | tf_op jit(solution)/shard_map/ppermute | solution.py:25
  70.3 15.3 %collective-permute-start.5 = (f32[16,8,128]{2,1,0:T(8,128)S(1)}, f32[16,8,128]{2,1,0:T(8,128)S(1)}, u32[]{:S(2)}, u32[]{:S(2)}) collective-permute-start(f32[16,8,128]{2,1,0:T(8,128)S(1)} %get-tuple-element.63), channel_id=1, source_target_pairs={{0,4},{2,6},{4,0},{6,2},{8,12},{10,14},{12,8},{14,10},{1,5},{3,7},... | collective-permute-start | bytes 196616 | tf_op jit(solution)/shard_map/ppermute | solution.py:25
  72.7 13.7 %collective-permute-start.6 = (f32[16,8,128]{2,1,0:T(8,128)S(1)}, f32[16,8,128]{2,1,0:T(8,128)S(1)}, u32[]{:S(2)}, u32[]{:S(2)}) collective-permute-start(f32[16,8,128]{2,1,0:T(8,128)S(1)} %get-tuple-element.62), channel_id=1, source_target_pairs={{0,6},{2,4},{4,2},{6,0},{8,14},{10,12},{12,10},{14,8},{1,7},{3,5},... | collective-permute-start | bytes 196616 | tf_op jit(solution)/shard_map/ppermute | solution.py:25
  72.7 18.4 %collective-permute-start.7 = (f32[16,8,128]{2,1,0:T(8,128)S(1)}, f32[16,8,128]{2,1,0:T(8,128)S(1)}, u32[]{:S(2)}, u32[]{:S(2)}) collective-permute-start(f32[16,8,128]{2,1,0:T(8,128)S(1)} %get-tuple-element.61), channel_id=1, source_target_pairs={{0,8},{2,10},{4,12},{6,14},{8,0},{10,2},{12,4},{14,6},{1,9},{3,11}... | collective-permute-start | bytes 196616 | tf_op jit(solution)/shard_map/ppermute | solution.py:25
  80.6 15.7 %copy-start.6 = (f32[16,8,128]{2,1,0:T(8,128)}, f32[16,8,128]{2,1,0:T(8,128)S(1)}, u32[]{:S(2)}) copy-start(f32[16,8,128]{2,1,0:T(8,128)S(1)} %collective-permute-done.4.refs_2_) | copy-start | bytes 196612
  80.6 10.5 %collective-permute-start.8 = (f32[16,8,128]{2,1,0:T(8,128)S(1)}, f32[16,8,128]{2,1,0:T(8,128)S(1)}, u32[]{:S(2)}, u32[]{:S(2)}) collective-permute-start(f32[16,8,128]{2,1,0:T(8,128)S(1)} %get-tuple-element.60), channel_id=1, source_target_pairs={{0,10},{2,8},{4,14},{6,12},{8,2},{10,0},{12,6},{14,4},{1,11},{3,9}... | collective-permute-start | bytes 196616 | tf_op jit(solution)/shard_map/ppermute | solution.py:25
  85.6 10.7 %copy-start.7 = (f32[16,8,128]{2,1,0:T(8,128)}, f32[16,8,128]{2,1,0:T(8,128)S(1)}, u32[]{:S(2)}) copy-start(f32[16,8,128]{2,1,0:T(8,128)S(1)} %collective-permute-done.5.refs_3_) | copy-start | bytes 196612
  85.6 6.3 %collective-permute-start.9 = (f32[16,8,128]{2,1,0:T(8,128)S(1)}, f32[16,8,128]{2,1,0:T(8,128)S(1)}, u32[]{:S(2)}, u32[]{:S(2)}) collective-permute-start(f32[16,8,128]{2,1,0:T(8,128)S(1)} %get-tuple-element.59), channel_id=1, source_target_pairs={{0,12},{2,14},{4,8},{6,10},{8,4},{10,6},{12,0},{14,2},{1,13},{3,15... | collective-permute-start | bytes 196616 | tf_op jit(solution)/shard_map/ppermute | solution.py:25
  86.3 10.0 %copy-start.8 = (f32[16,8,128]{2,1,0:T(8,128)}, f32[16,8,128]{2,1,0:T(8,128)S(1)}, u32[]{:S(2)}) copy-start(f32[16,8,128]{2,1,0:T(8,128)S(1)} %collective-permute-done.6.refs_4_) | copy-start | bytes 196612
  86.3 8.0 %collective-permute-start.10 = (f32[16,8,128]{2,1,0:T(8,128)S(1)}, f32[16,8,128]{2,1,0:T(8,128)S(1)}, u32[]{:S(2)}, u32[]{:S(2)}) collective-permute-start(f32[16,8,128]{2,1,0:T(8,128)S(1)} %get-tuple-element.58), channel_id=1, source_target_pairs={{0,14},{2,12},{4,10},{6,8},{8,6},{10,4},{12,2},{14,0},{1,15},{3,13... | collective-permute-start | bytes 196616 | tf_op jit(solution)/shard_map/ppermute | solution.py:25
  91.1 5.2 %copy-start.9 = (f32[16,8,128]{2,1,0:T(8,128)}, f32[16,8,128]{2,1,0:T(8,128)S(1)}, u32[]{:S(2)}) copy-start(f32[16,8,128]{2,1,0:T(8,128)S(1)} %collective-permute-done.7.refs_5_) | copy-start | bytes 196612
  91.1 5.2 %copy-start.10 = (f32[16,8,128]{2,1,0:T(8,128)}, f32[16,8,128]{2,1,0:T(8,128)S(1)}, u32[]{:S(2)}) copy-start(f32[16,8,128]{2,1,0:T(8,128)S(1)} %collective-permute-done.8.refs_6_) | copy-start | bytes 196612
  91.9 4.5 %copy-start.11 = (f32[16,8,128]{2,1,0:T(8,128)}, f32[16,8,128]{2,1,0:T(8,128)S(1)}, u32[]{:S(2)}) copy-start(f32[16,8,128]{2,1,0:T(8,128)S(1)} %collective-permute-done.9.refs_7_) | copy-start | bytes 196612
  95.0 18.7 %collective-permute-start.18 = (f32[4,2,64,256]{3,2,1,0:T(8,128)}, f32[4,2,64,256]{3,2,1,0:T(8,128)}, u32[]{:S(2)}, u32[]{:S(2)}) collective-permute-start(f32[4,2,64,256]{3,2,1,0:T(8,128)} %get-tuple-element.43), channel_id=1, source_target_pairs={{2,0},{4,2},{6,4},{8,6},{10,8},{12,10},{14,12},{3,1},{5,3},{7,5},{... | collective-permute-start | bytes 1572872 | tf_op jit(solution)/shard_map/ppermute | solution.py:20
  98.4 1.4 %collective-permute-start.13 = (f32[32,32]{1,0:T(8,128)}, f32[32,32]{1,0:T(8,128)S(1)}, u32[]{:S(2)}, u32[]{:S(2)}) collective-permute-start(f32[32,32]{1,0:T(8,128)} %get-tuple-element.41), channel_id=1, source_target_pairs={{0,1},{1,0},{2,3},{3,2},{4,5},{5,4},{6,7},{7,6},{8,9},{9,8},{10,11... | collective-permute-start | bytes 12296 | tf_op jit(solution)/shard_map/ppermute | solution.py:25
  100.5 13.0 %collective-permute-start.15 = (f32[32,32]{1,0:T(8,128)S(1)}, f32[32,32]{1,0:T(8,128)S(1)}, u32[]{:S(2)}, u32[]{:S(2)}) collective-permute-start(f32[32,32]{1,0:T(8,128)S(1)} %add.161), channel_id=1, source_target_pairs={{0,8},{2,10},{4,12},{6,14},{8,0},{10,2},{12,4},{14,6},{1,9},{3,11}... | collective-permute-start | bytes 12296 | tf_op jit(solution)/shard_map/ppermute | solution.py:25
  104.9 8.7 %collective-permute-start.16 = (f32[32,32]{1,0:T(8,128)S(1)}, f32[32,32]{1,0:T(8,128)S(1)}, u32[]{:S(2)}, u32[]{:S(2)}) collective-permute-start(f32[32,32]{1,0:T(8,128)S(1)} %add.161), channel_id=1, source_target_pairs={{0,12},{2,14},{4,8},{6,10},{8,4},{10,6},{12,0},{14,2},{1,13},{3,15... | collective-permute-start | bytes 12296 | tf_op jit(solution)/shard_map/ppermute | solution.py:25
  105.5 8.1 %collective-permute-start.14 = (f32[32,32]{1,0:T(8,128)S(1)}, f32[32,32]{1,0:T(8,128)S(1)}, u32[]{:S(2)}, u32[]{:S(2)}) collective-permute-start(f32[32,32]{1,0:T(8,128)S(1)} %add.161), channel_id=1, source_target_pairs={{0,4},{2,6},{4,0},{6,2},{8,12},{10,14},{12,8},{14,10},{1,5},{3,7},... | collective-permute-start | bytes 12296 | tf_op jit(solution)/shard_map/ppermute | solution.py:25
  113.6 3.8 %collective-permute-start.17 = (f32[32,32]{1,0:T(8,128)S(1)}, f32[32,32]{1,0:T(8,128)S(1)}, u32[]{:S(2)}, u32[]{:S(2)}) collective-permute-start(f32[32,32]{1,0:T(8,128)S(1)} %add_add_fusion.refs_0_), channel_id=1, source_target_pairs={{0,2},{2,0},{4,6},{6,4},{8,10},{10,8},{12,14},{14,12},{1,3},{3,1},... | collective-permute-start | bytes 12296 | tf_op jit(solution)/shard_map/ppermute | solution.py:25
  (3 other events, 3.7 us)

commit v8 on v7

--- a/solution.py
+++ b/solution.py
@@ -297,8 +297,7 @@
     )(probe, *parts)
 
 
-def ortho_kernel(*refs, modes, scale):
-    *grams, probe, grad, out = refs
+def ortho_update(grams, probe, grad, out, modes, scale):
     m = modes
     s = grams[0][...]
     for other in grams[1:]:
@@ -357,14 +356,46 @@
         out[:, 1, i * n : (i + 1) * n] = new[m:]
 
 
-def ortho(grams, probe, grad, modes, scale):
-    def body(*refs):
-        ortho_kernel(*refs, modes=modes, scale=scale)
-
+def finish(side, grams, probe, grad, gown, beside, above, below, modes, scale):
+    slices, _, rows, tile_cols = gown.shape
+    half = above.shape[2]
+    tile_rows = rows - 2 * half
+    n = beside.shape[3]
     pixels = probe.shape[1] * probe.shape[2]
+    count = len(grams)
+
+    def body(side_ref, *refs):
+        gram_refs, rest = refs[:count], refs[count:]
+        probe_ref, grad_ref, own_ref, beside_ref, above_ref, below_ref, new_ref, out = rest
+        near = pl.multiple_of(jnp.where(side_ref[0] == 0, tile_cols - n, 0), n)
+        out[...] = own_ref[:, :, half : half + tile_rows]
+        out[:, :, :, pl.ds(near, n)] += beside_ref[:, :, half : half + tile_rows]
+        out[:, :, :half] += above_ref[...]
+        out[:, :, tile_rows - half :] += below_ref[...]
+
+        @pl.when(pl.program_id(0) == 0)
+        def _():
+            ortho_update(gram_refs, probe_ref, grad_ref, new_ref, modes, scale)
+
+    def whole(shape):
+        return pl.BlockSpec(shape, lambda s, *_: (0,) * len(shape))
+
+    def one_slice(shape):
+        return pl.BlockSpec((1,) + shape[1:], lambda s, *_: (s,) + (0,) * (len(shape) - 1))
+
+    outs = [(modes, 2, pixels), (slices, 2, tile_rows, tile_cols)]
+    small, large = (*grams, probe, grad), (gown, beside, above, below)
     return pl.pallas_call(
-        body, out_shape=jax.ShapeDtypeStruct((modes, 2, pixels), F32), name="ortho"
-    )(*grams, probe, grad)
+        body,
+        out_shape=[jax.ShapeDtypeStruct(s, F32) for s in outs],
+        grid_spec=pltpu.PrefetchScalarGridSpec(
+            num_scalar_prefetch=1,
+            grid=(slices,),
+            in_specs=[whole(x.shape) for x in small] + [one_slice(x.shape) for x in large],
+            out_specs=[whole(outs[0]), one_slice(outs[1])],
+        ),
+        name="finish",
+    )(side, *small, *large)
 
 
 def take(array, which, dim):
@@ -380,7 +411,7 @@
     return block.transpose(1, 0, 2, 3).reshape(2 * modes, share, width)
 
 
-def updates(own_probe, keep, send, bottom, top, middle):
+def updates(own_probe, keep, send, bottom, top, side, gown, beside):
     rows, share, width = own_probe.shape
     modes = rows // 2
     row_devices = lax.axis_size("row")
@@ -388,7 +419,6 @@
     row_idx, col_idx = lax.axis_index("row"), lax.axis_index("col")
     row_bits = [1 << b for b in range(row_devices.bit_length() - 1)]
 
-    from_above = shifted(bottom, "row", 1)
     if share == SUBLANES and row_devices <= 8:
         received = swapped(send, "col", 1)
         parts = []
@@ -407,7 +437,8 @@
             grad = take(grad, mine, 0) + swapped(take(grad, 1 - mine, 0), "row", bit)
         parts = [grad.reshape(2 * modes, share, width)]
 
-    parts, top, from_above = lax.optimization_barrier((parts, top, from_above))
+    parts, bottom, top = lax.optimization_barrier((parts, bottom, top))
+    from_above = shifted(bottom, "row", 1)
     from_below = shifted(top, "row", -1)
     total, own_grad = gram(own_probe, parts)
     total = total + swapped(total, "col", 1)
@@ -419,10 +450,9 @@
         near, far, both = (swapped(total, "row", k) for k in (a, b, a ^ b))
         total = (total + near) + (far + both)
     grams = [total, swapped(total, "row", row_bits[0])]
-    object_grad = middle() + jnp.concatenate([from_above, from_below], axis=2)
-    grams, object_grad = lax.optimization_barrier((grams, object_grad))
-    new_probe = ortho(grams, own_probe, own_grad, modes, float(width))
-    return new_probe, object_grad
+    return finish(
+        side, grams, own_probe, own_grad, gown, beside, from_above, from_below, modes, float(width)
+    )
 
 
 def per_device(object_slices, probe, taps, measured, positions):
@@ -461,7 +491,7 @@
 
     bottom, top = folded(half + tile_rows, tile_rows + 2 * half), folded(0, half)
     new_probe, object_grad = updates(
-        own_probe, gkeep, gsend, bottom, top, lambda: folded(half, half + tile_rows)
+        own_probe, gkeep, gsend, bottom, top, side, gown, got
     )
     return (object_grad, new_probe)
 

time: 122 us -> 116 us (0.951)
  other arithmetic: 9.82 us -> 6.11 us
  starting transfers between devices: 34.4 us -> 31.3 us
  waiting for transfers between devices: 37.8 us -> 34.7 us
  Pallas kernels: 27.7 us -> 30.2 us
    ppermute x15, waiting for transfers between devices: 24.7 us -> 21.5 us  [swapped(): return lax.ppermute(value, axis, [(i, i ^ bit) for i in range(count)])]
    pallas_call x1, Pallas kernels: 2.92 us -> 5.49 us  [finish(): pl.pallas_call(body, out_shape=[jax.ShapeDtypeStruct(s, F32) for s in out...]
    add x1 -> x0, other arithmetic: 2.39 us -> none  [updates(): object_grad = middle() + jnp.concatenate([from_above, from_below], axis=2)]
    ppermute x15, starting transfers between devices: 22.3 us -> 20 us  [swapped(): return lax.ppermute(value, axis, [(i, i ^ bit) for i in range(count)])]
    unnamed x37 -> x43, local copies, waits for them, and re-layouts: 4.05 us -> 4.43 us
  transfers between devices with their start and end apart: 19 -> 19, of which waited for: 9 -> 8; matrix products, arithmetic and copies ran while one was open for 13% -> 11% of each run, Pallas kernels for 2% -> 2%
where the time goes in v8:
time: 116 us; the launch traced here: 114 us
  waiting for transfers between devices  34.7 us (30%)
  starting transfers between devices  31.3 us (27%)
  Pallas kernels  30.2 us (26%)
  local copies, waits for them, and re-layouts  10.5 us (9%)
  other arithmetic  6.11 us (5%)
    pallas_call x1, Pallas kernels, fields(): pl.pallas_call(field_kernel, out_shape=[jax.ShapeDtypeStruct(s, F32) for...  22.6 us
    ppermute x15, waiting for transfers between devices, swapped(): return lax.ppermute(value, axis, [(i, i ^ bit) for i in range(count)])  21.5 us
    ppermute x15, starting transfers between devices, swapped(): return lax.ppermute(value, axis, [(i, i ^ bit) for i in range(count)])  20 us
    ppermute x4, waiting for transfers between devices, shifted(): return lax.ppermute(value, axis, pairs)  13.2 us
    ppermute x4, starting transfers between devices, shifted(): return lax.ppermute(value, axis, pairs)  11.3 us
    pallas_call x1, Pallas kernels, finish(): pl.pallas_call(body, out_shape=[jax.ShapeDtypeStruct(s, F32) for s in out...  5.49 us
    unnamed x43, local copies, waits for them, and re-layouts  4.43 us
  transfers between devices with their start and end apart: 19, of which 8 were waited for; matrix products, arithmetic and copies ran while one was open for 11% of the time, Pallas kernels for 2%

profile of v8, /device:TPU:0, one launch (start us, length us, event | category | flops | bytes accessed | tf_op | source)
XLA Modules:
  0.0 113.8 jit_solution(18080421142440212412)
XLA Ops:
  0.6 2.3 %fusion.4 = (f32[4,2,64,256]{3,2,1,0:T(8,128)}, f32[4,2,64,256]{3,2,1,0:T(8,128)}) fusion(f32[4,2,128,256]{3,2,1,0:T(8,128)} %own.1), kind=kLoop, calls=%fused_computation.47 | loop fusion | bytes 2097152 | tf_op jit(solution)/shard_map/slice | solution.py:466
  2.9 4.9 %collective-permute-start = (f32[4,2,64,256]{3,2,1,0:T(8,128)}, f32[4,2,64,256]{3,2,1,0:T(8,128)S(1)}, u32[]{:S(2)}, u32[]{:S(2)}) collective-permute-start(f32[4,2,64,256]{3,2,1,0:T(8,128)} %get-tuple-element.63), channel_id=1, source_target_pairs={{0,2},{2,4},{4,6},{6,8},{8,10},{10,12},{12,14},{1,3},{3,5},{5,7},{... | collective-permute-start | bytes 1572872 | tf_op jit(solution)/shard_map/ppermute | solution.py:20
  7.8 1.3 %collective-permute-start.1 = (f32[4,2,64,256]{3,2,1,0:T(8,128)}, f32[4,2,64,256]{3,2,1,0:T(8,128)S(1)}, u32[]{:S(2)}, u32[]{:S(2)}) collective-permute-start(f32[4,2,64,256]{3,2,1,0:T(8,128)} %get-tuple-element.62), channel_id=1, source_target_pairs={{2,0},{4,2},{6,4},{8,6},{10,8},{12,10},{14,12},{3,1},{5,3},{7,5},{... | collective-permute-start | bytes 1572872 | tf_op jit(solution)/shard_map/ppermute | solution.py:20
  11.0 1.0 copy.17
  12.1 0.9 constant_dynamic-update-slice_fusion.3
  13.0 0.9 dynamic-slice_bitcast_fusion
  14.5 0.9 constant_dynamic-update-slice_fusion.2
  15.4 0.9 constant_dynamic-update-slice_fusion.1
  16.3 0.9 constant_dynamic-update-slice_fusion.tab
  17.3 13.2 %collective-permute-done.above = f32[4,2,64,256]{3,2,1,0:T(8,128)S(1)} collective-permute-done((f32[4,2,64,256]{3,2,1,0:T(8,128)}, f32[4,2,64,256]{3,2,1,0:T(8,128)S(1)}, u32[]{:S(2)}, u32[]{:S(2)}) %collective-permute-start) | collective-permute-done | bytes 524320 | tf_op jit(solution)/shard_map/ppermute | solution.py:20
  31.4 2.1 %collective-permute-done.2.beside = f32[4,2,256,128]{3,2,1,0:T(8,128)} collective-permute-done((f32[4,2,256,128]{3,2,1,0:T(8,128)S(1)}, f32[4,2,256,128]{3,2,1,0:T(8,128)}, u32[]{:S(2)}, u32[]{:S(2)}) %collective-permute-start.2) | collective-permute-done | bytes 1048608 | tf_op jit(solution)/shard_map/ppermute | solution.py:25
  33.5 22.6 %fields.1 = (f32[4,2,256,256]{3,2,1,0:T(8,128)}, f32[4,2,256,128]{3,2,1,0:T(8,128)}, f32[8,16,8,128]{3,2,1,0:T(8,128)}, f32[8,16,8,128]{3,2,1,0:T(8,128)}) custom-call(s32[2,2]{1,0:T(2,128)} %broadcast_subtract_fusion.places, s32[1]{0:T(128)} %bitcast.side.side_ref, f32[4,2,128,256]{3,2,1,0:T(8,128)} %own.1, f32[4,2,64,256]{3,2,1,0:T(8,128)} %copy-done.4, ...), custom_call_target="tpu_custom_call" | custom-call | tf_op jit(solution)/shard_map/fields/pallas_call | solution.py:246
  56.6 3.2 %collective-permute-done.3 = f32[8,16,8,128]{3,2,1,0:T(8,128)} collective-permute-done((f32[8,16,8,128]{3,2,1,0:T(8,128)}, f32[8,16,8,128]{3,2,1,0:T(8,128)}, u32[]{:S(2)}, u32[]{:S(2)}) %collective-permute-start.3) | collective-permute-done | bytes 524320 | tf_op jit(solution)/shard_map/ppermute | solution.py:25
  59.9 1.9 %add_bitcast_fusion = (f32[16,8,128]{2,1,0:T(8,128)S(1)}, f32[16,8,128]{2,1,0:T(8,128)S(1)}, f32[16,8,128]{2,1,0:T(8,128)S(1)}, f32[16,8,128]{2,1,0:T(8,128)S(1)...) fusion(f32[8,16,8,128]{3,2,1,0:T(8,128)} %collective-permute-don, ...), kind=kLoop, calls=%fused_computation.23 | loop fusion | flops 131072 | bytes 1572896 | tf_op jit(solution)/shard_map/add | solution.py:426
  61.8 2.4 %collective-permute-start.4 = (f32[16,8,128]{2,1,0:T(8,128)S(1)}, f32[16,8,128]{2,1,0:T(8,128)S(1)}, u32[]{:S(2)}, u32[]{:S(2)}) collective-permute-start(f32[16,8,128]{2,1,0:T(8,128)S(1)} %get-tuple-element.60), channel_id=1, source_target_pairs={{0,2},{2,0},{4,6},{6,4},{8,10},{10,8},{12,14},{14,12},{1,3},{3,1},... | collective-permute-start | bytes 196616 | tf_op jit(solution)/shard_map/ppermute | solution.py:25
  64.2 1.6 %collective-permute-start.5 = (f32[16,8,128]{2,1,0:T(8,128)S(1)}, f32[16,8,128]{2,1,0:T(8,128)S(1)}, u32[]{:S(2)}, u32[]{:S(2)}) collective-permute-start(f32[16,8,128]{2,1,0:T(8,128)S(1)} %get-tuple-element.59), channel_id=1, source_target_pairs={{0,4},{2,6},{4,0},{6,2},{8,12},{10,14},{12,8},{14,10},{1,5},{3,7},... | collective-permute-start | bytes 196616 | tf_op jit(solution)/shard_map/ppermute | solution.py:25
  65.8 0.9 collective-permute-start.6
  66.7 3.0 %collective-permute-start.7 = (f32[16,8,128]{2,1,0:T(8,128)S(1)}, f32[16,8,128]{2,1,0:T(8,128)S(1)}, u32[]{:S(2)}, u32[]{:S(2)}) collective-permute-start(f32[16,8,128]{2,1,0:T(8,128)S(1)} %get-tuple-element.57), channel_id=1, source_target_pairs={{0,8},{2,10},{4,12},{6,14},{8,0},{10,2},{12,4},{14,6},{1,9},{3,11}... | collective-permute-start | bytes 196616 | tf_op jit(solution)/shard_map/ppermute | solution.py:25
  70.2 3.1 %collective-permute-start.9 = (f32[16,8,128]{2,1,0:T(8,128)S(1)}, f32[16,8,128]{2,1,0:T(8,128)S(1)}, u32[]{:S(2)}, u32[]{:S(2)}) collective-permute-start(f32[16,8,128]{2,1,0:T(8,128)S(1)} %get-tuple-element.55), channel_id=1, source_target_pairs={{0,12},{2,14},{4,8},{6,10},{8,4},{10,6},{12,0},{14,2},{1,13},{3,15... | collective-permute-start | bytes 196616 | tf_op jit(solution)/shard_map/ppermute | solution.py:25
  73.4 1.5 %collective-permute-start.10 = (f32[16,8,128]{2,1,0:T(8,128)S(1)}, f32[16,8,128]{2,1,0:T(8,128)S(1)}, u32[]{:S(2)}, u32[]{:S(2)}) collective-permute-start(f32[16,8,128]{2,1,0:T(8,128)S(1)} %get-tuple-element.54), channel_id=1, source_target_pairs={{0,14},{2,12},{4,10},{6,8},{8,6},{10,4},{12,2},{14,0},{1,15},{3,13... | collective-permute-start | bytes 196616 | tf_op jit(solution)/shard_map/ppermute | solution.py:25
  74.9 1.1 maximum_add_fusion.1
  76.0 3.2 %collective-permute-done.8.refs_6_ = f32[16,8,128]{2,1,0:T(8,128)S(1)} collective-permute-done((f32[16,8,128]{2,1,0:T(8,128)S(1)}, f32[16,8,128]{2,1,0:T(8,128)S(1)}, u32[]{:S(2)}, u32[]{:S(2)}) %collective-permute-start.8) | collective-permute-done | bytes 65568 | tf_op jit(solution)/shard_map/ppermute | solution.py:25
  79.2 1.3 %collective-permute-done.10.refs_8_ = f32[16,8,128]{2,1,0:T(8,128)S(1)} collective-permute-done((f32[16,8,128]{2,1,0:T(8,128)S(1)}, f32[16,8,128]{2,1,0:T(8,128)S(1)}, u32[]{:S(2)}, u32[]{:S(2)}) %collective-permute-start.10) | collective-permute-done | bytes 65568 | tf_op jit(solution)/shard_map/ppermute | solution.py:25
  81.1 3.9 %collective-permute-start.17 = (f32[4,2,64,256]{3,2,1,0:T(8,128)}, f32[4,2,64,256]{3,2,1,0:T(8,128)S(1)}, u32[]{:S(2)}, u32[]{:S(2)}) collective-permute-start(f32[4,2,64,256]{3,2,1,0:T(8,128)} %get-tuple-element.42), channel_id=1, source_target_pairs={{0,2},{2,4},{4,6},{6,8},{8,10},{10,12},{12,14},{1,3},{3,5},{5,7},{... | collective-permute-start | bytes 1572872 | tf_op jit(solution)/shard_map/ppermute | solution.py:20
  85.0 1.3 %collective-permute-start.18 = (f32[4,2,64,256]{3,2,1,0:T(8,128)}, f32[4,2,64,256]{3,2,1,0:T(8,128)S(1)}, u32[]{:S(2)}, u32[]{:S(2)}) collective-permute-start(f32[4,2,64,256]{3,2,1,0:T(8,128)} %get-tuple-element.43), channel_id=1, source_target_pairs={{2,0},{4,2},{6,4},{8,6},{10,8},{12,10},{14,12},{3,1},{5,3},{7,5},{... | collective-permute-start | bytes 1572872 | tf_op jit(solution)/shard_map/ppermute | solution.py:20
  86.3 2.1 %gram.1 = (f32[32,32]{1,0:T(8,128)}, f32[16,8,128]{2,1,0:T(8,128)}) custom-call(f32[16,8,128]{2,1,0:T(8,128)} %bitcast.48, f32[16,8,128]{2,1,0:T(8,128)} %get-tuple-element.32.refs_1_, f32[16,8,128]{2,1,0:T(8,128)} %copy-done.9, f32[16,8,128]{2,1,0:T(8,128)} %copy-done.10, f32[16,8,128]{2,1,0:T(8,128)} %copy-done.11, f32[16,8,128]{2,1,0:T(8,128)} %copy-done.12, ...), custom_call_target="tpu_custom_call" | custom-call | tf_op jit(solution)/shard_map/gram/pallas_call | solution.py:290
  88.4 1.4 %collective-permute-done.12 = f32[32,32]{1,0:T(8,128)S(1)} collective-permute-done((f32[32,32]{1,0:T(8,128)}, f32[32,32]{1,0:T(8,128)S(1)}, u32[]{:S(2)}, u32[]{:S(2)}) %collective-permute-start.12) | collective-permute-done | bytes 4128 | tf_op jit(solution)/shard_map/ppermute | solution.py:25
  90.5 4.7 %collective-permute-start.14 = (f32[32,32]{1,0:T(8,128)S(1)}, f32[32,32]{1,0:T(8,128)S(1)}, u32[]{:S(2)}, u32[]{:S(2)}) collective-permute-start(f32[32,32]{1,0:T(8,128)S(1)} %add.155), channel_id=1, source_target_pairs={{0,8},{2,10},{4,12},{6,14},{8,0},{10,2},{12,4},{14,6},{1,9},{3,11}... | collective-permute-start | bytes 12296 | tf_op jit(solution)/shard_map/ppermute | solution.py:25
  95.2 1.7 %collective-permute-start.15 = (f32[32,32]{1,0:T(8,128)S(1)}, f32[32,32]{1,0:T(8,128)S(1)}, u32[]{:S(2)}, u32[]{:S(2)}) collective-permute-start(f32[32,32]{1,0:T(8,128)S(1)} %add.155), channel_id=1, source_target_pairs={{0,12},{2,14},{4,8},{6,10},{8,4},{10,6},{12,0},{14,2},{1,13},{3,15... | collective-permute-start | bytes 12296 | tf_op jit(solution)/shard_map/ppermute | solution.py:25
  96.9 6.6 %collective-permute-done.14 = f32[32,32]{1,0:T(8,128)S(1)} collective-permute-done((f32[32,32]{1,0:T(8,128)S(1)}, f32[32,32]{1,0:T(8,128)S(1)}, u32[]{:S(2)}, u32[]{:S(2)}) %collective-permute-start.14) | collective-permute-done | bytes 4128 | tf_op jit(solution)/shard_map/ppermute | solution.py:25
  103.6 3.7 %collective-permute-done.16.refs_1_ = f32[32,32]{1,0:T(8,128)S(1)} collective-permute-done((f32[32,32]{1,0:T(8,128)S(1)}, f32[32,32]{1,0:T(8,128)S(1)}, u32[]{:S(2)}, u32[]{:S(2)}) %collective-permute-start.16) | collective-permute-done | bytes 4128 | tf_op jit(solution)/shard_map/ppermute | solution.py:25
  108.3 5.5 %finish.1 = (f32[8,2,1024]{2,1,0:T(2,128)}, f32[4,2,128,256]{3,2,1,0:T(8,128)}) custom-call(s32[1]{0:T(128)} %bitcast.side.side_ref, f32[32,32]{1,0:T(8,128)} %copy-done.8, f32[32,32]{1,0:T(8,128)} %copy-done.16, f32[16,8,128]{2,1,0:T(8,128)} %bitcast.49, f32[16,8,128]{2,1,0:T(8,128)} %get-tuple-element.41.refs_3_, ...), custom_call_target="tpu_custom_call" | custom-call | tf_op jit(solution)/shard_map/finish/pallas_call | solution.py:388
  (78 shorter events, 6.8 us)
Async XLA Ops:
  0.6 8.5 %copy-start.17 = (f32[2,63]{1,0:T(2,128)S(1)}, f32[2,63]{1,0:T(2,128)}, u32[]{:S(2)}) copy-start(f32[2,63]{1,0:T(2,128)} %param.9) | copy-start | bytes 1516
  2.9 27.6 %collective-permute-start = (f32[4,2,64,256]{3,2,1,0:T(8,128)}, f32[4,2,64,256]{3,2,1,0:T(8,128)S(1)}, u32[]{:S(2)}, u32[]{:S(2)}) collective-permute-start(f32[4,2,64,256]{3,2,1,0:T(8,128)} %get-tuple-element.63), channel_id=1, source_target_pairs={{0,2},{2,4},{4,6},{6,8},{8,10},{10,12},{12,14},{1,3},{3,5},{5,7},{... | collective-permute-start | bytes 1572872 | tf_op jit(solution)/shard_map/ppermute | solution.py:20
  7.8 22.7 %collective-permute-start.1 = (f32[4,2,64,256]{3,2,1,0:T(8,128)}, f32[4,2,64,256]{3,2,1,0:T(8,128)S(1)}, u32[]{:S(2)}, u32[]{:S(2)}) collective-permute-start(f32[4,2,64,256]{3,2,1,0:T(8,128)} %get-tuple-element.62), channel_id=1, source_target_pairs={{2,0},{4,2},{6,4},{8,6},{10,8},{12,10},{14,12},{3,1},{5,3},{7,5},{... | collective-permute-start | bytes 1572872 | tf_op jit(solution)/shard_map/ppermute | solution.py:20
  10.0 7.2 %copy-start = (f32[4,2,128,256]{3,2,1,0:T(8,128)S(1)}, f32[4,2,128,256]{3,2,1,0:T(8,128)}, u32[]{:S(2)}) copy-start(f32[4,2,128,256]{3,2,1,0:T(8,128)} %own.1) | copy-start | bytes 3145732
  17.2 13.4 %copy-start.3 = (bf16[8,256,256]{2,1,0:T(8,128)(2,1)}, bf16[8,256,256]{2,1,0:T(8,128)(2,1)S(1)}, u32[]{:S(2)}) copy-start(bf16[8,256,256]{2,1,0:T(8,128)(2,1)S(1)} %constant_dynamic-update-slice_fusion.tab) | copy-start | bytes 3145732
  17.3 13.5 %copy-start.18 = (s32[2,2]{1,0:T(2,128)S(1)}, s32[2,2]{1,0:T(2,128)}, u32[]{:S(2)}) copy-start(s32[2,2]{1,0:T(2,128)} %param.11) | copy-start | bytes 52
  30.6 2.9 %collective-permute-start.2 = (f32[4,2,256,128]{3,2,1,0:T(8,128)S(1)}, f32[4,2,256,128]{3,2,1,0:T(8,128)}, u32[]{:S(2)}, u32[]{:S(2)}) collective-permute-start(f32[4,2,256,128]{3,2,1,0:T(8,128)S(1)} %pad_maximum_fusion), channel_id=1, source_target_pairs={{0,1},{1,0},{2,3},{3,2},{4,5},{5,4},{6,7},{7,6},{8,9},{9,8},{10,11... | collective-permute-start | bytes 3145736 | tf_op jit(solution)/shard_map/ppermute | solution.py:25
  56.1 18.7 %copy-start.1 = (f32[4,2,256,256]{3,2,1,0:T(8,128)S(1)}, f32[4,2,256,256]{3,2,1,0:T(8,128)}, u32[]{:S(2)}) copy-start(f32[4,2,256,256]{3,2,1,0:T(8,128)} %get-tuple-element.30.refs_4_) | copy-start | bytes 6291460
  56.1 13.6 %collective-permute-start.11 = (f32[4,2,256,128]{3,2,1,0:T(8,128)}, f32[4,2,256,128]{3,2,1,0:T(8,128)S(1)}, u32[]{:S(2)}, u32[]{:S(2)}) collective-permute-start(f32[4,2,256,128]{3,2,1,0:T(8,128)} %get-tuple-element.31), channel_id=1, source_target_pairs={{0,1},{1,0},{2,3},{3,2},{4,5},{5,4},{6,7},{7,6},{8,9},{9,8},{10,11... | collective-permute-start | bytes 3145736 | tf_op jit(solution)/shard_map/ppermute | solution.py:25
  56.3 3.5 %collective-permute-start.3 = (f32[8,16,8,128]{3,2,1,0:T(8,128)}, f32[8,16,8,128]{3,2,1,0:T(8,128)}, u32[]{:S(2)}, u32[]{:S(2)}) collective-permute-start(f32[8,16,8,128]{3,2,1,0:T(8,128)} %get-tuple-element.29), channel_id=1, source_target_pairs={{0,1},{1,0},{2,3},{3,2},{4,5},{5,4},{6,7},{7,6},{8,9},{9,8},{10,11... | collective-permute-start | bytes 1572872 | tf_op jit(solution)/shard_map/ppermute | solution.py:25
  61.8 8.4 %collective-permute-start.4 = (f32[16,8,128]{2,1,0:T(8,128)S(1)}, f32[16,8,128]{2,1,0:T(8,128)S(1)}, u32[]{:S(2)}, u32[]{:S(2)}) collective-permute-start(f32[16,8,128]{2,1,0:T(8,128)S(1)} %get-tuple-element.60), channel_id=1, source_target_pairs={{0,2},{2,0},{4,6},{6,4},{8,10},{10,8},{12,14},{14,12},{1,3},{3,1},... | collective-permute-start | bytes 196616 | tf_op jit(solution)/shard_map/ppermute | solution.py:25
  64.2 9.1 %collective-permute-start.5 = (f32[16,8,128]{2,1,0:T(8,128)S(1)}, f32[16,8,128]{2,1,0:T(8,128)S(1)}, u32[]{:S(2)}, u32[]{:S(2)}) collective-permute-start(f32[16,8,128]{2,1,0:T(8,128)S(1)} %get-tuple-element.59), channel_id=1, source_target_pairs={{0,4},{2,6},{4,0},{6,2},{8,12},{10,14},{12,8},{14,10},{1,5},{3,7},... | collective-permute-start | bytes 196616 | tf_op jit(solution)/shard_map/ppermute | solution.py:25
  65.8 10.2 %collective-permute-start.6 = (f32[16,8,128]{2,1,0:T(8,128)S(1)}, f32[16,8,128]{2,1,0:T(8,128)S(1)}, u32[]{:S(2)}, u32[]{:S(2)}) collective-permute-start(f32[16,8,128]{2,1,0:T(8,128)S(1)} %get-tuple-element.58), channel_id=1, source_target_pairs={{0,6},{2,4},{4,2},{6,0},{8,14},{10,12},{12,10},{14,8},{1,7},{3,5},... | collective-permute-start | bytes 196616 | tf_op jit(solution)/shard_map/ppermute | solution.py:25
  66.7 9.3 %collective-permute-start.7 = (f32[16,8,128]{2,1,0:T(8,128)S(1)}, f32[16,8,128]{2,1,0:T(8,128)S(1)}, u32[]{:S(2)}, u32[]{:S(2)}) collective-permute-start(f32[16,8,128]{2,1,0:T(8,128)S(1)} %get-tuple-element.57), channel_id=1, source_target_pairs={{0,8},{2,10},{4,12},{6,14},{8,0},{10,2},{12,4},{14,6},{1,9},{3,11}... | collective-permute-start | bytes 196616 | tf_op jit(solution)/shard_map/ppermute | solution.py:25
  69.7 6.2 %copy-start.2 = (f32[4,2,256,128]{3,2,1,0:T(8,128)}, f32[4,2,256,128]{3,2,1,0:T(8,128)S(1)}, u32[]{:S(2)}) copy-start(f32[4,2,256,128]{3,2,1,0:T(8,128)S(1)} %collective-permute-done.11.refs_5_) | copy-start | bytes 3145732
  69.7 9.4 %collective-permute-start.8 = (f32[16,8,128]{2,1,0:T(8,128)S(1)}, f32[16,8,128]{2,1,0:T(8,128)S(1)}, u32[]{:S(2)}, u32[]{:S(2)}) collective-permute-start(f32[16,8,128]{2,1,0:T(8,128)S(1)} %get-tuple-element.56), channel_id=1, source_target_pairs={{0,10},{2,8},{4,14},{6,12},{8,2},{10,0},{12,6},{14,4},{1,11},{3,9}... | collective-permute-start | bytes 196616 | tf_op jit(solution)/shard_map/ppermute | solution.py:25
  70.2 16.1 %copy-start.9 = (f32[16,8,128]{2,1,0:T(8,128)}, f32[16,8,128]{2,1,0:T(8,128)S(1)}, u32[]{:S(2)}) copy-start(f32[16,8,128]{2,1,0:T(8,128)S(1)} %collective-permute-done.4.refs_2_) | copy-start | bytes 196612
  70.2 9.0 %collective-permute-start.9 = (f32[16,8,128]{2,1,0:T(8,128)S(1)}, f32[16,8,128]{2,1,0:T(8,128)S(1)}, u32[]{:S(2)}, u32[]{:S(2)}) collective-permute-start(f32[16,8,128]{2,1,0:T(8,128)S(1)} %get-tuple-element.55), channel_id=1, source_target_pairs={{0,12},{2,14},{4,8},{6,10},{8,4},{10,6},{12,0},{14,2},{1,13},{3,15... | collective-permute-start | bytes 196616 | tf_op jit(solution)/shard_map/ppermute | solution.py:25
  73.4 12.9 %copy-start.10 = (f32[16,8,128]{2,1,0:T(8,128)}, f32[16,8,128]{2,1,0:T(8,128)S(1)}, u32[]{:S(2)}) copy-start(f32[16,8,128]{2,1,0:T(8,128)S(1)} %collective-permute-done.5.refs_3_) | copy-start | bytes 196612
  73.4 7.1 %collective-permute-start.10 = (f32[16,8,128]{2,1,0:T(8,128)S(1)}, f32[16,8,128]{2,1,0:T(8,128)S(1)}, u32[]{:S(2)}, u32[]{:S(2)}) collective-permute-start(f32[16,8,128]{2,1,0:T(8,128)S(1)} %get-tuple-element.54), channel_id=1, source_target_pairs={{0,14},{2,12},{4,10},{6,8},{8,6},{10,4},{12,2},{14,0},{1,15},{3,13... | collective-permute-start | bytes 196616 | tf_op jit(solution)/shard_map/ppermute | solution.py:25
  76.0 10.3 %copy-start.11 = (f32[16,8,128]{2,1,0:T(8,128)}, f32[16,8,128]{2,1,0:T(8,128)S(1)}, u32[]{:S(2)}) copy-start(f32[16,8,128]{2,1,0:T(8,128)S(1)} %collective-permute-done.6.refs_4_) | copy-start | bytes 196612
  76.0 10.3 %copy-start.12 = (f32[16,8,128]{2,1,0:T(8,128)}, f32[16,8,128]{2,1,0:T(8,128)S(1)}, u32[]{:S(2)}) copy-start(f32[16,8,128]{2,1,0:T(8,128)S(1)} %collective-permute-done.7.refs_5_) | copy-start | bytes 196612
  79.2 7.1 %copy-start.13 = (f32[16,8,128]{2,1,0:T(8,128)}, f32[16,8,128]{2,1,0:T(8,128)S(1)}, u32[]{:S(2)}) copy-start(f32[16,8,128]{2,1,0:T(8,128)S(1)} %collective-permute-done.8.refs_6_) | copy-start | bytes 196612
  79.2 7.1 %copy-start.14 = (f32[16,8,128]{2,1,0:T(8,128)}, f32[16,8,128]{2,1,0:T(8,128)S(1)}, u32[]{:S(2)}) copy-start(f32[16,8,128]{2,1,0:T(8,128)S(1)} %collective-permute-done.9.refs_7_) | copy-start | bytes 196612
  81.1 26.3 %collective-permute-start.17 = (f32[4,2,64,256]{3,2,1,0:T(8,128)}, f32[4,2,64,256]{3,2,1,0:T(8,128)S(1)}, u32[]{:S(2)}, u32[]{:S(2)}) collective-permute-start(f32[4,2,64,256]{3,2,1,0:T(8,128)} %get-tuple-element.42), channel_id=1, source_target_pairs={{0,2},{2,4},{4,6},{6,8},{8,10},{10,12},{12,14},{1,3},{3,5},{5,7},{... | collective-permute-start | bytes 1572872 | tf_op jit(solution)/shard_map/ppermute | solution.py:20
  85.0 22.4 %collective-permute-start.18 = (f32[4,2,64,256]{3,2,1,0:T(8,128)}, f32[4,2,64,256]{3,2,1,0:T(8,128)S(1)}, u32[]{:S(2)}, u32[]{:S(2)}) collective-permute-start(f32[4,2,64,256]{3,2,1,0:T(8,128)} %get-tuple-element.43), channel_id=1, source_target_pairs={{2,0},{4,2},{6,4},{8,6},{10,8},{12,10},{14,12},{3,1},{5,3},{7,5},{... | collective-permute-start | bytes 1572872 | tf_op jit(solution)/shard_map/ppermute | solution.py:20
  88.4 1.4 %collective-permute-start.12 = (f32[32,32]{1,0:T(8,128)}, f32[32,32]{1,0:T(8,128)S(1)}, u32[]{:S(2)}, u32[]{:S(2)}) collective-permute-start(f32[32,32]{1,0:T(8,128)} %get-tuple-element.40), channel_id=1, source_target_pairs={{0,1},{1,0},{2,3},{3,2},{4,5},{5,4},{6,7},{7,6},{8,9},{9,8},{10,11... | collective-permute-start | bytes 12296 | tf_op jit(solution)/shard_map/ppermute | solution.py:25
  90.5 13.0 %collective-permute-start.14 = (f32[32,32]{1,0:T(8,128)S(1)}, f32[32,32]{1,0:T(8,128)S(1)}, u32[]{:S(2)}, u32[]{:S(2)}) collective-permute-start(f32[32,32]{1,0:T(8,128)S(1)} %add.155), channel_id=1, source_target_pairs={{0,8},{2,10},{4,12},{6,14},{8,0},{10,2},{12,4},{14,6},{1,9},{3,11}... | collective-permute-start | bytes 12296 | tf_op jit(solution)/shard_map/ppermute | solution.py:25
  95.2 8.3 %collective-permute-start.15 = (f32[32,32]{1,0:T(8,128)S(1)}, f32[32,32]{1,0:T(8,128)S(1)}, u32[]{:S(2)}, u32[]{:S(2)}) collective-permute-start(f32[32,32]{1,0:T(8,128)S(1)} %add.155), channel_id=1, source_target_pairs={{0,12},{2,14},{4,8},{6,10},{8,4},{10,6},{12,0},{14,2},{1,13},{3,15... | collective-permute-start | bytes 12296 | tf_op jit(solution)/shard_map/ppermute | solution.py:25
  96.9 6.6 %collective-permute-start.13 = (f32[32,32]{1,0:T(8,128)S(1)}, f32[32,32]{1,0:T(8,128)S(1)}, u32[]{:S(2)}, u32[]{:S(2)}) collective-permute-start(f32[32,32]{1,0:T(8,128)S(1)} %add.155), channel_id=1, source_target_pairs={{0,4},{2,6},{4,0},{6,2},{8,12},{10,14},{12,8},{14,10},{1,5},{3,7},... | collective-permute-start | bytes 12296 | tf_op jit(solution)/shard_map/ppermute | solution.py:25
  103.5 3.8 %copy-start.8 = (f32[32,32]{1,0:T(8,128)}, f32[32,32]{1,0:T(8,128)S(1)}, u32[]{:S(2)}) copy-start(f32[32,32]{1,0:T(8,128)S(1)} %add_add_fusion.refs_0_) | copy-start | bytes 12292
  103.5 3.8 %collective-permute-start.16 = (f32[32,32]{1,0:T(8,128)S(1)}, f32[32,32]{1,0:T(8,128)S(1)}, u32[]{:S(2)}, u32[]{:S(2)}) collective-permute-start(f32[32,32]{1,0:T(8,128)S(1)} %add_add_fusion.refs_0_), channel_id=1, source_target_pairs={{0,2},{2,0},{4,6},{6,4},{8,10},{10,8},{12,14},{14,12},{1,3},{3,1},... | collective-permute-start | bytes 12296 | tf_op jit(solution)/shard_map/ppermute | solution.py:25
  (6 other events, 9.0 us)

commit v9 on v7

--- a/solution.py
+++ b/solution.py
@@ -388,7 +388,6 @@
     row_idx, col_idx = lax.axis_index("row"), lax.axis_index("col")
     row_bits = [1 << b for b in range(row_devices.bit_length() - 1)]
 
-    from_above = shifted(bottom, "row", 1)
     if share == SUBLANES and row_devices <= 8:
         received = swapped(send, "col", 1)
         parts = []
@@ -407,7 +406,8 @@
             grad = take(grad, mine, 0) + swapped(take(grad, 1 - mine, 0), "row", bit)
         parts = [grad.reshape(2 * modes, share, width)]
 
-    parts, top, from_above = lax.optimization_barrier((parts, top, from_above))
+    parts, bottom, top = lax.optimization_barrier((parts, bottom, top))
+    from_above = shifted(bottom, "row", 1)
     from_below = shifted(top, "row", -1)
     total, own_grad = gram(own_probe, parts)
     total = total + swapped(total, "col", 1)
@@ -419,9 +419,8 @@
         near, far, both = (swapped(total, "row", k) for k in (a, b, a ^ b))
         total = (total + near) + (far + both)
     grams = [total, swapped(total, "row", row_bits[0])]
+    new_probe = ortho(grams, own_probe, own_grad, modes, float(width))
     object_grad = middle() + jnp.concatenate([from_above, from_below], axis=2)
-    grams, object_grad = lax.optimization_barrier((grams, object_grad))
-    new_probe = ortho(grams, own_probe, own_grad, modes, float(width))
     return new_probe, object_grad
 
 

time: 122 us -> 113 us (0.926)
  starting transfers between devices: 34.4 us -> 28.8 us
  waiting for transfers between devices: 37.8 us -> 34.5 us
    ppermute x15, starting transfers between devices: 22.3 us -> 18.7 us  [swapped(): return lax.ppermute(value, axis, [(i, i ^ bit) for i in range(count)])]
    ppermute x15, waiting for transfers between devices: 24.7 us -> 21.3 us  [swapped(): return lax.ppermute(value, axis, [(i, i ^ bit) for i in range(count)])]
    ppermute x4, starting transfers between devices: 12.1 us -> 10.1 us  [shifted(): return lax.ppermute(value, axis, pairs)]
    unnamed x37 -> x39, local copies, waits for them, and re-layouts: 4.05 us -> 4.06 us
  transfers between devices with their start and end apart: 19 -> 19, of which waited for: 9 -> 11; matrix products, arithmetic and copies ran while one was open for 13% -> 12% of each run, Pallas kernels for 2% -> 4%
where the time goes in v9:
time: 113 us; the launch traced here: 112 us
  waiting for transfers between devices  34.5 us (31%)
  starting transfers between devices  28.8 us (25%)
  Pallas kernels  27.6 us (24%)
  local copies, waits for them, and re-layouts  10.1 us (9%)
  other arithmetic  9.64 us (9%)
    pallas_call x1, Pallas kernels, fields(): pl.pallas_call(field_kernel, out_shape=[jax.ShapeDtypeStruct(s, F32) for...  22.6 us
    ppermute x15, waiting for transfers between devices, swapped(): return lax.ppermute(value, axis, [(i, i ^ bit) for i in range(count)])  21.3 us
    ppermute x15, starting transfers between devices, swapped(): return lax.ppermute(value, axis, [(i, i ^ bit) for i in range(count)])  18.7 us
    ppermute x4, waiting for transfers between devices, shifted(): return lax.ppermute(value, axis, pairs)  13.2 us
    ppermute x4, starting transfers between devices, shifted(): return lax.ppermute(value, axis, pairs)  10.1 us
    unnamed x39, local copies, waits for them, and re-layouts  4.06 us
    pallas_call x1, Pallas kernels, ortho(): pl.pallas_call(body, out_shape=jax.ShapeDtypeStruct((modes, 2, pixels), F...  2.92 us
    add x1, other arithmetic, updates(): object_grad = middle() + jnp.concatenate([from_above, from_below], axis=2)  2.34 us
  transfers between devices with their start and end apart: 19, of which 11 were waited for; matrix products, arithmetic and copies ran while one was open for 12% of the time, Pallas kernels for 4%

profile of v9, /device:TPU:0, one launch (start us, length us, event | category | flops | bytes accessed | tf_op | source)
XLA Modules:
  0.0 111.7 jit_solution(6288617790303849960)
XLA Ops:
  0.6 2.3 %fusion.5 = (f32[4,2,64,256]{3,2,1,0:T(8,128)}, f32[4,2,64,256]{3,2,1,0:T(8,128)}) fusion(f32[4,2,128,256]{3,2,1,0:T(8,128)} %own.1), kind=kLoop, calls=%fused_computation.51 | loop fusion | bytes 2097152 | tf_op jit(solution)/shard_map/slice | solution.py:435
  2.9 4.9 %collective-permute-start = (f32[4,2,64,256]{3,2,1,0:T(8,128)}, f32[4,2,64,256]{3,2,1,0:T(8,128)S(1)}, u32[]{:S(2)}, u32[]{:S(2)}) collective-permute-start(f32[4,2,64,256]{3,2,1,0:T(8,128)} %get-tuple-element.61), channel_id=1, source_target_pairs={{0,2},{2,4},{4,6},{6,8},{8,10},{10,12},{12,14},{1,3},{3,5},{5,7},{... | collective-permute-start | bytes 1572872 | tf_op jit(solution)/shard_map/ppermute | solution.py:20
  7.8 1.3 %collective-permute-start.1 = (f32[4,2,64,256]{3,2,1,0:T(8,128)}, f32[4,2,64,256]{3,2,1,0:T(8,128)S(1)}, u32[]{:S(2)}, u32[]{:S(2)}) collective-permute-start(f32[4,2,64,256]{3,2,1,0:T(8,128)} %get-tuple-element.60), channel_id=1, source_target_pairs={{2,0},{4,2},{6,4},{8,6},{10,8},{12,10},{14,12},{3,1},{5,3},{7,5},{... | collective-permute-start | bytes 1572872 | tf_op jit(solution)/shard_map/ppermute | solution.py:20
  11.0 1.0 copy.17
  15.4 0.9 constant_dynamic-update-slice_fusion.1
  16.3 0.9 constant_dynamic-update-slice_fusion.tab
  17.3 13.2 %collective-permute-done.above = f32[4,2,64,256]{3,2,1,0:T(8,128)S(1)} collective-permute-done((f32[4,2,64,256]{3,2,1,0:T(8,128)}, f32[4,2,64,256]{3,2,1,0:T(8,128)S(1)}, u32[]{:S(2)}, u32[]{:S(2)}) %collective-permute-start) | collective-permute-done | bytes 524320 | tf_op jit(solution)/shard_map/ppermute | solution.py:20
  31.4 2.1 %collective-permute-done.2.beside = f32[4,2,256,128]{3,2,1,0:T(8,128)} collective-permute-done((f32[4,2,256,128]{3,2,1,0:T(8,128)S(1)}, f32[4,2,256,128]{3,2,1,0:T(8,128)}, u32[]{:S(2)}, u32[]{:S(2)}) %collective-permute-start.2) | collective-permute-done | bytes 1048608 | tf_op jit(solution)/shard_map/ppermute | solution.py:25
  33.5 22.6 %fields.1 = (f32[4,2,256,256]{3,2,1,0:T(8,128)}, f32[4,2,256,128]{3,2,1,0:T(8,128)}, f32[8,16,8,128]{3,2,1,0:T(8,128)}, f32[8,16,8,128]{3,2,1,0:T(8,128)}) custom-call(s32[2,2]{1,0:T(2,128)} %broadcast_subtract_fusion.places, s32[1]{0:T(128)} %bitcast.2.side, f32[4,2,128,256]{3,2,1,0:T(8,128)} %own.1, f32[4,2,64,256]{3,2,1,0:T(8,128)} %copy-done.3, ...), custom_call_target="tpu_custom_call" | custom-call | tf_op jit(solution)/shard_map/fields/pallas_call | solution.py:246
  56.6 3.2 %collective-permute-done.4 = f32[8,16,8,128]{3,2,1,0:T(8,128)} collective-permute-done((f32[8,16,8,128]{3,2,1,0:T(8,128)}, f32[8,16,8,128]{3,2,1,0:T(8,128)}, u32[]{:S(2)}, u32[]{:S(2)}) %collective-permute-start.4) | collective-permute-done | bytes 524320 | tf_op jit(solution)/shard_map/ppermute | solution.py:25
  59.9 1.9 %add_bitcast_fusion = (f32[16,8,128]{2,1,0:T(8,128)S(1)}, f32[16,8,128]{2,1,0:T(8,128)S(1)}, f32[16,8,128]{2,1,0:T(8,128)S(1)}, f32[16,8,128]{2,1,0:T(8,128)S(1)...) fusion(f32[8,16,8,128]{3,2,1,0:T(8,128)} %collective-permute-don, ...), kind=kLoop, calls=%fused_computation.27 | loop fusion | flops 131072 | bytes 1572896 | tf_op jit(solution)/shard_map/add | solution.py:395
  61.8 5.5 %collective-permute-start.10 = (f32[16,8,128]{2,1,0:T(8,128)S(1)}, f32[16,8,128]{2,1,0:T(8,128)S(1)}, u32[]{:S(2)}, u32[]{:S(2)}) collective-permute-start(f32[16,8,128]{2,1,0:T(8,128)S(1)} %get-tuple-element.51), channel_id=1, source_target_pairs={{0,12},{2,14},{4,8},{6,10},{8,4},{10,6},{12,0},{14,2},{1,13},{3,15... | collective-permute-start | bytes 196616 | tf_op jit(solution)/shard_map/ppermute | solution.py:25
  67.4 1.3 %collective-permute-start.5 = (f32[16,8,128]{2,1,0:T(8,128)S(1)}, f32[16,8,128]{2,1,0:T(8,128)S(1)}, u32[]{:S(2)}, u32[]{:S(2)}) collective-permute-start(f32[16,8,128]{2,1,0:T(8,128)S(1)} %get-tuple-element.56), channel_id=1, source_target_pairs={{0,2},{2,0},{4,6},{6,4},{8,10},{10,8},{12,14},{14,12},{1,3},{3,1},... | collective-permute-start | bytes 196616 | tf_op jit(solution)/shard_map/ppermute | solution.py:25
  68.8 2.1 %collective-permute-start.7 = (f32[16,8,128]{2,1,0:T(8,128)S(1)}, f32[16,8,128]{2,1,0:T(8,128)S(1)}, u32[]{:S(2)}, u32[]{:S(2)}) collective-permute-start(f32[16,8,128]{2,1,0:T(8,128)S(1)} %get-tuple-element.54), channel_id=1, source_target_pairs={{0,6},{2,4},{4,2},{6,0},{8,14},{10,12},{12,10},{14,8},{1,7},{3,5},... | collective-permute-start | bytes 196616 | tf_op jit(solution)/shard_map/ppermute | solution.py:25
  71.1 2.2 %collective-permute-start.8 = (f32[16,8,128]{2,1,0:T(8,128)S(1)}, f32[16,8,128]{2,1,0:T(8,128)S(1)}, u32[]{:S(2)}, u32[]{:S(2)}) collective-permute-start(f32[16,8,128]{2,1,0:T(8,128)S(1)} %get-tuple-element.53), channel_id=1, source_target_pairs={{0,8},{2,10},{4,12},{6,14},{8,0},{10,2},{12,4},{14,6},{1,9},{3,11}... | collective-permute-start | bytes 196616 | tf_op jit(solution)/shard_map/ppermute | solution.py:25
  73.3 1.2 %collective-permute-done.11.refs_8_ = f32[16,8,128]{2,1,0:T(8,128)S(1)} collective-permute-done((f32[16,8,128]{2,1,0:T(8,128)S(1)}, f32[16,8,128]{2,1,0:T(8,128)S(1)}, u32[]{:S(2)}, u32[]{:S(2)}) %collective-permute-start.11) | collective-permute-done | bytes 65568 | tf_op jit(solution)/shard_map/ppermute | solution.py:25
  74.5 1.0 collective-permute-start.9
  75.5 1.1 %maximum_add_fusion.2 = (f32[4,2,64,256]{3,2,1,0:T(8,128)}, f32[4,2,64,256]{3,2,1,0:T(8,128)}) fusion(f32[4,2,64,128]{3,2,1,0:T(8,128)S(1)} %get-tuple-element.48, f32[4,2,64,128]{3,2,1,0:T(8,128)S(1)} %get-tuple-element.46, f32[4,2,256,256]{3,2,1,0:T(8,128)S(1)} %copy-done.1, f32[4,2,64,128]{3,2,1,0:T(8,128)S(1)} %get-tuple-element.47, ...), kind=kLoop, calls=%fused_computation.7 | loop fusion | flops 524288 | bytes 3145728 | tf_op jit(solution)/shard_map/add | solution.py:459
  77.5 3.4 %collective-permute-done.9.refs_6_ = f32[16,8,128]{2,1,0:T(8,128)S(1)} collective-permute-done((f32[16,8,128]{2,1,0:T(8,128)S(1)}, f32[16,8,128]{2,1,0:T(8,128)S(1)}, u32[]{:S(2)}, u32[]{:S(2)}) %collective-permute-start.9) | collective-permute-done | bytes 65568 | tf_op jit(solution)/shard_map/ppermute | solution.py:25
  81.6 2.7 %collective-permute-start.12 = (f32[4,2,64,256]{3,2,1,0:T(8,128)}, f32[4,2,64,256]{3,2,1,0:T(8,128)}, u32[]{:S(2)}, u32[]{:S(2)}) collective-permute-start(f32[4,2,64,256]{3,2,1,0:T(8,128)} %get-tuple-element.29), channel_id=1, source_target_pairs={{0,2},{2,4},{4,6},{6,8},{8,10},{10,12},{12,14},{1,3},{3,5},{5,7},{... | collective-permute-start | bytes 1572872 | tf_op jit(solution)/shard_map/ppermute | solution.py:20
  84.3 1.3 %collective-permute-start.13 = (f32[4,2,64,256]{3,2,1,0:T(8,128)}, f32[4,2,64,256]{3,2,1,0:T(8,128)}, u32[]{:S(2)}, u32[]{:S(2)}) collective-permute-start(f32[4,2,64,256]{3,2,1,0:T(8,128)} %get-tuple-element.30), channel_id=1, source_target_pairs={{2,0},{4,2},{6,4},{8,6},{10,8},{12,10},{14,12},{3,1},{5,3},{7,5},{... | collective-permute-start | bytes 1572872 | tf_op jit(solution)/shard_map/ppermute | solution.py:20
  85.6 2.1 %gram.1 = (f32[32,32]{1,0:T(8,128)}, f32[16,8,128]{2,1,0:T(8,128)}) custom-call(f32[16,8,128]{2,1,0:T(8,128)} %bitcast.48, f32[16,8,128]{2,1,0:T(8,128)} %get-tuple-element.32.refs_1_, f32[16,8,128]{2,1,0:T(8,128)} %copy-done.9, f32[16,8,128]{2,1,0:T(8,128)} %copy-done.10, f32[16,8,128]{2,1,0:T(8,128)} %copy-done.11, f32[16,8,128]{2,1,0:T(8,128)} %copy-done.12, ...), custom_call_target="tpu_custom_call" | custom-call | tf_op jit(solution)/shard_map/gram/pallas_call | solution.py:290
  87.7 1.4 %collective-permute-done.14 = f32[32,32]{1,0:T(8,128)S(1)} collective-permute-done((f32[32,32]{1,0:T(8,128)}, f32[32,32]{1,0:T(8,128)S(1)}, u32[]{:S(2)}, u32[]{:S(2)}) %collective-permute-start.14) | collective-permute-done | bytes 4128 | tf_op jit(solution)/shard_map/ppermute | solution.py:25
  89.8 2.6 %collective-permute-start.15 = (f32[32,32]{1,0:T(8,128)S(1)}, f32[32,32]{1,0:T(8,128)S(1)}, u32[]{:S(2)}, u32[]{:S(2)}) collective-permute-start(f32[32,32]{1,0:T(8,128)S(1)} %add.163), channel_id=1, source_target_pairs={{0,4},{2,6},{4,0},{6,2},{8,12},{10,14},{12,8},{14,10},{1,5},{3,7},... | collective-permute-start | bytes 12296 | tf_op jit(solution)/shard_map/ppermute | solution.py:25
  92.4 3.1 %collective-permute-start.16 = (f32[32,32]{1,0:T(8,128)S(1)}, f32[32,32]{1,0:T(8,128)S(1)}, u32[]{:S(2)}, u32[]{:S(2)}) collective-permute-start(f32[32,32]{1,0:T(8,128)S(1)} %add.163), channel_id=1, source_target_pairs={{0,8},{2,10},{4,12},{6,14},{8,0},{10,2},{12,4},{14,6},{1,9},{3,11}... | collective-permute-start | bytes 12296 | tf_op jit(solution)/shard_map/ppermute | solution.py:25
  95.6 3.3 %collective-permute-done.15 = f32[32,32]{1,0:T(8,128)S(1)} collective-permute-done((f32[32,32]{1,0:T(8,128)S(1)}, f32[32,32]{1,0:T(8,128)S(1)}, u32[]{:S(2)}, u32[]{:S(2)}) %collective-permute-start.15) | collective-permute-done | bytes 4128 | tf_op jit(solution)/shard_map/ppermute | solution.py:25
  98.9 1.2 %collective-permute-done.16 = f32[32,32]{1,0:T(8,128)S(1)} collective-permute-done((f32[32,32]{1,0:T(8,128)S(1)}, f32[32,32]{1,0:T(8,128)S(1)}, u32[]{:S(2)}, u32[]{:S(2)}) %collective-permute-start.16) | collective-permute-done | bytes 4128 | tf_op jit(solution)/shard_map/ppermute | solution.py:25
  100.0 2.0 %collective-permute-done.17 = f32[32,32]{1,0:T(8,128)S(1)} collective-permute-done((f32[32,32]{1,0:T(8,128)S(1)}, f32[32,32]{1,0:T(8,128)S(1)}, u32[]{:S(2)}, u32[]{:S(2)}) %collective-permute-start.17) | collective-permute-done | bytes 4128 | tf_op jit(solution)/shard_map/ppermute | solution.py:25
  102.1 1.1 %slice_select_fusion.1 = (f32[4,2,128,128]{3,2,1,0:T(8,128)S(1)}, f32[4,2,128,128]{3,2,1,0:T(8,128)S(1)}) fusion(f32[4,2,256,128]{3,2,1,0:T(8,128)} %copy-done.5, pred[]{:T(512)S(6)} %eq.30), kind=kLoop, calls=%fused_computation.9 | loop fusion | flops 262144 | bytes 1572865 | tf_op jit(solution)/shard_map/jit(_where)/select_n | solution.py:456
  103.3 2.6 %collective-permute-done.18.refs_1_ = f32[32,32]{1,0:T(8,128)S(1)} collective-permute-done((f32[32,32]{1,0:T(8,128)S(1)}, f32[32,32]{1,0:T(8,128)S(1)}, u32[]{:S(2)}, u32[]{:S(2)}) %collective-permute-start.18) | collective-permute-done | bytes 4128 | tf_op jit(solution)/shard_map/ppermute | solution.py:25
  106.5 2.9 %ortho.1 = f32[8,2,1024]{2,1,0:T(2,128)} custom-call(f32[32,32]{1,0:T(8,128)} %copy-done.6, f32[32,32]{1,0:T(8,128)} %copy-done.14, f32[16,8,128]{2,1,0:T(8,128)} %bitcast.49, f32[16,8,128]{2,1,0:T(8,128)} %get-tuple-element.41.refs_3_), custom_call_target="tpu_custom_call" | custom-call | tf_op jit(solution)/shard_map/ortho/pallas_call | solution.py:365
  109.4 2.3 %fusion = f32[4,2,128,256]{3,2,1,0:T(8,128)} fusion(f32[4,2,128,128]{3,2,1,0:T(8,128)S(1)} %get-tuple-element.59, f32[4,2,128,128]{3,2,1,0:T(8,128)S(1)} %get-tuple-element.58, f32[4,2,64,256]{3,2,1,0:T(8,128)} %collective-permute-done.13, f32[4,2,64,256]{3,2,1,0:T(8,128)} %collective-permute-done.12, f32[4,2,256,256]{3,2,1,0:T(8,128)S(1)} %copy-done.1), kind=kLoop, calls=%fused_computation.5 | loop fusion | flops 1048576 | bytes 4194304 | tf_op jit(solution)/shard_map/add | solution.py:423
  (76 shorter events, 9.8 us)
Async XLA Ops:
  0.6 8.5 %copy-start.15 = (f32[2,63]{1,0:T(2,128)S(1)}, f32[2,63]{1,0:T(2,128)}, u32[]{:S(2)}) copy-start(f32[2,63]{1,0:T(2,128)} %param.9) | copy-start | bytes 1516
  2.9 27.6 %collective-permute-start = (f32[4,2,64,256]{3,2,1,0:T(8,128)}, f32[4,2,64,256]{3,2,1,0:T(8,128)S(1)}, u32[]{:S(2)}, u32[]{:S(2)}) collective-permute-start(f32[4,2,64,256]{3,2,1,0:T(8,128)} %get-tuple-element.61), channel_id=1, source_target_pairs={{0,2},{2,4},{4,6},{6,8},{8,10},{10,12},{12,14},{1,3},{3,5},{5,7},{... | collective-permute-start | bytes 1572872 | tf_op jit(solution)/shard_map/ppermute | solution.py:20
  7.8 22.7 %collective-permute-start.1 = (f32[4,2,64,256]{3,2,1,0:T(8,128)}, f32[4,2,64,256]{3,2,1,0:T(8,128)S(1)}, u32[]{:S(2)}, u32[]{:S(2)}) collective-permute-start(f32[4,2,64,256]{3,2,1,0:T(8,128)} %get-tuple-element.60), channel_id=1, source_target_pairs={{2,0},{4,2},{6,4},{8,6},{10,8},{12,10},{14,12},{3,1},{5,3},{7,5},{... | collective-permute-start | bytes 1572872 | tf_op jit(solution)/shard_map/ppermute | solution.py:20
  10.0 7.2 %copy-start = (f32[4,2,128,256]{3,2,1,0:T(8,128)S(1)}, f32[4,2,128,256]{3,2,1,0:T(8,128)}, u32[]{:S(2)}) copy-start(f32[4,2,128,256]{3,2,1,0:T(8,128)} %own.1) | copy-start | bytes 3145732
  17.2 13.4 %copy-start.2 = (bf16[8,256,256]{2,1,0:T(8,128)(2,1)}, bf16[8,256,256]{2,1,0:T(8,128)(2,1)S(1)}, u32[]{:S(2)}) copy-start(bf16[8,256,256]{2,1,0:T(8,128)(2,1)S(1)} %constant_dynamic-update-slice_fusion.tab) | copy-start | bytes 3145732
  17.3 13.6 %copy-start.16 = (s32[2,2]{1,0:T(2,128)S(1)}, s32[2,2]{1,0:T(2,128)}, u32[]{:S(2)}) copy-start(s32[2,2]{1,0:T(2,128)} %param.11) | copy-start | bytes 52
  30.6 2.9 %collective-permute-start.2 = (f32[4,2,256,128]{3,2,1,0:T(8,128)S(1)}, f32[4,2,256,128]{3,2,1,0:T(8,128)}, u32[]{:S(2)}, u32[]{:S(2)}) collective-permute-start(f32[4,2,256,128]{3,2,1,0:T(8,128)S(1)} %pad_maximum_fusion), channel_id=1, source_target_pairs={{0,1},{1,0},{2,3},{3,2},{4,5},{5,4},{6,7},{7,6},{8,9},{9,8},{10,11... | collective-permute-start | bytes 3145736 | tf_op jit(solution)/shard_map/ppermute | solution.py:25
  56.1 19.4 %copy-start.1 = (f32[4,2,256,256]{3,2,1,0:T(8,128)S(1)}, f32[4,2,256,256]{3,2,1,0:T(8,128)}, u32[]{:S(2)}) copy-start(f32[4,2,256,256]{3,2,1,0:T(8,128)} %get-tuple-element.25) | copy-start | bytes 6291460
  56.1 12.7 %collective-permute-start.3 = (f32[4,2,256,128]{3,2,1,0:T(8,128)}, f32[4,2,256,128]{3,2,1,0:T(8,128)S(1)}, u32[]{:S(2)}, u32[]{:S(2)}) collective-permute-start(f32[4,2,256,128]{3,2,1,0:T(8,128)} %get-tuple-element.26), channel_id=1, source_target_pairs={{0,1},{1,0},{2,3},{3,2},{4,5},{5,4},{6,7},{7,6},{8,9},{9,8},{10,11... | collective-permute-start | bytes 3145736 | tf_op jit(solution)/shard_map/ppermute | solution.py:25
  56.3 3.6 %collective-permute-start.4 = (f32[8,16,8,128]{3,2,1,0:T(8,128)}, f32[8,16,8,128]{3,2,1,0:T(8,128)}, u32[]{:S(2)}, u32[]{:S(2)}) collective-permute-start(f32[8,16,8,128]{3,2,1,0:T(8,128)} %get-tuple-element.28), channel_id=1, source_target_pairs={{0,1},{1,0},{2,3},{3,2},{4,5},{5,4},{6,7},{7,6},{8,9},{9,8},{10,11... | collective-permute-start | bytes 1572872 | tf_op jit(solution)/shard_map/ppermute | solution.py:25
  61.8 9.3 %collective-permute-start.10 = (f32[16,8,128]{2,1,0:T(8,128)S(1)}, f32[16,8,128]{2,1,0:T(8,128)S(1)}, u32[]{:S(2)}, u32[]{:S(2)}) collective-permute-start(f32[16,8,128]{2,1,0:T(8,128)S(1)} %get-tuple-element.51), channel_id=1, source_target_pairs={{0,12},{2,14},{4,8},{6,10},{8,4},{10,6},{12,0},{14,2},{1,13},{3,15... | collective-permute-start | bytes 196616 | tf_op jit(solution)/shard_map/ppermute | solution.py:25
  67.2 7.3 %collective-permute-start.11 = (f32[16,8,128]{2,1,0:T(8,128)S(1)}, f32[16,8,128]{2,1,0:T(8,128)S(1)}, u32[]{:S(2)}, u32[]{:S(2)}) collective-permute-start(f32[16,8,128]{2,1,0:T(8,128)S(1)} %get-tuple-element.50), channel_id=1, source_target_pairs={{0,14},{2,12},{4,10},{6,8},{8,6},{10,4},{12,2},{14,0},{1,15},{3,13... | collective-permute-start | bytes 196616 | tf_op jit(solution)/shard_map/ppermute | solution.py:25
  67.4 9.2 %collective-permute-start.5 = (f32[16,8,128]{2,1,0:T(8,128)S(1)}, f32[16,8,128]{2,1,0:T(8,128)S(1)}, u32[]{:S(2)}, u32[]{:S(2)}) collective-permute-start(f32[16,8,128]{2,1,0:T(8,128)S(1)} %get-tuple-element.56), channel_id=1, source_target_pairs={{0,2},{2,0},{4,6},{6,4},{8,10},{10,8},{12,14},{14,12},{1,3},{3,1},... | collective-permute-start | bytes 196616 | tf_op jit(solution)/shard_map/ppermute | solution.py:25
  68.8 7.9 %collective-permute-start.6 = (f32[16,8,128]{2,1,0:T(8,128)S(1)}, f32[16,8,128]{2,1,0:T(8,128)S(1)}, u32[]{:S(2)}, u32[]{:S(2)}) collective-permute-start(f32[16,8,128]{2,1,0:T(8,128)S(1)} %get-tuple-element.55), channel_id=1, source_target_pairs={{0,4},{2,6},{4,0},{6,2},{8,12},{10,14},{12,8},{14,10},{1,5},{3,7},... | collective-permute-start | bytes 196616 | tf_op jit(solution)/shard_map/ppermute | solution.py:25
  68.8 7.9 %copy-start.5 = (f32[4,2,256,128]{3,2,1,0:T(8,128)}, f32[4,2,256,128]{3,2,1,0:T(8,128)S(1)}, u32[]{:S(2)}) copy-start(f32[4,2,256,128]{3,2,1,0:T(8,128)S(1)} %collective-permute-done.3) | copy-start | bytes 3145732
  68.8 7.9 %collective-permute-start.7 = (f32[16,8,128]{2,1,0:T(8,128)S(1)}, f32[16,8,128]{2,1,0:T(8,128)S(1)}, u32[]{:S(2)}, u32[]{:S(2)}) collective-permute-start(f32[16,8,128]{2,1,0:T(8,128)S(1)} %get-tuple-element.54), channel_id=1, source_target_pairs={{0,6},{2,4},{4,2},{6,0},{8,14},{10,12},{12,10},{14,8},{1,7},{3,5},... | collective-permute-start | bytes 196616 | tf_op jit(solution)/shard_map/ppermute | solution.py:25
  71.0 14.5 %copy-start.7 = (f32[16,8,128]{2,1,0:T(8,128)}, f32[16,8,128]{2,1,0:T(8,128)S(1)}, u32[]{:S(2)}) copy-start(f32[16,8,128]{2,1,0:T(8,128)S(1)} %collective-permute-done.10.refs_7_) | copy-start | bytes 196612
  71.1 6.5 %collective-permute-start.8 = (f32[16,8,128]{2,1,0:T(8,128)S(1)}, f32[16,8,128]{2,1,0:T(8,128)S(1)}, u32[]{:S(2)}, u32[]{:S(2)}) collective-permute-start(f32[16,8,128]{2,1,0:T(8,128)S(1)} %get-tuple-element.53), channel_id=1, source_target_pairs={{0,8},{2,10},{4,12},{6,14},{8,0},{10,2},{12,4},{14,6},{1,9},{3,11}... | collective-permute-start | bytes 196616 | tf_op jit(solution)/shard_map/ppermute | solution.py:25
  74.5 11.0 %copy-start.8 = (f32[16,8,128]{2,1,0:T(8,128)}, f32[16,8,128]{2,1,0:T(8,128)S(1)}, u32[]{:S(2)}) copy-start(f32[16,8,128]{2,1,0:T(8,128)S(1)} %collective-permute-done.11.refs_8_) | copy-start | bytes 196612
  74.5 6.4 %collective-permute-start.9 = (f32[16,8,128]{2,1,0:T(8,128)S(1)}, f32[16,8,128]{2,1,0:T(8,128)S(1)}, u32[]{:S(2)}, u32[]{:S(2)}) collective-permute-start(f32[16,8,128]{2,1,0:T(8,128)S(1)} %get-tuple-element.52), channel_id=1, source_target_pairs={{0,10},{2,8},{4,14},{6,12},{8,2},{10,0},{12,6},{14,4},{1,11},{3,9}... | collective-permute-start | bytes 196616 | tf_op jit(solution)/shard_map/ppermute | solution.py:25
  76.6 8.9 %copy-start.9 = (f32[16,8,128]{2,1,0:T(8,128)}, f32[16,8,128]{2,1,0:T(8,128)S(1)}, u32[]{:S(2)}) copy-start(f32[16,8,128]{2,1,0:T(8,128)S(1)} %collective-permute-done.5.refs_2_) | copy-start | bytes 196612
  76.6 8.9 %copy-start.10 = (f32[16,8,128]{2,1,0:T(8,128)}, f32[16,8,128]{2,1,0:T(8,128)S(1)}, u32[]{:S(2)}) copy-start(f32[16,8,128]{2,1,0:T(8,128)S(1)} %collective-permute-done.6.refs_3_) | copy-start | bytes 196612
  76.7 8.9 %copy-start.11 = (f32[16,8,128]{2,1,0:T(8,128)}, f32[16,8,128]{2,1,0:T(8,128)S(1)}, u32[]{:S(2)}) copy-start(f32[16,8,128]{2,1,0:T(8,128)S(1)} %collective-permute-done.7.refs_4_) | copy-start | bytes 196612
  77.5 8.1 %copy-start.12 = (f32[16,8,128]{2,1,0:T(8,128)}, f32[16,8,128]{2,1,0:T(8,128)S(1)}, u32[]{:S(2)}) copy-start(f32[16,8,128]{2,1,0:T(8,128)S(1)} %collective-permute-done.8.refs_5_) | copy-start | bytes 196612
  81.6 27.8 %collective-permute-start.12 = (f32[4,2,64,256]{3,2,1,0:T(8,128)}, f32[4,2,64,256]{3,2,1,0:T(8,128)}, u32[]{:S(2)}, u32[]{:S(2)}) collective-permute-start(f32[4,2,64,256]{3,2,1,0:T(8,128)} %get-tuple-element.29), channel_id=1, source_target_pairs={{0,2},{2,4},{4,6},{6,8},{8,10},{10,12},{12,14},{1,3},{3,5},{5,7},{... | collective-permute-start | bytes 1572872 | tf_op jit(solution)/shard_map/ppermute | solution.py:20
  84.3 25.1 %collective-permute-start.13 = (f32[4,2,64,256]{3,2,1,0:T(8,128)}, f32[4,2,64,256]{3,2,1,0:T(8,128)}, u32[]{:S(2)}, u32[]{:S(2)}) collective-permute-start(f32[4,2,64,256]{3,2,1,0:T(8,128)} %get-tuple-element.30), channel_id=1, source_target_pairs={{2,0},{4,2},{6,4},{8,6},{10,8},{12,10},{14,12},{3,1},{5,3},{7,5},{... | collective-permute-start | bytes 1572872 | tf_op jit(solution)/shard_map/ppermute | solution.py:20
  87.7 1.4 %collective-permute-start.14 = (f32[32,32]{1,0:T(8,128)}, f32[32,32]{1,0:T(8,128)S(1)}, u32[]{:S(2)}, u32[]{:S(2)}) collective-permute-start(f32[32,32]{1,0:T(8,128)} %get-tuple-element.40), channel_id=1, source_target_pairs={{0,1},{1,0},{2,3},{3,2},{4,5},{5,4},{6,7},{7,6},{8,9},{9,8},{10,11... | collective-permute-start | bytes 12296 | tf_op jit(solution)/shard_map/ppermute | solution.py:25
  89.8 9.1 %collective-permute-start.15 = (f32[32,32]{1,0:T(8,128)S(1)}, f32[32,32]{1,0:T(8,128)S(1)}, u32[]{:S(2)}, u32[]{:S(2)}) collective-permute-start(f32[32,32]{1,0:T(8,128)S(1)} %add.163), channel_id=1, source_target_pairs={{0,4},{2,6},{4,0},{6,2},{8,12},{10,14},{12,8},{14,10},{1,5},{3,7},... | collective-permute-start | bytes 12296 | tf_op jit(solution)/shard_map/ppermute | solution.py:25
  92.4 7.6 %collective-permute-start.16 = (f32[32,32]{1,0:T(8,128)S(1)}, f32[32,32]{1,0:T(8,128)S(1)}, u32[]{:S(2)}, u32[]{:S(2)}) collective-permute-start(f32[32,32]{1,0:T(8,128)S(1)} %add.163), channel_id=1, source_target_pairs={{0,8},{2,10},{4,12},{6,14},{8,0},{10,2},{12,4},{14,6},{1,9},{3,11}... | collective-permute-start | bytes 12296 | tf_op jit(solution)/shard_map/ppermute | solution.py:25
  95.5 6.5 %collective-permute-start.17 = (f32[32,32]{1,0:T(8,128)S(1)}, f32[32,32]{1,0:T(8,128)S(1)}, u32[]{:S(2)}, u32[]{:S(2)}) collective-permute-start(f32[32,32]{1,0:T(8,128)S(1)} %add.163), channel_id=1, source_target_pairs={{0,12},{2,14},{4,8},{6,10},{8,4},{10,6},{12,0},{14,2},{1,13},{3,15... | collective-permute-start | bytes 12296 | tf_op jit(solution)/shard_map/ppermute | solution.py:25
  102.0 3.8 %copy-start.6 = (f32[32,32]{1,0:T(8,128)}, f32[32,32]{1,0:T(8,128)S(1)}, u32[]{:S(2)}) copy-start(f32[32,32]{1,0:T(8,128)S(1)} %add_add_fusion.refs_0_) | copy-start | bytes 12292
  102.0 3.8 %collective-permute-start.18 = (f32[32,32]{1,0:T(8,128)S(1)}, f32[32,32]{1,0:T(8,128)S(1)}, u32[]{:S(2)}, u32[]{:S(2)}) collective-permute-start(f32[32,32]{1,0:T(8,128)S(1)} %add_add_fusion.refs_0_), channel_id=1, source_target_pairs={{0,2},{2,0},{4,6},{6,4},{8,10},{10,8},{12,14},{14,12},{1,3},{3,1},... | collective-permute-start | bytes 12296 | tf_op jit(solution)/shard_map/ppermute | solution.py:25
  (4 other events, 7.2 us)

commit v10 on v9

--- a/solution.py
+++ b/solution.py
@@ -406,7 +406,9 @@
             grad = take(grad, mine, 0) + swapped(take(grad, 1 - mine, 0), "row", bit)
         parts = [grad.reshape(2 * modes, share, width)]
 
-    parts, bottom, top = lax.optimization_barrier((parts, bottom, top))
+    late = parts[4:6]
+    early, bottom, top = lax.optimization_barrier((parts[:4] + parts[6:], bottom, top))
+    parts = early + late
     from_above = shifted(bottom, "row", 1)
     from_below = shifted(top, "row", -1)
     total, own_grad = gram(own_probe, parts)

time: 113 us -> 109 us (0.965)
  waiting for transfers between devices: 34.5 us -> 28.9 us
  starting transfers between devices: 28.8 us -> 31.5 us
    ppermute x15, waiting for transfers between devices: 21.3 us -> 15.8 us  [swapped(): return lax.ppermute(value, axis, [(i, i ^ bit) for i in range(count)])]
    ppermute x15, starting transfers between devices: 18.7 us -> 21.8 us  [swapped(): return lax.ppermute(value, axis, [(i, i ^ bit) for i in range(count)])]
    unnamed x39 -> x37, local copies, waits for them, and re-layouts: 4.06 us -> 3.44 us
  transfers between devices with their start and end apart: 19 -> 19, of which waited for: 11 -> 10; matrix products, arithmetic and copies ran while one was open for 12% -> 13% of each run, Pallas kernels for 4% -> 5%
where the time goes in v10:
time: 109 us; the launch traced here: 108 us
  starting transfers between devices  31.5 us (29%)
  waiting for transfers between devices  28.9 us (27%)
  Pallas kernels  27.6 us (25%)
  other arithmetic  9.63 us (9%)
  local copies, waits for them, and re-layouts  9.5 us (9%)
    pallas_call x1, Pallas kernels, fields(): pl.pallas_call(field_kernel, out_shape=[jax.ShapeDtypeStruct(s, F32) for...  22.6 us
    ppermute x15, starting transfers between devices, swapped(): return lax.ppermute(value, axis, [(i, i ^ bit) for i in range(count)])  21.8 us
    ppermute x15, waiting for transfers between devices, swapped(): return lax.ppermute(value, axis, [(i, i ^ bit) for i in range(count)])  15.8 us
    ppermute x4, waiting for transfers between devices, shifted(): return lax.ppermute(value, axis, pairs)  13.2 us
    ppermute x4, starting transfers between devices, shifted(): return lax.ppermute(value, axis, pairs)  9.72 us
    unnamed x37, local copies, waits for them, and re-layouts  3.44 us
    pallas_call x1, Pallas kernels, ortho(): pl.pallas_call(body, out_shape=jax.ShapeDtypeStruct((modes, 2, pixels), F...  2.92 us
    add x1, other arithmetic, updates(): object_grad = middle() + jnp.concatenate([from_above, from_below], axis=2)  2.34 us
  transfers between devices with their start and end apart: 19, of which 10 were waited for; matrix products, arithmetic and copies ran while one was open for 13% of the time, Pallas kernels for 5%

profile of v10, /device:TPU:0, one launch (start us, length us, event | category | flops | bytes accessed | tf_op | source)
XLA Modules:
  0.0 108.2 jit_solution(3168981132911188157)
XLA Ops:
  0.6 2.3 %fusion.5 = (f32[4,2,64,256]{3,2,1,0:T(8,128)}, f32[4,2,64,256]{3,2,1,0:T(8,128)}) fusion(f32[4,2,128,256]{3,2,1,0:T(8,128)} %own.1), kind=kLoop, calls=%fused_computation.51 | loop fusion | bytes 2097152 | tf_op jit(solution)/shard_map/slice | solution.py:437
  2.9 4.9 %collective-permute-start = (f32[4,2,64,256]{3,2,1,0:T(8,128)}, f32[4,2,64,256]{3,2,1,0:T(8,128)S(1)}, u32[]{:S(2)}, u32[]{:S(2)}) collective-permute-start(f32[4,2,64,256]{3,2,1,0:T(8,128)} %get-tuple-element.57), channel_id=1, source_target_pairs={{0,2},{2,4},{4,6},{6,8},{8,10},{10,12},{12,14},{1,3},{3,5},{5,7},{... | collective-permute-start | bytes 1572872 | tf_op jit(solution)/shard_map/ppermute | solution.py:20
  7.8 1.3 %collective-permute-start.1 = (f32[4,2,64,256]{3,2,1,0:T(8,128)}, f32[4,2,64,256]{3,2,1,0:T(8,128)S(1)}, u32[]{:S(2)}, u32[]{:S(2)}) collective-permute-start(f32[4,2,64,256]{3,2,1,0:T(8,128)} %get-tuple-element.56), channel_id=1, source_target_pairs={{2,0},{4,2},{6,4},{8,6},{10,8},{12,10},{14,12},{3,1},{5,3},{7,5},{... | collective-permute-start | bytes 1572872 | tf_op jit(solution)/shard_map/ppermute | solution.py:20
  11.0 1.0 copy.17
  12.1 0.9 constant_dynamic-update-slice_fusion.3
  14.5 0.9 constant_dynamic-update-slice_fusion.2
  15.4 0.9 constant_dynamic-update-slice_fusion.1
  16.3 0.9 constant_dynamic-update-slice_fusion.tab
  17.3 13.2 %collective-permute-done.above = f32[4,2,64,256]{3,2,1,0:T(8,128)S(1)} collective-permute-done((f32[4,2,64,256]{3,2,1,0:T(8,128)}, f32[4,2,64,256]{3,2,1,0:T(8,128)S(1)}, u32[]{:S(2)}, u32[]{:S(2)}) %collective-permute-start) | collective-permute-done | bytes 524320 | tf_op jit(solution)/shard_map/ppermute | solution.py:20
  31.4 2.1 %collective-permute-done.2.beside = f32[4,2,256,128]{3,2,1,0:T(8,128)} collective-permute-done((f32[4,2,256,128]{3,2,1,0:T(8,128)S(1)}, f32[4,2,256,128]{3,2,1,0:T(8,128)}, u32[]{:S(2)}, u32[]{:S(2)}) %collective-permute-start.2) | collective-permute-done | bytes 1048608 | tf_op jit(solution)/shard_map/ppermute | solution.py:25
  33.5 22.6 %fields.1 = (f32[4,2,256,256]{3,2,1,0:T(8,128)}, f32[4,2,256,128]{3,2,1,0:T(8,128)}, f32[8,16,8,128]{3,2,1,0:T(8,128)}, f32[8,16,8,128]{3,2,1,0:T(8,128)}) custom-call(s32[2,2]{1,0:T(2,128)} %broadcast_subtract_fusion.places, s32[1]{0:T(128)} %bitcast.2.side, f32[4,2,128,256]{3,2,1,0:T(8,128)} %own.1, f32[4,2,64,256]{3,2,1,0:T(8,128)} %copy-done.3, ...), custom_call_target="tpu_custom_call" | custom-call | tf_op jit(solution)/shard_map/fields/pallas_call | solution.py:246
  56.6 3.2 %collective-permute-done.4 = f32[8,16,8,128]{3,2,1,0:T(8,128)} collective-permute-done((f32[8,16,8,128]{3,2,1,0:T(8,128)}, f32[8,16,8,128]{3,2,1,0:T(8,128)}, u32[]{:S(2)}, u32[]{:S(2)}) %collective-permute-start.4) | collective-permute-done | bytes 524320 | tf_op jit(solution)/shard_map/ppermute | solution.py:25
  59.8 1.9 %add_bitcast_fusion = (f32[16,8,128]{2,1,0:T(8,128)S(1)}, f32[16,8,128]{2,1,0:T(8,128)S(1)}, f32[16,8,128]{2,1,0:T(8,128)S(1)}, f32[16,8,128]{2,1,0:T(8,128)S(1)...) fusion(f32[8,16,8,128]{3,2,1,0:T(8,128)} %collective-permute-don, ...), kind=kLoop, calls=%fused_computation.27 | loop fusion | flops 131072 | bytes 1572896 | tf_op jit(solution)/shard_map/add | solution.py:395
  61.8 2.4 %collective-permute-start.5 = (f32[16,8,128]{2,1,0:T(8,128)S(1)}, f32[16,8,128]{2,1,0:T(8,128)S(1)}, u32[]{:S(2)}, u32[]{:S(2)}) collective-permute-start(f32[16,8,128]{2,1,0:T(8,128)S(1)} %get-tuple-element.48), channel_id=1, source_target_pairs={{0,2},{2,0},{4,6},{6,4},{8,10},{10,8},{12,14},{14,12},{1,3},{3,1},... | collective-permute-start | bytes 196616 | tf_op jit(solution)/shard_map/ppermute | solution.py:25
  64.2 1.5 %collective-permute-start.6 = (f32[16,8,128]{2,1,0:T(8,128)S(1)}, f32[16,8,128]{2,1,0:T(8,128)S(1)}, u32[]{:S(2)}, u32[]{:S(2)}) collective-permute-start(f32[16,8,128]{2,1,0:T(8,128)S(1)} %get-tuple-element.47), channel_id=1, source_target_pairs={{0,4},{2,6},{4,0},{6,2},{8,12},{10,14},{12,8},{14,10},{1,5},{3,7},... | collective-permute-start | bytes 196616 | tf_op jit(solution)/shard_map/ppermute | solution.py:25
  66.6 4.0 %collective-permute-start.8 = (f32[16,8,128]{2,1,0:T(8,128)S(1)}, f32[16,8,128]{2,1,0:T(8,128)S(1)}, u32[]{:S(2)}, u32[]{:S(2)}) collective-permute-start(f32[16,8,128]{2,1,0:T(8,128)S(1)} %get-tuple-element.45), channel_id=1, source_target_pairs={{0,12},{2,14},{4,8},{6,10},{8,4},{10,6},{12,0},{14,2},{1,13},{3,15... | collective-permute-start | bytes 196616 | tf_op jit(solution)/shard_map/ppermute | solution.py:25
  71.9 2.8 %collective-permute-start.13 = (f32[16,8,128]{2,1,0:T(8,128)S(1)}, f32[16,8,128]{2,1,0:T(8,128)}, u32[]{:S(2)}, u32[]{:S(2)}) collective-permute-start(f32[16,8,128]{2,1,0:T(8,128)S(1)} %get-tuple-element.42), channel_id=1, source_target_pairs={{0,10},{2,8},{4,14},{6,12},{8,2},{10,0},{12,6},{14,4},{1,11},{3,9}... | collective-permute-start | bytes 196616 | tf_op jit(solution)/shard_map/ppermute | solution.py:25
  74.8 1.1 %maximum_add_fusion.2 = (f32[4,2,64,256]{3,2,1,0:T(8,128)}, f32[4,2,64,256]{3,2,1,0:T(8,128)}) fusion(f32[4,2,64,128]{3,2,1,0:T(8,128)S(1)} %get-tuple-element.52, f32[4,2,64,128]{3,2,1,0:T(8,128)S(1)} %get-tuple-element.50, f32[4,2,256,256]{3,2,1,0:T(8,128)S(1)} %copy-done.1, f32[4,2,64,128]{3,2,1,0:T(8,128)S(1)} %get-tuple-element.51, ...), kind=kLoop, calls=%fused_computation.7 | loop fusion | flops 524288 | bytes 3145728 | tf_op jit(solution)/shard_map/add | solution.py:461
  75.9 2.2 %collective-permute-done.9.refs_6_ = f32[16,8,128]{2,1,0:T(8,128)S(1)} collective-permute-done((f32[16,8,128]{2,1,0:T(8,128)S(1)}, f32[16,8,128]{2,1,0:T(8,128)S(1)}, u32[]{:S(2)}, u32[]{:S(2)}) %collective-permute-start.9) | collective-permute-done | bytes 65568 | tf_op jit(solution)/shard_map/ppermute | solution.py:25
  78.1 2.3 %collective-permute-start.10 = (f32[4,2,64,256]{3,2,1,0:T(8,128)}, f32[4,2,64,256]{3,2,1,0:T(8,128)}, u32[]{:S(2)}, u32[]{:S(2)}) collective-permute-start(f32[4,2,64,256]{3,2,1,0:T(8,128)} %get-tuple-element.27), channel_id=1, source_target_pairs={{0,2},{2,4},{4,6},{6,8},{8,10},{10,12},{12,14},{1,3},{3,5},{5,7},{... | collective-permute-start | bytes 1572872 | tf_op jit(solution)/shard_map/ppermute | solution.py:20
  80.4 1.3 %collective-permute-start.11 = (f32[4,2,64,256]{3,2,1,0:T(8,128)}, f32[4,2,64,256]{3,2,1,0:T(8,128)}, u32[]{:S(2)}, u32[]{:S(2)}) collective-permute-start(f32[4,2,64,256]{3,2,1,0:T(8,128)} %get-tuple-element.28), channel_id=1, source_target_pairs={{2,0},{4,2},{6,4},{8,6},{10,8},{12,10},{14,12},{3,1},{5,3},{7,5},{... | collective-permute-start | bytes 1572872 | tf_op jit(solution)/shard_map/ppermute | solution.py:20
  82.3 2.1 %gram.1 = (f32[32,32]{1,0:T(8,128)}, f32[16,8,128]{2,1,0:T(8,128)}) custom-call(f32[16,8,128]{2,1,0:T(8,128)} %bitcast.48, f32[16,8,128]{2,1,0:T(8,128)} %get-tuple-element.30.refs_1_, f32[16,8,128]{2,1,0:T(8,128)} %copy-done.7, f32[16,8,128]{2,1,0:T(8,128)} %copy-done.8, f32[16,8,128]{2,1,0:T(8,128)} %copy-done.9, f32[16,8,128]{2,1,0:T(8,128)} %copy-done.10, ...), custom_call_target="tpu_custom_call" | custom-call | tf_op jit(solution)/shard_map/gram/pallas_call | solution.py:290
  84.4 1.4 %collective-permute-done.14 = f32[32,32]{1,0:T(8,128)S(1)} collective-permute-done((f32[32,32]{1,0:T(8,128)}, f32[32,32]{1,0:T(8,128)S(1)}, u32[]{:S(2)}, u32[]{:S(2)}) %collective-permute-start.14) | collective-permute-done | bytes 4128 | tf_op jit(solution)/shard_map/ppermute | solution.py:25
  86.5 4.7 %collective-permute-start.15 = (f32[32,32]{1,0:T(8,128)S(1)}, f32[32,32]{1,0:T(8,128)S(1)}, u32[]{:S(2)}, u32[]{:S(2)}) collective-permute-start(f32[32,32]{1,0:T(8,128)S(1)} %add.163), channel_id=1, source_target_pairs={{0,4},{2,6},{4,0},{6,2},{8,12},{10,14},{12,8},{14,10},{1,5},{3,7},... | collective-permute-start | bytes 12296 | tf_op jit(solution)/shard_map/ppermute | solution.py:25
  91.3 1.7 %collective-permute-start.16 = (f32[32,32]{1,0:T(8,128)S(1)}, f32[32,32]{1,0:T(8,128)S(1)}, u32[]{:S(2)}, u32[]{:S(2)}) collective-permute-start(f32[32,32]{1,0:T(8,128)S(1)} %add.163), channel_id=1, source_target_pairs={{0,8},{2,10},{4,12},{6,14},{8,0},{10,2},{12,4},{14,6},{1,9},{3,11}... | collective-permute-start | bytes 12296 | tf_op jit(solution)/shard_map/ppermute | solution.py:25
  93.0 1.3 %collective-permute-start.17 = (f32[32,32]{1,0:T(8,128)S(1)}, f32[32,32]{1,0:T(8,128)S(1)}, u32[]{:S(2)}, u32[]{:S(2)}) collective-permute-start(f32[32,32]{1,0:T(8,128)S(1)} %add.163), channel_id=1, source_target_pairs={{0,12},{2,14},{4,8},{6,10},{8,4},{10,6},{12,0},{14,2},{1,13},{3,15... | collective-permute-start | bytes 12296 | tf_op jit(solution)/shard_map/ppermute | solution.py:25
  94.8 1.2 %collective-permute-done.16 = f32[32,32]{1,0:T(8,128)S(1)} collective-permute-done((f32[32,32]{1,0:T(8,128)S(1)}, f32[32,32]{1,0:T(8,128)S(1)}, u32[]{:S(2)}, u32[]{:S(2)}) %collective-permute-start.16) | collective-permute-done | bytes 4128 | tf_op jit(solution)/shard_map/ppermute | solution.py:25
  96.0 2.5 %collective-permute-done.17 = f32[32,32]{1,0:T(8,128)S(1)} collective-permute-done((f32[32,32]{1,0:T(8,128)S(1)}, f32[32,32]{1,0:T(8,128)S(1)}, u32[]{:S(2)}, u32[]{:S(2)}) %collective-permute-start.17) | collective-permute-done | bytes 4128 | tf_op jit(solution)/shard_map/ppermute | solution.py:25
  99.1 1.1 %slice_select_fusion.1 = (f32[4,2,128,128]{3,2,1,0:T(8,128)S(1)}, f32[4,2,128,128]{3,2,1,0:T(8,128)S(1)}) fusion(f32[4,2,256,128]{3,2,1,0:T(8,128)} %copy-done.5, pred[]{:T(512)S(6)} %eq.30), kind=kLoop, calls=%fused_computation.9 | loop fusion | flops 262144 | bytes 1572865 | tf_op jit(solution)/shard_map/jit(_where)/select_n | solution.py:458
  100.3 2.0 %collective-permute-done.18.refs_1_ = f32[32,32]{1,0:T(8,128)S(1)} collective-permute-done((f32[32,32]{1,0:T(8,128)S(1)}, f32[32,32]{1,0:T(8,128)S(1)}, u32[]{:S(2)}, u32[]{:S(2)}) %collective-permute-start.18) | collective-permute-done | bytes 4128 | tf_op jit(solution)/shard_map/ppermute | solution.py:25
  102.9 2.9 %ortho.1 = f32[8,2,1024]{2,1,0:T(2,128)} custom-call(f32[32,32]{1,0:T(8,128)} %copy-done.6, f32[32,32]{1,0:T(8,128)} %copy-done.13, f32[16,8,128]{2,1,0:T(8,128)} %bitcast.49, f32[16,8,128]{2,1,0:T(8,128)} %get-tuple-element.37.refs_3_), custom_call_target="tpu_custom_call" | custom-call | tf_op jit(solution)/shard_map/ortho/pallas_call | solution.py:365
  105.8 2.3 %fusion = f32[4,2,128,256]{3,2,1,0:T(8,128)} fusion(f32[4,2,128,128]{3,2,1,0:T(8,128)S(1)} %get-tuple-element.55, f32[4,2,128,128]{3,2,1,0:T(8,128)S(1)} %get-tuple-element.54, f32[4,2,64,256]{3,2,1,0:T(8,128)} %collective-permute-done.11, f32[4,2,64,256]{3,2,1,0:T(8,128)} %collective-permute-done.10, f32[4,2,256,256]{3,2,1,0:T(8,128)S(1)} %copy-done.1), kind=kLoop, calls=%fused_computation.5 | loop fusion | flops 1048576 | bytes 4194304 | tf_op jit(solution)/shard_map/add | solution.py:425
  (74 shorter events, 9.9 us)
Async XLA Ops:
  0.6 8.5 %copy-start.14 = (f32[2,63]{1,0:T(2,128)S(1)}, f32[2,63]{1,0:T(2,128)}, u32[]{:S(2)}) copy-start(f32[2,63]{1,0:T(2,128)} %param.9) | copy-start | bytes 1516
  2.9 27.6 %collective-permute-start = (f32[4,2,64,256]{3,2,1,0:T(8,128)}, f32[4,2,64,256]{3,2,1,0:T(8,128)S(1)}, u32[]{:S(2)}, u32[]{:S(2)}) collective-permute-start(f32[4,2,64,256]{3,2,1,0:T(8,128)} %get-tuple-element.57), channel_id=1, source_target_pairs={{0,2},{2,4},{4,6},{6,8},{8,10},{10,12},{12,14},{1,3},{3,5},{5,7},{... | collective-permute-start | bytes 1572872 | tf_op jit(solution)/shard_map/ppermute | solution.py:20
  7.8 22.7 %collective-permute-start.1 = (f32[4,2,64,256]{3,2,1,0:T(8,128)}, f32[4,2,64,256]{3,2,1,0:T(8,128)S(1)}, u32[]{:S(2)}, u32[]{:S(2)}) collective-permute-start(f32[4,2,64,256]{3,2,1,0:T(8,128)} %get-tuple-element.56), channel_id=1, source_target_pairs={{2,0},{4,2},{6,4},{8,6},{10,8},{12,10},{14,12},{3,1},{5,3},{7,5},{... | collective-permute-start | bytes 1572872 | tf_op jit(solution)/shard_map/ppermute | solution.py:20
  10.0 7.2 %copy-start = (f32[4,2,128,256]{3,2,1,0:T(8,128)S(1)}, f32[4,2,128,256]{3,2,1,0:T(8,128)}, u32[]{:S(2)}) copy-start(f32[4,2,128,256]{3,2,1,0:T(8,128)} %own.1) | copy-start | bytes 3145732
  17.2 13.4 %copy-start.2 = (bf16[8,256,256]{2,1,0:T(8,128)(2,1)}, bf16[8,256,256]{2,1,0:T(8,128)(2,1)S(1)}, u32[]{:S(2)}) copy-start(bf16[8,256,256]{2,1,0:T(8,128)(2,1)S(1)} %constant_dynamic-update-slice_fusion.tab) | copy-start | bytes 3145732
  17.2 13.6 %copy-start.15 = (s32[2,2]{1,0:T(2,128)S(1)}, s32[2,2]{1,0:T(2,128)}, u32[]{:S(2)}) copy-start(s32[2,2]{1,0:T(2,128)} %param.11) | copy-start | bytes 52
  30.5 3.0 %copy-start.3 = (f32[4,2,64,256]{3,2,1,0:T(8,128)}, f32[4,2,64,256]{3,2,1,0:T(8,128)S(1)}, u32[]{:S(2)}) copy-start(f32[4,2,64,256]{3,2,1,0:T(8,128)S(1)} %collective-permute-done.above) | copy-start | bytes 1572868
  30.6 2.9 %collective-permute-start.2 = (f32[4,2,256,128]{3,2,1,0:T(8,128)S(1)}, f32[4,2,256,128]{3,2,1,0:T(8,128)}, u32[]{:S(2)}, u32[]{:S(2)}) collective-permute-start(f32[4,2,256,128]{3,2,1,0:T(8,128)S(1)} %pad_maximum_fusion), channel_id=1, source_target_pairs={{0,1},{1,0},{2,3},{3,2},{4,5},{5,4},{6,7},{7,6},{8,9},{9,8},{10,11... | collective-permute-start | bytes 3145736 | tf_op jit(solution)/shard_map/ppermute | solution.py:25
  56.1 18.7 %copy-start.1 = (f32[4,2,256,256]{3,2,1,0:T(8,128)S(1)}, f32[4,2,256,256]{3,2,1,0:T(8,128)}, u32[]{:S(2)}) copy-start(f32[4,2,256,256]{3,2,1,0:T(8,128)} %get-tuple-element.23) | copy-start | bytes 6291460
  56.1 14.5 %collective-permute-start.3 = (f32[4,2,256,128]{3,2,1,0:T(8,128)}, f32[4,2,256,128]{3,2,1,0:T(8,128)S(1)}, u32[]{:S(2)}, u32[]{:S(2)}) collective-permute-start(f32[4,2,256,128]{3,2,1,0:T(8,128)} %get-tuple-element.24), channel_id=1, source_target_pairs={{0,1},{1,0},{2,3},{3,2},{4,5},{5,4},{6,7},{7,6},{8,9},{9,8},{10,11... | collective-permute-start | bytes 3145736 | tf_op jit(solution)/shard_map/ppermute | solution.py:25
  56.3 3.6 %collective-permute-start.4 = (f32[8,16,8,128]{3,2,1,0:T(8,128)}, f32[8,16,8,128]{3,2,1,0:T(8,128)}, u32[]{:S(2)}, u32[]{:S(2)}) collective-permute-start(f32[8,16,8,128]{3,2,1,0:T(8,128)} %get-tuple-element.26), channel_id=1, source_target_pairs={{0,1},{1,0},{2,3},{3,2},{4,5},{5,4},{6,7},{7,6},{8,9},{9,8},{10,11... | collective-permute-start | bytes 1572872 | tf_op jit(solution)/shard_map/ppermute | solution.py:25
  61.8 9.3 %collective-permute-start.5 = (f32[16,8,128]{2,1,0:T(8,128)S(1)}, f32[16,8,128]{2,1,0:T(8,128)S(1)}, u32[]{:S(2)}, u32[]{:S(2)}) collective-permute-start(f32[16,8,128]{2,1,0:T(8,128)S(1)} %get-tuple-element.48), channel_id=1, source_target_pairs={{0,2},{2,0},{4,6},{6,4},{8,10},{10,8},{12,14},{14,12},{1,3},{3,1},... | collective-permute-start | bytes 196616 | tf_op jit(solution)/shard_map/ppermute | solution.py:25
  64.2 7.7 %collective-permute-start.6 = (f32[16,8,128]{2,1,0:T(8,128)S(1)}, f32[16,8,128]{2,1,0:T(8,128)S(1)}, u32[]{:S(2)}, u32[]{:S(2)}) collective-permute-start(f32[16,8,128]{2,1,0:T(8,128)S(1)} %get-tuple-element.47), channel_id=1, source_target_pairs={{0,4},{2,6},{4,0},{6,2},{8,12},{10,14},{12,8},{14,10},{1,5},{3,7},... | collective-permute-start | bytes 196616 | tf_op jit(solution)/shard_map/ppermute | solution.py:25
  65.7 10.2 %collective-permute-start.7 = (f32[16,8,128]{2,1,0:T(8,128)S(1)}, f32[16,8,128]{2,1,0:T(8,128)S(1)}, u32[]{:S(2)}, u32[]{:S(2)}) collective-permute-start(f32[16,8,128]{2,1,0:T(8,128)S(1)} %get-tuple-element.46), channel_id=1, source_target_pairs={{0,6},{2,4},{4,2},{6,0},{8,14},{10,12},{12,10},{14,8},{1,7},{3,5},... | collective-permute-start | bytes 196616 | tf_op jit(solution)/shard_map/ppermute | solution.py:25
  66.6 9.3 %collective-permute-start.8 = (f32[16,8,128]{2,1,0:T(8,128)S(1)}, f32[16,8,128]{2,1,0:T(8,128)S(1)}, u32[]{:S(2)}, u32[]{:S(2)}) collective-permute-start(f32[16,8,128]{2,1,0:T(8,128)S(1)} %get-tuple-element.45), channel_id=1, source_target_pairs={{0,12},{2,14},{4,8},{6,10},{8,4},{10,6},{12,0},{14,2},{1,13},{3,15... | collective-permute-start | bytes 196616 | tf_op jit(solution)/shard_map/ppermute | solution.py:25
  70.6 5.2 %copy-start.5 = (f32[4,2,256,128]{3,2,1,0:T(8,128)}, f32[4,2,256,128]{3,2,1,0:T(8,128)S(1)}, u32[]{:S(2)}) copy-start(f32[4,2,256,128]{3,2,1,0:T(8,128)S(1)} %collective-permute-done.3) | copy-start | bytes 3145732
  70.6 7.5 %collective-permute-start.9 = (f32[16,8,128]{2,1,0:T(8,128)S(1)}, f32[16,8,128]{2,1,0:T(8,128)S(1)}, u32[]{:S(2)}, u32[]{:S(2)}) collective-permute-start(f32[16,8,128]{2,1,0:T(8,128)S(1)} %get-tuple-element.44), channel_id=1, source_target_pairs={{0,14},{2,12},{4,10},{6,8},{8,6},{10,4},{12,2},{14,0},{1,15},{3,13... | collective-permute-start | bytes 196616 | tf_op jit(solution)/shard_map/ppermute | solution.py:25
  71.1 11.2 %copy-start.7 = (f32[16,8,128]{2,1,0:T(8,128)}, f32[16,8,128]{2,1,0:T(8,128)S(1)}, u32[]{:S(2)}) copy-start(f32[16,8,128]{2,1,0:T(8,128)S(1)} %collective-permute-done.5.refs_2_) | copy-start | bytes 196612
  71.1 10.6 %collective-permute-start.12 = (f32[16,8,128]{2,1,0:T(8,128)S(1)}, f32[16,8,128]{2,1,0:T(8,128)S(1)}, u32[]{:S(2)}, u32[]{:S(2)}) collective-permute-start(f32[16,8,128]{2,1,0:T(8,128)S(1)} %get-tuple-element.43), channel_id=1, source_target_pairs={{0,8},{2,10},{4,12},{6,14},{8,0},{10,2},{12,4},{14,6},{1,9},{3,11}... | collective-permute-start | bytes 196616 | tf_op jit(solution)/shard_map/ppermute | solution.py:25
  71.9 10.4 %copy-start.8 = (f32[16,8,128]{2,1,0:T(8,128)}, f32[16,8,128]{2,1,0:T(8,128)S(1)}, u32[]{:S(2)}) copy-start(f32[16,8,128]{2,1,0:T(8,128)S(1)} %collective-permute-done.6.refs_3_) | copy-start | bytes 196612
  71.9 10.4 %collective-permute-start.13 = (f32[16,8,128]{2,1,0:T(8,128)S(1)}, f32[16,8,128]{2,1,0:T(8,128)}, u32[]{:S(2)}, u32[]{:S(2)}) collective-permute-start(f32[16,8,128]{2,1,0:T(8,128)S(1)} %get-tuple-element.42), channel_id=1, source_target_pairs={{0,10},{2,8},{4,14},{6,12},{8,2},{10,0},{12,6},{14,4},{1,11},{3,9}... | collective-permute-start | bytes 196616 | tf_op jit(solution)/shard_map/ppermute | solution.py:25
  75.9 6.4 %copy-start.9 = (f32[16,8,128]{2,1,0:T(8,128)}, f32[16,8,128]{2,1,0:T(8,128)S(1)}, u32[]{:S(2)}) copy-start(f32[16,8,128]{2,1,0:T(8,128)S(1)} %collective-permute-done.7.refs_4_) | copy-start | bytes 196612
  75.9 6.4 %copy-start.10 = (f32[16,8,128]{2,1,0:T(8,128)}, f32[16,8,128]{2,1,0:T(8,128)S(1)}, u32[]{:S(2)}) copy-start(f32[16,8,128]{2,1,0:T(8,128)S(1)} %collective-permute-done.8.refs_5_) | copy-start | bytes 196612
  78.1 4.2 %copy-start.11 = (f32[16,8,128]{2,1,0:T(8,128)}, f32[16,8,128]{2,1,0:T(8,128)S(1)}, u32[]{:S(2)}) copy-start(f32[16,8,128]{2,1,0:T(8,128)S(1)} %collective-permute-done.9.refs_6_) | copy-start | bytes 196612
  78.1 27.7 %collective-permute-start.10 = (f32[4,2,64,256]{3,2,1,0:T(8,128)}, f32[4,2,64,256]{3,2,1,0:T(8,128)}, u32[]{:S(2)}, u32[]{:S(2)}) collective-permute-start(f32[4,2,64,256]{3,2,1,0:T(8,128)} %get-tuple-element.27), channel_id=1, source_target_pairs={{0,2},{2,4},{4,6},{6,8},{8,10},{10,12},{12,14},{1,3},{3,5},{5,7},{... | collective-permute-start | bytes 1572872 | tf_op jit(solution)/shard_map/ppermute | solution.py:20
  80.4 25.5 %collective-permute-start.11 = (f32[4,2,64,256]{3,2,1,0:T(8,128)}, f32[4,2,64,256]{3,2,1,0:T(8,128)}, u32[]{:S(2)}, u32[]{:S(2)}) collective-permute-start(f32[4,2,64,256]{3,2,1,0:T(8,128)} %get-tuple-element.28), channel_id=1, source_target_pairs={{2,0},{4,2},{6,4},{8,6},{10,8},{12,10},{14,12},{3,1},{5,3},{7,5},{... | collective-permute-start | bytes 1572872 | tf_op jit(solution)/shard_map/ppermute | solution.py:20
  84.4 1.4 %collective-permute-start.14 = (f32[32,32]{1,0:T(8,128)}, f32[32,32]{1,0:T(8,128)S(1)}, u32[]{:S(2)}, u32[]{:S(2)}) collective-permute-start(f32[32,32]{1,0:T(8,128)} %get-tuple-element.36), channel_id=1, source_target_pairs={{0,1},{1,0},{2,3},{3,2},{4,5},{5,4},{6,7},{7,6},{8,9},{9,8},{10,11... | collective-permute-start | bytes 12296 | tf_op jit(solution)/shard_map/ppermute | solution.py:25
  86.5 8.2 %collective-permute-start.15 = (f32[32,32]{1,0:T(8,128)S(1)}, f32[32,32]{1,0:T(8,128)S(1)}, u32[]{:S(2)}, u32[]{:S(2)}) collective-permute-start(f32[32,32]{1,0:T(8,128)S(1)} %add.163), channel_id=1, source_target_pairs={{0,4},{2,6},{4,0},{6,2},{8,12},{10,14},{12,8},{14,10},{1,5},{3,7},... | collective-permute-start | bytes 12296 | tf_op jit(solution)/shard_map/ppermute | solution.py:25
  91.3 4.7 %collective-permute-start.16 = (f32[32,32]{1,0:T(8,128)S(1)}, f32[32,32]{1,0:T(8,128)S(1)}, u32[]{:S(2)}, u32[]{:S(2)}) collective-permute-start(f32[32,32]{1,0:T(8,128)S(1)} %add.163), channel_id=1, source_target_pairs={{0,8},{2,10},{4,12},{6,14},{8,0},{10,2},{12,4},{14,6},{1,9},{3,11}... | collective-permute-start | bytes 12296 | tf_op jit(solution)/shard_map/ppermute | solution.py:25
  93.0 5.5 %collective-permute-start.17 = (f32[32,32]{1,0:T(8,128)S(1)}, f32[32,32]{1,0:T(8,128)S(1)}, u32[]{:S(2)}, u32[]{:S(2)}) collective-permute-start(f32[32,32]{1,0:T(8,128)S(1)} %add.163), channel_id=1, source_target_pairs={{0,12},{2,14},{4,8},{6,10},{8,4},{10,6},{12,0},{14,2},{1,13},{3,15... | collective-permute-start | bytes 12296 | tf_op jit(solution)/shard_map/ppermute | solution.py:25
  98.5 3.8 %copy-start.6 = (f32[32,32]{1,0:T(8,128)}, f32[32,32]{1,0:T(8,128)S(1)}, u32[]{:S(2)}) copy-start(f32[32,32]{1,0:T(8,128)S(1)} %add_add_fusion.refs_0_) | copy-start | bytes 12292
  98.5 3.8 %collective-permute-start.18 = (f32[32,32]{1,0:T(8,128)S(1)}, f32[32,32]{1,0:T(8,128)S(1)}, u32[]{:S(2)}, u32[]{:S(2)}) collective-permute-start(f32[32,32]{1,0:T(8,128)S(1)} %add_add_fusion.refs_0_), channel_id=1, source_target_pairs={{0,2},{2,0},{4,6},{6,4},{8,10},{10,8},{12,14},{14,12},{1,3},{3,1},... | collective-permute-start | bytes 12296 | tf_op jit(solution)/shard_map/ppermute | solution.py:25
  (3 other events, 4.2 us)

commit v11 on v10

--- a/solution.py
+++ b/solution.py
@@ -406,8 +406,8 @@
             grad = take(grad, mine, 0) + swapped(take(grad, 1 - mine, 0), "row", bit)
         parts = [grad.reshape(2 * modes, share, width)]
 
-    late = parts[4:6]
-    early, bottom, top = lax.optimization_barrier((parts[:4] + parts[6:], bottom, top))
+    late = parts[3:6]
+    early, bottom, top = lax.optimization_barrier((parts[:3] + parts[6:], bottom, top))
     parts = early + late
     from_above = shifted(bottom, "row", 1)
     from_below = shifted(top, "row", -1)

time: 109 us -> 109 us (level)
  waiting for transfers between devices: 28.9 us -> 27.4 us
    ppermute x4, starting transfers between devices: 9.72 us -> 12.8 us  [shifted(): return lax.ppermute(value, axis, pairs)]
    ppermute x15, starting transfers between devices: 21.8 us -> 19.7 us  [swapped(): return lax.ppermute(value, axis, [(i, i ^ bit) for i in range(count)])]
    ppermute x15, waiting for transfers between devices: 15.8 us -> 14.3 us  [swapped(): return lax.ppermute(value, axis, [(i, i ^ bit) for i in range(count)])]
  transfers between devices with their start and end apart: 19 -> 19, of which waited for: 10 -> 7; matrix products, arithmetic and copies ran while one was open for 13% -> 13% of each run, Pallas kernels for 5% -> 5%
where the time goes in v11:
time: 109 us; the launch traced here: 108 us
  starting transfers between devices  32.5 us (30%)
  Pallas kernels  27.5 us (25%)
  waiting for transfers between devices  27.4 us (25%)
  local copies, waits for them, and re-layouts  10.1 us (9%)
  other arithmetic  9.63 us (9%)
    pallas_call x1, Pallas kernels, fields(): pl.pallas_call(field_kernel, out_shape=[jax.ShapeDtypeStruct(s, F32) for...  22.6 us
    ppermute x15, starting transfers between devices, swapped(): return lax.ppermute(value, axis, [(i, i ^ bit) for i in range(count)])  19.7 us
    ppermute x15, waiting for transfers between devices, swapped(): return lax.ppermute(value, axis, [(i, i ^ bit) for i in range(count)])  14.3 us
    ppermute x4, waiting for transfers between devices, shifted(): return lax.ppermute(value, axis, pairs)  13.2 us
    ppermute x4, starting transfers between devices, shifted(): return lax.ppermute(value, axis, pairs)  12.8 us
    unnamed x37, local copies, waits for them, and re-layouts  4.02 us
    pallas_call x1, Pallas kernels, ortho(): pl.pallas_call(body, out_shape=jax.ShapeDtypeStruct((modes, 2, pixels), F...  2.92 us
    add x1, other arithmetic, updates(): object_grad = middle() + jnp.concatenate([from_above, from_below], axis=2)  2.34 us
  transfers between devices with their start and end apart: 19, of which 7 were waited for; matrix products, arithmetic and copies ran while one was open for 13% of the time, Pallas kernels for 5%

profile of v11, /device:TPU:0, one launch (start us, length us, event | category | flops | bytes accessed | tf_op | source)
XLA Modules:
  0.0 108.2 jit_solution(3641865429687474405)
XLA Ops:
  0.6 2.3 %fusion.5 = (f32[4,2,64,256]{3,2,1,0:T(8,128)}, f32[4,2,64,256]{3,2,1,0:T(8,128)}) fusion(f32[4,2,128,256]{3,2,1,0:T(8,128)} %own.1), kind=kLoop, calls=%fused_computation.51 | loop fusion | bytes 2097152 | tf_op jit(solution)/shard_map/slice | solution.py:437
  2.9 4.9 %collective-permute-start = (f32[4,2,64,256]{3,2,1,0:T(8,128)}, f32[4,2,64,256]{3,2,1,0:T(8,128)S(1)}, u32[]{:S(2)}, u32[]{:S(2)}) collective-permute-start(f32[4,2,64,256]{3,2,1,0:T(8,128)} %get-tuple-element.55), channel_id=1, source_target_pairs={{0,2},{2,4},{4,6},{6,8},{8,10},{10,12},{12,14},{1,3},{3,5},{5,7},{... | collective-permute-start | bytes 1572872 | tf_op jit(solution)/shard_map/ppermute | solution.py:20
  7.8 1.3 %collective-permute-start.1 = (f32[4,2,64,256]{3,2,1,0:T(8,128)}, f32[4,2,64,256]{3,2,1,0:T(8,128)S(1)}, u32[]{:S(2)}, u32[]{:S(2)}) collective-permute-start(f32[4,2,64,256]{3,2,1,0:T(8,128)} %get-tuple-element.54), channel_id=1, source_target_pairs={{2,0},{4,2},{6,4},{8,6},{10,8},{12,10},{14,12},{3,1},{5,3},{7,5},{... | collective-permute-start | bytes 1572872 | tf_op jit(solution)/shard_map/ppermute | solution.py:20
  11.0 1.0 copy.17
  12.1 0.9 constant_dynamic-update-slice_fusion.3
  15.4 0.9 constant_dynamic-update-slice_fusion.1
  16.3 0.9 constant_dynamic-update-slice_fusion.tab
  17.3 13.2 %collective-permute-done.above = f32[4,2,64,256]{3,2,1,0:T(8,128)S(1)} collective-permute-done((f32[4,2,64,256]{3,2,1,0:T(8,128)}, f32[4,2,64,256]{3,2,1,0:T(8,128)S(1)}, u32[]{:S(2)}, u32[]{:S(2)}) %collective-permute-start) | collective-permute-done | bytes 524320 | tf_op jit(solution)/shard_map/ppermute | solution.py:20
  31.4 2.1 %collective-permute-done.2.beside = f32[4,2,256,128]{3,2,1,0:T(8,128)} collective-permute-done((f32[4,2,256,128]{3,2,1,0:T(8,128)S(1)}, f32[4,2,256,128]{3,2,1,0:T(8,128)}, u32[]{:S(2)}, u32[]{:S(2)}) %collective-permute-start.2) | collective-permute-done | bytes 1048608 | tf_op jit(solution)/shard_map/ppermute | solution.py:25
  33.5 22.6 %fields.1 = (f32[4,2,256,256]{3,2,1,0:T(8,128)}, f32[4,2,256,128]{3,2,1,0:T(8,128)}, f32[8,16,8,128]{3,2,1,0:T(8,128)}, f32[8,16,8,128]{3,2,1,0:T(8,128)}) custom-call(s32[2,2]{1,0:T(2,128)} %broadcast_subtract_fusion.places, s32[1]{0:T(128)} %bitcast.2.side, f32[4,2,128,256]{3,2,1,0:T(8,128)} %own.1, f32[4,2,64,256]{3,2,1,0:T(8,128)} %copy-done.3, ...), custom_call_target="tpu_custom_call" | custom-call | tf_op jit(solution)/shard_map/fields/pallas_call | solution.py:246
  56.6 3.2 %collective-permute-done.4 = f32[8,16,8,128]{3,2,1,0:T(8,128)} collective-permute-done((f32[8,16,8,128]{3,2,1,0:T(8,128)}, f32[8,16,8,128]{3,2,1,0:T(8,128)}, u32[]{:S(2)}, u32[]{:S(2)}) %collective-permute-start.4) | collective-permute-done | bytes 524320 | tf_op jit(solution)/shard_map/ppermute | solution.py:25
  59.8 1.9 %add_bitcast_fusion = (f32[16,8,128]{2,1,0:T(8,128)S(1)}, f32[16,8,128]{2,1,0:T(8,128)S(1)}, f32[16,8,128]{2,1,0:T(8,128)S(1)}, f32[16,8,128]{2,1,0:T(8,128)S(1)...) fusion(f32[8,16,8,128]{3,2,1,0:T(8,128)} %collective-permute-don, ...), kind=kLoop, calls=%fused_computation.27 | loop fusion | flops 131072 | bytes 1572896 | tf_op jit(solution)/shard_map/add | solution.py:395
  61.7 2.4 %collective-permute-start.5 = (f32[16,8,128]{2,1,0:T(8,128)S(1)}, f32[16,8,128]{2,1,0:T(8,128)S(1)}, u32[]{:S(2)}, u32[]{:S(2)}) collective-permute-start(f32[16,8,128]{2,1,0:T(8,128)S(1)} %get-tuple-element.46), channel_id=1, source_target_pairs={{0,2},{2,0},{4,6},{6,4},{8,10},{10,8},{12,14},{14,12},{1,3},{3,1},... | collective-permute-start | bytes 196616 | tf_op jit(solution)/shard_map/ppermute | solution.py:25
  64.2 1.6 %collective-permute-start.6 = (f32[16,8,128]{2,1,0:T(8,128)S(1)}, f32[16,8,128]{2,1,0:T(8,128)S(1)}, u32[]{:S(2)}, u32[]{:S(2)}) collective-permute-start(f32[16,8,128]{2,1,0:T(8,128)S(1)} %get-tuple-element.45), channel_id=1, source_target_pairs={{0,4},{2,6},{4,0},{6,2},{8,12},{10,14},{12,8},{14,10},{1,5},{3,7},... | collective-permute-start | bytes 196616 | tf_op jit(solution)/shard_map/ppermute | solution.py:25
  65.7 2.5 %collective-permute-start.7 = (f32[16,8,128]{2,1,0:T(8,128)S(1)}, f32[16,8,128]{2,1,0:T(8,128)S(1)}, u32[]{:S(2)}, u32[]{:S(2)}) collective-permute-start(f32[16,8,128]{2,1,0:T(8,128)S(1)} %get-tuple-element.44), channel_id=1, source_target_pairs={{0,12},{2,14},{4,8},{6,10},{8,4},{10,6},{12,0},{14,2},{1,13},{3,15... | collective-permute-start | bytes 196616 | tf_op jit(solution)/shard_map/ppermute | solution.py:25
  68.3 2.2 %collective-permute-start.8 = (f32[16,8,128]{2,1,0:T(8,128)S(1)}, f32[16,8,128]{2,1,0:T(8,128)S(1)}, u32[]{:S(2)}, u32[]{:S(2)}) collective-permute-start(f32[16,8,128]{2,1,0:T(8,128)S(1)} %get-tuple-element.43), channel_id=1, source_target_pairs={{0,14},{2,12},{4,10},{6,8},{8,6},{10,4},{12,2},{14,0},{1,15},{3,13... | collective-permute-start | bytes 196616 | tf_op jit(solution)/shard_map/ppermute | solution.py:25
  70.6 3.1 %collective-permute-start.12 = (f32[16,8,128]{2,1,0:T(8,128)S(1)}, f32[16,8,128]{2,1,0:T(8,128)S(1)}, u32[]{:S(2)}, u32[]{:S(2)}) collective-permute-start(f32[16,8,128]{2,1,0:T(8,128)S(1)} %get-tuple-element.41), channel_id=1, source_target_pairs={{0,8},{2,10},{4,12},{6,14},{8,0},{10,2},{12,4},{14,6},{1,9},{3,11}... | collective-permute-start | bytes 196616 | tf_op jit(solution)/shard_map/ppermute | solution.py:25
  73.8 0.9 collective-permute-start.13
  74.7 1.1 %maximum_add_fusion.2 = (f32[4,2,64,256]{3,2,1,0:T(8,128)}, f32[4,2,64,256]{3,2,1,0:T(8,128)}) fusion(f32[4,2,64,128]{3,2,1,0:T(8,128)S(1)} %get-tuple-element.50, f32[4,2,64,128]{3,2,1,0:T(8,128)S(1)} %get-tuple-element.48, f32[4,2,256,256]{3,2,1,0:T(8,128)S(1)} %copy-done.1, f32[4,2,64,128]{3,2,1,0:T(8,128)S(1)} %get-tuple-element.49, ...), kind=kLoop, calls=%fused_computation.7 | loop fusion | flops 524288 | bytes 3145728 | tf_op jit(solution)/shard_map/add | solution.py:461
  75.9 1.3 %collective-permute-start.10 = (f32[4,2,64,256]{3,2,1,0:T(8,128)}, f32[4,2,64,256]{3,2,1,0:T(8,128)}, u32[]{:S(2)}, u32[]{:S(2)}) collective-permute-start(f32[4,2,64,256]{3,2,1,0:T(8,128)} %get-tuple-element.27), channel_id=1, source_target_pairs={{2,0},{4,2},{6,4},{8,6},{10,8},{12,10},{14,12},{3,1},{5,3},{7,5},{... | collective-permute-start | bytes 1572872 | tf_op jit(solution)/shard_map/ppermute | solution.py:20
  77.2 5.4 %collective-permute-start.9 = (f32[4,2,64,256]{3,2,1,0:T(8,128)}, f32[4,2,64,256]{3,2,1,0:T(8,128)}, u32[]{:S(2)}, u32[]{:S(2)}) collective-permute-start(f32[4,2,64,256]{3,2,1,0:T(8,128)} %get-tuple-element.26), channel_id=1, source_target_pairs={{0,2},{2,4},{4,6},{6,8},{8,10},{10,12},{12,14},{1,3},{3,5},{5,7},{... | collective-permute-start | bytes 1572872 | tf_op jit(solution)/shard_map/ppermute | solution.py:20
  83.2 2.1 %gram.1 = (f32[32,32]{1,0:T(8,128)}, f32[16,8,128]{2,1,0:T(8,128)}) custom-call(f32[16,8,128]{2,1,0:T(8,128)} %bitcast.48, f32[16,8,128]{2,1,0:T(8,128)} %get-tuple-element.29.refs_1_, f32[16,8,128]{2,1,0:T(8,128)} %copy-done.7, f32[16,8,128]{2,1,0:T(8,128)} %copy-done.8, f32[16,8,128]{2,1,0:T(8,128)} %copy-done.9, f32[16,8,128]{2,1,0:T(8,128)} %copy-done.10, ...), custom_call_target="tpu_custom_call" | custom-call | tf_op jit(solution)/shard_map/gram/pallas_call | solution.py:290
  85.3 1.4 %collective-permute-done.14 = f32[32,32]{1,0:T(8,128)S(1)} collective-permute-done((f32[32,32]{1,0:T(8,128)}, f32[32,32]{1,0:T(8,128)S(1)}, u32[]{:S(2)}, u32[]{:S(2)}) %collective-permute-start.14) | collective-permute-done | bytes 4128 | tf_op jit(solution)/shard_map/ppermute | solution.py:25
  87.4 2.2 %collective-permute-start.15 = (f32[32,32]{1,0:T(8,128)S(1)}, f32[32,32]{1,0:T(8,128)S(1)}, u32[]{:S(2)}, u32[]{:S(2)}) collective-permute-start(f32[32,32]{1,0:T(8,128)S(1)} %add.163), channel_id=1, source_target_pairs={{0,4},{2,6},{4,0},{6,2},{8,12},{10,14},{12,8},{14,10},{1,5},{3,7},... | collective-permute-start | bytes 12296 | tf_op jit(solution)/shard_map/ppermute | solution.py:25
  89.6 1.9 %collective-permute-start.16 = (f32[32,32]{1,0:T(8,128)S(1)}, f32[32,32]{1,0:T(8,128)S(1)}, u32[]{:S(2)}, u32[]{:S(2)}) collective-permute-start(f32[32,32]{1,0:T(8,128)S(1)} %add.163), channel_id=1, source_target_pairs={{0,8},{2,10},{4,12},{6,14},{8,0},{10,2},{12,4},{14,6},{1,9},{3,11}... | collective-permute-start | bytes 12296 | tf_op jit(solution)/shard_map/ppermute | solution.py:25
  91.5 1.5 %collective-permute-start.17 = (f32[32,32]{1,0:T(8,128)S(1)}, f32[32,32]{1,0:T(8,128)S(1)}, u32[]{:S(2)}, u32[]{:S(2)}) collective-permute-start(f32[32,32]{1,0:T(8,128)S(1)} %add.163), channel_id=1, source_target_pairs={{0,12},{2,14},{4,8},{6,10},{8,4},{10,6},{12,0},{14,2},{1,13},{3,15... | collective-permute-start | bytes 12296 | tf_op jit(solution)/shard_map/ppermute | solution.py:25
  92.9 1.3 %collective-permute-done.16 = f32[32,32]{1,0:T(8,128)S(1)} collective-permute-done((f32[32,32]{1,0:T(8,128)S(1)}, f32[32,32]{1,0:T(8,128)S(1)}, u32[]{:S(2)}, u32[]{:S(2)}) %collective-permute-start.16) | collective-permute-done | bytes 4128 | tf_op jit(solution)/shard_map/ppermute | solution.py:25
  94.2 2.8 %collective-permute-done.17 = f32[32,32]{1,0:T(8,128)S(1)} collective-permute-done((f32[32,32]{1,0:T(8,128)S(1)}, f32[32,32]{1,0:T(8,128)S(1)}, u32[]{:S(2)}, u32[]{:S(2)}) %collective-permute-start.17) | collective-permute-done | bytes 4128 | tf_op jit(solution)/shard_map/ppermute | solution.py:25
  97.7 1.1 %slice_select_fusion.1 = (f32[4,2,128,128]{3,2,1,0:T(8,128)S(1)}, f32[4,2,128,128]{3,2,1,0:T(8,128)S(1)}) fusion(f32[4,2,256,128]{3,2,1,0:T(8,128)} %copy-done.5, pred[]{:T(512)S(6)} %eq.30), kind=kLoop, calls=%fused_computation.9 | loop fusion | flops 262144 | bytes 1572865 | tf_op jit(solution)/shard_map/jit(_where)/select_n | solution.py:458
  98.9 3.4 %collective-permute-done.18.refs_1_ = f32[32,32]{1,0:T(8,128)S(1)} collective-permute-done((f32[32,32]{1,0:T(8,128)S(1)}, f32[32,32]{1,0:T(8,128)S(1)}, u32[]{:S(2)}, u32[]{:S(2)}) %collective-permute-start.18) | collective-permute-done | bytes 4128 | tf_op jit(solution)/shard_map/ppermute | solution.py:25
  102.9 2.9 %ortho.1 = f32[8,2,1024]{2,1,0:T(2,128)} custom-call(f32[32,32]{1,0:T(8,128)} %copy-done.6, f32[32,32]{1,0:T(8,128)} %copy-done.13, f32[16,8,128]{2,1,0:T(8,128)} %bitcast.49, f32[16,8,128]{2,1,0:T(8,128)} %get-tuple-element.35.refs_3_), custom_call_target="tpu_custom_call" | custom-call | tf_op jit(solution)/shard_map/ortho/pallas_call | solution.py:365
  105.9 2.3 %fusion = f32[4,2,128,256]{3,2,1,0:T(8,128)} fusion(f32[4,2,128,128]{3,2,1,0:T(8,128)S(1)} %get-tuple-element.53, f32[4,2,128,128]{3,2,1,0:T(8,128)S(1)} %get-tuple-element.52, f32[4,2,64,256]{3,2,1,0:T(8,128)} %collective-permute-done.10, f32[4,2,64,256]{3,2,1,0:T(8,128)} %collective-permute-done.9, f32[4,2,256,256]{3,2,1,0:T(8,128)S(1)} %copy-done.1), kind=kLoop, calls=%fused_computation.5 | loop fusion | flops 1048576 | bytes 4194304 | tf_op jit(solution)/shard_map/add | solution.py:425
  (74 shorter events, 8.5 us)
Async XLA Ops:
  0.6 8.5 %copy-start.14 = (f32[2,63]{1,0:T(2,128)S(1)}, f32[2,63]{1,0:T(2,128)}, u32[]{:S(2)}) copy-start(f32[2,63]{1,0:T(2,128)} %param.9) | copy-start | bytes 1516
  2.9 27.6 %collective-permute-start = (f32[4,2,64,256]{3,2,1,0:T(8,128)}, f32[4,2,64,256]{3,2,1,0:T(8,128)S(1)}, u32[]{:S(2)}, u32[]{:S(2)}) collective-permute-start(f32[4,2,64,256]{3,2,1,0:T(8,128)} %get-tuple-element.55), channel_id=1, source_target_pairs={{0,2},{2,4},{4,6},{6,8},{8,10},{10,12},{12,14},{1,3},{3,5},{5,7},{... | collective-permute-start | bytes 1572872 | tf_op jit(solution)/shard_map/ppermute | solution.py:20
  7.8 22.7 %collective-permute-start.1 = (f32[4,2,64,256]{3,2,1,0:T(8,128)}, f32[4,2,64,256]{3,2,1,0:T(8,128)S(1)}, u32[]{:S(2)}, u32[]{:S(2)}) collective-permute-start(f32[4,2,64,256]{3,2,1,0:T(8,128)} %get-tuple-element.54), channel_id=1, source_target_pairs={{2,0},{4,2},{6,4},{8,6},{10,8},{12,10},{14,12},{3,1},{5,3},{7,5},{... | collective-permute-start | bytes 1572872 | tf_op jit(solution)/shard_map/ppermute | solution.py:20
  10.0 7.2 %copy-start = (f32[4,2,128,256]{3,2,1,0:T(8,128)S(1)}, f32[4,2,128,256]{3,2,1,0:T(8,128)}, u32[]{:S(2)}) copy-start(f32[4,2,128,256]{3,2,1,0:T(8,128)} %own.1) | copy-start | bytes 3145732
  17.2 13.4 %copy-start.2 = (bf16[8,256,256]{2,1,0:T(8,128)(2,1)}, bf16[8,256,256]{2,1,0:T(8,128)(2,1)S(1)}, u32[]{:S(2)}) copy-start(bf16[8,256,256]{2,1,0:T(8,128)(2,1)S(1)} %constant_dynamic-update-slice_fusion.tab) | copy-start | bytes 3145732
  17.2 13.6 %copy-start.15 = (s32[2,2]{1,0:T(2,128)S(1)}, s32[2,2]{1,0:T(2,128)}, u32[]{:S(2)}) copy-start(s32[2,2]{1,0:T(2,128)} %param.11) | copy-start | bytes 52
  30.5 3.0 %copy-start.3 = (f32[4,2,64,256]{3,2,1,0:T(8,128)}, f32[4,2,64,256]{3,2,1,0:T(8,128)S(1)}, u32[]{:S(2)}) copy-start(f32[4,2,64,256]{3,2,1,0:T(8,128)S(1)} %collective-permute-done.above) | copy-start | bytes 1572868
  30.5 3.0 %copy-start.4 = (f32[4,2,64,256]{3,2,1,0:T(8,128)}, f32[4,2,64,256]{3,2,1,0:T(8,128)S(1)}, u32[]{:S(2)}) copy-start(f32[4,2,64,256]{3,2,1,0:T(8,128)S(1)} %collective-permute-done.1.below) | copy-start | bytes 1572868
  30.6 2.9 %collective-permute-start.2 = (f32[4,2,256,128]{3,2,1,0:T(8,128)S(1)}, f32[4,2,256,128]{3,2,1,0:T(8,128)}, u32[]{:S(2)}, u32[]{:S(2)}) collective-permute-start(f32[4,2,256,128]{3,2,1,0:T(8,128)S(1)} %pad_maximum_fusion), channel_id=1, source_target_pairs={{0,1},{1,0},{2,3},{3,2},{4,5},{5,4},{6,7},{7,6},{8,9},{9,8},{10,11... | collective-permute-start | bytes 3145736 | tf_op jit(solution)/shard_map/ppermute | solution.py:25
  56.0 18.7 %copy-start.1 = (f32[4,2,256,256]{3,2,1,0:T(8,128)S(1)}, f32[4,2,256,256]{3,2,1,0:T(8,128)}, u32[]{:S(2)}) copy-start(f32[4,2,256,256]{3,2,1,0:T(8,128)} %get-tuple-element.22) | copy-start | bytes 6291460
  56.0 14.4 %collective-permute-start.3 = (f32[4,2,256,128]{3,2,1,0:T(8,128)}, f32[4,2,256,128]{3,2,1,0:T(8,128)S(1)}, u32[]{:S(2)}, u32[]{:S(2)}) collective-permute-start(f32[4,2,256,128]{3,2,1,0:T(8,128)} %get-tuple-element.23), channel_id=1, source_target_pairs={{0,1},{1,0},{2,3},{3,2},{4,5},{5,4},{6,7},{7,6},{8,9},{9,8},{10,11... | collective-permute-start | bytes 3145736 | tf_op jit(solution)/shard_map/ppermute | solution.py:25
  56.3 3.5 %collective-permute-start.4 = (f32[8,16,8,128]{3,2,1,0:T(8,128)}, f32[8,16,8,128]{3,2,1,0:T(8,128)}, u32[]{:S(2)}, u32[]{:S(2)}) collective-permute-start(f32[8,16,8,128]{3,2,1,0:T(8,128)} %get-tuple-element.25), channel_id=1, source_target_pairs={{0,1},{1,0},{2,3},{3,2},{4,5},{5,4},{6,7},{7,6},{8,9},{9,8},{10,11... | collective-permute-start | bytes 1572872 | tf_op jit(solution)/shard_map/ppermute | solution.py:25
  61.7 8.9 %collective-permute-start.5 = (f32[16,8,128]{2,1,0:T(8,128)S(1)}, f32[16,8,128]{2,1,0:T(8,128)S(1)}, u32[]{:S(2)}, u32[]{:S(2)}) collective-permute-start(f32[16,8,128]{2,1,0:T(8,128)S(1)} %get-tuple-element.46), channel_id=1, source_target_pairs={{0,2},{2,0},{4,6},{6,4},{8,10},{10,8},{12,14},{14,12},{1,3},{3,1},... | collective-permute-start | bytes 196616 | tf_op jit(solution)/shard_map/ppermute | solution.py:25
  64.2 9.6 %collective-permute-start.6 = (f32[16,8,128]{2,1,0:T(8,128)S(1)}, f32[16,8,128]{2,1,0:T(8,128)S(1)}, u32[]{:S(2)}, u32[]{:S(2)}) collective-permute-start(f32[16,8,128]{2,1,0:T(8,128)S(1)} %get-tuple-element.45), channel_id=1, source_target_pairs={{0,4},{2,6},{4,0},{6,2},{8,12},{10,14},{12,8},{14,10},{1,5},{3,7},... | collective-permute-start | bytes 196616 | tf_op jit(solution)/shard_map/ppermute | solution.py:25
  65.7 10.1 %collective-permute-start.7 = (f32[16,8,128]{2,1,0:T(8,128)S(1)}, f32[16,8,128]{2,1,0:T(8,128)S(1)}, u32[]{:S(2)}, u32[]{:S(2)}) collective-permute-start(f32[16,8,128]{2,1,0:T(8,128)S(1)} %get-tuple-element.44), channel_id=1, source_target_pairs={{0,12},{2,14},{4,8},{6,10},{8,4},{10,6},{12,0},{14,2},{1,13},{3,15... | collective-permute-start | bytes 196616 | tf_op jit(solution)/shard_map/ppermute | solution.py:25
  68.3 7.6 %collective-permute-start.8 = (f32[16,8,128]{2,1,0:T(8,128)S(1)}, f32[16,8,128]{2,1,0:T(8,128)S(1)}, u32[]{:S(2)}, u32[]{:S(2)}) collective-permute-start(f32[16,8,128]{2,1,0:T(8,128)S(1)} %get-tuple-element.43), channel_id=1, source_target_pairs={{0,14},{2,12},{4,10},{6,8},{8,6},{10,4},{12,2},{14,0},{1,15},{3,13... | collective-permute-start | bytes 196616 | tf_op jit(solution)/shard_map/ppermute | solution.py:25
  70.5 5.4 %copy-start.5 = (f32[4,2,256,128]{3,2,1,0:T(8,128)}, f32[4,2,256,128]{3,2,1,0:T(8,128)S(1)}, u32[]{:S(2)}) copy-start(f32[4,2,256,128]{3,2,1,0:T(8,128)S(1)} %collective-permute-done.3) | copy-start | bytes 3145732
  70.5 12.1 %collective-permute-start.11 = (f32[16,8,128]{2,1,0:T(8,128)S(1)}, f32[16,8,128]{2,1,0:T(8,128)S(1)}, u32[]{:S(2)}, u32[]{:S(2)}) collective-permute-start(f32[16,8,128]{2,1,0:T(8,128)S(1)} %get-tuple-element.42), channel_id=1, source_target_pairs={{0,6},{2,4},{4,2},{6,0},{8,14},{10,12},{12,10},{14,8},{1,7},{3,5},... | collective-permute-start | bytes 196616 | tf_op jit(solution)/shard_map/ppermute | solution.py:25
  70.6 12.0 %copy-start.7 = (f32[16,8,128]{2,1,0:T(8,128)}, f32[16,8,128]{2,1,0:T(8,128)S(1)}, u32[]{:S(2)}) copy-start(f32[16,8,128]{2,1,0:T(8,128)S(1)} %collective-permute-done.5.refs_2_) | copy-start | bytes 196612
  70.6 11.9 %collective-permute-start.12 = (f32[16,8,128]{2,1,0:T(8,128)S(1)}, f32[16,8,128]{2,1,0:T(8,128)S(1)}, u32[]{:S(2)}, u32[]{:S(2)}) collective-permute-start(f32[16,8,128]{2,1,0:T(8,128)S(1)} %get-tuple-element.41), channel_id=1, source_target_pairs={{0,8},{2,10},{4,12},{6,14},{8,0},{10,2},{12,4},{14,6},{1,9},{3,11}... | collective-permute-start | bytes 196616 | tf_op jit(solution)/shard_map/ppermute | solution.py:25
  73.8 8.8 %copy-start.8 = (f32[16,8,128]{2,1,0:T(8,128)}, f32[16,8,128]{2,1,0:T(8,128)S(1)}, u32[]{:S(2)}) copy-start(f32[16,8,128]{2,1,0:T(8,128)S(1)} %collective-permute-done.6.refs_3_) | copy-start | bytes 196612
  73.8 8.8 %collective-permute-start.13 = (f32[16,8,128]{2,1,0:T(8,128)S(1)}, f32[16,8,128]{2,1,0:T(8,128)}, u32[]{:S(2)}, u32[]{:S(2)}) collective-permute-start(f32[16,8,128]{2,1,0:T(8,128)S(1)} %get-tuple-element.40), channel_id=1, source_target_pairs={{0,10},{2,8},{4,14},{6,12},{8,2},{10,0},{12,6},{14,4},{1,11},{3,9}... | collective-permute-start | bytes 196616 | tf_op jit(solution)/shard_map/ppermute | solution.py:25
  75.9 6.7 %copy-start.9 = (f32[16,8,128]{2,1,0:T(8,128)}, f32[16,8,128]{2,1,0:T(8,128)S(1)}, u32[]{:S(2)}) copy-start(f32[16,8,128]{2,1,0:T(8,128)S(1)} %collective-permute-done.7.refs_4_) | copy-start | bytes 196612
  75.9 6.7 %copy-start.10 = (f32[16,8,128]{2,1,0:T(8,128)}, f32[16,8,128]{2,1,0:T(8,128)S(1)}, u32[]{:S(2)}) copy-start(f32[16,8,128]{2,1,0:T(8,128)S(1)} %collective-permute-done.8.refs_5_) | copy-start | bytes 196612
  75.9 30.0 %collective-permute-start.10 = (f32[4,2,64,256]{3,2,1,0:T(8,128)}, f32[4,2,64,256]{3,2,1,0:T(8,128)}, u32[]{:S(2)}, u32[]{:S(2)}) collective-permute-start(f32[4,2,64,256]{3,2,1,0:T(8,128)} %get-tuple-element.27), channel_id=1, source_target_pairs={{2,0},{4,2},{6,4},{8,6},{10,8},{12,10},{14,12},{3,1},{5,3},{7,5},{... | collective-permute-start | bytes 1572872 | tf_op jit(solution)/shard_map/ppermute | solution.py:20
  77.2 28.7 %collective-permute-start.9 = (f32[4,2,64,256]{3,2,1,0:T(8,128)}, f32[4,2,64,256]{3,2,1,0:T(8,128)}, u32[]{:S(2)}, u32[]{:S(2)}) collective-permute-start(f32[4,2,64,256]{3,2,1,0:T(8,128)} %get-tuple-element.26), channel_id=1, source_target_pairs={{0,2},{2,4},{4,6},{6,8},{8,10},{10,12},{12,14},{1,3},{3,5},{5,7},{... | collective-permute-start | bytes 1572872 | tf_op jit(solution)/shard_map/ppermute | solution.py:20
  85.3 1.4 %collective-permute-start.14 = (f32[32,32]{1,0:T(8,128)}, f32[32,32]{1,0:T(8,128)S(1)}, u32[]{:S(2)}, u32[]{:S(2)}) collective-permute-start(f32[32,32]{1,0:T(8,128)} %get-tuple-element.34), channel_id=1, source_target_pairs={{0,1},{1,0},{2,3},{3,2},{4,5},{5,4},{6,7},{7,6},{8,9},{9,8},{10,11... | collective-permute-start | bytes 12296 | tf_op jit(solution)/shard_map/ppermute | solution.py:25
  87.4 5.6 %collective-permute-start.15 = (f32[32,32]{1,0:T(8,128)S(1)}, f32[32,32]{1,0:T(8,128)S(1)}, u32[]{:S(2)}, u32[]{:S(2)}) collective-permute-start(f32[32,32]{1,0:T(8,128)S(1)} %add.163), channel_id=1, source_target_pairs={{0,4},{2,6},{4,0},{6,2},{8,12},{10,14},{12,8},{14,10},{1,5},{3,7},... | collective-permute-start | bytes 12296 | tf_op jit(solution)/shard_map/ppermute | solution.py:25
  89.6 4.6 %collective-permute-start.16 = (f32[32,32]{1,0:T(8,128)S(1)}, f32[32,32]{1,0:T(8,128)S(1)}, u32[]{:S(2)}, u32[]{:S(2)}) collective-permute-start(f32[32,32]{1,0:T(8,128)S(1)} %add.163), channel_id=1, source_target_pairs={{0,8},{2,10},{4,12},{6,14},{8,0},{10,2},{12,4},{14,6},{1,9},{3,11}... | collective-permute-start | bytes 12296 | tf_op jit(solution)/shard_map/ppermute | solution.py:25
  91.5 5.5 %collective-permute-start.17 = (f32[32,32]{1,0:T(8,128)S(1)}, f32[32,32]{1,0:T(8,128)S(1)}, u32[]{:S(2)}, u32[]{:S(2)}) collective-permute-start(f32[32,32]{1,0:T(8,128)S(1)} %add.163), channel_id=1, source_target_pairs={{0,12},{2,14},{4,8},{6,10},{8,4},{10,6},{12,0},{14,2},{1,13},{3,15... | collective-permute-start | bytes 12296 | tf_op jit(solution)/shard_map/ppermute | solution.py:25
  97.0 5.3 %copy-start.6 = (f32[32,32]{1,0:T(8,128)}, f32[32,32]{1,0:T(8,128)S(1)}, u32[]{:S(2)}) copy-start(f32[32,32]{1,0:T(8,128)S(1)} %add_add_fusion.refs_0_) | copy-start | bytes 12292
  97.0 5.3 %collective-permute-start.18 = (f32[32,32]{1,0:T(8,128)S(1)}, f32[32,32]{1,0:T(8,128)S(1)}, u32[]{:S(2)}, u32[]{:S(2)}) collective-permute-start(f32[32,32]{1,0:T(8,128)S(1)} %add_add_fusion.refs_0_), channel_id=1, source_target_pairs={{0,2},{2,0},{4,6},{6,4},{8,10},{10,8},{12,14},{14,12},{1,3},{3,1},... | collective-permute-start | bytes 12296 | tf_op jit(solution)/shard_map/ppermute | solution.py:25
  (3 other events, 1.9 us)
